TPU v7x, 32 devices: a whole 2x2x4 slice. The times are simulated.
32 devices in a mesh: pb: 8 (over y, x, core), pa: 4 (over z).
Axes of the slice: x: 2, y: 2, z: 4, core: 2. Of those that a mesh axis runs over, the one named last changes fastest.
Arguments:
- query_tokens: bfloat16 [128, 32, 768], P(('pb', 'pa')), may hold values from -6 to 6
- passage_tokens: bfloat16 [32, 1024, 768], P(('pb', 'pa')), may hold values from -6 to 6
- passage_lengths: int32 [32, 8], replicated, may hold values from 1 to 512, 1024 in all within a row
- positives: int32 [128], replicated, may hold values from 0 to 255
- qkv_weight: float32 [768, 2304], P(('pb', 'pa')), may hold values from -0.21875 to 0.21875
- qkv_first: float32 [768, 2304], P(('pb', 'pa')), may hold values from -4.7683716e-06 to 4.7683716e-06
- qkv_second: float32 [768, 2304], P(('pb', 'pa')), may hold values from 5.5668377e-14 to 2.2267351e-13
- out_weight: float32 [768, 768], P(('pb', 'pa')), may hold values from -0.875 to 0.875
- out_first: float32 [768, 768], P(('pb', 'pa')), may hold values from -4.7683716e-06 to 4.7683716e-06
- out_second: float32 [768, 768], P(('pb', 'pa')), may hold values from 5.5668377e-14 to 2.2267351e-13
- up_weight: float32 [768, 3072], P(('pb', 'pa')), may hold values from -0.21875 to 0.21875
- up_first: float32 [768, 3072], P(('pb', 'pa')), may hold values from -4.7683716e-06 to 4.7683716e-06
- up_second: float32 [768, 3072], P(('pb', 'pa')), may hold values from 5.5668377e-14 to 2.2267351e-13
- down_weight: float32 [3072, 768], P(('pb', 'pa')), may hold values from -0.109375 to 0.109375
- down_first: float32 [3072, 768], P(('pb', 'pa')), may hold values from -4.7683716e-06 to 4.7683716e-06
- down_second: float32 [3072, 768], P(('pb', 'pa')), may hold values from 5.5668377e-14 to 2.2267351e-13
- proj_weight: float32 [768, 128], P(('pb', 'pa')), may hold values from -0.21875 to 0.21875
- proj_first: float32 [768, 128], P(('pb', 'pa')), may hold values from -4.7683716e-06 to 4.7683716e-06
- proj_second: float32 [768, 128], P(('pb', 'pa')), may hold values from 5.5668377e-14 to 2.2267351e-13
- vector_params: float32 [12, 768], P(None, ('pb', 'pa')), may hold values from -1.2 to 1.4, as said below
- vector_first: float32 [12, 768], P(None, ('pb', 'pa')), may hold values from -1.9073486e-05 to 1.9073486e-05
- vector_second: float32 [12, 768], P(None, ('pb', 'pa')), may hold values from 8.9069404e-13 to 3.5627762e-12
Outputs:
- grad_norm: float32 [], replicated
- qkv_next: float32 [768, 2304], P(('pb', 'pa'))
- qkv_first_next: float32 [768, 2304], P(('pb', 'pa'))
- qkv_second_next: float32 [768, 2304], P(('pb', 'pa'))
- out_next: float32 [768, 768], P(('pb', 'pa'))
- out_first_next: float32 [768, 768], P(('pb', 'pa'))
- out_second_next: float32 [768, 768], P(('pb', 'pa'))
- up_next: float32 [768, 3072], P(('pb', 'pa'))
- up_first_next: float32 [768, 3072], P(('pb', 'pa'))
- up_second_next: float32 [768, 3072], P(('pb', 'pa'))
- down_next: float32 [3072, 768], P(('pb', 'pa'))
- down_first_next: float32 [3072, 768], P(('pb', 'pa'))
- down_second_next: float32 [3072, 768], P(('pb', 'pa'))
- proj_next: float32 [768, 128], P(('pb', 'pa'))
- proj_first_next: float32 [768, 128], P(('pb', 'pa'))
- proj_second_next: float32 [768, 128], P(('pb', 'pa'))
- vector_next: float32 [12, 768], P(None, ('pb', 'pa'))
- vector_first_next: float32 [12, 768], P(None, ('pb', 'pa'))
- vector_second_next: float32 [12, 768], P(None, ('pb', 'pa'))
Inputs may be any that keep to these rules, and one draw needn't show every extreme that they name: `passage_lengths`: each row sums to 1024; one passage of each row is the longest. `positives`: any passage id. `vector_params`: rows 3 and 10 are gains between 0.6 and 1.4, the other rows biases of both signs.
All inputs are finite; a program needn't handle non-finite values.
Results may differ from a plain program's by a relative error of at most 0.0093.
Values may be sent and summed in bfloat16 or wider, within the bound.
No kernel may reach another device: no remote copies, remote signals or barrier semaphores. Data moves between devices by JAX's collectives and lax.ppermute only.
A program may use at most 320 MiB of HBM per device.

v0:
```python
import math

import jax
import jax.numpy as jnp
from jax import lax
from jax.sharding import PartitionSpec as P

D = 768
HEAD_DIM = 64
QLEN = 32
BIN = 1024
PPB = 8
STEP = 10
QPD = 4


full_accuracy_flag = lax.Precision.HIGHEST
sharpness_divisor = 0.1
clip_max = 0.02
learn_rate = 0.04
vector_rate = 0.4
beta_one = 0.9
beta_two = 0.999
adam_eps = 1e-08
decay_rate = 0.01
norm_eps = 1e-12


def merged(part, axis, combine):
    gathered = jax.tree.map(lambda a: lax.all_gather(a, axis), part)

    def take(source):
        return jax.tree.map(lambda a: lax.dynamic_index_in_dim(a, source, 0, False), gathered)

    return lax.fori_loop(
        1, lax.axis_size(axis), lambda source, state: combine(state, take(source)), take(0)
    )


def layer_norm(hidden, gain, shift):
    centred = hidden - jnp.mean(hidden, -1, keepdims=True)
    spread = jnp.mean(centred * centred, -1, keepdims=True)
    return centred * lax.rsqrt(spread + norm_eps) * gain + shift


def normalize(projected):
    return projected * lax.rsqrt(jnp.sum(projected * projected, -1, keepdims=True) + 1e-06)


def exact_gelu(value):
    return jax.nn.gelu(value, approximate=False)


def segment_table(lengths_row, span):
    ends = jnp.cumsum(lengths_row)
    places = jnp.arange(span, dtype=jnp.int32)
    segment = jnp.sum((places[:, None] >= ends[None, :]).astype(jnp.int32), 1)
    belonging_mask = (
        segment[:, None] == jnp.arange(lengths_row.shape[0], dtype=jnp.int32)[None, :]
    ).astype(jnp.float32)
    return (segment, belonging_mask)


def attend_forward(query, keys, values, segment):
    token_count = query.shape[0]
    block_rows = min(token_count, 512)
    scaling = HEAD_DIM ** (-0.5)

    def one_block(block_index):
        offset = block_index * block_rows
        block_query = lax.dynamic_slice_in_dim(query, offset, block_rows, 0)
        block_seg = lax.dynamic_slice_in_dim(segment, offset, block_rows, 0)
        raw_scores = jnp.einsum(
            "qhd,khd->hqk", block_query, keys, preferred_element_type=jnp.float32
        )
        logits = jnp.where(
            (block_seg[:, None] == segment[None, :])[None], raw_scores * scaling, -1e30
        )
        highest = jnp.max(logits, -1, keepdims=True)
        exponential_terms = jnp.exp(logits - highest)
        denominator = jnp.sum(exponential_terms, -1, keepdims=True)
        attention = (exponential_terms / denominator).astype(jnp.bfloat16)
        result = jnp.einsum("hqk,khd->qhd", attention, values, preferred_element_type=jnp.float32)
        return (result, highest[..., 0] + jnp.log(denominator[..., 0]))

    results, log_total = lax.map(one_block, jnp.arange(token_count // block_rows))
    return (results.reshape(token_count, -1), log_total)


def attend_backward(query, keys, values, segment, log_total, grad_out):
    token_count = query.shape[0]
    block_rows = min(token_count, 512)
    scaling = HEAD_DIM ** (-0.5)

    def one_block(running, block_index):
        grad_keys, grad_values = running
        offset = block_index * block_rows
        block_query = lax.dynamic_slice_in_dim(query, offset, block_rows, 0)
        block_seg = lax.dynamic_slice_in_dim(segment, offset, block_rows, 0)
        block_grad = lax.dynamic_slice_in_dim(grad_out, offset, block_rows, 0)
        block_total = lax.dynamic_index_in_dim(log_total, block_index, 0, keepdims=False)
        raw_scores = jnp.einsum(
            "qhd,khd->hqk", block_query, keys, preferred_element_type=jnp.float32
        )
        logits = jnp.where(
            (block_seg[:, None] == segment[None, :])[None], raw_scores * scaling, -1e30
        )
        attention = jnp.exp(logits - block_total[..., None])
        grad_values = grad_values + jnp.einsum(
            "hqk,qhd->khd",
            attention.astype(jnp.bfloat16),
            block_grad,
            preferred_element_type=jnp.float32,
        )
        grad_attention = jnp.einsum(
            "qhd,khd->hqk", block_grad, values, preferred_element_type=jnp.float32
        )
        row_dot = jnp.sum(attention * grad_attention, -1, keepdims=True)
        grad_raw = (attention * (grad_attention - row_dot) * scaling).astype(jnp.bfloat16)
        block_dquery = jnp.einsum(
            "hqk,khd->qhd", grad_raw, keys, preferred_element_type=jnp.float32
        )
        grad_keys = grad_keys + jnp.einsum(
            "hqk,qhd->khd", grad_raw, block_query, preferred_element_type=jnp.float32
        )
        return ((grad_keys, grad_values), block_dquery)

    empty_sum = jnp.zeros(keys.shape, jnp.float32)
    finals, grad_query = lax.scan(
        one_block, (empty_sum, empty_sum), jnp.arange(token_count // block_rows)
    )
    return (grad_query.reshape(query.shape), finals[0], finals[1])


def encode_forward(tokens, segment, weights):
    qkv_matrix, out_matrix, up_matrix, down_matrix, proj_matrix, vectors = weights
    token_count = tokens.shape[0]
    bias_qkv = jnp.concatenate([vectors[0], jnp.zeros_like(vectors[0]), vectors[1]])
    mixed = (jnp.dot(tokens, qkv_matrix, preferred_element_type=jnp.float32) + bias_qkv).astype(
        jnp.bfloat16
    )
    split_heads = mixed.reshape(token_count, 3, D // HEAD_DIM, HEAD_DIM)
    attended, log_total = attend_forward(
        split_heads[:, 0], split_heads[:, 1], split_heads[:, 2], segment
    )
    attended_low = attended.astype(jnp.bfloat16)
    resid_one = (
        tokens.astype(jnp.float32)
        + jnp.dot(attended_low, out_matrix, preferred_element_type=jnp.float32)
        + vectors[2]
    )
    normed_one = layer_norm(resid_one, vectors[3], vectors[4])
    normed_low = normed_one.astype(jnp.bfloat16)
    hidden = jnp.dot(normed_low, up_matrix, preferred_element_type=jnp.float32) + vectors[
        5:9
    ].reshape(-1)
    activated = exact_gelu(hidden).astype(jnp.bfloat16)
    resid_two = (
        normed_one
        + jnp.dot(activated, down_matrix, preferred_element_type=jnp.float32)
        + vectors[9]
    )
    normed_two = layer_norm(resid_two, vectors[10], vectors[11])
    normed_out = normed_two.astype(jnp.bfloat16)
    projected = jnp.dot(normed_out, proj_matrix, preferred_element_type=jnp.float32)
    kept = (
        mixed,
        log_total,
        attended_low,
        resid_one,
        normed_low,
        hidden,
        activated,
        resid_two,
        normed_out,
        projected,
    )
    return (normalize(projected).astype(jnp.bfloat16), kept)


def encode_backward(tokens, segment, weights, kept, grad_unit):
    qkv_matrix, out_matrix, up_matrix, down_matrix, proj_matrix, vectors = weights
    (
        mixed,
        log_total,
        attended_low,
        resid_one,
        normed_low,
        hidden,
        activated,
        resid_two,
        normed_out,
        projected,
    ) = kept
    token_count = tokens.shape[0]
    grad_proj = jax.vjp(normalize, projected)[1](grad_unit)[0].astype(jnp.bfloat16)
    proj_grad = jnp.dot(normed_out.T, grad_proj, preferred_element_type=jnp.float32)
    grad_normed = jnp.dot(grad_proj, proj_matrix.T, preferred_element_type=jnp.float32)
    grad_resid_two, gain_two, shift_two = jax.vjp(layer_norm, resid_two, vectors[10], vectors[11])[
        1
    ](grad_normed)
    grad_two_low = grad_resid_two.astype(jnp.bfloat16)
    down_grad = jnp.dot(activated.T, grad_two_low, preferred_element_type=jnp.float32)
    grad_activated = jnp.dot(grad_two_low, down_matrix.T, preferred_element_type=jnp.float32)
    grad_hidden = jax.vjp(exact_gelu, hidden)[1](grad_activated)[0]
    grad_hidden_low = grad_hidden.astype(jnp.bfloat16)
    up_grad = jnp.dot(normed_low.T, grad_hidden_low, preferred_element_type=jnp.float32)
    grad_normed_one = grad_resid_two + jnp.dot(
        grad_hidden_low, up_matrix.T, preferred_element_type=jnp.float32
    )
    grad_resid_one, gain_one, shift_one = jax.vjp(layer_norm, resid_one, vectors[3], vectors[4])[1](
        grad_normed_one
    )
    grad_one_low = grad_resid_one.astype(jnp.bfloat16)
    out_grad = jnp.dot(attended_low.T, grad_one_low, preferred_element_type=jnp.float32)
    grad_attended = jnp.dot(grad_one_low, out_matrix.T, preferred_element_type=jnp.float32).astype(
        jnp.bfloat16
    )
    split_heads = mixed.reshape(token_count, 3, D // HEAD_DIM, HEAD_DIM)
    grad_query, grad_keys, grad_values = attend_backward(
        split_heads[:, 0],
        split_heads[:, 1],
        split_heads[:, 2],
        segment,
        log_total,
        grad_attended.reshape(token_count, D // HEAD_DIM, HEAD_DIM),
    )
    grad_mixed = jnp.stack([grad_query, grad_keys, grad_values], 1).reshape(token_count, 3 * D)
    qkv_grad = jnp.dot(
        tokens.T, grad_mixed.astype(jnp.bfloat16), preferred_element_type=jnp.float32
    )
    vector_grad = jnp.concatenate(
        [
            jnp.sum(grad_query, 0).reshape(1, D),
            jnp.sum(grad_values, 0).reshape(1, D),
            jnp.sum(grad_resid_one, 0)[None],
            gain_one[None],
            shift_one[None],
            jnp.sum(grad_hidden, 0).reshape(4, D),
            jnp.sum(grad_resid_two, 0)[None],
            gain_two[None],
            shift_two[None],
        ],
        0,
    )
    return (qkv_grad, out_grad, up_grad, down_grad, proj_grad, vector_grad)


def block_size(query_rows, passage_rows):
    per_block = math.gcd(query_rows // QLEN, max(1, 8388608 // (passage_rows * QLEN)))
    return per_block * QLEN


def score_forward(query_unit, passage_normalized, belonging_mask):
    block_rows = block_size(query_unit.shape[0], passage_normalized.shape[0])
    bin_count, bin_span, per_bin = belonging_mask.shape

    def one_block(block_index):
        query_block = lax.dynamic_slice_in_dim(query_unit, block_index * block_rows, block_rows, 0)
        angle_agreement = jnp.einsum(
            "re,te->rt", query_block, passage_normalized, preferred_element_type=jnp.float32
        )
        exponential_terms = jnp.exp((angle_agreement - 1.0) / sharpness_divisor).reshape(
            block_rows, bin_count, bin_span
        )
        accumulated_sums = jnp.einsum(
            "rbt,btp->rbp", exponential_terms, belonging_mask, precision=full_accuracy_flag
        ).reshape(block_rows, bin_count * per_bin)
        smoothed_maximum = sharpness_divisor * jnp.log(accumulated_sums) + 1.0
        return (
            jnp.sum(smoothed_maximum.reshape(block_rows // QLEN, QLEN, -1), 1),
            accumulated_sums,
        )

    scores, accumulated_sums = lax.map(one_block, jnp.arange(query_unit.shape[0] // block_rows))
    return (scores.reshape(-1, bin_count * per_bin), accumulated_sums)


def score_backward(query_unit, passage_normalized, belonging_mask, accumulated_sums, grad_scores):
    block_rows = block_size(query_unit.shape[0], passage_normalized.shape[0])
    per_block = block_rows // QLEN
    bin_count, bin_span, per_bin = belonging_mask.shape
    passages = bin_count * per_bin

    def one_block(running, block_index):
        query_block = lax.dynamic_slice_in_dim(query_unit, block_index * block_rows, block_rows, 0)
        angle_agreement = jnp.einsum(
            "re,te->rt", query_block, passage_normalized, preferred_element_type=jnp.float32
        )
        exponential_terms = jnp.exp((angle_agreement - 1.0) / sharpness_divisor)
        grad_block = lax.dynamic_slice_in_dim(grad_scores, block_index * per_block, per_block, 0)
        grad_soft = jnp.broadcast_to(grad_block[:, None, :], (per_block, QLEN, passages)).reshape(
            block_rows, passages
        )
        ratio = grad_soft / lax.dynamic_index_in_dim(
            accumulated_sums, block_index, 0, keepdims=False
        )
        spread = jnp.einsum(
            "rbp,btp->rbt",
            ratio.reshape(block_rows, bin_count, per_bin),
            belonging_mask,
            precision=full_accuracy_flag,
        ).reshape(block_rows, bin_count * bin_span)
        grad_cosine = (exponential_terms * spread).astype(jnp.bfloat16)
        query_grad = jnp.dot(grad_cosine, passage_normalized, preferred_element_type=jnp.float32)
        running = running + jnp.einsum(
            "rt,re->te", grad_cosine, query_block, preferred_element_type=jnp.float32
        )
        return (running, query_grad)

    passage_grad, query_grads = lax.scan(
        one_block,
        jnp.zeros(passage_normalized.shape, jnp.float32),
        jnp.arange(query_unit.shape[0] // block_rows),
    )
    return (query_grads.reshape(query_unit.shape), passage_grad)


def cross_terms(scores):
    highest = jnp.max(scores, 1)
    partition = jnp.sum(jnp.exp(scores - highest[:, None]), 1)
    return (highest, partition)


def combine_terms(left_terms, right_terms):
    highest = jnp.maximum(left_terms[0], right_terms[0])
    partition = left_terms[1] * jnp.exp(left_terms[0] - highest) + right_terms[1] * jnp.exp(
        right_terms[0] - highest
    )
    return (highest, partition)


def cross_grad(scores, highest, partition, passage_ids, chosen_ids, query_total):
    log_total = highest + jnp.log(partition)
    onehot = (passage_ids[None, :] == chosen_ids[:, None]).astype(jnp.float32)
    return (jnp.exp(scores - log_total[:, None]) - onehot) / query_total


def adam_update(weight, moment_one, moment_two, gradient, factor, rate):
    clipped = gradient * factor
    new_one = beta_one * moment_one + (1.0 - beta_one) * clipped
    new_two = beta_two * moment_two + (1.0 - beta_two) * clipped * clipped
    direction = (
        new_one / (1.0 - beta_one**STEP) / (jnp.sqrt(new_two / (1.0 - beta_two**STEP)) + adam_eps)
    )
    return (weight - rate * (direction + decay_rate * weight), new_one, new_two)


def body(
    query_tokens,
    passage_tokens,
    passage_lengths,
    positives,
    qkv_weight,
    qkv_first,
    qkv_second,
    out_weight,
    out_first,
    out_second,
    up_weight,
    up_first,
    up_second,
    down_weight,
    down_first,
    down_second,
    proj_weight,
    proj_first,
    proj_second,
    vector_params,
    vector_first,
    vector_second,
):
    gathered = (
        lax.all_gather(qkv_weight.astype(jnp.bfloat16), ("pb", "pa"), axis=0, tiled=True),
        lax.all_gather(out_weight.astype(jnp.bfloat16), ("pb", "pa"), axis=0, tiled=True),
        lax.all_gather(up_weight.astype(jnp.bfloat16), ("pb", "pa"), axis=0, tiled=True),
        lax.all_gather(down_weight.astype(jnp.bfloat16), ("pb", "pa"), axis=0, tiled=True),
        lax.all_gather(proj_weight.astype(jnp.bfloat16), ("pb", "pa"), axis=0, tiled=True),
        lax.all_gather(vector_params.astype(jnp.bfloat16), ("pb", "pa"), axis=1, tiled=True),
    )
    weights = (
        gathered[0],
        gathered[1],
        gathered[2],
        gathered[3],
        gathered[4],
        gathered[5].astype(jnp.float32),
    )
    own_index = lax.axis_index(("pb", "pa"))
    row_count = lax.axis_size("pb")
    column_count = lax.axis_size("pa")
    query_total = QPD * row_count * column_count
    query_flat = query_tokens.reshape(QPD * QLEN, D)
    query_seg = jnp.arange(QPD * QLEN, dtype=jnp.int32) // QLEN
    own_lengths = lax.dynamic_index_in_dim(passage_lengths, own_index, 0, keepdims=False)
    own_seg, own_member = segment_table(own_lengths, BIN)
    query_unit, query_kept = encode_forward(query_flat, query_seg, weights)
    passage_normalized, passage_kept = encode_forward(passage_tokens[0], own_seg, weights)
    every_query = lax.all_gather(query_unit, ("pb", "pa"), axis=0, tiled=True)
    passage_ids = own_index * PPB + jnp.arange(PPB, dtype=jnp.int32)
    bin_member = own_member[None]
    scores, accumulated_sums = score_forward(every_query, passage_normalized, bin_member)
    highest, partition = cross_terms(scores)
    highest, partition = merged((highest, partition), ("pb", "pa"), combine_terms)
    grad_scores = cross_grad(scores, highest, partition, passage_ids, positives, query_total)
    grad_every, grad_passage = score_backward(
        every_query, passage_normalized, bin_member, accumulated_sums, grad_scores
    )
    grad_query = lax.psum_scatter(grad_every, ("pb", "pa"), scatter_dimension=0, tiled=True)
    query_grads = encode_backward(query_flat, query_seg, weights, query_kept, grad_query)
    passage_grads = encode_backward(passage_tokens[0], own_seg, weights, passage_kept, grad_passage)
    local_sums = tuple(
        (query_part + passage_part for query_part, passage_part in zip(query_grads, passage_grads))
    )
    reduced = (
        lax.psum_scatter(local_sums[0], ("pb", "pa"), scatter_dimension=0, tiled=True),
        lax.psum_scatter(local_sums[1], ("pb", "pa"), scatter_dimension=0, tiled=True),
        lax.psum_scatter(local_sums[2], ("pb", "pa"), scatter_dimension=0, tiled=True),
        lax.psum_scatter(local_sums[3], ("pb", "pa"), scatter_dimension=0, tiled=True),
        lax.psum_scatter(local_sums[4], ("pb", "pa"), scatter_dimension=0, tiled=True),
        lax.psum_scatter(local_sums[5], ("pb", "pa"), scatter_dimension=1, tiled=True),
    )
    square = sum((jnp.sum(gradient * gradient) for gradient in reduced))
    norm_value = jnp.sqrt(lax.psum(square, ("pb", "pa")))
    factor = jnp.minimum(1.0, clip_max / (norm_value + 1e-06))
    qkv_res = adam_update(qkv_weight, qkv_first, qkv_second, reduced[0], factor, learn_rate)
    out_res = adam_update(out_weight, out_first, out_second, reduced[1], factor, learn_rate)
    up_res = adam_update(up_weight, up_first, up_second, reduced[2], factor, learn_rate)
    down_res = adam_update(down_weight, down_first, down_second, reduced[3], factor, learn_rate)
    proj_res = adam_update(proj_weight, proj_first, proj_second, reduced[4], factor, learn_rate)
    vector_res = adam_update(
        vector_params, vector_first, vector_second, reduced[5], factor, vector_rate
    )
    return (
        norm_value,
        qkv_res[0],
        qkv_res[1],
        qkv_res[2],
        out_res[0],
        out_res[1],
        out_res[2],
        up_res[0],
        up_res[1],
        up_res[2],
        down_res[0],
        down_res[1],
        down_res[2],
        proj_res[0],
        proj_res[1],
        proj_res[2],
        vector_res[0],
        vector_res[1],
        vector_res[2],
    )


def solution(mesh):
    placed = (
        P(("pb", "pa"), None, None),
        P(("pb", "pa"), None, None),
        P(),
        P(),
        P(("pb", "pa"), None),
        P(("pb", "pa"), None),
        P(("pb", "pa"), None),
        P(("pb", "pa"), None),
        P(("pb", "pa"), None),
        P(("pb", "pa"), None),
        P(("pb", "pa"), None),
        P(("pb", "pa"), None),
        P(("pb", "pa"), None),
        P(("pb", "pa"), None),
        P(("pb", "pa"), None),
        P(("pb", "pa"), None),
        P(("pb", "pa"), None),
        P(("pb", "pa"), None),
        P(("pb", "pa"), None),
        P(None, ("pb", "pa")),
        P(None, ("pb", "pa")),
        P(None, ("pb", "pa")),
    )
    return jax.shard_map(
        body,
        mesh=mesh,
        in_specs=placed,
        out_specs=(
            P(),
            P(("pb", "pa"), None),
            P(("pb", "pa"), None),
            P(("pb", "pa"), None),
            P(("pb", "pa"), None),
            P(("pb", "pa"), None),
            P(("pb", "pa"), None),
            P(("pb", "pa"), None),
            P(("pb", "pa"), None),
            P(("pb", "pa"), None),
            P(("pb", "pa"), None),
            P(("pb", "pa"), None),
            P(("pb", "pa"), None),
            P(("pb", "pa"), None),
            P(("pb", "pa"), None),
            P(("pb", "pa"), None),
            P(None, ("pb", "pa")),
            P(None, ("pb", "pa")),
            P(None, ("pb", "pa")),
        ),
        check_vma=False,
    )
```

profile of v0, /device:TPU:0, one launch (start us, length us, event | category | flops | bytes accessed | tf_op | source)
XLA Modules:
  0.0 1553.4 jit_solution(11949622915725330376)
XLA Ops:
  14.8 71.0 %all-gather.2 = bf16[32,24,12]{1,2,0:T(8,128)(2,1)S(1)} all-gather(bf16[1,24,12]{1,2,0:T(8,128)(2,1)S(1)} %convert_bitcast_fusion.4), channel_id=1, replica_groups=mesh['pb'=8,'pa'=4] {'pb','pa'}, dimensions={0}, use_global_device_ids=true | all-gather | bytes 19008 | tf_op jit(solution)/shard_map/all_gather | solution.py:379
  90.6 70.2 %all_gather.38 = bf16[768,128]{1,0:T(8,128)(2,1)} all-gather(bf16[24,128]{1,0:T(8,128)(2,1)S(1)} %convert_element_type.173), channel_id=1, replica_groups=mesh['pb'=8,'pa'=4] {'pb','pa'}, dimensions={0}, use_global_device_ids=true | all-gather | bytes 202752 | tf_op jit(solution)/shard_map/all_gather | solution.py:378
  162.6 7.5 add_convert_fusion
  170.1 6.6 copy.140
  176.7 4.8 slice_bitcast_fusion
  181.5 78.8 %while.14 = (s32[]{:T(128)}, bf16[2,512,12,64]{1,3,2,0:T(8,128)(2,1)}, f32[2,12,512]{2,1,0:T(8,128)S(1)}, s32[2]{0:T(128)S(1)}, s32[1024]{0:T(1024)S(1)}, /*inde...) while((s32[]{:T(128)}, ...), condition=%wide.region_12.13_spmd.clone, body=%wide.region_9.12_spmd.sunk.clone | while | flops 1686628352 | bytes 196593904 | solution.py:86
  183.2 12.3 fusion.257
  195.5 12.4 fusion.258
  211.2 8.2 bitcast_dynamic-update-slice_fusion.9
  222.2 12.2 fusion.257
  234.4 12.8 fusion.258
  250.5 8.2 bitcast_dynamic-update-slice_fusion.9
  260.4 4.7 fusion.62
  282.3 8.6 multiply_convert_fusion.2
  297.4 37.6 %multiply_convert_fusion.1 = (bf16[1024,3072]{1,0:T(8,128)(2,1)S(1)}, f32[1024,3072]{1,0:T(8,128)}, f32[1024,3072]{1,0:T(8,128)}) fusion(f32[3072]{0:T(1024)} %add.510, bf16[768,3072]{1,0:T(8,128)(2,1)} %all-gather.15.cloned.1.call-done, f32[1024,768]{0,1:T(8,128)S(1)} %get-tuple-element.579, f32[768]{0:T(1024)S(1)} %copy-done.81, f32[768]{0:T(1024)S(1)} %copy-done.74, ...), kind=kOutput, calls=%fused_computation.60 | convolution fusion | flops 5043388416 | bytes 39348224 | tf_op jit(solution)/shard_map/dot_general | solution.py:154
  335.0 10.7 fusion.158
  353.1 10.9 multiply_add_fusion.7
  367.1 64.9 %all-gather.4 = f32[32,1,128]{2,1,0:T(1,128)S(1)} all-gather(f32[1,1,128]{2,1,0:T(1,128)S(1)} %bitcast.262), channel_id=3, replica_groups=mesh['pb'=8,'pa'=4] {'pb','pa'}, dimensions={0}, use_global_device_ids=true | all-gather | bytes 16896 | tf_op jit(solution)/shard_map/all_gather | solution.py:30
  432.0 63.3 %all-gather.3 = f32[32,1,128]{2,1,0:T(1,128)S(1)} all-gather(f32[1,1,128]{2,1,0:T(1,128)S(1)} %bitcast.261), channel_id=2, replica_groups=mesh['pb'=8,'pa'=4] {'pb','pa'}, dimensions={0}, use_global_device_ids=true | all-gather | bytes 16896 | tf_op jit(solution)/shard_map/all_gather | solution.py:30
  500.4 12.5 fusion.51
  520.4 5.8 multiply_reduce_fusion.9
  540.6 19.7 %fusion.163 = (f32[3072]{0:T(1024)}, bf16[1024,3072]{1,0:T(8,128)(2,1)}) fusion(f32[1024,3072]{1,0:T(8,128)} %get-tuple-element.564, bf16[3072,768]{1,0:T(8,128)(2,1)} %all-gather.17.cloned.1.call-done, f32[1024,768]{0,1:T(8,128)} %get-tuple-element.560, f32[1024]{0:T(1024)S(1)} %negate_multiply_fusion.3, f32[1024,3072]{1,0:T(8,128)} %get-tuple-element.580, ...), kind=kOutput, calls=%fused_computation.313 | convolution fusion | flops 4883739648 | bytes 39350272 | tf_op jit(solution)/shard_map/dot_general | solution.py:204
  560.4 10.8 multiply_reduce_fusion.2
  575.6 292.0 %while.32 = (s32[]{:T(128)}, f32[1024,12,64]{0,2,1:T(8,128)}, f32[1024,12,64]{0,2,1:T(8,128)}, f32[2,512,12,64]{1,3,2,0:T(8,128)}, s32[2]{0:T(128)S(1)}, /*index...) while((s32[]{:T(128)}, f32[1024,12,64]{0,2,1:T(8,128)}, ...), condition=%wide.region_37.38_spmd.clone.clone, body=%wide.region_35.37_spmd.clone.sunk.clone | while | flops 4193794048 | bytes 335767904 | solution.py:129
  579.4 11.6 fusion.271
  591.0 11.6 bitcast_add_fusion.7
  604.3 10.1 fusion.270
  614.4 55.0 %bitcast_add_fusion.6 = f32[1024,12,64]{0,2,1:T(8,128)} fusion(f32[1024,12,64]{0,2,1:T(8,128)} %get-tuple-element.891, f32[12,512,1024]{2,1,0:T(8,128)} %fusion.270, f32[12,512]{1,0:T(8,128)S(1)} %dynamic-slice_bitcast_fusion.3, f32[12,512,1024]{2,1,0:T(8,128)} %fusion.271, pred[512,1024]{1,0:T(8,128)(4,1)} %copy-done.15, pred[]{:T(512)S(6)} %compare.10, ...), kind=kOutput, calls=%fused_computation.30.clone.1.clone | convolution fusion | flops 876092416 | bytes 108855304 | tf_op jit(solution)/shard_map/while/body/eval_jaxpr/hqk,qhd->khd/dot_general | solution.py:123
  669.4 52.1 %bitcast_dynamic-update-slice_fusion.11 = f32[2,512,12,64]{1,3,2,0:T(8,128)} fusion(f32[2,512,12,64]{1,3,2,0:T(8,128)} %get-tuple-element.893, s32[]{:T(128)S(6)} %copy.190, bf16[1024,12,64]{0,2,1:T(8,128)(2,1)S(1)} %get-tuple-element.908, f32[12,512,1024]{2,1,0:T(8,128)} %fusion.270, f32[12,512]{1,0:T(8,128)S(1)} %dynamic-slice_bitcast_fusion.3, ...), kind=kOutput, calls=%fused_computation.31.clone.1.clone | convolution fusion | flops 874519552 | bytes 104923136 | tf_op jit(solution)/shard_map/while/body/eval_jaxpr/hqk,khd->qhd/dot_general | solution.py:120
  725.1 11.5 fusion.271
  736.7 11.6 bitcast_add_fusion.7
  750.0 10.0 fusion.270
  760.0 55.3 %bitcast_add_fusion.6 = f32[1024,12,64]{0,2,1:T(8,128)} fusion(f32[1024,12,64]{0,2,1:T(8,128)} %get-tuple-element.891, f32[12,512,1024]{2,1,0:T(8,128)} %fusion.270, f32[12,512]{1,0:T(8,128)S(1)} %dynamic-slice_bitcast_fusion.3, f32[12,512,1024]{2,1,0:T(8,128)} %fusion.271, pred[512,1024]{1,0:T(8,128)(4,1)} %copy-done.15, pred[]{:T(512)S(6)} %compare.10, ...), kind=kOutput, calls=%fused_computation.30.clone.1.clone | convolution fusion | flops 876092416 | bytes 108855304 | tf_op jit(solution)/shard_map/while/body/eval_jaxpr/hqk,qhd->khd/dot_general | solution.py:123
  815.3 52.1 %bitcast_dynamic-update-slice_fusion.11 = f32[2,512,12,64]{1,3,2,0:T(8,128)} fusion(f32[2,512,12,64]{1,3,2,0:T(8,128)} %get-tuple-element.893, s32[]{:T(128)S(6)} %copy.190, bf16[1024,12,64]{0,2,1:T(8,128)(2,1)S(1)} %get-tuple-element.908, f32[12,512,1024]{2,1,0:T(8,128)} %fusion.270, f32[12,512]{1,0:T(8,128)S(1)} %dynamic-slice_bitcast_fusion.3, ...), kind=kOutput, calls=%fused_computation.31.clone.1.clone | convolution fusion | flops 874519552 | bytes 104923136 | tf_op jit(solution)/shard_map/while/body/eval_jaxpr/hqk,khd->qhd/dot_general | solution.py:120
  889.0 6.0 fusion.162
  905.8 5.9 fusion.71
  916.3 7.0 add_bitcast_fusion
  923.3 8.0 copy.160
  933.3 7.6 fusion.63
  940.9 5.1 convolution_add_fusion.1
  947.9 7.7 fusion.92
  955.7 5.1 convolution_add_fusion
  978.6 40.0 %all-reduce.1 = f32[12,768]{1,0:T(8,128)S(1)} all-reduce(f32[12,768]{1,0:T(8,128)S(1)} %add.558), channel_id=10, replica_groups=mesh['pb'=8,'pa'=4] {'pb','pa'}, use_global_device_ids=true, to_apply=%region_66.67.clone | all-reduce | flops 9216 | bytes 73728
  1020.8 64.1 %reduce-scatter.14.cloned.1.call-done = f32[24,768]{1,0:T(8,128)} async-done(((f32[768,768]{1,0:T(8,128)}), f32[24,768]{1,0:T(8,128)}) %reduce-scatter.14.cloned.1.call-update) | async-done | bytes 73744 | tf_op jit(solution)/shard_map/reduce_scatter | solution.py:417
  1086.4 123.2 %reduce-scatter.20.cloned.1.call-done = f32[24,2304]{1,0:T(8,128)} async-done(((f32[768,2304]{1,0:T(8,128)}), f32[24,2304]{1,0:T(8,128)}) %reduce-scatter.20.cloned.1.call-update) | async-done | bytes 221200 | tf_op jit(solution)/shard_map/reduce_scatter | solution.py:416
  1213.2 137.0 %reduce-scatter.16.cloned.1.call-done = f32[24,3072]{1,0:T(8,128)} async-done(((f32[768,3072]{1,0:T(8,128)}), f32[24,3072]{1,0:T(8,128)}) %reduce-scatter.16.cloned.1.call-update) | async-done | bytes 294928 | tf_op jit(solution)/shard_map/reduce_scatter | solution.py:418
  1352.6 139.2 %reduce-scatter.18.cloned.1.call-done = f32[96,768]{1,0:T(8,128)} async-done(((f32[3072,768]{1,0:T(8,128)}), f32[96,768]{1,0:T(8,128)}) %reduce-scatter.18.cloned.1.call-update) | async-done | bytes 294928 | tf_op jit(solution)/shard_map/reduce_scatter | solution.py:419
  1495.4 39.8 %psum.7 = f32[]{:T(128)} all-reduce(f32[]{:T(128)S(6)} %add.559), channel_id=1, replica_groups=mesh['pb'=8,'pa'=4] {'pb','pa'}, use_global_device_ids=true, to_apply=%region_68.69 | all-reduce | flops 1 | bytes 8 | tf_op jit(solution)/shard_map/psum | solution.py:424
  (515 shorter events, 172.9 us)
Async XLA Ops:
  7.2 81.6 %copy-start = (s32[32,8]{0,1:T(8,128)S(1)}, s32[32,8]{0,1:T(8,128)}, u32[]{:S(2)}) copy-start(s32[32,8]{0,1:T(8,128)} %param.30) | copy-start | bytes 3076
  7.2 82.1 %copy-start.78 = (f32[24,128]{1,0:T(8,128)S(1)}, f32[24,128]{1,0:T(8,128)}, u32[]{:S(2)}) copy-start(f32[24,128]{1,0:T(8,128)} %param.44) | copy-start | bytes 36868
  7.2 153.6 %copy-start.50 = (bf16[1,1024,768]{2,1,0:T(8,128)(2,1)S(1)}, bf16[1,1024,768]{2,1,0:T(8,128)(2,1)}, u32[]{:S(2)}) copy-start(bf16[1,1024,768]{2,1,0:T(8,128)(2,1)} %param.29) | copy-start | bytes 4718596
  7.2 155.3 %all-gather.11.cloned.1.call-start = ((), (), s32[]{:S(2)}) async-start(), calls=%async_computation.6 | async-start | bytes 3649536 | tf_op jit(solution)/shard_map/all_gather | solution.py:374
  9.0 264.4 %all-gather.13.cloned.1.call-start = ((), (), s32[]{:S(2)}) async-start(), calls=%async_computation.7 | async-start | bytes 1216512 | tf_op jit(solution)/shard_map/all_gather | solution.py:375
  10.6 271.7 %all-gather.15.cloned.1.call-start = ((), (), s32[]{:S(2)}) async-start(), calls=%async_computation.8 | async-start | bytes 4866048 | tf_op jit(solution)/shard_map/all_gather | solution.py:376
  12.3 278.6 %all-gather.17.cloned.1.call-start = ((), (), s32[]{:S(2)}) async-start(), calls=%async_computation.9 | async-start | bytes 4866048 | tf_op jit(solution)/shard_map/all_gather | solution.py:377
  14.0 335.3 %all-gather.19.cloned.1.call-start = ((), (), s32[]{:S(2)}) async-start(), calls=%async_computation.10 | async-start | bytes 1081344 | tf_op jit(solution)/shard_map/all_gather | solution.py:399
  181.5 78.9 %copy-start.46 = (bf16[4,32,768]{2,1,0:T(8,128)(2,1)S(1)}, bf16[4,32,768]{2,1,0:T(8,128)(2,1)}, u32[]{:S(2)}) copy-start(bf16[4,32,768]{2,1,0:T(8,128)(2,1)} %param.28) | copy-start | bytes 589828
  181.5 78.9 %copy-start.77 = (f32[2304]{0:T(1024)S(1)}, f32[2304]{0:T(1024)}, u32[]{:S(2)}) copy-start(f32[2304]{0:T(1024)} %copy-done.76) | copy-start | bytes 27652
  183.2 24.7 %copy-start.25 = (bf16[2,512,12,64]{1,3,2,0:T(8,128)(2,1)S(1)}, bf16[2,512,12,64]{1,3,2,0:T(8,128)(2,1)}, u32[]{:S(2)}) copy-start(bf16[2,512,12,64]{1,3,2,0:T(8,128)(2,1)} %get-tuple-element.847) | copy-start | bytes 4718596 | tf_op jit(solution)/shard_map/while
  195.5 15.6 %copy-start.2 = (f32[12,512,1024]{2,1,0:T(8,128)S(1)}, f32[12,512,1024]{2,1,0:T(8,128)}, u32[]{:S(2)}) copy-start(f32[12,512,1024]{2,1,0:T(8,128)} %get-tuple-element.778) | copy-start | bytes 75497472 | tf_op jit(solution)/shard_map/while
  222.2 25.0 %copy-start.25 = (bf16[2,512,12,64]{1,3,2,0:T(8,128)(2,1)S(1)}, bf16[2,512,12,64]{1,3,2,0:T(8,128)(2,1)}, u32[]{:S(2)}) copy-start(bf16[2,512,12,64]{1,3,2,0:T(8,128)(2,1)} %get-tuple-element.847) | copy-start | bytes 4718596 | tf_op jit(solution)/shard_map/while
  234.4 16.1 %copy-start.2 = (f32[12,512,1024]{2,1,0:T(8,128)S(1)}, f32[12,512,1024]{2,1,0:T(8,128)}, u32[]{:S(2)}) copy-start(f32[12,512,1024]{2,1,0:T(8,128)} %get-tuple-element.778) | copy-start | bytes 75497472 | tf_op jit(solution)/shard_map/while
  275.2 15.6 %copy-start.12 = (f32[128,768]{1,0:T(8,128)}, f32[128,768]{1,0:T(8,128)S(1)}, u32[]{:S(2)}) copy-start(f32[128,768]{1,0:T(8,128)S(1)} %get-tuple-element.586) | copy-start | bytes 1179652
  280.0 17.4 %copy-start.16 = (f32[1024,768]{0,1:T(8,128)}, f32[1024,768]{0,1:T(8,128)S(1)}, u32[]{:S(2)}) copy-start(f32[1024,768]{0,1:T(8,128)S(1)} %get-tuple-element.579) | copy-start | bytes 9437188
  297.3 587.5 %reduce-scatter.12.cloned.1.call-start = ((), (), s32[]{:S(2)}) async-start(), calls=%async_computation.11 | async-start | bytes 2162688 | tf_op jit(solution)/shard_map/reduce_scatter | solution.py:409
  297.4 37.7 %copy-start.86 = (f32[1024]{0:T(1024)S(1)}, f32[1024]{0:T(1024)}, u32[]{:S(2)}) copy-start(f32[1024]{0:T(1024)} %copy-done.85) | copy-start | bytes 12292
  297.4 37.7 %copy-start.96 = (f32[768]{0:T(1024)S(1)}, f32[768]{0:T(1024)}, u32[]{:S(2)}) copy-start(f32[768]{0:T(1024)} %get-tuple-element.479) | copy-start | bytes 9220
  297.4 37.7 %copy-start.99 = (f32[1024]{0:T(1024)S(1)}, f32[1024]{0:T(1024)}, u32[]{:S(2)}) copy-start(f32[1024]{0:T(1024)} %fusion.125) | copy-start | bytes 12292
  353.1 143.6 %copy-start.132 = (s32[128]{0:T(128)S(1)}, s32[128]{0:T(128)}, u32[]{:S(2)}) copy-start(s32[128]{0:T(128)} %param.31) | copy-start | bytes 1540
  500.4 15.8 %copy-start.14 = (f32[1024,128]{0,1:T(8,128)S(1)}, f32[1024,128]{0,1:T(8,128)}, u32[]{:S(2)}) copy-start(f32[1024,128]{0,1:T(8,128)} %get-tuple-element.593) | copy-start | bytes 1572868
  526.2 493.2 %reduce-scatter.22.cloned.1.call-start = ((), (), s32[]{:S(2)}) async-start(), calls=%async_computation.16 | async-start | bytes 405504
  540.6 19.8 %copy-start.102 = (f32[1024]{0:T(1024)}, f32[1024]{0:T(1024)S(1)}, u32[]{:S(2)}) copy-start(f32[1024]{0:T(1024)S(1)} %negate_multiply_fusion.3) | copy-start | bytes 12292
  540.6 19.8 %copy-start.17 = (f32[1024,768]{0,1:T(8,128)S(1)}, f32[1024,768]{0,1:T(8,128)}, u32[]{:S(2)}) copy-start(f32[1024,768]{0,1:T(8,128)} %copy-done.16) | copy-start | bytes 9437188
  540.6 19.8 %copy-start.87 = (f32[1024]{0:T(1024)S(1)}, f32[1024]{0:T(1024)}, u32[]{:S(2)}) copy-start(f32[1024]{0:T(1024)} %copy-done.85) | copy-start | bytes 12292
  540.6 19.8 %copy-start.100 = (f32[1024]{0:T(1024)S(1)}, f32[1024]{0:T(1024)}, u32[]{:S(2)}) copy-start(f32[1024]{0:T(1024)} %fusion.125) | copy-start | bytes 12292
  579.4 11.6 copy-start.15
  579.4 11.6 copy-start.24
  888.6 196.3 %reduce-scatter.14.cloned.1.call-start = ((), (), s32[]{:S(2)}) async-start(), calls=%async_computation.12 | async-start | bytes 2433024 | tf_op jit(solution)/shard_map/reduce_scatter | solution.py:417
  897.6 14.0 copy-start.27
  897.7 14.0 copy-start.121
  899.6 310.0 %reduce-scatter.20.cloned.1.call-start = ((), (), s32[]{:S(2)}) async-start(), calls=%async_computation.15 | async-start | bytes 7299072 | tf_op jit(solution)/shard_map/reduce_scatter | solution.py:416
  931.4 418.9 %reduce-scatter.16.cloned.1.call-start = ((), (), s32[]{:S(2)}) async-start(), calls=%async_computation.13 | async-start | bytes 9732096 | tf_op jit(solution)/shard_map/reduce_scatter | solution.py:418
  946.1 545.7 %reduce-scatter.18.cloned.1.call-start = ((), (), s32[]{:S(2)}) async-start(), calls=%async_computation.14 | async-start | bytes 9732096 | tf_op jit(solution)/shard_map/reduce_scatter | solution.py:419
  964.4 11.7 copy-start.28
  967.2 570.1 %copy-start.79 = (f32[24,128]{1,0:T(8,128)S(1)}, f32[24,128]{1,0:T(8,128)}, u32[]{:S(2)}) copy-start(f32[24,128]{1,0:T(8,128)} %param.44) | copy-start | bytes 36868
  968.2 572.2 %copy-start.61 = (f32[24,2304]{1,0:T(8,128)S(1)}, f32[24,2304]{1,0:T(8,128)}, u32[]{:S(2)}) copy-start(f32[24,2304]{1,0:T(8,128)} %param.32) | copy-start | bytes 663556
  974.6 567.8 %copy-start.54 = (f32[96,768]{1,0:T(8,128)S(1)}, f32[96,768]{1,0:T(8,128)}, u32[]{:S(2)}) copy-start(f32[96,768]{1,0:T(8,128)} %param.41) | copy-start | bytes 884740
  974.6 567.7 %copy-start.67 = (f32[96,768]{1,0:T(8,128)S(1)}, f32[96,768]{1,0:T(8,128)}, u32[]{:S(2)}) copy-start(f32[96,768]{1,0:T(8,128)} %param.42) | copy-start | bytes 884740
  974.7 567.7 %copy-start.68 = (f32[96,768]{1,0:T(8,128)S(1)}, f32[96,768]{1,0:T(8,128)}, u32[]{:S(2)}) copy-start(f32[96,768]{1,0:T(8,128)} %param.43) | copy-start | bytes 884740
  1019.4 518.0 %copy-start.80 = (f32[24,128]{1,0:T(8,128)S(1)}, f32[24,128]{1,0:T(8,128)}, u32[]{:S(2)}) copy-start(f32[24,128]{1,0:T(8,128)} %reduce-scatter.22.cloned.1.call-done) | copy-start | bytes 36868
  1084.8 453.9 %copy-start.71 = (f32[24,768]{1,0:T(8,128)S(1)}, f32[24,768]{1,0:T(8,128)}, u32[]{:S(2)}) copy-start(f32[24,768]{1,0:T(8,128)} %reduce-scatter.14.cloned.1.call-done) | copy-start | bytes 221188
  1209.6 330.8 %copy-start.62 = (f32[24,2304]{1,0:T(8,128)S(1)}, f32[24,2304]{1,0:T(8,128)}, u32[]{:S(2)}) copy-start(f32[24,2304]{1,0:T(8,128)} %reduce-scatter.20.cloned.1.call-done) | copy-start | bytes 663556
  1211.0 333.4 %copy-start.55 = (f32[24,3072]{1,0:T(8,128)S(1)}, f32[24,3072]{1,0:T(8,128)}, u32[]{:S(2)}) copy-start(f32[24,3072]{1,0:T(8,128)} %param.38) | copy-start | bytes 884740
  1211.0 333.4 %copy-start.69 = (f32[24,3072]{1,0:T(8,128)S(1)}, f32[24,3072]{1,0:T(8,128)}, u32[]{:S(2)}) copy-start(f32[24,3072]{1,0:T(8,128)} %param.39) | copy-start | bytes 884740
  1211.0 333.4 %copy-start.70 = (f32[24,3072]{1,0:T(8,128)S(1)}, f32[24,3072]{1,0:T(8,128)}, u32[]{:S(2)}) copy-start(f32[24,3072]{1,0:T(8,128)} %param.40) | copy-start | bytes 884740
  1350.2 194.2 %copy-start.56 = (f32[24,3072]{1,0:T(8,128)S(1)}, f32[24,3072]{1,0:T(8,128)}, u32[]{:S(2)}) copy-start(f32[24,3072]{1,0:T(8,128)} %reduce-scatter.16.cloned.1.call-done) | copy-start | bytes 884740
  (108 other events, 464.6 us)
Sparse Core Ops, SparseCore 0:
  11.4 63.1 all-gather.10
  78.0 52.8 all-gather.12
  134.3 62.6 all-gather.14
  200.2 62.4 all-gather.16
  297.4 46.4 all-gather.18
  526.3 136.2 reduce-scatter.11
  888.7 92.5 reduce-scatter.21
  986.6 98.1 reduce-scatter.13
  1091.5 118.1 reduce-scatter.19
  1215.4 134.8 reduce-scatter.15
  1357.1 134.5 reduce-scatter.17
where the time goes:
time: 1560 us; the launch traced here: 1550 us
  matrix products  533 us (34%)
  waiting for transfers between devices  464 us (30%)
  blocking collectives  349 us (22%)
  other arithmetic  91.5 us (6%)
  local copies, waits for them, and re-layouts  85.6 us (5%)
  between operations  21.4 us (1%)
    reduce_scatter x1, waiting for transfers between devices, body(): lax.psum_scatter(local_sums[3], ('pb', 'pa'), scatter_dimension=0, tiled=...  139 us
    reduce_scatter x1, waiting for transfers between devices, body(): lax.psum_scatter(local_sums[2], ('pb', 'pa'), scatter_dimension=0, tiled=...  137 us
    all_gather x2, blocking collectives, merged(): gathered = jax.tree.map(lambda a: lax.all_gather(a, axis), part)  128 us
    reduce_scatter x1, waiting for transfers between devices, body(): lax.psum_scatter(local_sums[0], ('pb', 'pa'), scatter_dimension=0, tiled=...  123 us
    dot_general x3, matrix products, one_block(): jnp.einsum('hqk,qhd->khd', grad_raw, block_query, preferred_element_type=...  111 us
    dot_general x3, matrix products, one_block(): jnp.einsum('hqk,khd->qhd', grad_raw, keys, preferred_element_type=jnp.flo...  106 us
    all_gather x1, blocking collectives, body(): lax.all_gather(vector_params.astype(jnp.bfloat16), ('pb', 'pa'), axis=1,...  71 us
    all_gather x1, blocking collectives, body(): lax.all_gather(proj_weight.astype(jnp.bfloat16), ('pb', 'pa'), axis=0, ti...  70.2 us
  transfers between devices with their start and end apart: 11, of which 4 were waited for; matrix products, arithmetic and copies ran while one was open for 40% of the time, Pallas kernels for 0%

commit v1 on v0

v1 whole, which is shorter than its diff:
```python
import functools

import jax
import jax.numpy as jnp
from jax import lax
from jax.experimental import pallas as pl
from jax.experimental.pallas import tpu as pltpu
from jax.sharding import PartitionSpec as P

D = 768
HEAD_DIM = 64
QLEN = 32
BIN = 1024
PPB = 8
STEP = 10
QPD = 4
ATTEND_TILE = 512
FEED_ROWS = 512
BACK_ROWS = 256


sharpness_divisor = 0.1
clip_max = 0.02
learn_rate = 0.04
vector_rate = 0.4
beta_one = 0.9
beta_two = 0.999
adam_eps = 1e-08
decay_rate = 0.01
norm_eps = 1e-12


def shift_pairs(amount):
    return [(i, (i + amount) % 4) for i in range(4)]


FIRST_STEP = [(i, i ^ 2 if i % 2 == 0 else i ^ 4) for i in range(8)]
SECOND_STEP = [(i, i ^ 4 if i % 2 == 0 else i ^ 2) for i in range(8)]
CORE_PAIR = [(i, i ^ 1) for i in range(8)]


def staged_mesh():
    return lax.axis_size("pb") == 8 and lax.axis_size("pa") == 4


def position():
    row = lax.axis_index("pb")
    core, x_bit, y_bit = row % 2, (row // 2) % 2, row // 4
    return (
        lax.axis_index("pa"),
        core,
        jnp.where(core == 0, x_bit, y_bit),
        jnp.where(core == 0, y_bit, x_bit),
    )


def in_order(bit, own, other):
    first = bit == 0
    return jnp.stack([jnp.where(first, own, other), jnp.where(first, other, own)])


def gather_rows(part, columns):
    if not staged_mesh():
        whole = lax.all_gather(part, ("pb", "pa"), axis=0, tiled=True)
        return [whole[:, low:high] for low, high in columns]
    depth, core, first_bit, second_bit = position()
    moved = [lax.ppermute(part, "pa", shift_pairs(k)) for k in (1, 2, 3)]
    around = [part, moved[2], moved[1], moved[0]]
    line = jnp.stack([lax.select_n((place - depth) % 4, *around) for place in range(4)])
    pair = in_order(first_bit, line, lax.ppermute(line, "pb", FIRST_STEP))
    quad = in_order(second_bit, pair, lax.ppermute(pair, "pb", SECOND_STEP))
    partner = lax.ppermute(quad, "pb", CORE_PAIR)
    results = []
    for low, high in columns:
        own, other = quad[..., low:high], partner[..., low:high]
        even = jnp.where(core == 0, own, other)
        odd = jnp.where(core == 0, other, own).swapaxes(0, 1)
        results.append(jnp.stack([even, odd], 2).reshape(32 * part.shape[0], high - low))
    return results


def scatter_rows(terms):
    if not staged_mesh():
        return lax.psum_scatter(
            terms.astype(jnp.float32), ("pb", "pa"), scatter_dimension=0, tiled=True
        )
    depth, core, first_bit, second_bit = position()
    blocks = terms.reshape((2, 2, 2, 4, terms.shape[0] // 32) + terms.shape[1:])
    even, odd = blocks[:, :, 0], blocks[:, :, 1].swapaxes(0, 1)
    keep = jnp.where(core == 0, even, odd)
    send = jnp.where(core == 0, odd, even).astype(jnp.bfloat16)

    def block(array, place):
        return lax.dynamic_index_in_dim(array, place, 0, False)

    def sent(array, place):
        return block(array, place).astype(jnp.bfloat16)

    def joined(own, moved):
        return own.astype(jnp.float32) + moved.astype(jnp.float32)

    quad = joined(keep, lax.ppermute(send, "pb", CORE_PAIR))
    pair = joined(
        block(quad, second_bit), lax.ppermute(sent(quad, 1 - second_bit), "pb", SECOND_STEP)
    )
    line = joined(
        block(pair, first_bit), lax.ppermute(sent(pair, 1 - first_bit), "pb", FIRST_STEP)
    )
    total = block(line, depth)
    for k in (1, 2, 3):
        moved = lax.ppermute(sent(line, (depth + k) % 4), "pa", shift_pairs(k))
        total = joined(total, moved)
    return total


def sum_everywhere(value):
    count = lax.axis_size(("pb", "pa"))
    copies = jnp.broadcast_to(value[None], (count,) + value.shape)
    return jnp.sum(lax.all_to_all(copies, ("pb", "pa"), 0, 0), 0)


F32 = jnp.float32
LOW = jnp.bfloat16
ACROSS = (((1,), (1,)), ((), ()))
PLAIN = (((1,), (0,)), ((), ()))


def dot(left, right, dims=PLAIN):
    return lax.dot_general(left, right, dims, preferred_element_type=F32)


def standard(hidden):
    centred = hidden - jnp.mean(hidden, -1, keepdims=True)
    spread = jnp.mean(centred * centred, -1, keepdims=True)
    scale = lax.rsqrt(spread + norm_eps)
    return centred * scale, scale


def standard_backward(grad, unit, scale):
    return scale * (
        grad
        - jnp.mean(grad, -1, keepdims=True)
        - unit * jnp.mean(grad * unit, -1, keepdims=True)
    )


def gelu_with_slope(value):
    below = 0.5 + 0.5 * lax.erf(value * 0.7071067811865476)
    density = 0.3989422804014327 * jnp.exp(-0.5 * value * value)
    return value * below, below + value * density


def whole_block(array):
    return pl.BlockSpec(array.shape, lambda *_: (0,) * array.ndim, pipeline_mode=pl.Buffered(1))


def row_block(rows, width):
    return pl.BlockSpec((rows, width), lambda i: (i, 0))


def row_call(kernel, count, rows, inputs, weights, outputs, sums=(), flops=0, limit=56):
    moved = count * sum(a.shape[1] * a.dtype.itemsize for a in inputs)
    moved += sum(w.size * w.dtype.itemsize for w in weights)
    moved += count * sum(w * jnp.dtype(t).itemsize for w, t in outputs)
    return pl.pallas_call(
        kernel,
        grid=(count // rows,),
        in_specs=[row_block(rows, a.shape[1]) for a in inputs] + [whole_block(w) for w in weights],
        out_specs=[row_block(rows, w) for w, _ in outputs]
        + [pl.BlockSpec((8, w), lambda i: (0, 0)) for w in sums],
        out_shape=[jax.ShapeDtypeStruct((count, w), t) for w, t in outputs]
        + [jax.ShapeDtypeStruct((8, w), F32) for w in sums],
        compiler_params=pltpu.CompilerParams(vmem_limit_bytes=limit << 20),
        cost_estimate=pl.CostEstimate(flops=flops, transcendentals=0, bytes_accessed=moved),
    )(*inputs, *weights)


def widen_kernel(x_ref, att_ref, out_w, up_w, vec, wide, resid_ref, low_ref, act_ref, slope_ref):
    resid = x_ref[...].astype(F32) + dot(att_ref[...], out_w[...]) + vec[2:3]
    resid_ref[...] = resid
    low = (standard(resid)[0] * vec[3:4] + vec[4:5]).astype(LOW)
    low_ref[...] = low
    for at in range(0, up_w.shape[1], 512):
        part = slice(at, at + 512)
        value, slope = gelu_with_slope(dot(low, up_w[:, part]) + wide[0:1, part])
        act_ref[:, part] = value.astype(LOW)
        slope_ref[:, part] = slope.astype(LOW)


def narrow_kernel(act_ref, resid_ref, down_w, proj_w, vec, two_ref, low_ref, proj_ref, unit_ref):
    normed = standard(resid_ref[...])[0] * vec[3:4] + vec[4:5]
    two = normed + dot(act_ref[...], down_w[...]) + vec[9:10]
    two_ref[...] = two
    low = (standard(two)[0] * vec[10:11] + vec[11:12]).astype(LOW)
    low_ref[...] = low
    projected = dot(low, proj_w[...])
    proj_ref[...] = projected
    square = jnp.sum(projected * projected, -1, keepdims=True) + 1e-06
    unit_ref[...] = (projected * lax.rsqrt(square)).astype(LOW)


def back_kernel(
    grad_ref, proj_ref, two_ref, slope_ref, resid_ref,
    proj_w, down_w, up_w, out_w, vec,
    gproj_ref, gtwo_ref, ghid_ref, gone_ref, gatt_ref, sum_ref, wide_ref,
):
    @pl.when(pl.program_id(0) == 0)
    def _():
        sum_ref[...] = jnp.zeros_like(sum_ref)
        wide_ref[...] = jnp.zeros_like(wide_ref)

    def add(row, value):
        sum_ref[row : row + 1, :] += jnp.sum(value, 0, keepdims=True)

    grad, projected = grad_ref[...], proj_ref[...]
    scale = lax.rsqrt(jnp.sum(projected * projected, -1, keepdims=True) + 1e-06)
    along = jnp.sum(projected * grad, -1, keepdims=True)
    gproj = (scale * grad - projected * (scale * scale * scale * along)).astype(LOW)
    gproj_ref[...] = gproj
    gnormed = dot(gproj, proj_w[...], ACROSS)
    unit, scale = standard(two_ref[...])
    add(4, gnormed * unit)
    add(5, gnormed)
    gtwo = standard_backward(gnormed * vec[10:11], unit, scale)
    add(3, gtwo)
    gtwo_low = gtwo.astype(LOW)
    gtwo_ref[...] = gtwo_low
    gnormed = gtwo
    for at in range(0, up_w.shape[1], 512):
        part = slice(at, at + 512)
        ghid = dot(gtwo_low, down_w[part, :], ACROSS) * slope_ref[:, part].astype(F32)
        wide_ref[0:1, part] += jnp.sum(ghid, 0, keepdims=True)
        ghid_low = ghid.astype(LOW)
        ghid_ref[:, part] = ghid_low
        gnormed = gnormed + dot(ghid_low, up_w[:, part], ACROSS)
    unit, scale = standard(resid_ref[...])
    add(1, gnormed * unit)
    add(2, gnormed)
    gone = standard_backward(gnormed * vec[3:4], unit, scale)
    add(0, gone)
    gone_low = gone.astype(LOW)
    gone_ref[...] = gone_low
    gatt_ref[...] = dot(gone_low, out_w[...], ACROSS).astype(LOW)


def attend_kernel(tile, spans, q_ref, k_ref, v_ref, col, row, out_ref, total_ref, logits, flipped):
    flipped[...] = v_ref[...].T
    lane = lax.broadcasted_iota(jnp.int32, (tile, 128), 1)

    def block(index, carry):
        here = pl.ds(pl.multiple_of(index * tile, tile), tile)
        query = q_ref[here, :] * jnp.asarray(0.125, LOW)
        zero = jnp.zeros_like(query)
        pair = (jnp.where(lane < 64, query, zero), jnp.where(lane < 64, zero, query))
        segment = row[0:1, here]
        low, high = spans[index, 0], spans[index, 1]

        def score(step, tops):
            there = pl.ds(pl.multiple_of(step * tile, tile), tile)
            keys = k_ref[there, :]
            same = col[there, :] == segment
            result = []
            for head in range(2):
                value = jnp.where(same, dot(keys, pair[head], ACROSS), -1e30)
                logits[head, there, :] = value
                result.append(jnp.maximum(tops[head], jnp.max(value, 0, keepdims=True)))
            return tuple(result)

        lowest = jnp.full((1, tile), -1e30, F32)
        tops = lax.fori_loop(low, high, score, (lowest, lowest))

        def mix(step, state):
            there = pl.ds(pl.multiple_of(step * tile, tile), tile)
            result = []
            for head in range(2):
                term = jnp.exp(logits[head, there, :] - tops[head])
                result.append(state[2 * head] + jnp.sum(term, 0, keepdims=True))
                values = flipped[64 * head : 64 * head + 64, there]
                result.append(state[2 * head + 1] + dot(values, term.astype(LOW)))
            return tuple(result)

        none, empty = jnp.zeros((1, tile), F32), jnp.zeros((64, tile), F32)
        sum0, mix0, sum1, mix1 = lax.fori_loop(low, high, mix, (none, empty, none, empty))
        both = jnp.concatenate([mix0 / sum0, mix1 / sum1], 0)
        out_ref[here, :] = both.T.astype(LOW)
        total_ref[0, 0:1, here] = tops[0] + jnp.log(sum0)
        total_ref[0, 1:2, here] = tops[1] + jnp.log(sum1)
        return carry

    lax.fori_loop(0, q_ref.shape[0] // tile, block, 0)


def head_pair(count, third):
    return pl.BlockSpec((count, 128), lambda h, s: (0, third * 6 + h))


def attend_forward(mixed, spans, col, row, tile):
    count = mixed.shape[0]
    return pl.pallas_call(
        functools.partial(attend_kernel, tile),
        out_shape=(
            jax.ShapeDtypeStruct((count, D), LOW),
            jax.ShapeDtypeStruct((6, 8, count), F32),
        ),
        grid_spec=pltpu.PrefetchScalarGridSpec(
            num_scalar_prefetch=1,
            grid=(6,),
            in_specs=[head_pair(count, third) for third in range(3)]
            + [
                pl.BlockSpec((count, tile), lambda h, s: (0, 0)),
                pl.BlockSpec((8, count), lambda h, s: (0, 0)),
            ],
            out_specs=[head_pair(count, 0), pl.BlockSpec((1, 8, count), lambda h, s: (h, 0, 0))],
            scratch_shapes=[pltpu.VMEM((2, count, tile), F32), pltpu.VMEM((128, count), LOW)],
        ),
        compiler_params=pltpu.CompilerParams(vmem_limit_bytes=40 << 20),
        cost_estimate=pl.CostEstimate(
            flops=8 * count * count * D,
            transcendentals=12 * count * count,
            bytes_accessed=8 * count * D,
        ),
    )(spans, mixed, mixed, mixed, col, row)


def attend_back_kernel(
    tile, spans, q_ref, k_ref, v_ref, g_ref, total_ref, col, row,
    grad_ref, sum_ref, flipped, gkey, gvalue, probs, gprobs,
):
    flipped[...] = k_ref[...].T
    gkey[...] = jnp.zeros_like(gkey)
    gvalue[...] = jnp.zeros_like(gvalue)
    lane = lax.broadcasted_iota(jnp.int32, (tile, 128), 1)

    def block(index, query_sum):
        here = pl.ds(pl.multiple_of(index * tile, tile), tile)
        query = q_ref[here, :] * jnp.asarray(0.125, LOW)
        zero = jnp.zeros_like(query)
        queries = (jnp.where(lane < 64, query, zero), jnp.where(lane < 64, zero, query))
        grad = g_ref[here, :]
        grads = (jnp.where(lane < 64, grad, zero), jnp.where(lane < 64, zero, grad))
        totals = (total_ref[0, 0:1, here], total_ref[0, 1:2, here])
        segment = row[0:1, here]
        low, high = spans[index, 0], spans[index, 1]

        def first(step, dots):
            there = pl.ds(pl.multiple_of(step * tile, tile), tile)
            keys, values = k_ref[there, :], v_ref[there, :]
            same = col[there, :] == segment
            result = []
            part = None
            for head in range(2):
                logit = dot(keys, queries[head], ACROSS)
                prob = jnp.where(same, jnp.exp(logit - totals[head]), 0.0)
                gprob = dot(values, grads[head], ACROSS)
                probs[head, there, :] = prob
                gprobs[head, there, :] = gprob
                result.append(dots[head] + jnp.sum(prob * gprob, 0, keepdims=True))
                more = dot(prob.astype(LOW), grads[head])
                part = more if part is None else part + more
            gvalue[there, :] += part
            return tuple(result)

        none = jnp.zeros((1, tile), F32)
        dots = lax.fori_loop(low, high, first, (none, none))

        def second(step, state):
            there = pl.ds(pl.multiple_of(step * tile, tile), tile)
            result = []
            part = None
            for head in range(2):
                delta = probs[head, there, :] * (gprobs[head, there, :] - dots[head])
                delta = delta.astype(LOW)
                more = dot(delta, queries[head])
                part = more if part is None else part + more
                keys = flipped[64 * head : 64 * head + 64, there]
                result.append(state[head] + dot(keys, delta))
            gkey[there, :] += part
            return tuple(result)

        empty = jnp.zeros((64, tile), F32)
        both = lax.fori_loop(low, high, second, (empty, empty))
        whole = jnp.concatenate(both, 0).T * 0.125
        grad_ref[0, here, :] = whole.astype(LOW)
        return query_sum + jnp.sum(whole, 0, keepdims=True)

    count = q_ref.shape[0]
    query_sum = lax.fori_loop(0, count // tile, block, jnp.zeros((1, 128), F32))
    grad_ref[1] = gkey[...].astype(LOW)
    grad_ref[2] = gvalue[...].astype(LOW)
    sum_ref[...] = jnp.zeros_like(sum_ref)
    sum_ref[0:1, :] = query_sum
    sum_ref[1:2, :] = jnp.sum(gvalue[...], 0, keepdims=True)


def attend_backward(mixed, grad, total, spans, col, row, tile):
    count = mixed.shape[0]
    return pl.pallas_call(
        functools.partial(attend_back_kernel, tile),
        out_shape=(
            jax.ShapeDtypeStruct((3, count, D), LOW),
            jax.ShapeDtypeStruct((8, D), F32),
        ),
        grid_spec=pltpu.PrefetchScalarGridSpec(
            num_scalar_prefetch=1,
            grid=(6,),
            in_specs=[head_pair(count, third) for third in range(3)]
            + [
                head_pair(count, 0),
                pl.BlockSpec((1, 8, count), lambda h, s: (h, 0, 0)),
                pl.BlockSpec((count, tile), lambda h, s: (0, 0)),
                pl.BlockSpec((8, count), lambda h, s: (0, 0)),
            ],
            out_specs=[
                pl.BlockSpec((3, count, 128), lambda h, s: (0, 0, h)),
                pl.BlockSpec((8, 128), lambda h, s: (0, h)),
            ],
            scratch_shapes=[
                pltpu.VMEM((128, count), LOW),
                pltpu.VMEM((count, 128), F32),
                pltpu.VMEM((count, 128), F32),
                pltpu.VMEM((2, count, tile), F32),
                pltpu.VMEM((2, count, tile), F32),
            ],
        ),
        compiler_params=pltpu.CompilerParams(vmem_limit_bytes=48 << 20),
        cost_estimate=pl.CostEstimate(
            flops=20 * count * count * D,
            transcendentals=12 * count * count,
            bytes_accessed=16 * count * D,
        ),
    )(spans, mixed, mixed, mixed, grad, total, col, row)


def segment_tables(segment, tile):
    count = segment.shape[0]
    ends = segment.reshape(count // tile, tile)
    first = jnp.sum((segment[None, :] < ends[:, :1]).astype(jnp.int32), 1)
    last = jnp.sum((segment[None, :] <= ends[:, -1:]).astype(jnp.int32), 1)
    return (
        jnp.stack([first // tile, (last + tile - 1) // tile], 1),
        jnp.broadcast_to(segment[:, None], (count, tile)),
        jnp.broadcast_to(segment[None, :], (8, count)),
    )


def split_low(value):
    high = value.astype(LOW)
    return high, (value - high.astype(F32)).astype(LOW)


def sharp(cosine):
    return jnp.exp(cosine * 10.0 - 10.0)


def score_kernel(query_ref, passage_ref, member_ref, score_ref, sums_ref):
    high, rest = split_low(sharp(dot(query_ref[...], passage_ref[...], ACROSS)))
    sums = dot(high, member_ref[...]) + dot(rest, member_ref[...])
    sums_ref[...] = sums
    lane = lax.broadcasted_iota(jnp.int32, sums.shape, 1)
    soft = jnp.where(lane < PPB, 0.1 * jnp.log(jnp.where(lane < PPB, sums, 1.0)) + 1.0, 0.0)
    score_ref[...] = jnp.sum(soft.reshape(-1, QLEN, 128), 1)


def score_ratio(grad_ref, sums_ref):
    rows = sums_ref.shape[0]
    lane = lax.broadcasted_iota(jnp.int32, (rows, 128), 1)
    grads = jnp.broadcast_to(grad_ref[...][:, None, :], (rows // QLEN, QLEN, 128))
    ratio = grads.reshape(rows, 128) / jnp.where(lane % 64 < PPB, sums_ref[...], 1.0)
    high, rest = split_low(ratio)
    return jnp.where(lane < 64, high, rest)


def score_query_kernel(query_ref, passage_ref, member_ref, grad_ref, sums_ref, out_ref):
    ratio = score_ratio(grad_ref, sums_ref)
    terms = sharp(dot(query_ref[...], passage_ref[...], ACROSS))
    terms = (terms * dot(ratio, member_ref[...], ACROSS)).astype(LOW)
    out_ref[...] = dot(terms, passage_ref[...])


def score_passage_kernel(query_ref, passage_ref, member_ref, grad_ref, sums_ref, out_ref):
    @pl.when(pl.program_id(0) == 0)
    def _():
        out_ref[...] = jnp.zeros_like(out_ref)

    ratio = score_ratio(grad_ref, sums_ref)
    terms = sharp(dot(passage_ref[...], query_ref[...], ACROSS))
    terms = (terms * dot(member_ref[...], ratio, ACROSS)).astype(LOW)
    out_ref[...] += dot(terms, query_ref[...])


SCORE_ROWS = 512


def score_call(kernel, inputs, in_specs, out_specs, out_shape, flops):
    return pl.pallas_call(
        kernel,
        grid=(inputs[0].shape[0] // SCORE_ROWS,),
        in_specs=in_specs,
        out_specs=out_specs,
        out_shape=out_shape,
        compiler_params=pltpu.CompilerParams(vmem_limit_bytes=40 << 20),
        cost_estimate=pl.CostEstimate(
            flops=flops,
            transcendentals=inputs[0].shape[0] * BIN,
            bytes_accessed=inputs[0].shape[0] * 1024,
        ),
    )(*inputs)


def score_specs():
    rows = SCORE_ROWS
    fixed = pl.BlockSpec((BIN, 128), lambda i: (0, 0))
    return (
        pl.BlockSpec((rows, 128), lambda i: (i, 0)),
        fixed,
        pl.BlockSpec((rows // QLEN, 128), lambda i: (i, 0)),
    )


def score_forward(queries, passages, member):
    rows, fixed, grads = score_specs()
    count = queries.shape[0]
    return score_call(
        score_kernel,
        (queries, passages, member),
        [rows, fixed, fixed],
        [grads, rows],
        [
            jax.ShapeDtypeStruct((count // QLEN, 128), F32),
            jax.ShapeDtypeStruct((count, 128), F32),
        ],
        6 * count * BIN * 128,
    )


def score_backward(queries, passages, member, grad_scores, sums):
    rows, fixed, grads = score_specs()
    count = queries.shape[0]
    inputs = (queries, passages, member, grad_scores, sums)
    in_specs = [rows, fixed, fixed, grads, rows]
    flops = 6 * count * BIN * 128
    out = jax.ShapeDtypeStruct((count, 128), F32)
    grad_queries = score_call(score_query_kernel, inputs, in_specs, rows, out, flops)
    out = jax.ShapeDtypeStruct((BIN, 128), F32)
    grad_passages = score_call(score_passage_kernel, inputs, in_specs, fixed, out, flops)
    return grad_queries, grad_passages


def encode_forward(tokens, tables, tile, rows, weights):
    qkv_matrix, out_matrix, up_matrix, down_matrix, proj_matrix, vectors, wide = weights
    count = tokens.shape[0]
    bias_qkv = jnp.concatenate([vectors[0], jnp.zeros_like(vectors[0]), vectors[1]])
    mixed = (dot(tokens, qkv_matrix) + bias_qkv).astype(LOW)
    attended, total = attend_forward(mixed, *tables, tile)
    resid, normed, active, slope = row_call(
        widen_kernel,
        count,
        rows,
        (tokens, attended),
        (out_matrix, up_matrix, vectors, wide),
        [(D, F32), (D, LOW), (4 * D, LOW), (4 * D, LOW)],
        flops=10 * count * D * D,
    )
    two, normed_out, projected, unit = row_call(
        narrow_kernel,
        count,
        rows,
        (active, resid),
        (down_matrix, proj_matrix, vectors),
        [(D, F32), (D, LOW), (128, F32), (128, LOW)],
        flops=8 * count * D * D,
    )
    kept = (tokens, mixed, total, attended, resid, normed, active, slope, two, normed_out, projected)
    return unit, kept


def encode_backward(tables, tile, rows, weights, kept, grad_unit):
    qkv_matrix, out_matrix, up_matrix, down_matrix, proj_matrix, vectors, wide = weights
    tokens, mixed, total, attended, resid, normed, active, slope, two, normed_out, projected = kept
    count = tokens.shape[0]
    gproj, gtwo, ghid, gone, gatt, sums, wide_sums = row_call(
        back_kernel,
        count,
        rows,
        (grad_unit, projected, two, slope, resid),
        (proj_matrix, down_matrix, up_matrix, out_matrix, vectors),
        [(128, LOW), (D, LOW), (4 * D, LOW), (D, LOW), (D, LOW)],
        (D, 4 * D),
        flops=18 * count * D * D,
    )
    gmixed, attend_sums = attend_backward(mixed, gatt, total, *tables, tile)
    vector_grad = jnp.concatenate(
        [attend_sums[:2], sums[:3], wide_sums[:1].reshape(4, D), sums[3:6]], 0
    )
    pairs = (
        (tokens, gmixed),
        (attended, gone),
        (normed, ghid),
        (active, gtwo),
        (normed_out, gproj),
    )
    return pairs, vector_grad


def cross_grad(scores, partition, passage_ids, chosen_ids, query_total):
    onehot = (passage_ids[None, :] == chosen_ids[:, None]).astype(jnp.float32)
    return (jnp.exp(scores) / partition[:, None] - onehot) / query_total


def adam_update(weight, moment_one, moment_two, gradient, factor, rate):
    clipped = gradient * factor
    new_one = beta_one * moment_one + (1.0 - beta_one) * clipped
    new_two = beta_two * moment_two + (1.0 - beta_two) * clipped * clipped
    direction = (
        new_one / (1.0 - beta_one**STEP) / (jnp.sqrt(new_two / (1.0 - beta_two**STEP)) + adam_eps)
    )
    return (weight - rate * (direction + decay_rate * weight), new_one, new_two)


def body(
    query_tokens,
    passage_tokens,
    passage_lengths,
    positives,
    qkv_weight,
    qkv_first,
    qkv_second,
    out_weight,
    out_first,
    out_second,
    up_weight,
    up_first,
    up_second,
    down_weight,
    down_first,
    down_second,
    proj_weight,
    proj_first,
    proj_second,
    vector_params,
    vector_first,
    vector_second,
):
    low = jnp.bfloat16
    vector_part = jnp.pad(vector_params.T, ((0, 0), (0, 116))).astype(low)
    qkv_matrix, vectors = gather_rows(
        jnp.concatenate([qkv_weight.astype(low), vector_part], 1), [(0, 2304), (2304, 2432)]
    )
    up_matrix, out_matrix, proj_matrix = gather_rows(
        jnp.concatenate([up_weight, out_weight, proj_weight], 1).astype(low),
        [(0, 3072), (3072, 3840), (3840, 3968)],
    )
    (down_matrix,) = gather_rows(down_weight.astype(low), [(0, 768)])
    weights = (
        qkv_matrix,
        out_matrix,
        up_matrix,
        down_matrix,
        proj_matrix,
        vectors[:, :12].T.astype(F32),
        vectors[:, 5:9].T.astype(F32).reshape(1, 4 * D),
    )
    own_index = lax.axis_index(("pb", "pa"))
    query_total = QPD * lax.axis_size(("pb", "pa"))
    query_flat = query_tokens.reshape(QPD * QLEN, D)
    query_tables = segment_tables(jnp.arange(QPD * QLEN, dtype=jnp.int32) // QLEN, QPD * QLEN)
    own_lengths = lax.dynamic_index_in_dim(passage_lengths, own_index, 0, keepdims=False)
    ends = jnp.cumsum(own_lengths)
    places = jnp.arange(BIN, dtype=jnp.int32)
    own_seg = jnp.sum((places[:, None] >= ends[None, :]).astype(jnp.int32), 1)
    passage_tables = segment_tables(own_seg, ATTEND_TILE)
    member = (own_seg[:, None] == jnp.arange(128, dtype=jnp.int32)[None, :] % 64).astype(low)
    query_unit, query_kept = encode_forward(
        query_flat, query_tables, QPD * QLEN, QPD * QLEN, weights
    )
    passage_unit, passage_kept = encode_forward(
        passage_tokens[0], passage_tables, ATTEND_TILE, FEED_ROWS, weights
    )
    (every_query,) = gather_rows(query_unit, [(0, 128)])
    passage_ids = own_index * PPB + jnp.arange(PPB, dtype=jnp.int32)
    scores, totals = score_forward(every_query, passage_unit, member)
    scores = scores[:, :PPB]
    partition = sum_everywhere(jnp.sum(jnp.exp(scores), 1))
    grad_scores = cross_grad(scores, partition, passage_ids, positives, query_total)
    grad_scores = jnp.tile(jnp.pad(grad_scores, ((0, 0), (0, 64 - PPB))), (1, 2))
    grad_every, grad_passage = score_backward(
        every_query, passage_unit, member, grad_scores, totals
    )
    grad_query = scatter_rows(grad_every)
    query_pairs, query_vector = encode_backward(
        query_tables, QPD * QLEN, QPD * QLEN, weights, query_kept, grad_query
    )
    passage_pairs, passage_vector = encode_backward(
        passage_tables, ATTEND_TILE, BACK_ROWS, weights, passage_kept, grad_passage
    )

    def weight_terms(index):
        (left, right), (left_more, right_more) = passage_pairs[index], query_pairs[index]
        left = jnp.concatenate([left, left_more], 0)
        right = jnp.concatenate([right, right_more], -2)
        if index == 0:
            return jnp.einsum("td,itk->dik", left, right, preferred_element_type=F32).reshape(
                D, 3 * D
            )
        return dot(left, right, (((0,), (0,)), ((), ())))

    down_sum = scatter_rows(weight_terms(3))
    proj_terms = weight_terms(4)
    proj_high = proj_terms.astype(low)
    proj_rest = (proj_terms - proj_high.astype(F32)).astype(low)
    middle = scatter_rows(
        jnp.concatenate(
            [weight_terms(2).astype(low), weight_terms(1).astype(low), proj_high, proj_rest], 1
        )
    )
    vector_terms = jnp.pad((query_vector + passage_vector).T, ((0, 0), (0, 116)))
    first = scatter_rows(
        jnp.concatenate([weight_terms(0).astype(low), vector_terms.astype(low)], 1)
    )
    reduced = (
        first[:, :2304],
        middle[:, 3072:3840],
        middle[:, :3072],
        down_sum,
        middle[:, 3840:3968] + middle[:, 3968:],
        first[:, 2304:2316].T,
    )
    square = sum((jnp.sum(gradient * gradient) for gradient in reduced))
    norm_value = jnp.sqrt(sum_everywhere(jnp.full((1, 128), square))[0, 0])
    factor = jnp.minimum(1.0, clip_max / (norm_value + 1e-06))
    qkv_res = adam_update(qkv_weight, qkv_first, qkv_second, reduced[0], factor, learn_rate)
    out_res = adam_update(out_weight, out_first, out_second, reduced[1], factor, learn_rate)
    up_res = adam_update(up_weight, up_first, up_second, reduced[2], factor, learn_rate)
    down_res = adam_update(down_weight, down_first, down_second, reduced[3], factor, learn_rate)
    proj_res = adam_update(proj_weight, proj_first, proj_second, reduced[4], factor, learn_rate)
    vector_res = adam_update(
        vector_params, vector_first, vector_second, reduced[5], factor, vector_rate
    )
    return (
        norm_value,
        qkv_res[0],
        qkv_res[1],
        qkv_res[2],
        out_res[0],
        out_res[1],
        out_res[2],
        up_res[0],
        up_res[1],
        up_res[2],
        down_res[0],
        down_res[1],
        down_res[2],
        proj_res[0],
        proj_res[1],
        proj_res[2],
        vector_res[0],
        vector_res[1],
        vector_res[2],
    )


def solution(mesh):
    placed = (
        P(("pb", "pa"), None, None),
        P(("pb", "pa"), None, None),
        P(),
        P(),
        P(("pb", "pa"), None),
        P(("pb", "pa"), None),
        P(("pb", "pa"), None),
        P(("pb", "pa"), None),
        P(("pb", "pa"), None),
        P(("pb", "pa"), None),
        P(("pb", "pa"), None),
        P(("pb", "pa"), None),
        P(("pb", "pa"), None),
        P(("pb", "pa"), None),
        P(("pb", "pa"), None),
        P(("pb", "pa"), None),
        P(("pb", "pa"), None),
        P(("pb", "pa"), None),
        P(("pb", "pa"), None),
        P(None, ("pb", "pa")),
        P(None, ("pb", "pa")),
        P(None, ("pb", "pa")),
    )
    return jax.shard_map(
        body,
        mesh=mesh,
        in_specs=placed,
        out_specs=(
            P(),
            P(("pb", "pa"), None),
            P(("pb", "pa"), None),
            P(("pb", "pa"), None),
            P(("pb", "pa"), None),
            P(("pb", "pa"), None),
            P(("pb", "pa"), None),
            P(("pb", "pa"), None),
            P(("pb", "pa"), None),
            P(("pb", "pa"), None),
            P(("pb", "pa"), None),
            P(("pb", "pa"), None),
            P(("pb", "pa"), None),
            P(("pb", "pa"), None),
            P(("pb", "pa"), None),
            P(("pb", "pa"), None),
            P(None, ("pb", "pa")),
            P(None, ("pb", "pa")),
            P(None, ("pb", "pa")),
        ),
        check_vma=False,
    )
```

time: 1560 us -> 557 us (0.36)
  matrix products: 533 us -> 38.8 us
  waiting for transfers between devices: 464 us -> 107 us
  blocking collectives: 349 us -> 0 us
  Pallas kernels: 0 us -> 194 us
  starting transfers between devices: 0.46 us -> 85.9 us
  other arithmetic: 91.5 us -> 58.3 us
  local copies, waits for them, and re-layouts: 85.6 us -> 54 us
    dot_general x53 -> x7, matrix products: 533 us -> 38.8 us  [the longest x6 29.7 us: dot(): return lax.dot_general(left, right, dims, preferred_element_type=F32)]
    reduce_scatter x5 -> x0, waiting for transfers between devices: 463 us -> none  [the longest x1 139 us: body(): lax.psum_scatter(local_sums[3], ('pb', 'pa'), scatter_dimension=0, tiled=...]
    all_gather x4 -> x0, blocking collectives: 269 us -> none  [the longest x2 128 us: merged(): gathered = jax.tree.map(lambda a: lax.all_gather(a, axis), part)]
    pallas_call x0 -> x13, Pallas kernels: none -> 194 us  [the longest x6 75 us: row_call(): pl.pallas_call(kernel, grid=(count // rows,), in_specs=[row_block(rows, a...]
    ppermute x0 -> x48, waiting for transfers between devices: none -> 97.7 us  [the longest x4 25 us: gather_rows(): pair = in_order(first_bit, line, lax.ppermute(line, 'pb', FIRST_STEP))]
    ppermute x0 -> x48, starting transfers between devices: none -> 77.5 us  [the longest x12 27.6 us: gather_rows(): moved = [lax.ppermute(part, 'pa', shift_pairs(k)) for k in (1, 2, 3)]]
    reduce_sum x22 -> x6, other arithmetic: 49 us -> 2.39 us  [the longest x2 2.16 us: segment_tables(): first = jnp.sum((segment[None, :] < ends[:, :1]).astype(jnp.int32), 1)]
    unnamed x1 -> x0, blocking collectives: 40 us -> none
  transfers between devices with their start and end apart: 11 -> 50, of which waited for: 4 -> 26; matrix products, arithmetic and copies ran while one was open for 40% -> 16% of each run, Pallas kernels for 0% -> 25%
where the time goes in v1:
time: 557 us; the launch traced here: 549 us
  Pallas kernels  194 us (35%)
  waiting for transfers between devices  107 us (19%)
  starting transfers between devices  85.9 us (15%)
  other arithmetic  58.3 us (10%)
  local copies, waits for them, and re-layouts  54 us (10%)
  matrix products  38.8 us (7%)
  between operations  10.8 us (2%)
    pallas_call x6, Pallas kernels, row_call(): pl.pallas_call(kernel, grid=(count // rows,), in_specs=[row_block(rows, a...  75 us
    pallas_call x2, Pallas kernels, attend_backward(): pl.pallas_call(functools.partial(attend_back_kernel, tile), out_shape=(ja...  57.8 us
    pallas_call x2, Pallas kernels, attend_forward(): pl.pallas_call(functools.partial(attend_kernel, tile), out_shape=(jax.Sha...  31.2 us
    pallas_call x3, Pallas kernels, score_call(): pl.pallas_call(kernel, grid=(inputs[0].shape[0] // SCORE_ROWS,), in_specs...  29.9 us
    dot_general x6, matrix products, dot(): return lax.dot_general(left, right, dims, preferred_element_type=F32)  29.7 us
    unnamed x137, local copies, waits for them, and re-layouts  28.2 us
    ppermute x12, starting transfers between devices, gather_rows(): moved = [lax.ppermute(part, 'pa', shift_pairs(k)) for k in (1, 2, 3)]  27.6 us
    ppermute x4, waiting for transfers between devices, gather_rows(): pair = in_order(first_bit, line, lax.ppermute(line, 'pb', FIRST_STEP))  25 us
  transfers between devices with their start and end apart: 50, of which 26 were waited for; matrix products, arithmetic and copies ran while one was open for 16% of the time, Pallas kernels for 25%

profile of v1, /device:TPU:0, one launch (start us, length us, event | category | flops | bytes accessed | tf_op | source)
XLA Modules:
  0.0 548.6 jit_solution(16129621863290079124)
XLA Ops:
  3.3 5.1 collective-permute-start.6
  25.1 6.1 %collective-permute-done.1 = bf16[24,2432]{1,0:T(8,128)(2,1)S(1)} collective-permute-done((bf16[24,2432]{1,0:T(8,128)(2,1)S(1)}, bf16[24,2432]{1,0:T(8,128)(2,1)S(1)}, u32[]{:S(2)}, u32[]{:S(2)}) %collective-permute-start.1) | collective-permute-done | bytes 116768 | tf_op jit(solution)/shard_map/ppermute | solution.py:67
  31.2 8.3 %collective-permute-start.14 = (bf16[96,768]{1,0:T(8,128)(2,1)S(1)}, bf16[96,768]{1,0:T(8,128)(2,1)S(1)}, u32[]{:S(2)}, u32[]{:S(2)}) collective-permute-start(bf16[96,768]{1,0:T(8,128)(2,1)S(1)} %convert_element_type.299), channel_id=1, source_target_pairs={{0,1},{1,2},{2,3},{3,0},{4,5},{5,6},{6,7},{7,4},{8,9},{9,10},{10,1... | collective-permute-start | bytes 442376 | tf_op jit(solution)/shard_map/ppermute | solution.py:67
  42.9 2.7 collective-permute-done.14
  51.8 10.5 %collective-permute-done.15 = bf16[4,96,768]{2,1,0:T(8,128)(2,1)S(1)} collective-permute-done((bf16[4,96,768]{2,1,0:T(8,128)(2,1)S(1)}, bf16[4,96,768]{2,1,0:T(8,128)(2,1)S(1)}, u32[]{:S(2)}, u32[]{:S(2)}) %collective-permute-start.15) | collective-permute-done | bytes 589856 | tf_op jit(solution)/shard_map/ppermute | solution.py:70
  64.4 14.2 %collective-permute-done.9 = bf16[4,24,3968]{2,1,0:T(8,128)(2,1)S(1)} collective-permute-done((bf16[4,24,3968]{2,1,0:T(8,128)(2,1)S(1)}, bf16[4,24,3968]{2,1,0:T(8,128)(2,1)S(1)}, u32[]{:S(2)}, u32[]{:S(2)}) %collective-permute-start.9) | collective-permute-done | bytes 761888 | tf_op jit(solution)/shard_map/ppermute | solution.py:70
  84.4 3.3 collective-permute-start.17
  87.7 12.7 %collective-permute-done.10 = bf16[2,4,24,3968]{3,2,1,0:T(8,128)(2,1)S(1)} collective-permute-done((bf16[2,4,24,3968]{3,2,1,0:T(8,128)(2,1)S(1)}, bf16[2,4,24,3968]{3,2,1,0:T(8,128)(2,1)S(1)}, u32[]{:S(2)}, u32[]{:S(2)}) %collective-permute-start.10) | collective-permute-done | bytes 1523744 | tf_op jit(solution)/shard_map/ppermute | solution.py:71
  101.2 3.0 collective-permute-start.11
  108.6 2.7 copy.551
  113.3 2.9 fusion.26
  126.3 3.9 shard_map.357
  130.9 5.8 %shard_map.358 = (f32[128,768]{1,0:T(8,128)}, bf16[128,768]{1,0:T(8,128)(2,1)}, bf16[128,3072]{1,0:T(8,128)(2,1)}, bf16[128,3072]{1,0:T(8,128)(2,1)}) custom-call(bf16[128,768]{1,0:T(8,128)(2,1)} %bitcast.349, bf16[128,768]{1,0:T(8,128)(2,1)} %copy-done.4, bf16[768,768]{1,0:T(8,128)(2,1)} %bitcast.338, bf16[768,3072]{1,0:T(8,128)(2,1)} %bitcast.326, ...), custom_call_target="tpu_custom_call" | custom-call | flops 754974720 | bytes 8503296 | tf_op jit(solution)/shard_map/pallas_call | solution.py:165
  136.7 4.8 shard_map.359
  141.6 5.1 collective-permute-start.18
  148.6 3.1 collective-permute-done.19
  155.0 6.5 %fusion.16.q_ref.k_ref.v_ref = bf16[1024,2304]{1,0:T(8,128)(2,1)S(1)} fusion(bf16[768,2304]{1,0:T(8,128)(2,1)} %bitcast.337, f32[2304]{0:T(1024)S(1)} %pad_maximum_fusion.21, bf16[1,1024,768]{2,1,0:T(8,128)(2,1)S(1)} %copy-done.48), kind=kOutput, calls=%fused_computation.18 | convolution fusion | flops 3628597248 | bytes 9839616 | tf_op jit(solution)/shard_map/dot_general | solution.py:129
  163.4 27.3 %shard_map.360 = (bf16[1024,768]{1,0:T(8,128)(2,1)S(1)}, f32[6,8,1024]{2,1,0:T(8,128)S(1)}) custom-call(s32[2,2]{1,0:T(2,128)S(1)} %pad_add_fusion.spans, bf16[1024,2304]{1,0:T(8,128)(2,1)S(1)} %fusion.16.q_ref.k_ref.v_ref, bf16[1024,2304]{1,0:T(8,128)(2,1)S(1)} %fusion.16.q_ref.k_ref.v_ref, bf16[1024,2304]{1,0:T(8,128)(2,1)S(1)} %fusion.16.q_ref.k_ref.v_ref, ...), custom_call_target="tpu_custom_call" | custom-call | flops 6442450944 | bytes 6291456 | tf_op jit(solution)/shard_map/pallas_call | solution.py:299
  192.8 17.4 %shard_map.361 = (f32[1024,768]{1,0:T(8,128)}, bf16[1024,768]{1,0:T(8,128)(2,1)}, bf16[1024,3072]{1,0:T(8,128)(2,1)}, bf16[1024,3072]{1,0:T(8,128)(2,1)}) custom-call(bf16[1024,768]{1,0:T(8,128)(2,1)} %bitcast.362, bf16[1024,768]{1,0:T(8,128)(2,1)} %copy-done.10, bf16[768,768]{1,0:T(8,128)(2,1)} %bitcast.339, bf16[768,3072]{1,0:T(8,128)(2,1)} %bitcast.327, ...), custom_call_target="tpu_custom_call" | custom-call | flops 6039797760 | bytes 26394624 | tf_op jit(solution)/shard_map/pallas_call | solution.py:165
  210.2 12.3 %shard_map.362 = (f32[1024,768]{1,0:T(8,128)}, bf16[1024,768]{1,0:T(8,128)(2,1)}, f32[1024,128]{1,0:T(8,128)}, bf16[1024,128]{1,0:T(8,128)(2,1)}) custom-call(bf16[1024,3072]{1,0:T(8,128)(2,1)} %get-tuple-element.64.act_ref, f32[1024,768]{1,0:T(8,128)} %get-tuple-element.65.resid_ref, bf16[3072,768]{1,0:T(8,128)(2,1)} %bitcast.323, ...), custom_call_target="tpu_custom_call" | custom-call | flops 4831838208 | bytes 19894272 | tf_op jit(solution)/shard_map/pallas_call | solution.py:165
  223.7 11.3 %shard_map.363 = (f32[128,128]{1,0:T(8,128)S(1)}, f32[4096,128]{1,0:T(8,128)S(1)}) custom-call(bf16[4096,128]{1,0:T(8,128)(2,1)S(1)} %bitcast.317, bf16[1024,128]{1,0:T(8,128)(2,1)S(1)} %copy-done.12, bf16[1024,128]{1,0:T(8,128)(2,1)S(1)} %compare_convert_fusion.member_ref), custom_call_target="tpu_custom_call" | custom-call | flops 3221225472 | bytes 4194304 | tf_op jit(solution)/shard_map/pallas_call | solution.py:495
  239.7 7.0 %all-to-all-done = f32[32,1,128]{2,1,0:T(1,128)S(1)} async-done(((f32[32,1,128]{2,1,0:T(1,128)}), f32[32,1,128]{2,1,0:T(1,128)S(1)}, u32[]{:S(2)}, u32[]{:S(2)}) %all-to-all-start) | async-done | bytes 16416 | tf_op jit(solution)/shard_map/all_to_all | solution.py:119
  249.8 10.0 %shard_map.367 = f32[4096,128]{1,0:T(8,128)S(1)} custom-call(bf16[4096,128]{1,0:T(8,128)(2,1)S(1)} %bitcast.318, bf16[1024,128]{1,0:T(8,128)(2,1)S(1)} %copy-done.12, bf16[1024,128]{1,0:T(8,128)(2,1)S(1)} %compare_convert_fusion.member_ref, f32[128,128]{1,0:T(8,128)S(1)} %copy.563.grad_ref, f32[4096,128]{1,0:T(8,128)S(1)} %copy-done.9), custom_call_target="tpu_custom_call" | custom-call | flops 3221225472 | bytes 4194304 | tf_op jit(solution)/shard_map/pallas_call | solution.py:495
  259.9 8.6 %shard_map.364.grad_ref = f32[1024,128]{1,0:T(8,128)S(1)} custom-call(bf16[4096,128]{1,0:T(8,128)(2,1)S(1)} %bitcast.319, bf16[1024,128]{1,0:T(8,128)(2,1)S(1)} %copy-done.12, bf16[1024,128]{1,0:T(8,128)(2,1)S(1)} %compare_convert_fusion.member_ref, f32[128,128]{1,0:T(8,128)S(1)} %copy.563.grad_ref, f32[4096,128]{1,0:T(8,128)S(1)} %copy-done.9), custom_call_target="tpu_custom_call" | custom-call | flops 3221225472 | bytes 4194304 | tf_op jit(solution)/shard_map/pallas_call | solution.py:495
  269.3 24.9 %shard_map.365 = (bf16[1024,128]{1,0:T(8,128)(2,1)}, bf16[1024,768]{1,0:T(8,128)(2,1)}, bf16[1024,3072]{1,0:T(8,128)(2,1)}, bf16[1024,768]{1,0:T(8,128)(2,1)}, b...) custom-call(f32[1024,128]{1,0:T(8,128)} %copy-done.13, f32[1024,128]{1,0:T(8,128)} %get-tuple-element.69.proj_ref, ...), custom_call_target="tpu_custom_call" | custom-call | flops 10871635968 | bytes 35753984 | tf_op jit(solution)/shard_map/pallas_call | solution.py:165
  296.3 52.6 %shard_map.366 = (bf16[3,1024,768]{2,1,0:T(8,128)(2,1)}, f32[8,768]{1,0:T(8,128)S(1)}) custom-call(s32[2,2]{1,0:T(2,128)S(1)} %pad_add_fusion.spans, bf16[1024,2304]{1,0:T(8,128)(2,1)} %copy-done.7, bf16[1024,2304]{1,0:T(8,128)(2,1)} %copy-done.7, bf16[1024,2304]{1,0:T(8,128)(2,1)} %copy-done.7, bf16[1024,768]{1,0:T(8,128)(2,1)S(1)} %copy-done.14, ...), custom_call_target="tpu_custom_call" | custom-call | flops 16106127360 | bytes 12582912 | tf_op jit(solution)/shard_map/pallas_call | solution.py:397
  349.6 4.4 collective-permute-done.26
  355.2 2.8 collective-permute-start.29
  361.1 9.8 %shard_map.368 = (bf16[128,128]{1,0:T(8,128)(2,1)}, bf16[128,768]{1,0:T(8,128)(2,1)}, bf16[128,3072]{1,0:T(8,128)(2,1)}, bf16[128,768]{1,0:T(8,128)(2,1)}, bf16[...) custom-call(f32[128,128]{1,0:T(8,128)} %fusion.94.grad_ref, f32[128,128]{1,0:T(8,128)} %get-tuple-element.75.proj_ref, ...), custom_call_target="tpu_custom_call" | custom-call | flops 1358954496 | bytes 13963264 | tf_op jit(solution)/shard_map/pallas_call | solution.py:165
  370.9 9.0 %fusion.5 = f32[3072,768]{1,0:T(8,128)S(1)} fusion(bf16[128,3072]{1,0:T(8,128)(2,1)S(1)} %copy-done.35, bf16[1024,3072]{1,0:T(8,128)(2,1)} %get-tuple-element.64.act_ref, bf16[128,768]{1,0:T(8,128)(2,1)} %get-tuple-element.98, bf16[1024,768]{1,0:T(8,128)(2,1)S(1)} %copy-done.59), kind=kOutput, calls=%fused_computation.7 | convolution fusion | flops 5453512704 | bytes 18284544 | tf_op jit(solution)/shard_map/dot_general | solution.py:129
  380.5 3.3 copy-done.19
  383.8 5.3 shard_map.369
  389.1 9.0 %fusion.20 = bf16[768,3,768]{0,2,1:T(8,128)(2,1)} fusion(bf16[3,128,768]{2,1,0:T(8,128)(2,1)S(1)} %get-tuple-element.80, bf16[3,1024,768]{2,1,0:T(8,128)(2,1)} %get-tuple-element.74, bf16[128,768]{1,0:T(8,128)(2,1)S(1)} %bitcast.351, bf16[1024,768]{1,0:T(8,128)(2,1)S(1)} %bitcast.363), kind=kOutput, calls=%fused_computation.43 | convolution fusion | flops 4092788736 | bytes 10616832 | tf_op jit(solution)/shard_map/td,itk->dik/dot_general | solution.py:702
  398.1 5.8 %copy.568 = bf16[768,2304]{1,0:T(8,128)(2,1)} copy(bf16[768,2304]{0,1:T(8,128)(2,1)} %bitcast.342) | data formatting | bytes 7077888 | tf_op jit(solution)/shard_map/convert_element_type | solution.py:718
  410.2 9.1 %fusion.13 = bf16[768,3072]{1,0:T(8,128)(2,1)S(1)} fusion(bf16[128,3072]{1,0:T(8,128)(2,1)S(1)} %copy-done.50, bf16[1024,3072]{1,0:T(8,128)(2,1)} %get-tuple-element.89, bf16[128,768]{1,0:T(8,128)(2,1)S(1)} %copy-done.52, bf16[1024,768]{1,0:T(8,128)(2,1)S(1)} %copy-done.58), kind=kOutput, calls=%fused_computation.17 | convolution fusion | flops 5455872000 | bytes 13565952 | tf_op jit(solution)/shard_map/dot_general | solution.py:129
  422.6 2.9 broadcast_select_fusion
  428.5 2.7 convert_add_fusion.1
  433.9 6.5 %collective-permute-done.31 = bf16[2,4,24,2432]{3,2,1,0:T(8,128)(2,1)S(1)} collective-permute-done((bf16[2,4,24,2432]{3,2,1,0:T(8,128)(2,1)S(1)}, bf16[2,4,24,2432]{3,2,1,0:T(8,128)(2,1)S(1)}, u32[]{:S(2)}, u32[]{:S(2)}) %collective-permute-start.31) | collective-permute-done | bytes 933920 | tf_op jit(solution)/shard_map/ppermute | solution.py:104
  442.7 2.9 convert_add_fusion
  450.9 4.9 collective-permute-done.32
  461.1 2.8 collective-permute-done.33
  464.3 2.8 collective-permute-done.34
  472.4 4.2 collective-permute-done.37
  483.3 4.8 collective-permute-start.46
  492.9 5.4 collective-permute-start.40
  503.6 7.9 %collective-permute-done.40 = bf16[24,4096]{1,0:T(8,128)(2,1)S(1)} collective-permute-done((bf16[24,4096]{1,0:T(8,128)(2,1)S(1)}, bf16[24,4096]{1,0:T(8,128)(2,1)S(1)}, u32[]{:S(2)}, u32[]{:S(2)}) %collective-permute-start.40) | collective-permute-done | bytes 196640 | tf_op jit(solution)/shard_map/ppermute | solution.py:111
  518.0 5.9 %all-to-all-start.1 = ((f32[32,1,128]{2,1,0:T(1,128)}), f32[32,1,128]{2,1,0:T(1,128)S(1)}, u32[]{:S(2)}, u32[]{:S(2)}) async-start(f32[32,1,128]{2,1,0:T(1,128)} %broadcast_in_dim_broadcast_in_dim_broadcast_in_dim.3), calls=%async_computation.1 | async-start | bytes 32768 | tf_op jit(solution)/shard_map/all_to_all | solution.py:119
  531.1 4.1 multiply_subtract_fusion
  (369 shorter events, 149.3 us)
Async XLA Ops:
  3.3 44.0 %collective-permute-start.6 = (bf16[24,3968]{1,0:T(8,128)(2,1)S(1)}, bf16[24,3968]{1,0:T(8,128)(2,1)S(1)}, u32[]{:S(2)}, u32[]{:S(2)}) collective-permute-start(bf16[24,3968]{1,0:T(8,128)(2,1)S(1)} %pad_maximum_fusion.19), channel_id=1, source_target_pairs={{0,3},{1,0},{2,1},{3,2},{4,7},{5,4},{6,5},{7,6},{8,11},{9,8},{10,9... | collective-permute-start | bytes 571400 | tf_op jit(solution)/shard_map/ppermute | solution.py:67
  8.4 38.9 %collective-permute-start.7 = (bf16[24,3968]{1,0:T(8,128)(2,1)S(1)}, bf16[24,3968]{1,0:T(8,128)(2,1)S(1)}, u32[]{:S(2)}, u32[]{:S(2)}) collective-permute-start(bf16[24,3968]{1,0:T(8,128)(2,1)S(1)} %pad_maximum_fusion.19), channel_id=1, source_target_pairs={{0,2},{1,3},{2,0},{3,1},{4,6},{5,7},{6,4},{7,5},{8,10},{9,11},{10,... | collective-permute-start | bytes 571400 | tf_op jit(solution)/shard_map/ppermute | solution.py:67
  10.2 12.9 %collective-permute-start = (bf16[24,2432]{1,0:T(8,128)(2,1)S(1)}, bf16[24,2432]{1,0:T(8,128)(2,1)S(1)}, u32[]{:S(2)}, u32[]{:S(2)}) collective-permute-start(bf16[24,2432]{1,0:T(8,128)(2,1)S(1)} %fusion.82), channel_id=1, source_target_pairs={{0,3},{1,0},{2,1},{3,2},{4,7},{5,4},{6,5},{7,6},{8,11},{9,8},{10,9... | collective-permute-start | bytes 350216 | tf_op jit(solution)/shard_map/ppermute | solution.py:67
  10.7 20.4 %collective-permute-start.1 = (bf16[24,2432]{1,0:T(8,128)(2,1)S(1)}, bf16[24,2432]{1,0:T(8,128)(2,1)S(1)}, u32[]{:S(2)}, u32[]{:S(2)}) collective-permute-start(bf16[24,2432]{1,0:T(8,128)(2,1)S(1)} %fusion.82), channel_id=1, source_target_pairs={{0,2},{1,3},{2,0},{3,1},{4,6},{5,7},{6,4},{7,5},{8,10},{9,11},{10,... | collective-permute-start | bytes 350216 | tf_op jit(solution)/shard_map/ppermute | solution.py:67
  13.3 17.9 %collective-permute-start.2 = (bf16[24,2432]{1,0:T(8,128)(2,1)S(1)}, bf16[24,2432]{1,0:T(8,128)(2,1)S(1)}, u32[]{:S(2)}, u32[]{:S(2)}) collective-permute-start(bf16[24,2432]{1,0:T(8,128)(2,1)S(1)} %fusion.82), channel_id=1, source_target_pairs={{0,1},{1,2},{2,3},{3,0},{4,5},{5,6},{6,7},{7,4},{8,9},{9,10},{10,1... | collective-permute-start | bytes 350216 | tf_op jit(solution)/shard_map/ppermute | solution.py:67
  23.1 16.6 %collective-permute-start.12 = (bf16[96,768]{1,0:T(8,128)(2,1)S(1)}, bf16[96,768]{1,0:T(8,128)(2,1)S(1)}, u32[]{:S(2)}, u32[]{:S(2)}) collective-permute-start(bf16[96,768]{1,0:T(8,128)(2,1)S(1)} %convert_element_type.299), channel_id=1, source_target_pairs={{0,3},{1,0},{2,1},{3,2},{4,7},{5,4},{6,5},{7,6},{8,11},{9,8},{10,9... | collective-permute-start | bytes 442376 | tf_op jit(solution)/shard_map/ppermute | solution.py:67
  31.2 10.2 %collective-permute-start.13 = (bf16[96,768]{1,0:T(8,128)(2,1)S(1)}, bf16[96,768]{1,0:T(8,128)(2,1)S(1)}, u32[]{:S(2)}, u32[]{:S(2)}) collective-permute-start(bf16[96,768]{1,0:T(8,128)(2,1)S(1)} %convert_element_type.299), channel_id=1, source_target_pairs={{0,2},{1,3},{2,0},{3,1},{4,6},{5,7},{6,4},{7,5},{8,10},{9,11},{10,... | collective-permute-start | bytes 442376 | tf_op jit(solution)/shard_map/ppermute | solution.py:67
  31.2 14.5 %collective-permute-start.14 = (bf16[96,768]{1,0:T(8,128)(2,1)S(1)}, bf16[96,768]{1,0:T(8,128)(2,1)S(1)}, u32[]{:S(2)}, u32[]{:S(2)}) collective-permute-start(bf16[96,768]{1,0:T(8,128)(2,1)S(1)} %convert_element_type.299), channel_id=1, source_target_pairs={{0,1},{1,2},{2,3},{3,0},{4,5},{5,6},{6,7},{7,4},{8,9},{9,10},{10,1... | collective-permute-start | bytes 442376 | tf_op jit(solution)/shard_map/ppermute | solution.py:67
  39.7 7.9 %collective-permute-start.8 = (bf16[24,3968]{1,0:T(8,128)(2,1)S(1)}, bf16[24,3968]{1,0:T(8,128)(2,1)S(1)}, u32[]{:S(2)}, u32[]{:S(2)}) collective-permute-start(bf16[24,3968]{1,0:T(8,128)(2,1)S(1)} %pad_maximum_fusion.19), channel_id=1, source_target_pairs={{0,1},{1,2},{2,3},{3,0},{4,5},{5,6},{6,7},{7,4},{8,9},{9,10},{10,1... | collective-permute-start | bytes 571400 | tf_op jit(solution)/shard_map/ppermute | solution.py:67
  41.4 8.6 %collective-permute-start.3 = (bf16[4,24,2432]{2,1,0:T(8,128)(2,1)S(1)}, bf16[4,24,2432]{2,1,0:T(8,128)(2,1)S(1)}, u32[]{:S(2)}, u32[]{:S(2)}) collective-permute-start(bf16[4,24,2432]{2,1,0:T(8,128)(2,1)S(1)} %pad_maximum_fusion.15), channel_id=1, source_target_pairs={{0,8},{4,20},{8,0},{12,28},{16,24},{20,4},{24,16},{28,12},{1,9},{5... | collective-permute-start | bytes 1400840 | tf_op jit(solution)/shard_map/ppermute | solution.py:70
  45.8 16.5 %collective-permute-start.15 = (bf16[4,96,768]{2,1,0:T(8,128)(2,1)S(1)}, bf16[4,96,768]{2,1,0:T(8,128)(2,1)S(1)}, u32[]{:S(2)}, u32[]{:S(2)}) collective-permute-start(bf16[4,96,768]{2,1,0:T(8,128)(2,1)S(1)} %pad_maximum_fusion.13), channel_id=1, source_target_pairs={{0,8},{4,20},{8,0},{12,28},{16,24},{20,4},{24,16},{28,12},{1,9},{5... | collective-permute-start | bytes 1769480 | tf_op jit(solution)/shard_map/ppermute | solution.py:70
  48.1 30.5 %collective-permute-start.9 = (bf16[4,24,3968]{2,1,0:T(8,128)(2,1)S(1)}, bf16[4,24,3968]{2,1,0:T(8,128)(2,1)S(1)}, u32[]{:S(2)}, u32[]{:S(2)}) collective-permute-start(bf16[4,24,3968]{2,1,0:T(8,128)(2,1)S(1)} %pad_maximum_fusion.12), channel_id=1, source_target_pairs={{0,8},{4,20},{8,0},{12,28},{16,24},{20,4},{24,16},{28,12},{1,9},{5... | collective-permute-start | bytes 2285576 | tf_op jit(solution)/shard_map/ppermute | solution.py:70
  50.2 30.7 %collective-permute-start.4 = (bf16[2,4,24,2432]{3,2,1,0:T(8,128)(2,1)S(1)}, bf16[2,4,24,2432]{3,2,1,0:T(8,128)(2,1)S(1)}, u32[]{:S(2)}, u32[]{:S(2)}) collective-permute-start(bf16[2,4,24,2432]{3,2,1,0:T(8,128)(2,1)S(1)} %pad_maximum_fusion.11), channel_id=1, source_target_pairs={{0,16},{4,12},{8,24},{12,4},{16,0},{20,28},{24,8},{28,20},{1,17},{... | collective-permute-start | bytes 2801672 | tf_op jit(solution)/shard_map/ppermute | solution.py:71
  62.5 21.5 %collective-permute-start.16 = (bf16[2,4,96,768]{3,2,1,0:T(8,128)(2,1)S(1)}, bf16[2,4,96,768]{3,2,1,0:T(8,128)(2,1)S(1)}, u32[]{:S(2)}, u32[]{:S(2)}) collective-permute-start(bf16[2,4,96,768]{3,2,1,0:T(8,128)(2,1)S(1)} %pad_maximum_fusion.9), channel_id=1, source_target_pairs={{0,16},{4,12},{8,24},{12,4},{16,0},{20,28},{24,8},{28,20},{1,17},{... | collective-permute-start | bytes 3538952 | tf_op jit(solution)/shard_map/ppermute | solution.py:71
  79.0 21.3 %collective-permute-start.10 = (bf16[2,4,24,3968]{3,2,1,0:T(8,128)(2,1)S(1)}, bf16[2,4,24,3968]{3,2,1,0:T(8,128)(2,1)S(1)}, u32[]{:S(2)}, u32[]{:S(2)}) collective-permute-start(bf16[2,4,24,3968]{3,2,1,0:T(8,128)(2,1)S(1)} %pad_maximum_fusion.7), channel_id=1, source_target_pairs={{0,16},{4,12},{8,24},{12,4},{16,0},{20,28},{24,8},{28,20},{1,17},{... | collective-permute-start | bytes 4571144 | tf_op jit(solution)/shard_map/ppermute | solution.py:71
  81.4 23.0 %collective-permute-start.5 = (bf16[2,2,4,24,2432]{4,3,2,0,1:T(8,128)(2,1)S(1)}, bf16[2,2,4,24,2432]{4,3,2,0,1:T(8,128)(2,1)S(1)}, u32[]{:S(2)}, u32[]{:S(2)}) collective-permute-start(bf16[2,2,4,24,2432]{4,3,2,0,1:T(8,128)(2,1)S(1)} %copy.527), channel_id=1, source_target_pairs={{0,4},{4,0},{8,12},{12,8},{16,20},{20,16},{24,28},{28,24},{1,5},{5... | collective-permute-start | bytes 5603336 | tf_op jit(solution)/shard_map/ppermute | solution.py:72
  84.4 22.8 %collective-permute-start.17 = (bf16[2,2,4,96,768]{4,3,2,0,1:T(8,128)(2,1)S(1)}, bf16[2,2,4,96,768]{4,3,2,0,1:T(8,128)(2,1)S(1)}, u32[]{:S(2)}, u32[]{:S(2)}) collective-permute-start(bf16[2,2,4,96,768]{4,3,2,0,1:T(8,128)(2,1)S(1)} %pad_maximum_fusion.5), channel_id=1, source_target_pairs={{0,4},{4,0},{8,12},{12,8},{16,20},{20,16},{24,28},{28,24},{1,5},{5... | collective-permute-start | bytes 7077896 | tf_op jit(solution)/shard_map/ppermute | solution.py:72
  101.2 10.1 %collective-permute-start.11 = (bf16[2,2,4,24,3968]{4,3,2,0,1:T(8,128)(2,1)S(1)}, bf16[2,2,4,24,3968]{4,3,2,0,1:T(8,128)(2,1)S(1)}, u32[]{:S(2)}, u32[]{:S(2)}) collective-permute-start(bf16[2,2,4,24,3968]{4,3,2,0,1:T(8,128)(2,1)S(1)} %copy.537), channel_id=1, source_target_pairs={{0,4},{4,0},{8,12},{12,8},{16,20},{20,16},{24,28},{28,24},{1,5},{5... | collective-permute-start | bytes 9142280 | tf_op jit(solution)/shard_map/ppermute | solution.py:72
  141.6 7.0 %collective-permute-start.18 = (bf16[128,128]{1,0:T(8,128)(2,1)}, bf16[128,128]{1,0:T(8,128)(2,1)S(1)}, u32[]{:S(2)}, u32[]{:S(2)}) collective-permute-start(bf16[128,128]{1,0:T(8,128)(2,1)} %get-tuple-element.62), channel_id=1, source_target_pairs={{0,3},{1,0},{2,1},{3,2},{4,7},{5,4},{6,5},{7,6},{8,11},{9,8},{10,9... | collective-permute-start | bytes 98312 | tf_op jit(solution)/shard_map/ppermute | solution.py:67
  146.7 5.9 %collective-permute-start.20 = (bf16[128,128]{1,0:T(8,128)(2,1)}, bf16[128,128]{1,0:T(8,128)(2,1)S(1)}, u32[]{:S(2)}, u32[]{:S(2)}) collective-permute-start(bf16[128,128]{1,0:T(8,128)(2,1)} %get-tuple-element.62), channel_id=1, source_target_pairs={{0,1},{1,2},{2,3},{3,0},{4,5},{5,6},{6,7},{7,4},{8,9},{9,10},{10,1... | collective-permute-start | bytes 98312 | tf_op jit(solution)/shard_map/ppermute | solution.py:67
  153.4 8.1 %collective-permute-start.21 = (bf16[4,128,128]{2,1,0:T(8,128)(2,1)S(1)}, bf16[4,128,128]{2,1,0:T(8,128)(2,1)S(1)}, u32[]{:S(2)}, u32[]{:S(2)}) collective-permute-start(bf16[4,128,128]{2,1,0:T(8,128)(2,1)S(1)} %pad_maximum_fusion.20), channel_id=1, source_target_pairs={{0,8},{4,20},{8,0},{12,28},{16,24},{20,4},{24,16},{28,12},{1,9},{5... | collective-permute-start | bytes 393224 | tf_op jit(solution)/shard_map/ppermute | solution.py:70
  161.6 31.0 %collective-permute-start.22 = (bf16[2,4,128,128]{3,2,1,0:T(8,128)(2,1)S(1)}, bf16[2,4,128,128]{3,2,1,0:T(8,128)(2,1)S(1)}, u32[]{:S(2)}, u32[]{:S(2)}) collective-permute-start(bf16[2,4,128,128]{3,2,1,0:T(8,128)(2,1)S(1)} %pad_maximum_fusion.16), channel_id=1, source_target_pairs={{0,16},{4,12},{8,24},{12,4},{16,0},{20,28},{24,8},{28,20},{1,17},{... | collective-permute-start | bytes 786440 | tf_op jit(solution)/shard_map/ppermute | solution.py:71
  192.7 29.7 %collective-permute-start.23 = (bf16[2,2,4,128,128]{4,3,2,0,1:T(8,128)(2,1)S(1)}, bf16[2,2,4,128,128]{4,3,2,0,1:T(8,128)(2,1)S(1)}, u32[]{:S(2)}, u32[]{:S(2)}) collective-permute-start(bf16[2,2,4,128,128]{4,3,2,0,1:T(8,128)(2,1)S(1)} %pad_maximum_fusion.14), channel_id=1, source_target_pairs={{0,4},{4,0},{8,12},{12,8},{16,20},{20,16},{24,28},{28,24},{1,5},{5... | collective-permute-start | bytes 1572872 | tf_op jit(solution)/shard_map/ppermute | solution.py:72
  237.1 9.6 %all-to-all-start = ((f32[32,1,128]{2,1,0:T(1,128)}), f32[32,1,128]{2,1,0:T(1,128)S(1)}, u32[]{:S(2)}, u32[]{:S(2)}) async-start(f32[32,1,128]{2,1,0:T(1,128)} %broadcast_in_dim.18), calls=%async_computation | async-start | bytes 32768 | tf_op jit(solution)/shard_map/all_to_all | solution.py:119
  268.6 25.6 %collective-permute-start.24 = (bf16[2,2,4,128,128]{4,3,2,1,0:T(8,128)(2,1)S(1)}, bf16[2,2,4,128,128]{4,3,2,1,0:T(8,128)(2,1)}, u32[]{:S(2)}, u32[]{:S(2)}) collective-permute-start(bf16[2,2,4,128,128]{4,3,2,1,0:T(8,128)(2,1)S(1)} %select_convert_fusion.1), channel_id=1, source_target_pairs={{0,4},{4,0},{8,12},{12,8},{16,20},{20,16},{24,28},{28,24},{1,5},{5... | collective-permute-start | bytes 1572872 | tf_op jit(solution)/shard_map/ppermute | solution.py:102
  295.7 53.2 %collective-permute-start.25 = (bf16[2,4,128,128]{3,2,1,0:T(8,128)(2,1)S(1)}, bf16[2,4,128,128]{3,2,1,0:T(8,128)(2,1)S(1)}, u32[]{:S(2)}, u32[]{:S(2)}) collective-permute-start(bf16[2,4,128,128]{3,2,1,0:T(8,128)(2,1)S(1)} %fusion.73), channel_id=1, source_target_pairs={{0,16},{4,12},{8,24},{12,4},{16,0},{20,28},{24,8},{28,20},{1,17},{... | collective-permute-start | bytes 786440 | tf_op jit(solution)/shard_map/ppermute | solution.py:104
  354.1 5.8 %collective-permute-start.27 = (bf16[128,128]{1,0:T(8,128)(2,1)S(1)}, bf16[128,128]{1,0:T(8,128)(2,1)S(1)}, u32[]{:S(2)}, u32[]{:S(2)}) collective-permute-start(bf16[128,128]{1,0:T(8,128)(2,1)S(1)} %get-tuple-element.323), channel_id=1, source_target_pairs={{0,1},{1,2},{2,3},{3,0},{4,5},{5,6},{6,7},{7,4},{8,9},{9,10},{10,1... | collective-permute-start | bytes 98312 | tf_op jit(solution)/shard_map/ppermute | solution.py:111
  354.6 5.2 collective-permute-start.28
  355.2 5.2 collective-permute-start.29
  383.8 44.7 %collective-permute-start.42 = (bf16[2,2,4,96,768]{4,3,2,1,0:T(8,128)(2,1)S(1)}, bf16[2,2,4,96,768]{4,3,2,1,0:T(8,128)(2,1)}, u32[]{:S(2)}, u32[]{:S(2)}) collective-permute-start(bf16[2,2,4,96,768]{4,3,2,1,0:T(8,128)(2,1)S(1)} %select_convert_fusion), channel_id=1, source_target_pairs={{0,4},{4,0},{8,12},{12,8},{16,20},{20,16},{24,28},{28,24},{1,5},{5... | collective-permute-start | bytes 7077896 | tf_op jit(solution)/shard_map/ppermute | solution.py:102
  409.2 16.8 %collective-permute-start.30 = (bf16[2,2,4,24,2432]{4,3,2,1,0:T(8,128)(2,1)}, bf16[2,2,4,24,2432]{4,3,2,1,0:T(8,128)(2,1)S(1)}, u32[]{:S(2)}, u32[]{:S(2)}) collective-permute-start(bf16[2,2,4,24,2432]{4,3,2,1,0:T(8,128)(2,1)} %copy.571), channel_id=1, source_target_pairs={{0,4},{4,0},{8,12},{12,8},{16,20},{20,16},{24,28},{28,24},{1,5},{5... | collective-permute-start | bytes 5603336 | tf_op jit(solution)/shard_map/ppermute | solution.py:102
  425.5 17.2 %collective-permute-start.36 = (bf16[2,2,4,24,4096]{4,3,2,1,0:T(8,128)(2,1)}, bf16[2,2,4,24,4096]{4,3,2,1,0:T(8,128)(2,1)}, u32[]{:S(2)}, u32[]{:S(2)}) collective-permute-start(bf16[2,2,4,24,4096]{4,3,2,1,0:T(8,128)(2,1)} %broadcast_select_fusion), channel_id=1, source_target_pairs={{0,4},{4,0},{8,12},{12,8},{16,20},{20,16},{24,28},{28,24},{1,5},{5... | collective-permute-start | bytes 9437192 | tf_op jit(solution)/shard_map/ppermute | solution.py:102
  426.8 13.6 %collective-permute-start.31 = (bf16[2,4,24,2432]{3,2,1,0:T(8,128)(2,1)S(1)}, bf16[2,4,24,2432]{3,2,1,0:T(8,128)(2,1)S(1)}, u32[]{:S(2)}, u32[]{:S(2)}) collective-permute-start(bf16[2,4,24,2432]{3,2,1,0:T(8,128)(2,1)S(1)} %fusion.56), channel_id=1, source_target_pairs={{0,16},{4,12},{8,24},{12,4},{16,0},{20,28},{24,8},{28,20},{1,17},{... | collective-permute-start | bytes 2801672 | tf_op jit(solution)/shard_map/ppermute | solution.py:104
  432.5 36.8 %collective-permute-start.43 = (bf16[2,4,96,768]{3,2,1,0:T(8,128)(2,1)}, bf16[2,4,96,768]{3,2,1,0:T(8,128)(2,1)}, u32[]{:S(2)}, u32[]{:S(2)}) collective-permute-start(bf16[2,4,96,768]{3,2,1,0:T(8,128)(2,1)} %fusion.55), channel_id=1, source_target_pairs={{0,16},{4,12},{8,24},{12,4},{16,0},{20,28},{24,8},{28,20},{1,17},{... | collective-permute-start | bytes 3538952 | tf_op jit(solution)/shard_map/ppermute | solution.py:104
  442.1 13.7 %collective-permute-start.32 = (bf16[4,24,2432]{2,1,0:T(8,128)(2,1)S(1)}, bf16[4,24,2432]{2,1,0:T(8,128)(2,1)S(1)}, u32[]{:S(2)}, u32[]{:S(2)}) collective-permute-start(bf16[4,24,2432]{2,1,0:T(8,128)(2,1)S(1)} %fusion.63), channel_id=1, source_target_pairs={{0,8},{4,20},{8,0},{12,28},{16,24},{20,4},{24,16},{28,12},{1,9},{5... | collective-permute-start | bytes 1400840 | tf_op jit(solution)/shard_map/ppermute | solution.py:107
  449.6 26.9 %collective-permute-start.37 = (bf16[2,4,24,4096]{3,2,1,0:T(8,128)(2,1)}, bf16[2,4,24,4096]{3,2,1,0:T(8,128)(2,1)}, u32[]{:S(2)}, u32[]{:S(2)}) collective-permute-start(bf16[2,4,24,4096]{3,2,1,0:T(8,128)(2,1)} %fusion.46), channel_id=1, source_target_pairs={{0,16},{4,12},{8,24},{12,4},{16,0},{20,28},{24,8},{28,20},{1,17},{... | collective-permute-start | bytes 4718600 | tf_op jit(solution)/shard_map/ppermute | solution.py:104
  456.0 7.9 %collective-permute-start.33 = (bf16[24,2432]{1,0:T(8,128)(2,1)S(1)}, bf16[24,2432]{1,0:T(8,128)(2,1)S(1)}, u32[]{:S(2)}, u32[]{:S(2)}) collective-permute-start(bf16[24,2432]{1,0:T(8,128)(2,1)S(1)} %get-tuple-element.305), channel_id=1, source_target_pairs={{0,1},{1,2},{2,3},{3,0},{4,5},{5,6},{6,7},{7,4},{8,9},{9,10},{10,1... | collective-permute-start | bytes 350216 | tf_op jit(solution)/shard_map/ppermute | solution.py:111
  458.1 9.0 %collective-permute-start.34 = (bf16[24,2432]{1,0:T(8,128)(2,1)S(1)}, bf16[24,2432]{1,0:T(8,128)(2,1)S(1)}, u32[]{:S(2)}, u32[]{:S(2)}) collective-permute-start(bf16[24,2432]{1,0:T(8,128)(2,1)S(1)} %get-tuple-element.307), channel_id=1, source_target_pairs={{0,2},{1,3},{2,0},{3,1},{4,6},{5,7},{6,4},{7,5},{8,10},{9,11},{10,... | collective-permute-start | bytes 350216 | tf_op jit(solution)/shard_map/ppermute | solution.py:111
  459.9 8.3 %collective-permute-start.35 = (bf16[24,2432]{1,0:T(8,128)(2,1)S(1)}, bf16[24,2432]{1,0:T(8,128)(2,1)S(1)}, u32[]{:S(2)}, u32[]{:S(2)}) collective-permute-start(bf16[24,2432]{1,0:T(8,128)(2,1)S(1)} %get-tuple-element.306), channel_id=1, source_target_pairs={{0,3},{1,0},{2,1},{3,2},{4,7},{5,4},{6,5},{7,6},{8,11},{9,8},{10,9... | collective-permute-start | bytes 350216 | tf_op jit(solution)/shard_map/ppermute | solution.py:111
  471.8 9.9 %collective-permute-start.44 = (bf16[4,96,768]{2,1,0:T(8,128)(2,1)S(1)}, bf16[4,96,768]{2,1,0:T(8,128)(2,1)S(1)}, u32[]{:S(2)}, u32[]{:S(2)}) collective-permute-start(bf16[4,96,768]{2,1,0:T(8,128)(2,1)S(1)} %fusion.58), channel_id=1, source_target_pairs={{0,8},{4,20},{8,0},{12,28},{16,24},{20,4},{24,16},{28,12},{1,9},{5... | collective-permute-start | bytes 1769480 | tf_op jit(solution)/shard_map/ppermute | solution.py:107
  478.6 12.1 %collective-permute-start.38 = (bf16[4,24,4096]{2,1,0:T(8,128)(2,1)S(1)}, bf16[4,24,4096]{2,1,0:T(8,128)(2,1)S(1)}, u32[]{:S(2)}, u32[]{:S(2)}) collective-permute-start(bf16[4,24,4096]{2,1,0:T(8,128)(2,1)S(1)} %fusion.57), channel_id=1, source_target_pairs={{0,8},{4,20},{8,0},{12,28},{16,24},{20,4},{24,16},{28,12},{1,9},{5... | collective-permute-start | bytes 2359304 | tf_op jit(solution)/shard_map/ppermute | solution.py:107
  481.9 16.4 %collective-permute-start.45 = (bf16[96,768]{1,0:T(8,128)(2,1)S(1)}, bf16[96,768]{1,0:T(8,128)(2,1)S(1)}, u32[]{:S(2)}, u32[]{:S(2)}) collective-permute-start(bf16[96,768]{1,0:T(8,128)(2,1)S(1)} %get-tuple-element.300), channel_id=1, source_target_pairs={{0,1},{1,2},{2,3},{3,0},{4,5},{5,6},{6,7},{7,4},{8,9},{9,10},{10,1... | collective-permute-start | bytes 442376 | tf_op jit(solution)/shard_map/ppermute | solution.py:111
  483.3 17.1 %collective-permute-start.46 = (bf16[96,768]{1,0:T(8,128)(2,1)S(1)}, bf16[96,768]{1,0:T(8,128)(2,1)S(1)}, u32[]{:S(2)}, u32[]{:S(2)}) collective-permute-start(bf16[96,768]{1,0:T(8,128)(2,1)S(1)} %get-tuple-element.302), channel_id=1, source_target_pairs={{0,2},{1,3},{2,0},{3,1},{4,6},{5,7},{6,4},{7,5},{8,10},{9,11},{10,... | collective-permute-start | bytes 442376 | tf_op jit(solution)/shard_map/ppermute | solution.py:111
  488.1 12.3 %collective-permute-start.47 = (bf16[96,768]{1,0:T(8,128)(2,1)S(1)}, bf16[96,768]{1,0:T(8,128)(2,1)S(1)}, u32[]{:S(2)}, u32[]{:S(2)}) collective-permute-start(bf16[96,768]{1,0:T(8,128)(2,1)S(1)} %get-tuple-element.301), channel_id=1, source_target_pairs={{0,3},{1,0},{2,1},{3,2},{4,7},{5,4},{6,5},{7,6},{8,11},{9,8},{10,9... | collective-permute-start | bytes 442376 | tf_op jit(solution)/shard_map/ppermute | solution.py:111
  490.9 12.7 %collective-permute-start.39 = (bf16[24,4096]{1,0:T(8,128)(2,1)S(1)}, bf16[24,4096]{1,0:T(8,128)(2,1)S(1)}, u32[]{:S(2)}, u32[]{:S(2)}) collective-permute-start(bf16[24,4096]{1,0:T(8,128)(2,1)S(1)} %get-tuple-element.295), channel_id=1, source_target_pairs={{0,1},{1,2},{2,3},{3,0},{4,5},{5,6},{6,7},{7,4},{8,9},{9,10},{10,1... | collective-permute-start | bytes 589832 | tf_op jit(solution)/shard_map/ppermute | solution.py:111
  492.9 18.5 %collective-permute-start.40 = (bf16[24,4096]{1,0:T(8,128)(2,1)S(1)}, bf16[24,4096]{1,0:T(8,128)(2,1)S(1)}, u32[]{:S(2)}, u32[]{:S(2)}) collective-permute-start(bf16[24,4096]{1,0:T(8,128)(2,1)S(1)} %get-tuple-element.297), channel_id=1, source_target_pairs={{0,2},{1,3},{2,0},{3,1},{4,6},{5,7},{6,4},{7,5},{8,10},{9,11},{10,... | collective-permute-start | bytes 589832 | tf_op jit(solution)/shard_map/ppermute | solution.py:111
  498.3 13.1 %collective-permute-start.41 = (bf16[24,4096]{1,0:T(8,128)(2,1)S(1)}, bf16[24,4096]{1,0:T(8,128)(2,1)S(1)}, u32[]{:S(2)}, u32[]{:S(2)}) collective-permute-start(bf16[24,4096]{1,0:T(8,128)(2,1)S(1)} %get-tuple-element.296), channel_id=1, source_target_pairs={{0,3},{1,0},{2,1},{3,2},{4,7},{5,4},{6,5},{7,6},{8,11},{9,8},{10,9... | collective-permute-start | bytes 589832 | tf_op jit(solution)/shard_map/ppermute | solution.py:111
  518.0 13.0 %all-to-all-start.1 = ((f32[32,1,128]{2,1,0:T(1,128)}), f32[32,1,128]{2,1,0:T(1,128)S(1)}, u32[]{:S(2)}, u32[]{:S(2)}) async-start(f32[32,1,128]{2,1,0:T(1,128)} %broadcast_in_dim_broadcast_in_dim_broadcast_in_dim.3), calls=%async_computation.1 | async-start | bytes 32768 | tf_op jit(solution)/shard_map/all_to_all | solution.py:119
  (65 other events, 505.5 us)

commit v2 on v1

--- a/solution.py
+++ b/solution.py
@@ -14,11 +14,15 @@
 PPB = 8
 STEP = 10
 QPD = 4
+QUERY_ROWS = QPD * QLEN
+TOKENS = BIN + QUERY_ROWS
 ATTEND_TILE = 512
 FEED_ROWS = 512
 BACK_ROWS = 256
 
 
+F32 = jnp.float32
+LOW = jnp.bfloat16
 sharpness_divisor = 0.1
 clip_max = 0.02
 learn_rate = 0.04
@@ -54,62 +58,195 @@
     )
 
 
-def in_order(bit, own, other):
-    first = bit == 0
-    return jnp.stack([jnp.where(first, own, other), jnp.where(first, other, own)])
-
-
-def gather_rows(part, columns):
+def gate(value, *others):
+    return lax.optimization_barrier((value, others))[0]
+
+
+def place_blocks(sources, copies, outputs, index):
+    def run(scalars, *refs):
+        given, (results, sems) = refs[: len(sources)], (refs[len(sources) : -1], refs[-1])
+        moves = [
+            pltpu.make_async_copy(
+                given[source].at[where(scalars)], results[out].at[there(scalars)], sems.at[number]
+            )
+            for number, (source, where, out, there) in enumerate(copies)
+        ]
+        for move in moves:
+            move.start()
+        for move in moves:
+            move.wait()
+
+    anywhere = pl.BlockSpec(memory_space=pl.ANY)
+    return pl.pallas_call(
+        run,
+        grid_spec=pltpu.PrefetchScalarGridSpec(
+            num_scalar_prefetch=1,
+            grid=(),
+            in_specs=[anywhere] * len(sources),
+            out_specs=[anywhere] * len(outputs),
+            scratch_shapes=[pltpu.SemaphoreType.DMA((len(copies),))],
+        ),
+        out_shape=outputs,
+        compiler_params=pltpu.CompilerParams(vmem_limit_bytes=4 << 20),
+        cost_estimate=pl.CostEstimate(
+            flops=0,
+            transcendentals=0,
+            bytes_accessed=2 * sum(o.size * o.dtype.itemsize for o in outputs),
+        ),
+    )(index, *sources)
+
+
+def scalars_of_position():
+    return jnp.stack([jnp.asarray(v, jnp.int32) for v in position()])
+
+
+def send_line(part):
     if not staged_mesh():
-        whole = lax.all_gather(part, ("pb", "pa"), axis=0, tiled=True)
-        return [whole[:, low:high] for low, high in columns]
-    depth, core, first_bit, second_bit = position()
-    moved = [lax.ppermute(part, "pa", shift_pairs(k)) for k in (1, 2, 3)]
+        return [lax.all_gather(part, "pa", axis=0, tiled=True)]
+    return [lax.ppermute(part, "pa", shift_pairs(k)) for k in (1, 2, 3)]
+
+
+def line_of(part, moved):
+    if not staged_mesh():
+        return moved[0]
+    depth = position()[0]
     around = [part, moved[2], moved[1], moved[0]]
     line = jnp.stack([lax.select_n((place - depth) % 4, *around) for place in range(4)])
-    pair = in_order(first_bit, line, lax.ppermute(line, "pb", FIRST_STEP))
-    quad = in_order(second_bit, pair, lax.ppermute(pair, "pb", SECOND_STEP))
-    partner = lax.ppermute(quad, "pb", CORE_PAIR)
+    return line.reshape((4 * part.shape[0],) + part.shape[1:])
+
+
+def gather_rest(line):
+    return lax.all_gather(line, "pb", axis=0, tiled=True)
+
+
+def in_order(own, other, which):
+    both = jax.ShapeDtypeStruct((2,) + own.shape, own.dtype)
+    copies = [
+        (0, lambda s: Ellipsis, 0, lambda s: s[which]),
+        (1, lambda s: Ellipsis, 0, lambda s: 1 - s[which]),
+    ]
+    return place_blocks([own, other], copies, [both], scalars_of_position())[0]
+
+
+def gather_pair(line, *others):
+    if not staged_mesh():
+        return line
+    return in_order(line, gate(lax.ppermute(line, "pb", FIRST_STEP), others), 2)
+
+
+def gather_quad(pair, *others):
+    if not staged_mesh():
+        return pair
+    return in_order(pair, gate(lax.ppermute(pair, "pb", SECOND_STEP), others), 3)
+
+
+def gather_whole(quad, ranges, *others):
+    if not staged_mesh():
+        whole = gather_rest(quad)
+        return [whole[:, low:high] for low, high in ranges]
+    partner = gate(lax.ppermute(quad, "pb", CORE_PAIR), others)
+    rows = quad.shape[2]
+    copies, outputs = [], []
+    for number, (low, high) in enumerate(ranges):
+        outputs.append(jax.ShapeDtypeStruct((8, rows, high - low), quad.dtype))
+        for source in range(2):
+            for second in range(2):
+                for first in range(2):
+
+                    def where(s, second=second, first=first, low=low, high=high):
+                        return second, first, slice(None), slice(low, high)
+
+                    def there(s, source=source, second=second, first=first):
+                        core = s[1] if source == 0 else 1 - s[1]
+                        swapped = 4 * first + 2 * second
+                        return core + jnp.where(core == 0, 4 * second + 2 * first, swapped)
+
+                    copies.append((source, where, number, there))
+    results = place_blocks([quad, partner], copies, outputs, scalars_of_position())
+    return [a.reshape(8 * rows, a.shape[2]) for a in results]
+
+
+def split_low(value):
+    high = lax.reduce_precision(value, 8, 7)
+    return high.astype(LOW), (value - high).astype(LOW)
+
+
+def packed(arrays, exact):
+    pieces = []
+    for array, whole in zip(arrays, exact):
+        pieces += split_low(array) if whole else [array.astype(LOW)]
+    return pieces[0] if len(pieces) == 1 else jnp.concatenate(pieces, -1)
+
+
+def joined(arrays, exact, moved):
+    results, at = [], 0
+    for array, whole in zip(arrays, exact):
+        total = array.astype(F32)
+        for _ in range(2 if whole else 1):
+            total = total + moved[..., at : at + array.shape[-1]].astype(F32)
+            at += array.shape[-1]
+        results.append(total)
+    return results
+
+
+def blocks_at(arrays, place):
+    return [lax.dynamic_index_in_dim(array, place, 0, False) for array in arrays]
+
+
+def scatter_quad(arrays, exact, *others):
+    if not staged_mesh():
+        return [
+            lax.psum_scatter(a.astype(F32), "pb", scatter_dimension=0, tiled=True)
+            for a in arrays
+        ]
+    core = position()[1]
     results = []
-    for low, high in columns:
-        own, other = quad[..., low:high], partner[..., low:high]
-        even = jnp.where(core == 0, own, other)
-        odd = jnp.where(core == 0, other, own).swapaxes(0, 1)
-        results.append(jnp.stack([even, odd], 2).reshape(32 * part.shape[0], high - low))
+    for array, whole in zip(arrays, exact):
+        parts = array.reshape((4, 2, array.shape[0] // 8) + array.shape[1:])
+        keep, send = (lax.dynamic_index_in_dim(parts, c, 1, False) for c in (core, 1 - core))
+        moved = lax.ppermute(send if whole else send.astype(LOW), "pb", CORE_PAIR)
+        results.append(keep.astype(F32) + gate(moved, others).astype(F32))
     return results
 
 
-def scatter_rows(terms):
+def scatter_pair(arrays, exact, *others):
     if not staged_mesh():
-        return lax.psum_scatter(
-            terms.astype(jnp.float32), ("pb", "pa"), scatter_dimension=0, tiled=True
-        )
-    depth, core, first_bit, second_bit = position()
-    blocks = terms.reshape((2, 2, 2, 4, terms.shape[0] // 32) + terms.shape[1:])
-    even, odd = blocks[:, :, 0], blocks[:, :, 1].swapaxes(0, 1)
-    keep = jnp.where(core == 0, even, odd)
-    send = jnp.where(core == 0, odd, even).astype(jnp.bfloat16)
-
-    def block(array, place):
-        return lax.dynamic_index_in_dim(array, place, 0, False)
-
-    def sent(array, place):
-        return block(array, place).astype(jnp.bfloat16)
-
-    def joined(own, moved):
-        return own.astype(jnp.float32) + moved.astype(jnp.float32)
-
-    quad = joined(keep, lax.ppermute(send, "pb", CORE_PAIR))
-    pair = joined(
-        block(quad, second_bit), lax.ppermute(sent(quad, 1 - second_bit), "pb", SECOND_STEP)
-    )
-    line = joined(
-        block(pair, first_bit), lax.ppermute(sent(pair, 1 - first_bit), "pb", FIRST_STEP)
-    )
-    total = block(line, depth)
+        return arrays
+    _, core, _, bit = position()
+
+    def two_at(bit):
+        first = jnp.where(core == 0, 2 * bit, bit)
+        second = first + jnp.where(core == 0, 1, 2)
+        return [
+            jnp.stack([lax.dynamic_index_in_dim(a, i, 0, False) for i in (first, second)])
+            for a in arrays
+        ]
+
+    send = packed(two_at(1 - bit), exact)
+    return joined(two_at(bit), exact, gate(lax.ppermute(send, "pb", SECOND_STEP), others))
+
+
+def scatter_line(arrays, exact):
+    if not staged_mesh():
+        return arrays
+    bit = position()[2]
+    send = packed(blocks_at(arrays, 1 - bit), exact)
+    return joined(blocks_at(arrays, bit), exact, lax.ppermute(send, "pb", FIRST_STEP))
+
+
+def scatter_rest(arrays):
+    return [lax.psum_scatter(a, "pa", scatter_dimension=0, tiled=True) for a in arrays]
+
+
+def scatter_total(arrays, exact):
+    if not staged_mesh():
+        return scatter_rest(arrays)
+    depth = position()[0]
+    arrays = [a.reshape((4, a.shape[0] // 4) + a.shape[1:]) for a in arrays]
+    total = blocks_at(arrays, depth)
     for k in (1, 2, 3):
-        moved = lax.ppermute(sent(line, (depth + k) % 4), "pa", shift_pairs(k))
-        total = joined(total, moved)
+        send = packed(blocks_at(arrays, (depth + k) % 4), exact)
+        total = joined(total, exact, lax.ppermute(send, "pa", shift_pairs(k)))
     return total
 
 
@@ -119,8 +256,6 @@
     return jnp.sum(lax.all_to_all(copies, ("pb", "pa"), 0, 0), 0)
 
 
-F32 = jnp.float32
-LOW = jnp.bfloat16
 ACROSS = (((1,), (1,)), ((), ()))
 PLAIN = (((1,), (0,)), ((), ()))
 
@@ -150,39 +285,68 @@
     return value * below, below + value * density
 
 
-def whole_block(array):
-    return pl.BlockSpec(array.shape, lambda *_: (0,) * array.ndim, pipeline_mode=pl.Buffered(1))
-
-
-def row_block(rows, width):
-    return pl.BlockSpec((rows, width), lambda i: (i, 0))
-
-
-def row_call(kernel, count, rows, inputs, weights, outputs, sums=(), flops=0, limit=56):
-    moved = count * sum(a.shape[1] * a.dtype.itemsize for a in inputs)
-    moved += sum(w.size * w.dtype.itemsize for w in weights)
-    moved += count * sum(w * jnp.dtype(t).itemsize for w, t in outputs)
+def columns(array, low=0, high=None):
+    width = array.shape[1] - low if high is None else high - low
+    spec = pl.BlockSpec(
+        (array.shape[0], width), lambda i: (0, low // width), pipeline_mode=pl.Buffered(1)
+    )
+    return array, spec
+
+
+def row_call(kernel, rows, first, count, inputs, weights, outputs, sums=(), into=None, flops=0):
+    done = 0 if into is None else len(inputs) + len(weights)
+
+    def run(*refs):
+        given, results = refs[: len(inputs) + len(weights)], refs[-len(outputs) - len(sums) :]
+        if sums:
+
+            @pl.when(pl.program_id(0) == 0)
+            def _():
+                for place in range(len(sums)):
+                    place -= len(sums)
+                    start = refs[place - len(outputs) - len(sums)] if done else None
+                    here = results[place]
+                    here[...] = start[...] if done else jnp.zeros_like(here)
+
+        kernel(*given, *results)
+
+    moved = rows * count * sum(a.shape[1] * a.dtype.itemsize for a, _ in inputs)
+    moved += sum(w.size * w.dtype.itemsize for w, _ in weights)
+    moved += rows * count * sum(w * jnp.dtype(t).itemsize for w, t in outputs)
+
+    def rows_at(width, begin):
+        return pl.BlockSpec((rows, width), lambda i: (begin + i, 0))
+
+    sum_specs = [pl.BlockSpec((16, w), lambda i: (0, 0)) for w in sums]
+    in_specs = [rows_at(a.shape[1], begin) for a, begin in inputs]
+    in_specs += [spec for _, spec in weights]
+    arguments = [a for a, _ in inputs] + [w for w, _ in weights]
+    if into is not None:
+        in_specs += [pl.BlockSpec(memory_space=pl.ANY)] * len(outputs) + sum_specs
+        arguments += list(into)
     return pl.pallas_call(
-        kernel,
-        grid=(count // rows,),
-        in_specs=[row_block(rows, a.shape[1]) for a in inputs] + [whole_block(w) for w in weights],
-        out_specs=[row_block(rows, w) for w, _ in outputs]
-        + [pl.BlockSpec((8, w), lambda i: (0, 0)) for w in sums],
-        out_shape=[jax.ShapeDtypeStruct((count, w), t) for w, t in outputs]
-        + [jax.ShapeDtypeStruct((8, w), F32) for w in sums],
-        compiler_params=pltpu.CompilerParams(vmem_limit_bytes=limit << 20),
-        cost_estimate=pl.CostEstimate(flops=flops, transcendentals=0, bytes_accessed=moved),
-    )(*inputs, *weights)
-
-
-def widen_kernel(x_ref, att_ref, out_w, up_w, vec, wide, resid_ref, low_ref, act_ref, slope_ref):
+        run,
+        grid=(count,),
+        in_specs=in_specs,
+        out_specs=[rows_at(w, first) for w, _ in outputs] + sum_specs,
+        out_shape=[jax.ShapeDtypeStruct((TOKENS, w), t) for w, t in outputs]
+        + [jax.ShapeDtypeStruct((16, w), F32) for w in sums],
+        input_output_aliases={done + i: i for i in range(len(outputs) + len(sums))} if done else {},
+        compiler_params=pltpu.CompilerParams(vmem_limit_bytes=56 << 20),
+        cost_estimate=pl.CostEstimate(
+            flops=flops * rows * count, transcendentals=0, bytes_accessed=moved
+        ),
+    )(*arguments)
+
+
+def widen_kernel(x_ref, att_ref, out_w, up_w, vec, resid_ref, low_ref, act_ref, slope_ref):
     resid = x_ref[...].astype(F32) + dot(att_ref[...], out_w[...]) + vec[2:3]
     resid_ref[...] = resid
     low = (standard(resid)[0] * vec[3:4] + vec[4:5]).astype(LOW)
     low_ref[...] = low
-    for at in range(0, up_w.shape[1], 512):
-        part = slice(at, at + 512)
-        value, slope = gelu_with_slope(dot(low, up_w[:, part]) + wide[0:1, part])
+    for row in range(4):
+        part = slice(row * D, row * D + D)
+        value, slope = gelu_with_slope(dot(low, up_w[:, part]) + vec[5 + row : 6 + row])
         act_ref[:, part] = value.astype(LOW)
         slope_ref[:, part] = slope.astype(LOW)
 
@@ -202,13 +366,8 @@
 def back_kernel(
     grad_ref, proj_ref, two_ref, slope_ref, resid_ref,
     proj_w, down_w, up_w, out_w, vec,
-    gproj_ref, gtwo_ref, ghid_ref, gone_ref, gatt_ref, sum_ref, wide_ref,
+    gproj_ref, gtwo_ref, ghid_ref, gone_ref, gatt_ref, sum_ref,
 ):
-    @pl.when(pl.program_id(0) == 0)
-    def _():
-        sum_ref[...] = jnp.zeros_like(sum_ref)
-        wide_ref[...] = jnp.zeros_like(wide_ref)
-
     def add(row, value):
         sum_ref[row : row + 1, :] += jnp.sum(value, 0, keepdims=True)
 
@@ -219,25 +378,25 @@
     gproj_ref[...] = gproj
     gnormed = dot(gproj, proj_w[...], ACROSS)
     unit, scale = standard(two_ref[...])
-    add(4, gnormed * unit)
-    add(5, gnormed)
+    add(10, gnormed * unit)
+    add(11, gnormed)
     gtwo = standard_backward(gnormed * vec[10:11], unit, scale)
-    add(3, gtwo)
+    add(9, gtwo)
     gtwo_low = gtwo.astype(LOW)
     gtwo_ref[...] = gtwo_low
     gnormed = gtwo
-    for at in range(0, up_w.shape[1], 512):
-        part = slice(at, at + 512)
+    for row in range(4):
+        part = slice(row * D, row * D + D)
         ghid = dot(gtwo_low, down_w[part, :], ACROSS) * slope_ref[:, part].astype(F32)
-        wide_ref[0:1, part] += jnp.sum(ghid, 0, keepdims=True)
+        add(5 + row, ghid)
         ghid_low = ghid.astype(LOW)
         ghid_ref[:, part] = ghid_low
         gnormed = gnormed + dot(ghid_low, up_w[:, part], ACROSS)
     unit, scale = standard(resid_ref[...])
-    add(1, gnormed * unit)
-    add(2, gnormed)
+    add(3, gnormed * unit)
+    add(4, gnormed)
     gone = standard_backward(gnormed * vec[3:4], unit, scale)
-    add(0, gone)
+    add(2, gone)
     gone_low = gone.astype(LOW)
     gone_ref[...] = gone_low
     gatt_ref[...] = dot(gone_low, out_w[...], ACROSS).astype(LOW)
@@ -290,36 +449,68 @@
     lax.fori_loop(0, q_ref.shape[0] // tile, block, 0)
 
 
-def head_pair(count, third):
-    return pl.BlockSpec((count, 128), lambda h, s: (0, third * 6 + h))
-
-
-def attend_forward(mixed, spans, col, row, tile):
-    count = mixed.shape[0]
+def head_pair(count, row, first):
+    return pl.BlockSpec((count, 128), lambda h, s: (row, first + h))
+
+
+def attend_call(kernel, tile, count, pairs, tables, arrays, specs, outputs, into, scratch, cost):
+    spans, col, row = tables
+    specs = specs + [
+        pl.BlockSpec((count, tile), lambda h, s: (0, 0)),
+        pl.BlockSpec((8, count), lambda h, s: (0, 0)),
+    ]
+    arguments = [spans, *arrays, col, row]
+    aliases = {}
+    used = len(arguments)
+    if into is not None:
+        aliases = {used + i: i for i in range(len(into))}
+        specs = specs + [pl.BlockSpec(memory_space=pl.ANY)] * len(into)
+        arguments += list(into)
+
+    def run(*refs):
+        kernel(tile, *refs[:used], *refs[len(arguments) :])
+
     return pl.pallas_call(
-        functools.partial(attend_kernel, tile),
-        out_shape=(
-            jax.ShapeDtypeStruct((count, D), LOW),
-            jax.ShapeDtypeStruct((6, 8, count), F32),
-        ),
+        run,
+        out_shape=[shape for shape, _ in outputs],
         grid_spec=pltpu.PrefetchScalarGridSpec(
             num_scalar_prefetch=1,
-            grid=(6,),
-            in_specs=[head_pair(count, third) for third in range(3)]
-            + [
-                pl.BlockSpec((count, tile), lambda h, s: (0, 0)),
-                pl.BlockSpec((8, count), lambda h, s: (0, 0)),
-            ],
-            out_specs=[head_pair(count, 0), pl.BlockSpec((1, 8, count), lambda h, s: (h, 0, 0))],
-            scratch_shapes=[pltpu.VMEM((2, count, tile), F32), pltpu.VMEM((128, count), LOW)],
+            grid=(pairs,),
+            in_specs=specs,
+            out_specs=[spec for _, spec in outputs],
+            scratch_shapes=scratch,
         ),
-        compiler_params=pltpu.CompilerParams(vmem_limit_bytes=40 << 20),
+        input_output_aliases=aliases,
+        compiler_params=pltpu.CompilerParams(vmem_limit_bytes=48 << 20),
         cost_estimate=pl.CostEstimate(
-            flops=8 * count * count * D,
-            transcendentals=12 * count * count,
-            bytes_accessed=8 * count * D,
+            flops=cost * pairs * count * count * 128,
+            transcendentals=0,
+            bytes_accessed=8 * pairs * count * 128,
         ),
-    )(spans, mixed, mixed, mixed, col, row)
+    )(*arguments)
+
+
+def attend_forward(mixed, tables, tile, first, pairs, row, into=None):
+    count = mixed.shape[0]
+    return attend_call(
+        attend_kernel,
+        tile,
+        count,
+        pairs,
+        tables,
+        [mixed] * 3,
+        [head_pair(count, 0, third * 6 + first) for third in range(3)],
+        [
+            (jax.ShapeDtypeStruct((TOKENS, D), LOW), head_pair(count, row, first)),
+            (
+                jax.ShapeDtypeStruct((6, 8, count), F32),
+                pl.BlockSpec((1, 8, count), lambda h, s: (first + h, 0, 0)),
+            ),
+        ],
+        into,
+        [pltpu.VMEM((2, count, tile), F32), pltpu.VMEM((128, count), LOW)],
+        40,
+    )
 
 
 def attend_back_kernel(
@@ -392,43 +583,40 @@
     sum_ref[1:2, :] = jnp.sum(gvalue[...], 0, keepdims=True)
 
 
-def attend_backward(mixed, grad, total, spans, col, row, tile):
+def attend_backward(mixed, grad, total, tables, tile, first, pairs, row, into=None):
     count = mixed.shape[0]
-    return pl.pallas_call(
-        functools.partial(attend_back_kernel, tile),
-        out_shape=(
-            jax.ShapeDtypeStruct((3, count, D), LOW),
-            jax.ShapeDtypeStruct((8, D), F32),
-        ),
-        grid_spec=pltpu.PrefetchScalarGridSpec(
-            num_scalar_prefetch=1,
-            grid=(6,),
-            in_specs=[head_pair(count, third) for third in range(3)]
-            + [
-                head_pair(count, 0),
-                pl.BlockSpec((1, 8, count), lambda h, s: (h, 0, 0)),
-                pl.BlockSpec((count, tile), lambda h, s: (0, 0)),
-                pl.BlockSpec((8, count), lambda h, s: (0, 0)),
-            ],
-            out_specs=[
-                pl.BlockSpec((3, count, 128), lambda h, s: (0, 0, h)),
-                pl.BlockSpec((8, 128), lambda h, s: (0, h)),
-            ],
-            scratch_shapes=[
-                pltpu.VMEM((128, count), LOW),
-                pltpu.VMEM((count, 128), F32),
-                pltpu.VMEM((count, 128), F32),
-                pltpu.VMEM((2, count, tile), F32),
-                pltpu.VMEM((2, count, tile), F32),
-            ],
-        ),
-        compiler_params=pltpu.CompilerParams(vmem_limit_bytes=48 << 20),
-        cost_estimate=pl.CostEstimate(
-            flops=20 * count * count * D,
-            transcendentals=12 * count * count,
-            bytes_accessed=16 * count * D,
-        ),
-    )(spans, mixed, mixed, mixed, grad, total, col, row)
+    return attend_call(
+        attend_back_kernel,
+        tile,
+        count,
+        pairs,
+        tables,
+        [mixed] * 3 + [grad, total],
+        [head_pair(count, 0, third * 6 + first) for third in range(3)]
+        + [
+            head_pair(count, row, first),
+            pl.BlockSpec((1, 8, count), lambda h, s: (first + h, 0, 0)),
+        ],
+        [
+            (
+                jax.ShapeDtypeStruct((3, TOKENS, D), LOW),
+                pl.BlockSpec((3, count, 128), lambda h, s: (0, row, first + h)),
+            ),
+            (
+                jax.ShapeDtypeStruct((16, D), F32),
+                pl.BlockSpec((16, 128), lambda h, s: (0, first + h)),
+            ),
+        ],
+        into,
+        [
+            pltpu.VMEM((128, count), LOW),
+            pltpu.VMEM((count, 128), F32),
+            pltpu.VMEM((count, 128), F32),
+            pltpu.VMEM((2, count, tile), F32),
+            pltpu.VMEM((2, count, tile), F32),
+        ],
+        80,
+    )
 
 
 def segment_tables(segment, tile):
@@ -443,7 +631,7 @@
     )
 
 
-def split_low(value):
+def two_terms(value):
     high = value.astype(LOW)
     return high, (value - high.astype(F32)).astype(LOW)
 
@@ -453,7 +641,7 @@
 
 
 def score_kernel(query_ref, passage_ref, member_ref, score_ref, sums_ref):
-    high, rest = split_low(sharp(dot(query_ref[...], passage_ref[...], ACROSS)))
+    high, rest = two_terms(sharp(dot(query_ref[...], passage_ref[...], ACROSS)))
     sums = dot(high, member_ref[...]) + dot(rest, member_ref[...])
     sums_ref[...] = sums
     lane = lax.broadcasted_iota(jnp.int32, sums.shape, 1)
@@ -466,7 +654,7 @@
     lane = lax.broadcasted_iota(jnp.int32, (rows, 128), 1)
     grads = jnp.broadcast_to(grad_ref[...][:, None, :], (rows // QLEN, QLEN, 128))
     ratio = grads.reshape(rows, 128) / jnp.where(lane % 64 < PPB, sums_ref[...], 1.0)
-    high, rest = split_low(ratio)
+    high, rest = two_terms(ratio)
     return jnp.where(lane < 64, high, rest)
 
 
@@ -533,73 +721,14 @@
     )
 
 
-def score_backward(queries, passages, member, grad_scores, sums):
+def score_backward(kernel, queries, passages, member, grad_scores, sums):
     rows, fixed, grads = score_specs()
     count = queries.shape[0]
     inputs = (queries, passages, member, grad_scores, sums)
     in_specs = [rows, fixed, fixed, grads, rows]
-    flops = 6 * count * BIN * 128
-    out = jax.ShapeDtypeStruct((count, 128), F32)
-    grad_queries = score_call(score_query_kernel, inputs, in_specs, rows, out, flops)
-    out = jax.ShapeDtypeStruct((BIN, 128), F32)
-    grad_passages = score_call(score_passage_kernel, inputs, in_specs, fixed, out, flops)
-    return grad_queries, grad_passages
-
-
-def encode_forward(tokens, tables, tile, rows, weights):
-    qkv_matrix, out_matrix, up_matrix, down_matrix, proj_matrix, vectors, wide = weights
-    count = tokens.shape[0]
-    bias_qkv = jnp.concatenate([vectors[0], jnp.zeros_like(vectors[0]), vectors[1]])
-    mixed = (dot(tokens, qkv_matrix) + bias_qkv).astype(LOW)
-    attended, total = attend_forward(mixed, *tables, tile)
-    resid, normed, active, slope = row_call(
-        widen_kernel,
-        count,
-        rows,
-        (tokens, attended),
-        (out_matrix, up_matrix, vectors, wide),
-        [(D, F32), (D, LOW), (4 * D, LOW), (4 * D, LOW)],
-        flops=10 * count * D * D,
-    )
-    two, normed_out, projected, unit = row_call(
-        narrow_kernel,
-        count,
-        rows,
-        (active, resid),
-        (down_matrix, proj_matrix, vectors),
-        [(D, F32), (D, LOW), (128, F32), (128, LOW)],
-        flops=8 * count * D * D,
-    )
-    kept = (tokens, mixed, total, attended, resid, normed, active, slope, two, normed_out, projected)
-    return unit, kept
-
-
-def encode_backward(tables, tile, rows, weights, kept, grad_unit):
-    qkv_matrix, out_matrix, up_matrix, down_matrix, proj_matrix, vectors, wide = weights
-    tokens, mixed, total, attended, resid, normed, active, slope, two, normed_out, projected = kept
-    count = tokens.shape[0]
-    gproj, gtwo, ghid, gone, gatt, sums, wide_sums = row_call(
-        back_kernel,
-        count,
-        rows,
-        (grad_unit, projected, two, slope, resid),
-        (proj_matrix, down_matrix, up_matrix, out_matrix, vectors),
-        [(128, LOW), (D, LOW), (4 * D, LOW), (D, LOW), (D, LOW)],
-        (D, 4 * D),
-        flops=18 * count * D * D,
-    )
-    gmixed, attend_sums = attend_backward(mixed, gatt, total, *tables, tile)
-    vector_grad = jnp.concatenate(
-        [attend_sums[:2], sums[:3], wide_sums[:1].reshape(4, D), sums[3:6]], 0
-    )
-    pairs = (
-        (tokens, gmixed),
-        (attended, gone),
-        (normed, ghid),
-        (active, gtwo),
-        (normed_out, gproj),
-    )
-    return pairs, vector_grad
+    width, spec = (BIN, fixed) if kernel is score_passage_kernel else (count, rows)
+    out = jax.ShapeDtypeStruct((width, 128), F32)
+    return score_call(kernel, inputs, in_specs, spec, out, 6 * count * BIN * 128)
 
 
 def cross_grad(scores, partition, passage_ids, chosen_ids, query_total):
@@ -641,90 +770,185 @@
     vector_first,
     vector_second,
 ):
-    low = jnp.bfloat16
-    vector_part = jnp.pad(vector_params.T, ((0, 0), (0, 116))).astype(low)
-    qkv_matrix, vectors = gather_rows(
-        jnp.concatenate([qkv_weight.astype(low), vector_part], 1), [(0, 2304), (2304, 2432)]
-    )
-    up_matrix, out_matrix, proj_matrix = gather_rows(
-        jnp.concatenate([up_weight, out_weight, proj_weight], 1).astype(low),
-        [(0, 3072), (3072, 3840), (3840, 3968)],
-    )
-    (down_matrix,) = gather_rows(down_weight.astype(low), [(0, 768)])
-    weights = (
-        qkv_matrix,
-        out_matrix,
-        up_matrix,
-        down_matrix,
-        proj_matrix,
-        vectors[:, :12].T.astype(F32),
-        vectors[:, 5:9].T.astype(F32).reshape(1, 4 * D),
-    )
     own_index = lax.axis_index(("pb", "pa"))
     query_total = QPD * lax.axis_size(("pb", "pa"))
-    query_flat = query_tokens.reshape(QPD * QLEN, D)
-    query_tables = segment_tables(jnp.arange(QPD * QLEN, dtype=jnp.int32) // QLEN, QPD * QLEN)
+    query_flat = query_tokens.reshape(QUERY_ROWS, D)
+    tokens = jnp.concatenate([passage_tokens[0], query_flat], 0)
+    query_tables = segment_tables(jnp.arange(QUERY_ROWS, dtype=jnp.int32) // QLEN, QUERY_ROWS)
     own_lengths = lax.dynamic_index_in_dim(passage_lengths, own_index, 0, keepdims=False)
     ends = jnp.cumsum(own_lengths)
     places = jnp.arange(BIN, dtype=jnp.int32)
     own_seg = jnp.sum((places[:, None] >= ends[None, :]).astype(jnp.int32), 1)
     passage_tables = segment_tables(own_seg, ATTEND_TILE)
-    member = (own_seg[:, None] == jnp.arange(128, dtype=jnp.int32)[None, :] % 64).astype(low)
-    query_unit, query_kept = encode_forward(
-        query_flat, query_tables, QPD * QLEN, QPD * QLEN, weights
-    )
-    passage_unit, passage_kept = encode_forward(
-        passage_tokens[0], passage_tables, ATTEND_TILE, FEED_ROWS, weights
-    )
-    (every_query,) = gather_rows(query_unit, [(0, 128)])
+    member = (own_seg[:, None] == jnp.arange(128, dtype=jnp.int32)[None, :] % 64).astype(LOW)
+
+    vector_part = jnp.pad(vector_params.T, ((0, 0), (0, 116))).astype(LOW)
+    first_part = jnp.concatenate([qkv_weight.astype(LOW), vector_part], 1)
+    middle_part = jnp.concatenate([up_weight, out_weight, proj_weight], 1).astype(LOW)
+    down_part = down_weight.astype(LOW)
+    first_line = line_of(first_part, send_line(first_part))
+    middle_moved = send_line(gate(middle_part, first_line))
+    first_pair = gather_pair(first_line)
+    ready = gate((tokens, query_tables, passage_tables, member), first_pair)
+    first_quad = gather_quad(first_pair, ready)
+    tokens, query_tables, passage_tables, member = ready
+    middle = gather_rest(line_of(middle_part, gate(middle_moved, first_quad)))
+    qkv_matrix, vectors = gather_whole(first_quad, [(0, 2304), (2304, 2432)])
+    vectors = vectors[:, :12].T.astype(F32)
+    bias_qkv = jnp.concatenate([vectors[0], jnp.zeros_like(vectors[0]), vectors[1]])
+
+    def mix(rows):
+        return (dot(rows, qkv_matrix) + bias_qkv).astype(LOW)
+
+    query_mixed = mix(query_flat)
+    down_moved = send_line(gate(down_part, query_mixed))
+    passage_mixed = mix(gate(passage_tokens[0], query_mixed))
+    attended, query_log = attend_forward(
+        gate(query_mixed, passage_mixed), query_tables, QUERY_ROWS, 0, 6, BIN // QUERY_ROWS
+    )
+    down_line = line_of(down_part, gate(down_moved, attended))
+    passage_state = attend_forward(
+        gate(passage_mixed, down_line), passage_tables, ATTEND_TILE, 0, 3, 0, (attended,)
+    )
+    down_pair = gather_pair(down_line, passage_state)
+    attended, passage_log = attend_forward(
+        gate(passage_mixed, down_pair), passage_tables, ATTEND_TILE, 3, 3, 0, passage_state
+    )
+    down_quad = gather_quad(down_pair, attended)
+    up = columns(middle, 0, 4 * D)
+    out = columns(middle, 4 * D, 5 * D)
+    proj = columns(middle, 5 * D, 5 * D + 128)
+    vector_rows = columns(vectors)
+
+    def widen(rows, first, count, att, into):
+        return row_call(
+            widen_kernel,
+            rows,
+            first,
+            count,
+            [(tokens, first), (att, first)],
+            (out, up, vector_rows),
+            [(D, F32), (D, LOW), (4 * D, LOW), (4 * D, LOW)],
+            into=into,
+            flops=10 * D * D,
+        )
+
+    def narrow(rows, first, count, wider, into):
+        return row_call(
+            narrow_kernel,
+            rows,
+            first,
+            count,
+            [(wider[2], first), (wider[0], first)],
+            (down, proj, vector_rows),
+            [(D, F32), (D, LOW), (128, F32), (128, LOW)],
+            into=into,
+            flops=8 * D * D,
+        )
+
+    wider = widen(QUERY_ROWS, BIN // QUERY_ROWS, 1, gate(attended, down_quad), None)
+    (down_matrix,) = gather_whole(down_quad, [(0, D)], wider)
+    down = columns(down_matrix)
+    narrower = narrow(QUERY_ROWS, BIN // QUERY_ROWS, 1, wider, None)
+    query_part = narrower[3][BIN:]
+    query_line = line_of(query_part, send_line(query_part))
+    every_query = gather_rest(query_line)
+    wider = widen(
+        FEED_ROWS, 0, BIN // FEED_ROWS, gate(attended, query_line), gate(wider, narrower)
+    )
+    narrower = narrow(FEED_ROWS, 0, BIN // FEED_ROWS, wider, narrower)
+    resid, normed, active, slope = wider
+    two, normed_out, projected, unit = narrower
+    passage_unit = unit[:BIN]
+
     passage_ids = own_index * PPB + jnp.arange(PPB, dtype=jnp.int32)
     scores, totals = score_forward(every_query, passage_unit, member)
     scores = scores[:, :PPB]
     partition = sum_everywhere(jnp.sum(jnp.exp(scores), 1))
     grad_scores = cross_grad(scores, partition, passage_ids, positives, query_total)
     grad_scores = jnp.tile(jnp.pad(grad_scores, ((0, 0), (0, 64 - PPB))), (1, 2))
-    grad_every, grad_passage = score_backward(
-        every_query, passage_unit, member, grad_scores, totals
-    )
-    grad_query = scatter_rows(grad_every)
-    query_pairs, query_vector = encode_backward(
-        query_tables, QPD * QLEN, QPD * QLEN, weights, query_kept, grad_query
-    )
-    passage_pairs, passage_vector = encode_backward(
-        passage_tables, ATTEND_TILE, BACK_ROWS, weights, passage_kept, grad_passage
-    )
-
-    def weight_terms(index):
-        (left, right), (left_more, right_more) = passage_pairs[index], query_pairs[index]
-        left = jnp.concatenate([left, left_more], 0)
-        right = jnp.concatenate([right, right_more], -2)
-        if index == 0:
-            return jnp.einsum("td,itk->dik", left, right, preferred_element_type=F32).reshape(
-                D, 3 * D
-            )
+    grad_every = score_backward(
+        score_query_kernel, every_query, passage_unit, member, grad_scores, totals
+    )
+    whole, rounded = (True,), (False,)
+    query_back = scatter_quad([grad_every], whole)
+    grad_passage = score_backward(
+        score_passage_kernel,
+        gate(every_query, query_back),
+        passage_unit,
+        member,
+        grad_scores,
+        totals,
+    )
+
+    def go_back(rows, first, count, grad, into):
+        return row_call(
+            back_kernel,
+            rows,
+            first,
+            count,
+            [grad, (projected, first), (two, first), (slope, first), (resid, first)],
+            (proj, down, up, out, vector_rows),
+            [(128, LOW), (D, LOW), (4 * D, LOW), (D, LOW), (D, LOW)],
+            (D,),
+            into=into,
+            flops=18 * D * D,
+        )
+
+    query_back = scatter_pair(query_back, whole)
+    back = go_back(
+        BACK_ROWS, 0, BIN // BACK_ROWS, (gate(grad_passage, query_back), 0), None
+    )
+    query_back = scatter_line(query_back, whole)
+    (grad_query,) = scatter_total(gate(query_back, back), whole)
+    back = go_back(QUERY_ROWS, BIN // QUERY_ROWS, 1, (grad_query, 0), back)
+    gproj, gtwo, ghid, gone, gatt, sums = back
+
+    def terms(left, right):
         return dot(left, right, (((0,), (0,)), ((), ())))
 
-    down_sum = scatter_rows(weight_terms(3))
-    proj_terms = weight_terms(4)
-    proj_high = proj_terms.astype(low)
-    proj_rest = (proj_terms - proj_high.astype(F32)).astype(low)
-    middle = scatter_rows(
-        jnp.concatenate(
-            [weight_terms(2).astype(low), weight_terms(1).astype(low), proj_high, proj_rest], 1
+    def attend_back(first, pairs, into, *others):
+        mixed = gate(passage_mixed, *others)
+        return attend_backward(
+            mixed, gatt, passage_log, passage_tables, ATTEND_TILE, first, pairs, 0, into
         )
-    )
-    vector_terms = jnp.pad((query_vector + passage_vector).T, ((0, 0), (0, 116)))
-    first = scatter_rows(
-        jnp.concatenate([weight_terms(0).astype(low), vector_terms.astype(low)], 1)
-    )
-    reduced = (
-        first[:, :2304],
-        middle[:, 3072:3840],
-        middle[:, :3072],
-        down_sum,
-        middle[:, 3840:3968] + middle[:, 3968:],
-        first[:, 2304:2316].T,
-    )
+
+    down_terms = terms(active, gtwo)
+    up_terms = terms(normed, gate(ghid, down_terms))
+    down_back = scatter_quad([down_terms], rounded, up_terms)
+    down_back = scatter_pair(down_back, rounded)
+    rest = gate((gone, gproj), up_terms)
+    out_terms, proj_terms = terms(attended, rest[0]), terms(normed_out, rest[1])
+    query_grads = attend_backward(
+        gate(query_mixed, out_terms, proj_terms),
+        gatt,
+        query_log,
+        query_tables,
+        QUERY_ROWS,
+        0,
+        6,
+        BIN // QUERY_ROWS,
+    )
+    kinds = (False, False, True)
+    middle_back = scatter_quad([up_terms, out_terms, proj_terms], kinds, query_grads)
+    middle_back = scatter_pair(middle_back, kinds)
+    down_back = scatter_line(down_back, rounded)
+    grads = attend_back(0, 2, query_grads[:1], query_grads)
+    (down_sum,) = scatter_total(gate(down_back, grads), rounded)
+    middle_back = scatter_line(gate(middle_back, grads), kinds)
+    grads = attend_back(2, 2, grads)
+    up_sum, out_sum, proj_sum = scatter_total(gate(middle_back, grads), kinds)
+    grads = attend_back(4, 2, grads, down_sum)
+    first_terms = [terms(tokens, grads[0][third]) for third in range(3)]
+    mixed_sums = grads[1] + query_grads[1]
+    vector_grad = jnp.concatenate([mixed_sums[:2], sums[2:12]], 0)
+    vector_terms = jnp.pad(vector_grad.T, ((0, 0), (0, 116)))
+    kinds = (False,) * 4
+    first_back = scatter_quad([*first_terms, vector_terms], kinds)
+    first_back = scatter_pair(first_back, kinds, up_sum)
+    *thirds, vector_sum = scatter_total(scatter_line(first_back, kinds), kinds)
+    qkv_sum = jnp.concatenate(thirds, 1)
+    reduced = (qkv_sum, out_sum, up_sum, down_sum, proj_sum, vector_sum[:, :12].T)
     square = sum((jnp.sum(gradient * gradient) for gradient in reduced))
     norm_value = jnp.sqrt(sum_everywhere(jnp.full((1, 128), square))[0, 0])
     factor = jnp.minimum(1.0, clip_max / (norm_value + 1e-06))

time: 557 us -> 504 us (0.905)
  waiting for transfers between devices: 107 us -> 74.6 us
  starting transfers between devices: 85.9 us -> 59.4 us
  local copies, waits for them, and re-layouts: 54 us -> 37.2 us
  Pallas kernels: 194 us -> 209 us
  other arithmetic: 58.3 us -> 43.9 us
  between operations: 10.8 us -> 24.5 us
  blocking collectives: 0 us -> 10.5 us
    ppermute x48 -> x47, waiting for transfers between devices: 97.7 us -> 67.4 us  [the longest x12 15.1 us: scatter_total(): total = joined(total, exact, lax.ppermute(send, 'pa', shift_pairs(k)))]
    ppermute x48 -> x47, starting transfers between devices: 77.5 us -> 53.5 us  [the longest x12 22.2 us: send_line(): return [lax.ppermute(part, 'pa', shift_pairs(k)) for k in (1, 2, 3)]]
    pallas_call x10 -> x19, Pallas kernels: 164 us -> 179 us  [the longest x7 97 us: attend_call(): pl.pallas_call(run, out_shape=[shape for shape, _ in outputs], grid_spec=...]
    unnamed x137, local copies, waits for them, and re-layouts: 28.2 us -> 16.1 us
    another operation x49 -> x16, other arithmetic: 16.3 us -> 4.65 us  [the longest x10 3.22 us: line_of(): jnp.stack([lax.select_n((place - depth) % 4, *around) for place in range(...]
    all_to_all x0 -> x1, blocking collectives: none -> 10.5 us  [sum_everywhere(): return jnp.sum(lax.all_to_all(copies, ('pb', 'pa'), 0, 0), 0)]
    dot_general x6 -> x9, matrix products: 29.7 us -> 39.4 us  [dot(): return lax.dot_general(left, right, dims, preferred_element_type=F32)]
    dot_general x1 -> x0, matrix products: 9.05 us -> none  [weight_terms(): jnp.einsum('td,itk->dik', left, right, preferred_element_type=F32)]
  transfers between devices with their start and end apart: 50 -> 50, of which waited for: 26 -> 20; matrix products, arithmetic and copies ran while one was open for 16% -> 11% of each run, Pallas kernels for 25% -> 30%
where the time goes in v2:
time: 504 us; the launch traced here: 498 us
  Pallas kernels  209 us (41%)
  waiting for transfers between devices  74.6 us (15%)
  starting transfers between devices  59.4 us (12%)
  other arithmetic  43.9 us (9%)
  matrix products  39.4 us (8%)
  local copies, waits for them, and re-layouts  37.2 us (7%)
  between operations  24.5 us (5%)
  blocking collectives  10.5 us (2%)
    pallas_call x7, Pallas kernels, attend_call(): pl.pallas_call(run, out_shape=[shape for shape, _ in outputs], grid_spec=...  97 us
    pallas_call x6, Pallas kernels, row_call(): pl.pallas_call(run, grid=(count,), in_specs=in_specs, out_specs=[rows_at(...  74.3 us
    dot_general x9, matrix products, dot(): return lax.dot_general(left, right, dims, preferred_element_type=F32)  39.4 us
    pallas_call x3, Pallas kernels, score_call(): pl.pallas_call(kernel, grid=(inputs[0].shape[0] // SCORE_ROWS,), in_specs...  29.7 us
    ppermute x12, starting transfers between devices, send_line(): return [lax.ppermute(part, 'pa', shift_pairs(k)) for k in (1, 2, 3)]  22.2 us
    unnamed x137, local copies, waits for them, and re-layouts  16.1 us
    ppermute x12, starting transfers between devices, scatter_total(): total = joined(total, exact, lax.ppermute(send, 'pa', shift_pairs(k)))  15.6 us
    ppermute x12, waiting for transfers between devices, scatter_total(): total = joined(total, exact, lax.ppermute(send, 'pa', shift_pairs(k)))  15.1 us
  transfers between devices with their start and end apart: 50, of which 20 were waited for; matrix products, arithmetic and copies ran while one was open for 11% of the time, Pallas kernels for 30%

profile of v2, /device:TPU:0, one launch (start us, length us, event | category | flops | bytes accessed | tf_op | source)
XLA Modules:
  0.0 498.3 jit_solution(14791209774103438231)
XLA Ops:
  9.1 4.1 collective-permute-start.1
  26.2 6.7 %collective-permute-done.3.refs_1_ = bf16[96,2432]{1,0:T(8,128)(2,1)S(1)} collective-permute-done((bf16[96,2432]{1,0:T(8,128)(2,1)S(1)}, bf16[96,2432]{1,0:T(8,128)(2,1)S(1)}, u32[]{:S(2)}, u32[]{:S(2)}) %collective-permute-start.3) | collective-permute-done | bytes 466976 | tf_op jit(solution)/shard_map/ppermute | solution.py:134
  43.5 4.1 collective-permute-done.4.refs_1_
  48.7 7.0 %collective-permute-done.12 = bf16[24,3968]{1,0:T(8,128)(2,1)S(1)} collective-permute-done((bf16[24,3968]{1,0:T(8,128)(2,1)S(1)}, bf16[24,3968]{1,0:T(8,128)(2,1)S(1)}, u32[]{:S(2)}, u32[]{:S(2)}) %collective-permute-start.12) | collective-permute-done | bytes 190496 | tf_op jit(solution)/shard_map/ppermute | solution.py:106
  57.8 3.1 collective-permute-done.5.refs_1_
  64.0 2.8 fusion.1.refs_1_.refs_2_.refs_3_
  70.1 7.3 %add_convert_fusion.refs_1_.refs_2_.refs_3_ = bf16[1024,2304]{1,0:T(8,128)(2,1)} fusion(bf16[1024,768]{1,0:T(8,128)(2,1)} %bitcast.391, bf16[768,2304]{1,0:T(8,128)(2,1)S(1)} %bitcast.366, f32[2304]{0:T(1024)S(1)} %pad_maximum_fusion.24), kind=kOutput, calls=%fused_computation | convolution fusion | flops 3628597248 | bytes 9839616 | tf_op jit(solution)/shard_map/dot_general | solution.py:264
  77.3 3.9 shard_map.360
  82.3 14.7 %shard_map.361 = (bf16[1152,768]{1,0:T(8,128)(2,1)S(1)}, f32[6,8,1024]{2,1,0:T(8,128)S(1)}) custom-call(s32[2,2]{1,0:T(2,128)S(1)} %pad_add_fusion.refs_0_, bf16[1024,2304]{1,0:T(8,128)(2,1)} %add_convert_fusion.refs_1_.refs_2_.refs_3_, bf16[1024,2304]{1,0:T(8,128)(2,1)} %add_convert_fusion.refs_1_.refs_2_.refs_3_, ...), custom_call_target="tpu_custom_call", output_to_operand_aliasing={{0}: (6, {})} | custom-call | flops 16106127360 | bytes 3145728 | tf_op jit(solution)/shard_map/pallas_call | solution.py:473
  97.0 6.8 %collective-permute-done.9.refs_1_ = bf16[384,768]{1,0:T(8,128)(2,1)S(1)} collective-permute-done((bf16[384,768]{1,0:T(8,128)(2,1)S(1)}, bf16[384,768]{1,0:T(8,128)(2,1)S(1)}, u32[]{:S(2)}, u32[]{:S(2)}) %collective-permute-start.9) | collective-permute-done | bytes 589856 | tf_op jit(solution)/shard_map/ppermute | solution.py:134
  106.0 14.7 %shard_map.363 = (bf16[1152,768]{1,0:T(8,128)(2,1)S(1)}, f32[6,8,1024]{2,1,0:T(8,128)S(1)}) custom-call(s32[2,2]{1,0:T(2,128)S(1)} %pad_add_fusion.refs_0_, bf16[1024,2304]{1,0:T(8,128)(2,1)} %add_convert_fusion.refs_1_.refs_2_.refs_3_, bf16[1024,2304]{1,0:T(8,128)(2,1)} %add_convert_fusion.refs_1_.refs_2_.refs_3_, ...), custom_call_target="tpu_custom_call", output_to_operand_aliasing={{0}: (6, {}), {1}: (7, {})} | custom-call | flops 16106127360 | bytes 3145728 | tf_op jit(solution)/shard_map/pallas_call | solution.py:473
  122.0 5.8 %shard_map.365 = (f32[1152,768]{1,0:T(8,128)}, bf16[1152,768]{1,0:T(8,128)(2,1)}, bf16[1152,3072]{1,0:T(8,128)(2,1)}, bf16[1152,3072]{1,0:T(8,128)(2,1)}) custom-call(bf16[1152,768]{1,0:T(8,128)(2,1)} %pad_maximum_fusion.refs_0_, bf16[1152,768]{1,0:T(8,128)(2,1)} %copy-done.3, ...), custom_call_target="tpu_custom_call" | custom-call | flops 754974720 | bytes 14782464 | tf_op jit(solution)/shard_map/pallas_call | solution.py:327
  127.8 2.7 shard_map.366
  132.7 4.8 shard_map.367
  138.3 2.3 collective-permute-start.16
  141.0 3.6 collective-permute-start.15
  147.8 18.2 %shard_map.368 = (f32[1152,768]{1,0:T(8,128)}, bf16[1152,768]{1,0:T(8,128)(2,1)}, bf16[1152,3072]{1,0:T(8,128)(2,1)}, bf16[1152,3072]{1,0:T(8,128)(2,1)}) custom-call(bf16[1152,768]{1,0:T(8,128)(2,1)} %pad_maximum_fusion.refs_0_, bf16[1152,768]{1,0:T(8,128)(2,1)} %copy-done.3, ...), custom_call_target="tpu_custom_call", output_to_operand_aliasing={{0}: (5, {}), {1}: (6, {}), {2}: (7, {}), {3}: (8, {})} | custom-call | flops 6039797760 | bytes 32673792 | tf_op jit(solution)/shard_map/pallas_call | solution.py:327
  166.0 13.0 %shard_map.369 = (f32[1152,768]{1,0:T(8,128)}, bf16[1152,768]{1,0:T(8,128)(2,1)}, f32[1152,128]{1,0:T(8,128)}, bf16[1152,128]{1,0:T(8,128)(2,1)}) custom-call(bf16[1152,3072]{1,0:T(8,128)(2,1)} %get-tuple-element.160.refs_0_, ...), custom_call_target="tpu_custom_call", output_to_operand_aliasing={{0}: (5, {}), {1}: (6, {}), {2}: (7, {}), {3}: (8, {})} | custom-call | flops 4831838208 | bytes 25792512 | tf_op jit(solution)/shard_map/pallas_call | solution.py:327
  181.2 11.1 %shard_map.370 = (f32[128,128]{1,0:T(8,128)S(1)}, f32[4096,128]{1,0:T(8,128)S(1)}) custom-call(bf16[4096,128]{1,0:T(8,128)(2,1)S(1)} %copy-done.10, bf16[1024,128]{1,0:T(8,128)(2,1)S(1)} %slice.209.passage_ref, bf16[1024,128]{1,0:T(8,128)(2,1)S(1)} %compare_convert_fusion.member_ref), custom_call_target="tpu_custom_call" | custom-call | flops 3221225472 | bytes 4194304 | tf_op jit(solution)/shard_map/pallas_call | solution.py:683
  194.3 5.8 %all-to-all-start = ((f32[32,1,128]{2,1,0:T(1,128)}), f32[32,1,128]{2,1,0:T(1,128)S(1)}, u32[]{:S(2)}, u32[]{:S(2)}) async-start(f32[32,1,128]{2,1,0:T(1,128)} %broadcast_in_dim.17), calls=%async_computation | async-start | bytes 32768 | tf_op jit(solution)/shard_map/all_to_all | solution.py:256
  200.2 7.1 %all-to-all-done = f32[32,1,128]{2,1,0:T(1,128)S(1)} async-done(((f32[32,1,128]{2,1,0:T(1,128)}), f32[32,1,128]{2,1,0:T(1,128)S(1)}, u32[]{:S(2)}, u32[]{:S(2)}) %all-to-all-start) | async-done | bytes 16416 | tf_op jit(solution)/shard_map/all_to_all | solution.py:256
  210.5 10.0 %shard_map.371 = f32[4096,128]{1,0:T(8,128)S(1)} custom-call(bf16[4096,128]{1,0:T(8,128)(2,1)S(1)} %copy-done.11, bf16[1024,128]{1,0:T(8,128)(2,1)S(1)} %slice.209.passage_ref, bf16[1024,128]{1,0:T(8,128)(2,1)S(1)} %compare_convert_fusion.member_ref, f32[128,128]{1,0:T(8,128)S(1)} %copy.288.grad_ref, f32[4096,128]{1,0:T(8,128)S(1)} %copy-done.15), custom_call_target="tpu_custom_call" | custom-call | flops 3221225472 | bytes 4194304 | tf_op jit(solution)/shard_map/pallas_call | solution.py:683
  221.6 3.0 collective-permute-done.18
  229.2 8.6 %shard_map.372.refs_0_ = f32[1024,128]{1,0:T(8,128)S(1)} custom-call(bf16[4096,128]{1,0:T(8,128)(2,1)S(1)} %copy-done.12, bf16[1024,128]{1,0:T(8,128)(2,1)S(1)} %slice.209.passage_ref, bf16[1024,128]{1,0:T(8,128)(2,1)S(1)} %compare_convert_fusion.member_ref, f32[128,128]{1,0:T(8,128)S(1)} %copy.288.grad_ref, f32[4096,128]{1,0:T(8,128)S(1)} %copy-done.16), custom_call_target="tpu_custom_call" | custom-call | flops 3221225472 | bytes 4194304 | tf_op jit(solution)/shard_map/pallas_call | solution.py:683
  238.6 23.1 %shard_map.373 = (bf16[1152,128]{1,0:T(8,128)(2,1)}, bf16[1152,768]{1,0:T(8,128)(2,1)}, bf16[1152,3072]{1,0:T(8,128)(2,1)}, bf16[1152,768]{1,0:T(8,128)(2,1)}, b...) custom-call(f32[1024,128]{1,0:T(8,128)} %copy-done.13, f32[1152,128]{1,0:T(8,128)} %get-tuple-element.167.refs_1_, ...), custom_call_target="tpu_custom_call" | custom-call | flops 10871635968 | bytes 47943680 | tf_op jit(solution)/shard_map/pallas_call | solution.py:327
  266.7 3.7 collective-permute-done.22
  271.0 9.5 %shard_map.374 = (bf16[1152,128]{1,0:T(8,128)(2,1)}, bf16[1152,768]{1,0:T(8,128)(2,1)}, bf16[1152,3072]{1,0:T(8,128)(2,1)}, bf16[1152,768]{1,0:T(8,128)(2,1)}, b...) custom-call(f32[128,128]{1,0:T(8,128)} %fusion.61.refs_0_, ...), custom_call_target="tpu_custom_call", output_to_operand_aliasing={{0}: (10, {}), {1}: (11, {}), {2}: (12, {}), {3}: (13, {}),... | custom-call | flops 1358954496 | bytes 26152960 | tf_op jit(solution)/shard_map/pallas_call | solution.py:327
  280.5 9.5 %fusion.120 = f32[3072,768]{1,0:T(8,128)S(1)} fusion(bf16[1152,3072]{1,0:T(8,128)(2,1)} %get-tuple-element.160.refs_0_, bf16[1152,768]{1,0:T(8,128)(2,1)} %get-tuple-element.177), kind=kOutput, calls=%fused_computation.350 | convolution fusion | flops 5435817984 | bytes 18284544 | tf_op jit(solution)/shard_map/dot_general | solution.py:264
  290.0 6.3 %fusion.121 = f32[768,3072]{1,0:T(8,128)S(1)} fusion(bf16[1152,768]{1,0:T(8,128)(2,1)S(1)} %copy-done.28, bf16[1152,3072]{1,0:T(8,128)(2,1)S(1)} %copy-done.20), kind=kOutput, calls=%fused_computation.351 | convolution fusion | flops 5435817984 | bytes 18284544 | tf_op jit(solution)/shard_map/dot_general | solution.py:264
  307.2 4.0 copy.283
  311.8 5.8 %shard_map.375 = (bf16[3,1152,768]{2,1,0:T(8,128)(2,1)}, f32[16,768]{1,0:T(8,128)S(1)}) custom-call(s32[1,2]{1,0:T(1,128)S(1)} %pad_add_fusion.1.refs_0_, bf16[128,2304]{1,0:T(8,128)(2,1)S(1)} %fusion.1.refs_1_.refs_2_.refs_3_, bf16[128,2304]{1,0:T(8,128)(2,1)S(1)} %fusion.1.refs_1_.refs_2_.refs_3_, bf16[128,2304]{1,0:T(8,128)(2,1)S(1)} %fusion.1.refs_1_.refs_2_.refs_3_, ...), custom_call_target="tpu_custom_call" | custom-call | flops 1006632960 | bytes 786432 | tf_op jit(solution)/shard_map/pallas_call | solution.py:473
  319.9 3.7 bitcast_add_fusion.1
  326.4 2.4 bitcast_add_fusion
  331.3 19.3 %shard_map.376 = (bf16[3,1152,768]{2,1,0:T(8,128)(2,1)}, f32[16,768]{1,0:T(8,128)S(1)}) custom-call(s32[2,2]{1,0:T(2,128)S(1)} %pad_add_fusion.refs_0_, bf16[1024,2304]{1,0:T(8,128)(2,1)} %add_convert_fusion.refs_1_.refs_2_.refs_3_, bf16[1024,2304]{1,0:T(8,128)(2,1)} %add_convert_fusion.refs_1_.refs_2_.refs_3_, ...), custom_call_target="tpu_custom_call", output_to_operand_aliasing={{0}: (8, {})} | custom-call | flops 21474836480 | bytes 2097152 | tf_op jit(solution)/shard_map/pallas_call | solution.py:473
  354.1 7.2 %collective-permute-done.38 = bf16[2,96,4096]{2,1,0:T(8,128)(2,1)} collective-permute-done((bf16[2,96,4096]{2,1,0:T(8,128)(2,1)}, bf16[2,96,4096]{2,1,0:T(8,128)(2,1)}, u32[]{:S(2)}, u32[]{:S(2)}) %collective-permute-start.38) | collective-permute-done | bytes 1572896 | tf_op jit(solution)/shard_map/ppermute | solution.py:226
  366.9 3.8 collective-permute-start.29
  370.7 19.4 %shard_map.377 = (bf16[3,1152,768]{2,1,0:T(8,128)(2,1)}, f32[16,768]{1,0:T(8,128)S(1)}) custom-call(s32[2,2]{1,0:T(2,128)S(1)} %pad_add_fusion.refs_0_, bf16[1024,2304]{1,0:T(8,128)(2,1)} %add_convert_fusion.refs_1_.refs_2_.refs_3_, bf16[1024,2304]{1,0:T(8,128)(2,1)} %add_convert_fusion.refs_1_.refs_2_.refs_3_, ...), custom_call_target="tpu_custom_call", output_to_operand_aliasing={{0}: (8, {}), {1}: (9, {})} | custom-call | flops 21474836480 | bytes 2097152 | tf_op jit(solution)/shard_map/pallas_call | solution.py:473
  392.1 19.3 %shard_map.378 = (bf16[3,1152,768]{2,1,0:T(8,128)(2,1)}, f32[16,768]{1,0:T(8,128)S(1)}) custom-call(s32[2,2]{1,0:T(2,128)S(1)} %pad_add_fusion.refs_0_, bf16[1024,2304]{1,0:T(8,128)(2,1)} %add_convert_fusion.refs_1_.refs_2_.refs_3_, bf16[1024,2304]{1,0:T(8,128)(2,1)} %add_convert_fusion.refs_1_.refs_2_.refs_3_, ...), custom_call_target="tpu_custom_call", output_to_operand_aliasing={{0}: (8, {}), {1}: (9, {})} | custom-call | flops 21474836480 | bytes 2097152 | tf_op jit(solution)/shard_map/pallas_call | solution.py:473
  411.3 4.7 fusion.4
  416.0 3.2 fusion.6
  419.2 3.1 fusion.8
  423.8 3.0 collective-permute-start.42
  435.7 5.5 %collective-permute-done.40 = bf16[24,4096]{1,0:T(8,128)(2,1)S(1)} collective-permute-done((bf16[24,4096]{1,0:T(8,128)(2,1)S(1)}, bf16[24,4096]{1,0:T(8,128)(2,1)S(1)}, u32[]{:S(2)}, u32[]{:S(2)}) %collective-permute-start.40) | collective-permute-done | bytes 196640 | tf_op jit(solution)/shard_map/ppermute | solution.py:249
  442.1 3.7 collective-permute-done.34
  447.2 7.6 %collective-permute-done.43 = bf16[96,2432]{1,0:T(8,128)(2,1)S(1)} collective-permute-done((bf16[96,2432]{1,0:T(8,128)(2,1)S(1)}, bf16[96,2432]{1,0:T(8,128)(2,1)S(1)}, u32[]{:S(2)}, u32[]{:S(2)}) %collective-permute-start.43) | collective-permute-done | bytes 466976 | tf_op jit(solution)/shard_map/ppermute | solution.py:234
  455.8 3.8 collective-permute-start.46
  461.0 3.7 collective-permute-done.45
  474.3 10.5 %all_to_all.11 = f32[32,1,128]{2,1,0:T(1,128)S(1)} all-to-all(f32[32,1,128]{2,1,0:T(1,128)S(1)} %broadcast_in_dim_broadcast_in_dim_broadcast_in_dim.3), channel_id=1, replica_groups=mesh['pb'=8,'pa'=4] {'pb','pa'}, dimensions={0} | all-to-all | bytes 32768 | tf_op jit(solution)/shard_map/all_to_all | solution.py:256
  (389 shorter events, 117.1 us)
Async XLA Ops:
  7.2 114.8 %all-gather.3.cloned.1.call-start = ((), (), s32[]{:S(2)}) async-start(), calls=%async_computation.2 | async-start | bytes 6856704 | tf_op jit(solution)/shard_map/all_gather | solution.py:119
  9.1 14.8 %collective-permute-start.1 = (bf16[24,2432]{1,0:T(8,128)(2,1)S(1)}, bf16[24,2432]{1,0:T(8,128)(2,1)S(1)}, u32[]{:S(2)}, u32[]{:S(2)}) collective-permute-start(bf16[24,2432]{1,0:T(8,128)(2,1)S(1)} %fusion.41), channel_id=1, source_target_pairs={{0,2},{1,3},{2,0},{3,1},{4,6},{5,7},{6,4},{7,5},{8,10},{9,11},{10,... | collective-permute-start | bytes 350216 | tf_op jit(solution)/shard_map/ppermute | solution.py:106
  13.2 10.7 %collective-permute-start.2 = (bf16[24,2432]{1,0:T(8,128)(2,1)S(1)}, bf16[24,2432]{1,0:T(8,128)(2,1)S(1)}, u32[]{:S(2)}, u32[]{:S(2)}) collective-permute-start(bf16[24,2432]{1,0:T(8,128)(2,1)S(1)} %fusion.41), channel_id=1, source_target_pairs={{0,1},{1,2},{2,3},{3,0},{4,5},{5,6},{6,7},{7,4},{8,9},{9,10},{10,1... | collective-permute-start | bytes 350216 | tf_op jit(solution)/shard_map/ppermute | solution.py:106
  14.8 9.1 %collective-permute-start = (bf16[24,2432]{1,0:T(8,128)(2,1)S(1)}, bf16[24,2432]{1,0:T(8,128)(2,1)S(1)}, u32[]{:S(2)}, u32[]{:S(2)}) collective-permute-start(bf16[24,2432]{1,0:T(8,128)(2,1)S(1)} %fusion.41), channel_id=1, source_target_pairs={{0,3},{1,0},{2,1},{3,2},{4,7},{5,4},{6,5},{7,6},{8,11},{9,8},{10,9... | collective-permute-start | bytes 350216 | tf_op jit(solution)/shard_map/ppermute | solution.py:106
  24.2 8.6 %collective-permute-start.3 = (bf16[96,2432]{1,0:T(8,128)(2,1)S(1)}, bf16[96,2432]{1,0:T(8,128)(2,1)S(1)}, u32[]{:S(2)}, u32[]{:S(2)}) collective-permute-start(bf16[96,2432]{1,0:T(8,128)(2,1)S(1)} %bitcast.371), channel_id=1, source_target_pairs={{0,8},{4,20},{8,0},{12,28},{16,24},{20,4},{24,16},{28,12},{1,9},{5... | collective-permute-start | bytes 1400840 | tf_op jit(solution)/shard_map/ppermute | solution.py:134
  34.0 13.6 %collective-permute-start.4 = (bf16[2,96,2432]{2,1,0:T(8,128)(2,1)S(1)}, bf16[2,96,2432]{2,1,0:T(8,128)(2,1)S(1)}, u32[]{:S(2)}, u32[]{:S(2)}) collective-permute-start(bf16[2,96,2432]{2,1,0:T(8,128)(2,1)S(1)} %shard_map.357.refs_0_), channel_id=1, source_target_pairs={{0,16},{4,12},{8,24},{12,4},{16,0},{20,28},{24,8},{28,20},{1,17},{... | collective-permute-start | bytes 2801672 | tf_op jit(solution)/shard_map/ppermute | solution.py:140
  36.9 11.8 %collective-permute-start.13 = (bf16[24,3968]{1,0:T(8,128)(2,1)S(1)}, bf16[24,3968]{1,0:T(8,128)(2,1)S(1)}, u32[]{:S(2)}, u32[]{:S(2)}) collective-permute-start(bf16[24,3968]{1,0:T(8,128)(2,1)S(1)} %pad_maximum_fusion.15), channel_id=1, source_target_pairs={{0,3},{1,0},{2,1},{3,2},{4,7},{5,4},{6,5},{7,6},{8,11},{9,8},{10,9... | collective-permute-start | bytes 571400 | tf_op jit(solution)/shard_map/ppermute | solution.py:106
  38.1 17.5 %collective-permute-start.12 = (bf16[24,3968]{1,0:T(8,128)(2,1)S(1)}, bf16[24,3968]{1,0:T(8,128)(2,1)S(1)}, u32[]{:S(2)}, u32[]{:S(2)}) collective-permute-start(bf16[24,3968]{1,0:T(8,128)(2,1)S(1)} %pad_maximum_fusion.15), channel_id=1, source_target_pairs={{0,2},{1,3},{2,0},{3,1},{4,6},{5,7},{6,4},{7,5},{8,10},{9,11},{10,... | collective-permute-start | bytes 571400 | tf_op jit(solution)/shard_map/ppermute | solution.py:106
  39.7 16.0 %collective-permute-start.11 = (bf16[24,3968]{1,0:T(8,128)(2,1)S(1)}, bf16[24,3968]{1,0:T(8,128)(2,1)S(1)}, u32[]{:S(2)}, u32[]{:S(2)}) collective-permute-start(bf16[24,3968]{1,0:T(8,128)(2,1)S(1)} %pad_maximum_fusion.15), channel_id=1, source_target_pairs={{0,1},{1,2},{2,3},{3,0},{4,5},{5,6},{6,7},{7,4},{8,9},{9,10},{10,1... | collective-permute-start | bytes 571400 | tf_op jit(solution)/shard_map/ppermute | solution.py:106
  57.0 122.9 %all-gather.5.cloned.1.call-start = ((), (), s32[]{:S(2)}) async-start(), calls=%async_computation.3 | async-start | bytes 1179648 | tf_op jit(solution)/shard_map/all_gather | solution.py:119
  57.1 3.9 collective-permute-start.5
  66.9 14.4 %collective-permute-start.8 = (bf16[96,768]{1,0:T(8,128)(2,1)S(1)}, bf16[96,768]{1,0:T(8,128)(2,1)S(1)}, u32[]{:S(2)}, u32[]{:S(2)}) collective-permute-start(bf16[96,768]{1,0:T(8,128)(2,1)S(1)} %copy-done.50), channel_id=1, source_target_pairs={{0,3},{1,0},{2,1},{3,2},{4,7},{5,4},{6,5},{7,6},{8,11},{9,8},{10,9... | collective-permute-start | bytes 442376 | tf_op jit(solution)/shard_map/ppermute | solution.py:106
  66.9 14.6 %collective-permute-start.7 = (bf16[96,768]{1,0:T(8,128)(2,1)S(1)}, bf16[96,768]{1,0:T(8,128)(2,1)S(1)}, u32[]{:S(2)}, u32[]{:S(2)}) collective-permute-start(bf16[96,768]{1,0:T(8,128)(2,1)S(1)} %copy-done.50), channel_id=1, source_target_pairs={{0,2},{1,3},{2,0},{3,1},{4,6},{5,7},{6,4},{7,5},{8,10},{9,11},{10,... | collective-permute-start | bytes 442376 | tf_op jit(solution)/shard_map/ppermute | solution.py:106
  68.0 13.6 %collective-permute-start.6 = (bf16[96,768]{1,0:T(8,128)(2,1)S(1)}, bf16[96,768]{1,0:T(8,128)(2,1)S(1)}, u32[]{:S(2)}, u32[]{:S(2)}) collective-permute-start(bf16[96,768]{1,0:T(8,128)(2,1)S(1)} %copy-done.50), channel_id=1, source_target_pairs={{0,1},{1,2},{2,3},{3,0},{4,5},{5,6},{6,7},{7,4},{8,9},{9,10},{10,1... | collective-permute-start | bytes 442376 | tf_op jit(solution)/shard_map/ppermute | solution.py:106
  81.7 22.1 %collective-permute-start.9 = (bf16[384,768]{1,0:T(8,128)(2,1)S(1)}, bf16[384,768]{1,0:T(8,128)(2,1)S(1)}, u32[]{:S(2)}, u32[]{:S(2)}) collective-permute-start(bf16[384,768]{1,0:T(8,128)(2,1)S(1)} %bitcast.367), channel_id=1, source_target_pairs={{0,8},{4,20},{8,0},{12,28},{16,24},{20,4},{24,16},{28,12},{1,9},{5... | collective-permute-start | bytes 1769480 | tf_op jit(solution)/shard_map/ppermute | solution.py:134
  104.6 16.3 %collective-permute-start.10 = (bf16[2,384,768]{2,1,0:T(8,128)(2,1)S(1)}, bf16[2,384,768]{2,1,0:T(8,128)(2,1)S(1)}, u32[]{:S(2)}, u32[]{:S(2)}) collective-permute-start(bf16[2,384,768]{2,1,0:T(8,128)(2,1)S(1)} %shard_map.362.refs_0_), channel_id=1, source_target_pairs={{0,16},{4,12},{8,24},{12,4},{16,0},{20,28},{24,8},{28,20},{1,17},{... | collective-permute-start | bytes 3538952 | tf_op jit(solution)/shard_map/ppermute | solution.py:140
  122.0 5.8 %collective-permute-start.14 = (bf16[2,2,384,768]{3,2,1,0:T(8,128)(2,1)S(1)}, bf16[2,2,384,768]{3,2,1,0:T(8,128)(2,1)}, u32[]{:S(2)}, u32[]{:S(2)}) collective-permute-start(bf16[2,2,384,768]{3,2,1,0:T(8,128)(2,1)S(1)} %shard_map.364.refs_0_), channel_id=1, source_target_pairs={{0,4},{4,0},{8,12},{12,8},{16,20},{20,16},{24,28},{28,24},{1,5},{5... | collective-permute-start | bytes 7077896 | tf_op jit(solution)/shard_map/ppermute | solution.py:147
  138.3 6.3 %collective-permute-start.16 = (bf16[128,128]{1,0:T(8,128)(2,1)S(1)}, bf16[128,128]{1,0:T(8,128)(2,1)S(1)}, u32[]{:S(2)}, u32[]{:S(2)}) collective-permute-start(bf16[128,128]{1,0:T(8,128)(2,1)S(1)} %slice.208), channel_id=1, source_target_pairs={{0,2},{1,3},{2,0},{3,1},{4,6},{5,7},{6,4},{7,5},{8,10},{9,11},{10,... | collective-permute-start | bytes 98312 | tf_op jit(solution)/shard_map/ppermute | solution.py:106
  140.6 5.7 %collective-permute-start.17 = (bf16[128,128]{1,0:T(8,128)(2,1)S(1)}, bf16[128,128]{1,0:T(8,128)(2,1)S(1)}, u32[]{:S(2)}, u32[]{:S(2)}) collective-permute-start(bf16[128,128]{1,0:T(8,128)(2,1)S(1)} %slice.208), channel_id=1, source_target_pairs={{0,1},{1,2},{2,3},{3,0},{4,5},{5,6},{6,7},{7,4},{8,9},{9,10},{10,1... | collective-permute-start | bytes 98312 | tf_op jit(solution)/shard_map/ppermute | solution.py:106
  141.0 5.3 %collective-permute-start.15 = (bf16[128,128]{1,0:T(8,128)(2,1)S(1)}, bf16[128,128]{1,0:T(8,128)(2,1)S(1)}, u32[]{:S(2)}, u32[]{:S(2)}) collective-permute-start(bf16[128,128]{1,0:T(8,128)(2,1)S(1)} %slice.208), channel_id=1, source_target_pairs={{0,3},{1,0},{2,1},{3,2},{4,7},{5,4},{6,5},{7,6},{8,11},{9,8},{10,9... | collective-permute-start | bytes 98312 | tf_op jit(solution)/shard_map/ppermute | solution.py:106
  194.3 13.0 %all-to-all-start = ((f32[32,1,128]{2,1,0:T(1,128)}), f32[32,1,128]{2,1,0:T(1,128)S(1)}, u32[]{:S(2)}, u32[]{:S(2)}) async-start(f32[32,1,128]{2,1,0:T(1,128)} %broadcast_in_dim.17), calls=%async_computation | async-start | bytes 32768 | tf_op jit(solution)/shard_map/all_to_all | solution.py:256
  221.6 3.0 collective-permute-start.18
  227.0 10.8 %collective-permute-start.19 = (bf16[2,512,256]{2,1,0:T(8,128)(2,1)}, bf16[2,512,256]{2,1,0:T(8,128)(2,1)S(1)}, u32[]{:S(2)}, u32[]{:S(2)}) collective-permute-start(bf16[2,512,256]{2,1,0:T(8,128)(2,1)} %pad_maximum_fusion.7), channel_id=1, source_target_pairs={{0,16},{4,12},{8,24},{12,4},{16,0},{20,28},{24,8},{28,20},{1,17},{... | collective-permute-start | bytes 1572872 | tf_op jit(solution)/shard_map/ppermute | solution.py:226
  238.0 23.7 %collective-permute-start.20 = (bf16[512,256]{1,0:T(8,128)(2,1)S(1)}, bf16[512,256]{1,0:T(8,128)(2,1)S(1)}, u32[]{:S(2)}, u32[]{:S(2)}) collective-permute-start(bf16[512,256]{1,0:T(8,128)(2,1)S(1)} %pad_maximum_fusion.10), channel_id=1, source_target_pairs={{0,8},{4,20},{8,0},{12,28},{16,24},{20,4},{24,16},{28,12},{1,9},{5... | collective-permute-start | bytes 786440 | tf_op jit(solution)/shard_map/ppermute | solution.py:234
  261.9 4.8 collective-permute-start.23
  262.6 7.8 %collective-permute-start.22 = (bf16[128,256]{1,0:T(8,128)(2,1)S(1)}, bf16[128,256]{1,0:T(8,128)(2,1)S(1)}, u32[]{:S(2)}, u32[]{:S(2)}) collective-permute-start(bf16[128,256]{1,0:T(8,128)(2,1)S(1)} %pad_maximum_fusion.22), channel_id=1, source_target_pairs={{0,2},{1,3},{2,0},{3,1},{4,6},{5,7},{6,4},{7,5},{8,10},{9,11},{10,... | collective-permute-start | bytes 196616 | tf_op jit(solution)/shard_map/ppermute | solution.py:249
  264.0 6.4 %collective-permute-start.21 = (bf16[128,256]{1,0:T(8,128)(2,1)S(1)}, bf16[128,256]{1,0:T(8,128)(2,1)S(1)}, u32[]{:S(2)}, u32[]{:S(2)}) collective-permute-start(bf16[128,256]{1,0:T(8,128)(2,1)S(1)} %pad_maximum_fusion.21), channel_id=1, source_target_pairs={{0,1},{1,2},{2,3},{3,0},{4,5},{5,6},{6,7},{7,4},{8,9},{9,10},{10,1... | collective-permute-start | bytes 196616 | tf_op jit(solution)/shard_map/ppermute | solution.py:249
  298.2 21.7 %collective-permute-start.24 = (bf16[4,384,768]{2,1,0:T(8,128)(2,1)}, bf16[4,384,768]{2,1,0:T(8,128)(2,1)}, u32[]{:S(2)}, u32[]{:S(2)}) collective-permute-start(bf16[4,384,768]{2,1,0:T(8,128)(2,1)} %fusion.2), channel_id=1, source_target_pairs={{0,4},{4,0},{8,12},{12,8},{16,20},{20,16},{24,28},{28,24},{1,5},{5... | collective-permute-start | bytes 7077896 | tf_op jit(solution)/shard_map/ppermute | solution.py:207
  299.9 26.5 %collective-permute-start.35 = (bf16[4,96,3072]{2,1,0:T(8,128)(2,1)}, bf16[4,96,3072]{2,1,0:T(8,128)(2,1)}, u32[]{:S(2)}, u32[]{:S(2)}) collective-permute-start(bf16[4,96,3072]{2,1,0:T(8,128)(2,1)} %fusion.3), channel_id=1, source_target_pairs={{0,4},{4,0},{8,12},{12,8},{16,20},{20,16},{24,28},{28,24},{1,5},{5... | collective-permute-start | bytes 7077896 | tf_op jit(solution)/shard_map/ppermute | solution.py:207
  302.6 14.9 %collective-permute-start.37 = (f32[4,96,128]{2,1,0:T(8,128)}, f32[4,96,128]{2,1,0:T(8,128)}, u32[]{:S(2)}, u32[]{:S(2)}) collective-permute-start(f32[4,96,128]{2,1,0:T(8,128)} %dynamic-slice_bitcast_fusion.1), channel_id=1, source_target_pairs={{0,4},{4,0},{8,12},{12,8},{16,20},{20,16},{24,28},{28,24},{1,5},{5... | collective-permute-start | bytes 589832 | tf_op jit(solution)/shard_map/ppermute | solution.py:207
  307.1 11.5 %collective-permute-start.36 = (bf16[4,96,768]{2,1,0:T(8,128)(2,1)S(1)}, bf16[4,96,768]{2,1,0:T(8,128)(2,1)}, u32[]{:S(2)}, u32[]{:S(2)}) collective-permute-start(bf16[4,96,768]{2,1,0:T(8,128)(2,1)S(1)} %fusion.18), channel_id=1, source_target_pairs={{0,4},{4,0},{8,12},{12,8},{16,20},{20,16},{24,28},{28,24},{1,5},{5... | collective-permute-start | bytes 1769480 | tf_op jit(solution)/shard_map/ppermute | solution.py:207
  325.0 26.0 %collective-permute-start.25 = (bf16[2,384,768]{2,1,0:T(8,128)(2,1)}, bf16[2,384,768]{2,1,0:T(8,128)(2,1)}, u32[]{:S(2)}, u32[]{:S(2)}) collective-permute-start(bf16[2,384,768]{2,1,0:T(8,128)(2,1)} %pad_maximum_fusion.2), channel_id=1, source_target_pairs={{0,16},{4,12},{8,24},{12,4},{16,0},{20,28},{24,8},{28,20},{1,17},{... | collective-permute-start | bytes 3538952 | tf_op jit(solution)/shard_map/ppermute | solution.py:226
  330.3 31.0 %collective-permute-start.38 = (bf16[2,96,4096]{2,1,0:T(8,128)(2,1)}, bf16[2,96,4096]{2,1,0:T(8,128)(2,1)}, u32[]{:S(2)}, u32[]{:S(2)}) collective-permute-start(bf16[2,96,4096]{2,1,0:T(8,128)(2,1)} %pad_maximum_fusion.1), channel_id=1, source_target_pairs={{0,16},{4,12},{8,24},{12,4},{16,0},{20,28},{24,8},{28,20},{1,17},{... | collective-permute-start | bytes 4718600 | tf_op jit(solution)/shard_map/ppermute | solution.py:226
  352.6 14.1 %collective-permute-start.26 = (bf16[384,768]{1,0:T(8,128)(2,1)S(1)}, bf16[384,768]{1,0:T(8,128)(2,1)S(1)}, u32[]{:S(2)}, u32[]{:S(2)}) collective-permute-start(bf16[384,768]{1,0:T(8,128)(2,1)S(1)} %fusion.13), channel_id=1, source_target_pairs={{0,8},{4,20},{8,0},{12,28},{16,24},{20,4},{24,16},{28,12},{1,9},{5... | collective-permute-start | bytes 1769480 | tf_op jit(solution)/shard_map/ppermute | solution.py:234
  364.9 25.9 %collective-permute-start.39 = (bf16[96,4096]{1,0:T(8,128)(2,1)S(1)}, bf16[96,4096]{1,0:T(8,128)(2,1)S(1)}, u32[]{:S(2)}, u32[]{:S(2)}) collective-permute-start(bf16[96,4096]{1,0:T(8,128)(2,1)S(1)} %pad_maximum_fusion.3), channel_id=1, source_target_pairs={{0,8},{4,20},{8,0},{12,28},{16,24},{20,4},{24,16},{28,12},{1,9},{5... | collective-permute-start | bytes 2359304 | tf_op jit(solution)/shard_map/ppermute | solution.py:234
  366.8 23.3 %collective-permute-start.27 = (bf16[96,768]{1,0:T(8,128)(2,1)S(1)}, bf16[96,768]{1,0:T(8,128)(2,1)S(1)}, u32[]{:S(2)}, u32[]{:S(2)}) collective-permute-start(bf16[96,768]{1,0:T(8,128)(2,1)S(1)} %get-tuple-element.388), channel_id=1, source_target_pairs={{0,1},{1,2},{2,3},{3,0},{4,5},{5,6},{6,7},{7,4},{8,9},{9,10},{10,1... | collective-permute-start | bytes 442376 | tf_op jit(solution)/shard_map/ppermute | solution.py:249
  366.9 23.3 %collective-permute-start.29 = (bf16[96,768]{1,0:T(8,128)(2,1)S(1)}, bf16[96,768]{1,0:T(8,128)(2,1)S(1)}, u32[]{:S(2)}, u32[]{:S(2)}) collective-permute-start(bf16[96,768]{1,0:T(8,128)(2,1)S(1)} %get-tuple-element.389), channel_id=1, source_target_pairs={{0,3},{1,0},{2,1},{3,2},{4,7},{5,4},{6,5},{7,6},{8,11},{9,8},{10,9... | collective-permute-start | bytes 442376 | tf_op jit(solution)/shard_map/ppermute | solution.py:249
  370.7 19.5 %collective-permute-start.28 = (bf16[96,768]{1,0:T(8,128)(2,1)S(1)}, bf16[96,768]{1,0:T(8,128)(2,1)S(1)}, u32[]{:S(2)}, u32[]{:S(2)}) collective-permute-start(bf16[96,768]{1,0:T(8,128)(2,1)S(1)} %get-tuple-element.390), channel_id=1, source_target_pairs={{0,2},{1,3},{2,0},{3,1},{4,6},{5,7},{6,4},{7,5},{8,10},{9,11},{10,... | collective-permute-start | bytes 442376 | tf_op jit(solution)/shard_map/ppermute | solution.py:249
  422.7 6.2 %collective-permute-start.33 = (bf16[4,96,128]{2,1,0:T(8,128)(2,1)S(1)}, bf16[4,96,128]{2,1,0:T(8,128)(2,1)S(1)}, u32[]{:S(2)}, u32[]{:S(2)}) collective-permute-start(bf16[4,96,128]{2,1,0:T(8,128)(2,1)S(1)} %fusion.43), channel_id=1, source_target_pairs={{0,4},{4,0},{8,12},{12,8},{16,20},{20,16},{24,28},{28,24},{1,5},{5... | collective-permute-start | bytes 294920 | tf_op jit(solution)/shard_map/ppermute | solution.py:207
  423.7 12.0 %collective-permute-start.41 = (bf16[24,4096]{1,0:T(8,128)(2,1)S(1)}, bf16[24,4096]{1,0:T(8,128)(2,1)S(1)}, u32[]{:S(2)}, u32[]{:S(2)}) collective-permute-start(bf16[24,4096]{1,0:T(8,128)(2,1)S(1)} %pad_maximum_fusion.13), channel_id=1, source_target_pairs={{0,2},{1,3},{2,0},{3,1},{4,6},{5,7},{6,4},{7,5},{8,10},{9,11},{10,... | collective-permute-start | bytes 589832 | tf_op jit(solution)/shard_map/ppermute | solution.py:249
  423.8 11.9 %collective-permute-start.42 = (bf16[24,4096]{1,0:T(8,128)(2,1)S(1)}, bf16[24,4096]{1,0:T(8,128)(2,1)S(1)}, u32[]{:S(2)}, u32[]{:S(2)}) collective-permute-start(bf16[24,4096]{1,0:T(8,128)(2,1)S(1)} %pad_maximum_fusion.14), channel_id=1, source_target_pairs={{0,3},{1,0},{2,1},{3,2},{4,7},{5,4},{6,5},{7,6},{8,11},{9,8},{10,9... | collective-permute-start | bytes 589832 | tf_op jit(solution)/shard_map/ppermute | solution.py:249
  428.3 3.3 collective-permute-start.31
  432.1 13.6 %collective-permute-start.34 = (bf16[2,96,2432]{2,1,0:T(8,128)(2,1)S(1)}, bf16[2,96,2432]{2,1,0:T(8,128)(2,1)S(1)}, u32[]{:S(2)}, u32[]{:S(2)}) collective-permute-start(bf16[2,96,2432]{2,1,0:T(8,128)(2,1)S(1)} %maximum_maximum_fusion), channel_id=1, source_target_pairs={{0,16},{4,12},{8,24},{12,4},{16,0},{20,28},{24,8},{28,20},{1,17},{... | collective-permute-start | bytes 2801672 | tf_op jit(solution)/shard_map/ppermute | solution.py:226
  433.7 7.6 %collective-permute-start.40 = (bf16[24,4096]{1,0:T(8,128)(2,1)S(1)}, bf16[24,4096]{1,0:T(8,128)(2,1)S(1)}, u32[]{:S(2)}, u32[]{:S(2)}) collective-permute-start(bf16[24,4096]{1,0:T(8,128)(2,1)S(1)} %pad_maximum_fusion.12), channel_id=1, source_target_pairs={{0,1},{1,2},{2,3},{3,0},{4,5},{5,6},{6,7},{7,4},{8,9},{9,10},{10,1... | collective-permute-start | bytes 589832 | tf_op jit(solution)/shard_map/ppermute | solution.py:249
  446.1 8.6 %collective-permute-start.43 = (bf16[96,2432]{1,0:T(8,128)(2,1)S(1)}, bf16[96,2432]{1,0:T(8,128)(2,1)S(1)}, u32[]{:S(2)}, u32[]{:S(2)}) collective-permute-start(bf16[96,2432]{1,0:T(8,128)(2,1)S(1)} %pad_maximum_fusion.9), channel_id=1, source_target_pairs={{0,8},{4,20},{8,0},{12,28},{16,24},{20,4},{24,16},{28,12},{1,9},{5... | collective-permute-start | bytes 1400840 | tf_op jit(solution)/shard_map/ppermute | solution.py:234
  455.1 9.6 %collective-permute-start.45 = (bf16[24,2432]{1,0:T(8,128)(2,1)S(1)}, bf16[24,2432]{1,0:T(8,128)(2,1)}, u32[]{:S(2)}, u32[]{:S(2)}) collective-permute-start(bf16[24,2432]{1,0:T(8,128)(2,1)S(1)} %pad_maximum_fusion.18), channel_id=1, source_target_pairs={{0,2},{1,3},{2,0},{3,1},{4,6},{5,7},{6,4},{7,5},{8,10},{9,11},{10,... | collective-permute-start | bytes 350216 | tf_op jit(solution)/shard_map/ppermute | solution.py:249
  455.8 9.7 %collective-permute-start.46 = (bf16[24,2432]{1,0:T(8,128)(2,1)}, bf16[24,2432]{1,0:T(8,128)(2,1)}, u32[]{:S(2)}, u32[]{:S(2)}) collective-permute-start(bf16[24,2432]{1,0:T(8,128)(2,1)} %pad_maximum_fusion.19), channel_id=1, source_target_pairs={{0,3},{1,0},{2,1},{3,2},{4,7},{5,4},{6,5},{7,6},{8,11},{9,8},{10,9... | collective-permute-start | bytes 350216 | tf_op jit(solution)/shard_map/ppermute | solution.py:249
  459.6 6.9 %collective-permute-start.44 = (bf16[24,2432]{1,0:T(8,128)(2,1)S(1)}, bf16[24,2432]{1,0:T(8,128)(2,1)}, u32[]{:S(2)}, u32[]{:S(2)}) collective-permute-start(bf16[24,2432]{1,0:T(8,128)(2,1)S(1)} %pad_maximum_fusion.17), channel_id=1, source_target_pairs={{0,1},{1,2},{2,3},{3,0},{4,5},{5,6},{6,7},{7,4},{8,9},{9,10},{10,1... | collective-permute-start | bytes 350216 | tf_op jit(solution)/shard_map/ppermute | solution.py:249
  (67 other events, 534.9 us)
Sparse Core Ops, SparseCore 0:
  57.1 48.3 all-gather.2
  147.9 24.2 all-gather.4

commit v3 on v2

--- a/solution.py
+++ b/solution.py
@@ -16,8 +16,8 @@
 QPD = 4
 QUERY_ROWS = QPD * QLEN
 TOKENS = BIN + QUERY_ROWS
-ATTEND_TILE = 512
-FEED_ROWS = 512
+ATTEND_TILE = 256
+FEED_ROWS = 256
 BACK_ROWS = 256
 
 
@@ -193,20 +193,29 @@
     return [lax.dynamic_index_in_dim(array, place, 0, False) for array in arrays]
 
 
-def scatter_quad(arrays, exact, *others):
+def core_blocks(array, other):
+    core = position()[1]
+    parts = array.reshape((4, 2, array.shape[0] // 8) + array.shape[1:])
+    return lax.dynamic_index_in_dim(parts, 1 - core if other else core, 1, False)
+
+
+def scatter_sends(arrays, exact):
+    if not staged_mesh():
+        return arrays
+    sends = [core_blocks(array, True) for array in arrays]
+    return [a if whole else a.astype(LOW) for a, whole in zip(sends, exact)]
+
+
+def scatter_quad(arrays, sends, *others):
     if not staged_mesh():
         return [
             lax.psum_scatter(a.astype(F32), "pb", scatter_dimension=0, tiled=True)
             for a in arrays
         ]
-    core = position()[1]
-    results = []
-    for array, whole in zip(arrays, exact):
-        parts = array.reshape((4, 2, array.shape[0] // 8) + array.shape[1:])
-        keep, send = (lax.dynamic_index_in_dim(parts, c, 1, False) for c in (core, 1 - core))
-        moved = lax.ppermute(send if whole else send.astype(LOW), "pb", CORE_PAIR)
-        results.append(keep.astype(F32) + gate(moved, others).astype(F32))
-    return results
+    moved = gate([lax.ppermute(a, "pb", CORE_PAIR) for a in sends], others)
+    return [
+        core_blocks(array, False).astype(F32) + m.astype(F32) for array, m in zip(arrays, moved)
+    ]
 
 
 def scatter_pair(arrays, exact, *others):
@@ -291,6 +300,17 @@
         (array.shape[0], width), lambda i: (0, low // width), pipeline_mode=pl.Buffered(1)
     )
     return array, spec
+
+
+def transposed(array):
+    rows, width = array.shape
+    return pl.pallas_call(
+        lambda x_ref, out_ref: out_ref.__setitem__(Ellipsis, x_ref[...].T),
+        grid=(width // 128,),
+        in_specs=[pl.BlockSpec((rows, 128), lambda i: (0, i))],
+        out_specs=pl.BlockSpec((128, rows), lambda i: (i, 0)),
+        out_shape=jax.ShapeDtypeStruct((width, rows), array.dtype),
+    )(array)
 
 
 def row_call(kernel, rows, first, count, inputs, weights, outputs, sums=(), into=None, flops=0):
@@ -402,48 +422,42 @@
     gatt_ref[...] = dot(gone_low, out_w[...], ACROSS).astype(LOW)
 
 
-def attend_kernel(tile, spans, q_ref, k_ref, v_ref, col, row, out_ref, total_ref, logits, flipped):
+def attend_kernel(
+    tile, lengths, spans, q_ref, k_ref, v_ref, col, row, out_ref, total_ref, logits, probs, flipped
+):
     flipped[...] = v_ref[...].T
     lane = lax.broadcasted_iota(jnp.int32, (tile, 128), 1)
 
     def block(index, carry):
         here = pl.ds(pl.multiple_of(index * tile, tile), tile)
-        query = q_ref[here, :] * jnp.asarray(0.125, LOW)
-        zero = jnp.zeros_like(query)
-        pair = (jnp.where(lane < 64, query, zero), jnp.where(lane < 64, zero, query))
-        segment = row[0:1, here]
-        low, high = spans[index, 0], spans[index, 1]
-
-        def score(step, tops):
-            there = pl.ds(pl.multiple_of(step * tile, tile), tile)
-            keys = k_ref[there, :]
-            same = col[there, :] == segment
-            result = []
+        low, kind = spans[index, 0], spans[index, 1]
+
+        def attend(length):
+            there = pl.ds(pl.multiple_of(low, 128), length)
+            query = q_ref[here, :] * jnp.asarray(0.125, LOW)
+            same = col[there, :] == row[0:1, here]
+            tops = []
             for head in range(2):
-                value = jnp.where(same, dot(keys, pair[head], ACROSS), -1e30)
-                logits[head, there, :] = value
-                result.append(jnp.maximum(tops[head], jnp.max(value, 0, keepdims=True)))
-            return tuple(result)
-
-        lowest = jnp.full((1, tile), -1e30, F32)
-        tops = lax.fori_loop(low, high, score, (lowest, lowest))
-
-        def mix(step, state):
-            there = pl.ds(pl.multiple_of(step * tile, tile), tile)
-            result = []
+                own = jnp.where((lane < 64) == (head == 0), query, jnp.zeros_like(query))
+                value = jnp.where(same, dot(k_ref[there, :], own, ACROSS), -1e30)
+                logits[head, 0:length, :] = value
+                top = jnp.max(value.reshape(-1, 8, tile), 0)
+                tops.append(jnp.max(top, 0, keepdims=True))
+            sums = []
             for head in range(2):
-                term = jnp.exp(logits[head, there, :] - tops[head])
-                result.append(state[2 * head] + jnp.sum(term, 0, keepdims=True))
+                term = jnp.exp(logits[head, 0:length, :] - tops[head])
+                sums.append(jnp.sum(term.reshape(-1, 8, tile), 0))
+                probs[head, 0:length, :] = term.astype(LOW)
+            parts = []
+            for head in range(2):
+                total = jnp.sum(sums[head], 0, keepdims=True)
                 values = flipped[64 * head : 64 * head + 64, there]
-                result.append(state[2 * head + 1] + dot(values, term.astype(LOW)))
-            return tuple(result)
-
-        none, empty = jnp.zeros((1, tile), F32), jnp.zeros((64, tile), F32)
-        sum0, mix0, sum1, mix1 = lax.fori_loop(low, high, mix, (none, empty, none, empty))
-        both = jnp.concatenate([mix0 / sum0, mix1 / sum1], 0)
-        out_ref[here, :] = both.T.astype(LOW)
-        total_ref[0, 0:1, here] = tops[0] + jnp.log(sum0)
-        total_ref[0, 1:2, here] = tops[1] + jnp.log(sum1)
+                parts.append(dot(values, probs[head, 0:length, :]) / total)
+                total_ref[0, head : head + 1, here] = tops[head] + jnp.log(total)
+            out_ref[here, :] = jnp.concatenate(parts, 0).T.astype(LOW)
+
+        for number, length in enumerate(lengths):
+            pl.when(kind == number)(functools.partial(attend, length))
         return carry
 
     lax.fori_loop(0, q_ref.shape[0] // tile, block, 0)
@@ -451,6 +465,12 @@
 
 def head_pair(count, row, first):
     return pl.BlockSpec((count, 128), lambda h, s: (row, first + h))
+
+
+def attend_lengths(count):
+    return [length for length in (128, 256, 384, 512, 640, 768, 1024) if count < 256 or length > 128][
+        : 1 if count < 256 else None
+    ]
 
 
 def attend_call(kernel, tile, count, pairs, tables, arrays, specs, outputs, into, scratch, cost):
@@ -468,7 +488,7 @@
         arguments += list(into)
 
     def run(*refs):
-        kernel(tile, *refs[:used], *refs[len(arguments) :])
+        kernel(tile, attend_lengths(count), *refs[:used], *refs[len(arguments) :])
 
     return pl.pallas_call(
         run,
@@ -508,78 +528,72 @@
             ),
         ],
         into,
-        [pltpu.VMEM((2, count, tile), F32), pltpu.VMEM((128, count), LOW)],
+        [
+            pltpu.VMEM((2, count, tile), F32),
+            pltpu.VMEM((2, count, tile), LOW),
+            pltpu.VMEM((128, count), LOW),
+        ],
         40,
     )
 
 
 def attend_back_kernel(
-    tile, spans, q_ref, k_ref, v_ref, g_ref, total_ref, col, row,
-    grad_ref, sum_ref, flipped, gkey, gvalue, probs, gprobs,
+    tile, lengths, spans, q_ref, k_ref, v_ref, g_ref, total_ref, col, row,
+    grad_ref, sum_ref, flipped, gkey, gvalue, probs, gprobs, low_probs, low_deltas,
 ):
     flipped[...] = k_ref[...].T
     gkey[...] = jnp.zeros_like(gkey)
     gvalue[...] = jnp.zeros_like(gvalue)
+    sum_ref[...] = jnp.zeros_like(sum_ref)
     lane = lax.broadcasted_iota(jnp.int32, (tile, 128), 1)
 
-    def block(index, query_sum):
+    def block(index, carry):
         here = pl.ds(pl.multiple_of(index * tile, tile), tile)
-        query = q_ref[here, :] * jnp.asarray(0.125, LOW)
-        zero = jnp.zeros_like(query)
-        queries = (jnp.where(lane < 64, query, zero), jnp.where(lane < 64, zero, query))
-        grad = g_ref[here, :]
-        grads = (jnp.where(lane < 64, grad, zero), jnp.where(lane < 64, zero, grad))
-        totals = (total_ref[0, 0:1, here], total_ref[0, 1:2, here])
-        segment = row[0:1, here]
-        low, high = spans[index, 0], spans[index, 1]
-
-        def first(step, dots):
-            there = pl.ds(pl.multiple_of(step * tile, tile), tile)
-            keys, values = k_ref[there, :], v_ref[there, :]
-            same = col[there, :] == segment
-            result = []
-            part = None
+        low, kind = spans[index, 0], spans[index, 1]
+
+        def attend(length):
+            there = pl.ds(pl.multiple_of(low, 128), length)
+            query, grad = q_ref[here, :] * jnp.asarray(0.125, LOW), g_ref[here, :]
+            zero = jnp.zeros_like(query)
+            same = col[there, :] == row[0:1, here]
+            own = [(lane < 64) == (head == 0) for head in range(2)]
+            queries = [jnp.where(mine, query, zero) for mine in own]
+            grads = [jnp.where(mine, grad, zero) for mine in own]
+            dots = []
             for head in range(2):
-                logit = dot(keys, queries[head], ACROSS)
-                prob = jnp.where(same, jnp.exp(logit - totals[head]), 0.0)
-                gprob = dot(values, grads[head], ACROSS)
-                probs[head, there, :] = prob
-                gprobs[head, there, :] = gprob
-                result.append(dots[head] + jnp.sum(prob * gprob, 0, keepdims=True))
-                more = dot(prob.astype(LOW), grads[head])
-                part = more if part is None else part + more
-            gvalue[there, :] += part
-            return tuple(result)
-
-        none = jnp.zeros((1, tile), F32)
-        dots = lax.fori_loop(low, high, first, (none, none))
-
-        def second(step, state):
-            there = pl.ds(pl.multiple_of(step * tile, tile), tile)
-            result = []
-            part = None
+                prob = dot(k_ref[there, :], queries[head], ACROSS)
+                prob = jnp.exp(prob - total_ref[0, head : head + 1, here])
+                prob = jnp.where(same, prob, 0.0)
+                gprob = dot(v_ref[there, :], grads[head], ACROSS)
+                total = jnp.sum((prob * gprob).reshape(-1, 8, tile), 0)
+                dots.append(jnp.sum(total, 0, keepdims=True))
+                probs[head, 0:length, :] = prob
+                gprobs[head, 0:length, :] = gprob
+                low_probs[head, 0:length, :] = prob.astype(LOW)
+
+            def both(terms, right):
+                return dot(terms[0, 0:length, :], right[0]) + dot(terms[1, 0:length, :], right[1])
+
+            gvalue[there, :] += both(low_probs, grads)
             for head in range(2):
-                delta = probs[head, there, :] * (gprobs[head, there, :] - dots[head])
-                delta = delta.astype(LOW)
-                more = dot(delta, queries[head])
-                part = more if part is None else part + more
+                delta = gprobs[head, 0:length, :] - dots[head]
+                low_deltas[head, 0:length, :] = (probs[head, 0:length, :] * delta).astype(LOW)
+            gkey[there, :] += both(low_deltas, queries)
+            parts = []
+            for head in range(2):
                 keys = flipped[64 * head : 64 * head + 64, there]
-                result.append(state[head] + dot(keys, delta))
-            gkey[there, :] += part
-            return tuple(result)
-
-        empty = jnp.zeros((64, tile), F32)
-        both = lax.fori_loop(low, high, second, (empty, empty))
-        whole = jnp.concatenate(both, 0).T * 0.125
-        grad_ref[0, here, :] = whole.astype(LOW)
-        return query_sum + jnp.sum(whole, 0, keepdims=True)
-
-    count = q_ref.shape[0]
-    query_sum = lax.fori_loop(0, count // tile, block, jnp.zeros((1, 128), F32))
+                parts.append(dot(keys, low_deltas[head, 0:length, :]))
+            whole = jnp.concatenate(parts, 0).T * 0.125
+            grad_ref[0, here, :] = whole.astype(LOW)
+            sum_ref[0:1, :] += jnp.sum(whole, 0, keepdims=True)
+
+        for number, length in enumerate(lengths):
+            pl.when(kind == number)(functools.partial(attend, length))
+        return carry
+
+    lax.fori_loop(0, q_ref.shape[0] // tile, block, 0)
     grad_ref[1] = gkey[...].astype(LOW)
     grad_ref[2] = gvalue[...].astype(LOW)
-    sum_ref[...] = jnp.zeros_like(sum_ref)
-    sum_ref[0:1, :] = query_sum
     sum_ref[1:2, :] = jnp.sum(gvalue[...], 0, keepdims=True)
 
 
@@ -614,6 +628,8 @@
             pltpu.VMEM((count, 128), F32),
             pltpu.VMEM((2, count, tile), F32),
             pltpu.VMEM((2, count, tile), F32),
+            pltpu.VMEM((2, count, tile), LOW),
+            pltpu.VMEM((2, count, tile), LOW),
         ],
         80,
     )
@@ -621,11 +637,15 @@
 
 def segment_tables(segment, tile):
     count = segment.shape[0]
+    lengths = jnp.asarray(attend_lengths(count), jnp.int32)
     ends = segment.reshape(count // tile, tile)
-    first = jnp.sum((segment[None, :] < ends[:, :1]).astype(jnp.int32), 1)
+    first = jnp.sum((segment[None, :] < ends[:, :1]).astype(jnp.int32), 1) // 128 * 128
     last = jnp.sum((segment[None, :] <= ends[:, -1:]).astype(jnp.int32), 1)
+    kind = jnp.sum((lengths[None, :] < (last - first)[:, None]).astype(jnp.int32), 1)
+    chosen = jnp.arange(lengths.shape[0], dtype=jnp.int32)[None, :] == kind[:, None]
+    keys = jnp.sum(jnp.where(chosen, lengths[None, :], 0), 1)
     return (
-        jnp.stack([first // tile, (last + tile - 1) // tile], 1),
+        jnp.stack([jnp.minimum(first, count - keys), kind], 1),
         jnp.broadcast_to(segment[:, None], (count, tile)),
         jnp.broadcast_to(segment[None, :], (8, count)),
     )
@@ -637,12 +657,12 @@
 
 
 def sharp(cosine):
-    return jnp.exp(cosine * 10.0 - 10.0)
+    return jnp.exp2(cosine * 14.426950408889634 - 14.426950408889634)
 
 
 def score_kernel(query_ref, passage_ref, member_ref, score_ref, sums_ref):
-    high, rest = two_terms(sharp(dot(query_ref[...], passage_ref[...], ACROSS)))
-    sums = dot(high, member_ref[...]) + dot(rest, member_ref[...])
+    terms = sharp(dot(query_ref[...], passage_ref[...], ACROSS)).astype(LOW)
+    sums = dot(terms, member_ref[...])
     sums_ref[...] = sums
     lane = lax.broadcasted_iota(jnp.int32, sums.shape, 1)
     soft = jnp.where(lane < PPB, 0.1 * jnp.log(jnp.where(lane < PPB, sums, 1.0)) + 1.0, 0.0)
@@ -789,9 +809,10 @@
     first_line = line_of(first_part, send_line(first_part))
     middle_moved = send_line(gate(middle_part, first_line))
     first_pair = gather_pair(first_line)
-    ready = gate((tokens, query_tables, passage_tables, member), first_pair)
+    turned = transposed(tokens)
+    ready = gate((tokens, turned, query_tables, passage_tables, member), first_pair)
     first_quad = gather_quad(first_pair, ready)
-    tokens, query_tables, passage_tables, member = ready
+    tokens, turned, query_tables, passage_tables, member = ready
     middle = gather_rest(line_of(middle_part, gate(middle_moved, first_quad)))
     qkv_matrix, vectors = gather_whole(first_quad, [(0, 2304), (2304, 2432)])
     vectors = vectors[:, :12].T.astype(F32)
@@ -871,7 +892,7 @@
         score_query_kernel, every_query, passage_unit, member, grad_scores, totals
     )
     whole, rounded = (True,), (False,)
-    query_back = scatter_quad([grad_every], whole)
+    query_back = scatter_quad([grad_every], scatter_sends([grad_every], whole))
     grad_passage = score_backward(
         score_passage_kernel,
         gate(every_query, query_back),
@@ -914,13 +935,17 @@
         )
 
     down_terms = terms(active, gtwo)
-    up_terms = terms(normed, gate(ghid, down_terms))
-    down_back = scatter_quad([down_terms], rounded, up_terms)
-    down_back = scatter_pair(down_back, rounded)
-    rest = gate((gone, gproj), up_terms)
-    out_terms, proj_terms = terms(attended, rest[0]), terms(normed_out, rest[1])
+    down_sends = scatter_sends([down_terms], rounded)
+    up_terms = terms(normed, gate(ghid, down_sends))
+    down_back = scatter_quad([down_terms], down_sends, up_terms)
+    down_pair = scatter_pair(down_back, rounded)
+    rest = gate((gone, gproj), down_back)
+    out_terms, proj_terms = terms(attended, rest[0]), terms(rest[1], normed_out).T
+    kinds = (False, False, True)
+    middle_terms = [up_terms, out_terms, proj_terms]
+    middle_sends = scatter_sends(middle_terms, kinds)
     query_grads = attend_backward(
-        gate(query_mixed, out_terms, proj_terms),
+        gate(query_mixed, middle_sends),
         gatt,
         query_log,
         query_tables,
@@ -929,22 +954,23 @@
         6,
         BIN // QUERY_ROWS,
     )
-    kinds = (False, False, True)
-    middle_back = scatter_quad([up_terms, out_terms, proj_terms], kinds, query_grads)
-    middle_back = scatter_pair(middle_back, kinds)
-    down_back = scatter_line(down_back, rounded)
-    grads = attend_back(0, 2, query_grads[:1], query_grads)
-    (down_sum,) = scatter_total(gate(down_back, grads), rounded)
-    middle_back = scatter_line(gate(middle_back, grads), kinds)
-    grads = attend_back(2, 2, grads)
-    up_sum, out_sum, proj_sum = scatter_total(gate(middle_back, grads), kinds)
-    grads = attend_back(4, 2, grads, down_sum)
-    first_terms = [terms(tokens, grads[0][third]) for third in range(3)]
+    middle_back = scatter_quad(middle_terms, middle_sends, query_grads)
+    middle_pair = scatter_pair(middle_back, kinds)
+    down_line = scatter_line(down_pair, rounded)
+    grads = attend_back(0, 2, query_grads[:1], query_grads, down_pair, middle_back)
+    (down_sum,) = scatter_total(gate(down_line, grads), rounded)
+    grads = attend_back(2, 2, grads, down_line)
+    middle_line = scatter_line(gate(middle_pair, grads), kinds)
+    grads = attend_back(4, 2, grads, middle_pair, down_sum)
+    up_sum, out_sum, proj_sum = scatter_total(middle_line, kinds)
+    mixed_grads = gate(grads[0], middle_line)
+    first_terms = [dot(turned, mixed_grads[third]) for third in range(3)]
     mixed_sums = grads[1] + query_grads[1]
     vector_grad = jnp.concatenate([mixed_sums[:2], sums[2:12]], 0)
     vector_terms = jnp.pad(vector_grad.T, ((0, 0), (0, 116)))
     kinds = (False,) * 4
-    first_back = scatter_quad([*first_terms, vector_terms], kinds)
+    first_terms.append(vector_terms)
+    first_back = scatter_quad(first_terms, scatter_sends(first_terms, kinds))
     first_back = scatter_pair(first_back, kinds, up_sum)
     *thirds, vector_sum = scatter_total(scatter_line(first_back, kinds), kinds)
     qkv_sum = jnp.concatenate(thirds, 1)

time: 504 us -> 477 us (0.946)
  Pallas kernels: 209 us -> 188 us
  waiting for transfers between devices: 74.6 us -> 67.9 us
    pallas_call x7, Pallas kernels: 97 us -> 75.4 us  [attend_call(): pl.pallas_call(run, out_shape=[shape for shape, _ in outputs], grid_spec=...]
    ppermute x4, waiting for transfers between devices: 10.9 us -> 2.64 us  [scatter_pair(): lax.ppermute(send, 'pb', SECOND_STEP)]
    ppermute x2, waiting for transfers between devices: 13.4 us -> 7.43 us  [gather_pair(): return in_order(line, gate(lax.ppermute(line, 'pb', FIRST_STEP), others), 2)]
    ppermute x12, waiting for transfers between devices: 8.92 us -> 14.8 us  [send_line(): return [lax.ppermute(part, 'pa', shift_pairs(k)) for k in (1, 2, 3)]]
    unnamed x137 -> x161, local copies, waits for them, and re-layouts: 16.1 us -> 19.8 us
  transfers between devices with their start and end apart: 50 -> 50, of which waited for: 20 -> 21; matrix products, arithmetic and copies ran while one was open for 11% -> 14% of each run, Pallas kernels for 30% -> 32%
where the time goes in v3:
time: 477 us; the launch traced here: 471 us
  Pallas kernels  188 us (39%)
  waiting for transfers between devices  67.9 us (14%)
  starting transfers between devices  59.3 us (12%)
  other arithmetic  47.5 us (10%)
  matrix products  37.8 us (8%)
  local copies, waits for them, and re-layouts  35.1 us (7%)
  between operations  24.6 us (5%)
  blocking collectives  11 us (2%)
    pallas_call x7, Pallas kernels, attend_call(): pl.pallas_call(run, out_shape=[shape for shape, _ in outputs], grid_spec=...  75.4 us
    pallas_call x6, Pallas kernels, row_call(): pl.pallas_call(run, grid=(count,), in_specs=in_specs, out_specs=[rows_at(...  74.3 us
    dot_general x9, matrix products, dot(): return lax.dot_general(left, right, dims, preferred_element_type=F32)  37.8 us
    pallas_call x3, Pallas kernels, score_call(): pl.pallas_call(kernel, grid=(inputs[0].shape[0] // SCORE_ROWS,), in_specs...  25.2 us
    ppermute x12, starting transfers between devices, send_line(): return [lax.ppermute(part, 'pa', shift_pairs(k)) for k in (1, 2, 3)]  22.8 us
    unnamed x161, local copies, waits for them, and re-layouts  19.8 us
    ppermute x12, waiting for transfers between devices, scatter_total(): total = joined(total, exact, lax.ppermute(send, 'pa', shift_pairs(k)))  18.6 us
    ppermute x12, starting transfers between devices, scatter_total(): total = joined(total, exact, lax.ppermute(send, 'pa', shift_pairs(k)))  15 us
  transfers between devices with their start and end apart: 50, of which 21 were waited for; matrix products, arithmetic and copies ran while one was open for 14% of the time, Pallas kernels for 32%

profile of v3, /device:TPU:0, one launch (start us, length us, event | category | flops | bytes accessed | tf_op | source)
XLA Modules:
  0.0 471.1 jit_solution(8813419745392178695)
XLA Ops:
  9.2 4.1 collective-permute-start.1
  14.8 2.2 collective-permute-start
  20.0 2.3 collective-permute-done.1
  35.1 4.9 %shard_map.375 = bf16[768,1152]{1,0:T(8,128)(2,1)} custom-call(bf16[1152,768]{1,0:T(8,128)(2,1)} %pad_maximum_fusion.x_ref.refs_0_), custom_call_target="tpu_custom_call" | custom-call | tf_op jit(solution)/shard_map/pallas_call | solution.py:307
  51.1 9.2 %collective-permute-done.12 = bf16[24,3968]{1,0:T(8,128)(2,1)S(1)} collective-permute-done((bf16[24,3968]{1,0:T(8,128)(2,1)S(1)}, bf16[24,3968]{1,0:T(8,128)(2,1)S(1)}, u32[]{:S(2)}, u32[]{:S(2)}) %collective-permute-start.12) | collective-permute-done | bytes 190496 | tf_op jit(solution)/shard_map/ppermute | solution.py:106
  62.5 3.1 collective-permute-done.5.refs_1_
  68.7 2.8 fusion.1.refs_1_.refs_2_.refs_3_
  74.6 7.3 %add_convert_fusion.refs_1_.refs_2_.refs_3_ = bf16[1024,2304]{1,0:T(8,128)(2,1)} fusion(bf16[1024,768]{1,0:T(8,128)(2,1)} %bitcast.387, bf16[768,2304]{1,0:T(8,128)(2,1)S(1)} %bitcast.367, f32[2304]{0:T(1024)S(1)} %pad_maximum_fusion.24), kind=kOutput, calls=%fused_computation | convolution fusion | flops 3628597248 | bytes 9839616 | tf_op jit(solution)/shard_map/dot_general | solution.py:273
  81.9 3.7 shard_map.379
  87.2 13.0 %shard_map.380 = (bf16[1152,768]{1,0:T(8,128)(2,1)S(1)}, f32[6,8,1024]{2,1,0:T(8,128)S(1)}) custom-call(s32[4,2]{1,0:T(4,128)S(1)} %pad_add_fusion.refs_0_, bf16[1024,2304]{1,0:T(8,128)(2,1)} %add_convert_fusion.refs_1_.refs_2_.refs_3_, bf16[1024,2304]{1,0:T(8,128)(2,1)} %add_convert_fusion.refs_1_.refs_2_.refs_3_, ...), custom_call_target="tpu_custom_call", output_to_operand_aliasing={{0}: (6, {})} | custom-call | flops 16106127360 | bytes 3145728 | tf_op jit(solution)/shard_map/pallas_call | solution.py:493
  100.2 7.4 %collective-permute-done.9.refs_1_ = bf16[384,768]{1,0:T(8,128)(2,1)S(1)} collective-permute-done((bf16[384,768]{1,0:T(8,128)(2,1)S(1)}, bf16[384,768]{1,0:T(8,128)(2,1)S(1)}, u32[]{:S(2)}, u32[]{:S(2)}) %collective-permute-start.9) | collective-permute-done | bytes 589856 | tf_op jit(solution)/shard_map/ppermute | solution.py:134
  110.0 13.0 %shard_map.382 = (bf16[1152,768]{1,0:T(8,128)(2,1)S(1)}, f32[6,8,1024]{2,1,0:T(8,128)S(1)}) custom-call(s32[4,2]{1,0:T(4,128)S(1)} %pad_add_fusion.refs_0_, bf16[1024,2304]{1,0:T(8,128)(2,1)} %add_convert_fusion.refs_1_.refs_2_.refs_3_, bf16[1024,2304]{1,0:T(8,128)(2,1)} %add_convert_fusion.refs_1_.refs_2_.refs_3_, ...), custom_call_target="tpu_custom_call", output_to_operand_aliasing={{0}: (6, {}), {1}: (7, {})} | custom-call | flops 16106127360 | bytes 3145728 | tf_op jit(solution)/shard_map/pallas_call | solution.py:493
  125.9 5.9 %shard_map.384 = (f32[1152,768]{1,0:T(8,128)}, bf16[1152,768]{1,0:T(8,128)(2,1)}, bf16[1152,3072]{1,0:T(8,128)(2,1)}, bf16[1152,3072]{1,0:T(8,128)(2,1)}) custom-call(bf16[1152,768]{1,0:T(8,128)(2,1)} %pad_maximum_fusion.x_ref.refs_0_, bf16[1152,768]{1,0:T(8,128)(2,1)} %copy-done.3, ...), custom_call_target="tpu_custom_call" | custom-call | flops 754974720 | bytes 14782464 | tf_op jit(solution)/shard_map/pallas_call | solution.py:347
  131.8 2.9 shard_map.385
  134.7 2.2 copy-done.2
  137.0 4.8 %shard_map.386 = (f32[1152,768]{1,0:T(8,128)}, bf16[1152,768]{1,0:T(8,128)(2,1)}, f32[1152,128]{1,0:T(8,128)}, bf16[1152,128]{1,0:T(8,128)(2,1)}) custom-call(bf16[1152,3072]{1,0:T(8,128)(2,1)} %get-tuple-element.163.refs_0_.refs_7_, f32[1152,768]{1,0:T(8,128)} %get-tuple-element.161.refs_1_.refs_5_, bf16[3072,768]{1,0:T(8,128)(2,1)} %bitcast.362, ...), custom_call_target="tpu_custom_call" | custom-call | flops 603979776 | bytes 12718080 | tf_op jit(solution)/shard_map/pallas_call | solution.py:347
  142.5 2.5 collective-permute-start.16
  145.7 3.1 collective-permute-start.15
  152.1 18.2 %shard_map.387 = (f32[1152,768]{1,0:T(8,128)}, bf16[1152,768]{1,0:T(8,128)(2,1)}, bf16[1152,3072]{1,0:T(8,128)(2,1)}, bf16[1152,3072]{1,0:T(8,128)(2,1)}) custom-call(bf16[1152,768]{1,0:T(8,128)(2,1)} %pad_maximum_fusion.x_ref.refs_0_, bf16[1152,768]{1,0:T(8,128)(2,1)} %copy-done.3, ...), custom_call_target="tpu_custom_call", output_to_operand_aliasing={{0}: (5, {}), {1}: (6, {}), {2}: (7, {}), {3}: (8, {})} | custom-call | flops 6039797760 | bytes 32673792 | tf_op jit(solution)/shard_map/pallas_call | solution.py:347
  170.3 12.9 %shard_map.388 = (f32[1152,768]{1,0:T(8,128)}, bf16[1152,768]{1,0:T(8,128)(2,1)}, f32[1152,128]{1,0:T(8,128)}, bf16[1152,128]{1,0:T(8,128)(2,1)}) custom-call(bf16[1152,3072]{1,0:T(8,128)(2,1)} %get-tuple-element.166.refs_0_, ...), custom_call_target="tpu_custom_call", output_to_operand_aliasing={{0}: (5, {}), {1}: (6, {}), {2}: (7, {}), {3}: (8, {})} | custom-call | flops 4831838208 | bytes 25792512 | tf_op jit(solution)/shard_map/pallas_call | solution.py:347
  185.5 6.7 %shard_map.389 = (f32[128,128]{1,0:T(8,128)S(1)}, f32[4096,128]{1,0:T(8,128)S(1)}) custom-call(bf16[4096,128]{1,0:T(8,128)(2,1)S(1)} %copy-done.19, bf16[1024,128]{1,0:T(8,128)(2,1)S(1)} %slice.209.passage_ref, bf16[1024,128]{1,0:T(8,128)(2,1)S(1)} %copy-done.13), custom_call_target="tpu_custom_call" | custom-call | flops 3221225472 | bytes 4194304 | tf_op jit(solution)/shard_map/pallas_call | solution.py:703
  194.3 5.5 %all-to-all-start = ((f32[32,1,128]{2,1,0:T(1,128)}), f32[32,1,128]{2,1,0:T(1,128)S(1)}, u32[]{:S(2)}, u32[]{:S(2)}) async-start(f32[32,1,128]{2,1,0:T(1,128)} %broadcast_in_dim.39), calls=%async_computation | async-start | bytes 32768 | tf_op jit(solution)/shard_map/all_to_all | solution.py:265
  199.8 7.1 %all-to-all-done = f32[32,1,128]{2,1,0:T(1,128)S(1)} async-done(((f32[32,1,128]{2,1,0:T(1,128)}), f32[32,1,128]{2,1,0:T(1,128)S(1)}, u32[]{:S(2)}, u32[]{:S(2)}) %all-to-all-start) | async-done | bytes 16416 | tf_op jit(solution)/shard_map/all_to_all | solution.py:265
  211.0 10.0 %shard_map.390 = f32[4096,128]{1,0:T(8,128)S(1)} custom-call(bf16[4096,128]{1,0:T(8,128)(2,1)S(1)} %copy-done.20, bf16[1024,128]{1,0:T(8,128)(2,1)S(1)} %copy-done.15, bf16[1024,128]{1,0:T(8,128)(2,1)S(1)} %copy-done.13, f32[128,128]{1,0:T(8,128)S(1)} %copy.267.grad_ref, f32[4096,128]{1,0:T(8,128)S(1)} %copy-done.26), custom_call_target="tpu_custom_call" | custom-call | flops 3221225472 | bytes 4194304 | tf_op jit(solution)/shard_map/pallas_call | solution.py:703
  222.1 3.0 collective-permute-done.18
  230.5 8.4 %shard_map.391.refs_0_ = f32[1024,128]{1,0:T(8,128)S(1)} custom-call(bf16[4096,128]{1,0:T(8,128)(2,1)S(1)} %copy-done.21, bf16[1024,128]{1,0:T(8,128)(2,1)S(1)} %copy-done.16, bf16[1024,128]{1,0:T(8,128)(2,1)S(1)} %copy-done.13, f32[128,128]{1,0:T(8,128)S(1)} %copy.267.grad_ref, f32[4096,128]{1,0:T(8,128)S(1)} %copy-done.27), custom_call_target="tpu_custom_call" | custom-call | flops 3221225472 | bytes 4194304 | tf_op jit(solution)/shard_map/pallas_call | solution.py:703
  241.0 23.1 %shard_map.392 = (bf16[1152,128]{1,0:T(8,128)(2,1)}, bf16[1152,768]{1,0:T(8,128)(2,1)}, bf16[1152,3072]{1,0:T(8,128)(2,1)}, bf16[1152,768]{1,0:T(8,128)(2,1)}, b...) custom-call(f32[1024,128]{1,0:T(8,128)} %copy-done.24, f32[1152,128]{1,0:T(8,128)} %get-tuple-element.173.refs_1_, ...), custom_call_target="tpu_custom_call" | custom-call | flops 10871635968 | bytes 47943680 | tf_op jit(solution)/shard_map/pallas_call | solution.py:347
  269.0 3.7 collective-permute-done.22
  273.3 9.5 %shard_map.393 = (bf16[1152,128]{1,0:T(8,128)(2,1)}, bf16[1152,768]{1,0:T(8,128)(2,1)}, bf16[1152,3072]{1,0:T(8,128)(2,1)}, bf16[1152,768]{1,0:T(8,128)(2,1)}, b...) custom-call(f32[128,128]{1,0:T(8,128)} %fusion.61.refs_0_, ...), custom_call_target="tpu_custom_call", output_to_operand_aliasing={{0}: (10, {}), {1}: (11, {}), {2}: (12, {}), {3}: (13, {}),... | custom-call | flops 1358954496 | bytes 26152960 | tf_op jit(solution)/shard_map/pallas_call | solution.py:347
  282.9 9.8 %fusion.122 = f32[3072,768]{1,0:T(8,128)S(1)} fusion(bf16[1152,3072]{1,0:T(8,128)(2,1)} %get-tuple-element.166.refs_0_, bf16[1152,768]{1,0:T(8,128)(2,1)} %get-tuple-element.184), kind=kOutput, calls=%fused_computation.357 | convolution fusion | flops 5435817984 | bytes 18284544 | tf_op jit(solution)/shard_map/dot_general | solution.py:273
  294.1 8.8 %fusion.123 = f32[768,3072]{1,0:T(8,128)} fusion(bf16[1152,768]{1,0:T(8,128)(2,1)S(1)} %copy-done.38, bf16[1152,3072]{1,0:T(8,128)(2,1)S(1)} %copy-done.31), kind=kOutput, calls=%fused_computation.358 | convolution fusion | flops 5435817984 | bytes 18284544 | tf_op jit(solution)/shard_map/dot_general | solution.py:273
  303.0 2.7 fusion.3
  315.6 5.3 %shard_map.394 = (bf16[3,1152,768]{2,1,0:T(8,128)(2,1)}, f32[16,768]{1,0:T(8,128)S(1)}) custom-call(s32[1,2]{1,0:T(1,128)S(1)} %pad_add_fusion.1.refs_0_, bf16[128,2304]{1,0:T(8,128)(2,1)S(1)} %copy-done.12, bf16[128,2304]{1,0:T(8,128)(2,1)S(1)} %copy-done.12, bf16[128,2304]{1,0:T(8,128)(2,1)S(1)} %copy-done.12, bf16[1152,768]{1,0:T(8,128)(2,1)S(1)} %copy-done.7, ...), custom_call_target="tpu_custom_call" | custom-call | flops 1006632960 | bytes 786432 | tf_op jit(solution)/shard_map/pallas_call | solution.py:493
  323.7 3.7 bitcast_add_fusion.1
  333.8 13.3 %shard_map.395 = (bf16[3,1152,768]{2,1,0:T(8,128)(2,1)}, f32[16,768]{1,0:T(8,128)S(1)}) custom-call(s32[4,2]{1,0:T(4,128)S(1)} %pad_add_fusion.refs_0_, bf16[1024,2304]{1,0:T(8,128)(2,1)} %add_convert_fusion.refs_1_.refs_2_.refs_3_, bf16[1024,2304]{1,0:T(8,128)(2,1)} %add_convert_fusion.refs_1_.refs_2_.refs_3_, ...), custom_call_target="tpu_custom_call", output_to_operand_aliasing={{0}: (8, {})} | custom-call | flops 21474836480 | bytes 2097152 | tf_op jit(solution)/shard_map/pallas_call | solution.py:493
  348.9 3.8 collective-permute-start.33
  352.7 13.7 %shard_map.396 = (bf16[3,1152,768]{2,1,0:T(8,128)(2,1)}, f32[16,768]{1,0:T(8,128)S(1)}) custom-call(s32[4,2]{1,0:T(4,128)S(1)} %pad_add_fusion.refs_0_, bf16[1024,2304]{1,0:T(8,128)(2,1)} %add_convert_fusion.refs_1_.refs_2_.refs_3_, bf16[1024,2304]{1,0:T(8,128)(2,1)} %add_convert_fusion.refs_1_.refs_2_.refs_3_, ...), custom_call_target="tpu_custom_call", output_to_operand_aliasing={{0}: (8, {}), {1}: (9, {})} | custom-call | flops 21474836480 | bytes 2097152 | tf_op jit(solution)/shard_map/pallas_call | solution.py:493
  372.7 13.4 %shard_map.397 = (bf16[3,1152,768]{2,1,0:T(8,128)(2,1)}, f32[16,768]{1,0:T(8,128)S(1)}) custom-call(s32[4,2]{1,0:T(4,128)S(1)} %pad_add_fusion.refs_0_, bf16[1024,2304]{1,0:T(8,128)(2,1)} %add_convert_fusion.refs_1_.refs_2_.refs_3_, bf16[1024,2304]{1,0:T(8,128)(2,1)} %add_convert_fusion.refs_1_.refs_2_.refs_3_, ...), custom_call_target="tpu_custom_call", output_to_operand_aliasing={{0}: (8, {}), {1}: (9, {})} | custom-call | flops 21474836480 | bytes 2097152 | tf_op jit(solution)/shard_map/pallas_call | solution.py:493
  389.9 3.3 fusion.4
  396.8 3.0 collective-permute-start.41
  404.3 2.9 collective-permute-start.39
  407.1 2.7 collective-permute-done.41
  409.8 5.5 %collective-permute-done.42 = bf16[24,4096]{1,0:T(8,128)(2,1)S(1)} collective-permute-done((bf16[24,4096]{1,0:T(8,128)(2,1)S(1)}, bf16[24,4096]{1,0:T(8,128)(2,1)S(1)}, u32[]{:S(2)}, u32[]{:S(2)}) %collective-permute-start.42) | collective-permute-done | bytes 196640 | tf_op jit(solution)/shard_map/ppermute | solution.py:258
  416.2 2.5 collective-permute-done.39
  420.3 7.3 %collective-permute-done.43 = bf16[96,2432]{1,0:T(8,128)(2,1)S(1)} collective-permute-done((bf16[96,2432]{1,0:T(8,128)(2,1)S(1)}, bf16[96,2432]{1,0:T(8,128)(2,1)S(1)}, u32[]{:S(2)}, u32[]{:S(2)}) %collective-permute-start.43) | collective-permute-done | bytes 466976 | tf_op jit(solution)/shard_map/ppermute | solution.py:243
  429.3 2.5 collective-permute-start.46
  433.1 4.6 collective-permute-done.45
  446.5 11.0 %all_to_all.11 = f32[32,1,128]{2,1,0:T(1,128)S(1)} all-to-all(f32[32,1,128]{2,1,0:T(1,128)S(1)} %broadcast_in_dim_broadcast_in_dim_broadcast_in_dim.3), channel_id=1, replica_groups=mesh['pb'=8,'pa'=4] {'pb','pa'}, dimensions={0} | all-to-all | bytes 32768 | tf_op jit(solution)/shard_map/all_to_all | solution.py:265
  (417 shorter events, 124.1 us)
Async XLA Ops:
  7.2 118.7 %all-gather.3.cloned.1.call-start = ((), (), s32[]{:S(2)}) async-start(), calls=%async_computation.2 | async-start | bytes 6856704 | tf_op jit(solution)/shard_map/all_gather | solution.py:119
  9.2 13.2 %collective-permute-start.1 = (bf16[24,2432]{1,0:T(8,128)(2,1)S(1)}, bf16[24,2432]{1,0:T(8,128)(2,1)S(1)}, u32[]{:S(2)}, u32[]{:S(2)}) collective-permute-start(bf16[24,2432]{1,0:T(8,128)(2,1)S(1)} %fusion.41), channel_id=1, source_target_pairs={{0,2},{1,3},{2,0},{3,1},{4,6},{5,7},{6,4},{7,5},{8,10},{9,11},{10,... | collective-permute-start | bytes 350216 | tf_op jit(solution)/shard_map/ppermute | solution.py:106
  13.3 9.1 %collective-permute-start.2 = (bf16[24,2432]{1,0:T(8,128)(2,1)S(1)}, bf16[24,2432]{1,0:T(8,128)(2,1)S(1)}, u32[]{:S(2)}, u32[]{:S(2)}) collective-permute-start(bf16[24,2432]{1,0:T(8,128)(2,1)S(1)} %fusion.41), channel_id=1, source_target_pairs={{0,1},{1,2},{2,3},{3,0},{4,5},{5,6},{6,7},{7,4},{8,9},{9,10},{10,1... | collective-permute-start | bytes 350216 | tf_op jit(solution)/shard_map/ppermute | solution.py:106
  14.8 8.2 %collective-permute-start = (bf16[24,2432]{1,0:T(8,128)(2,1)S(1)}, bf16[24,2432]{1,0:T(8,128)(2,1)S(1)}, u32[]{:S(2)}, u32[]{:S(2)}) collective-permute-start(bf16[24,2432]{1,0:T(8,128)(2,1)S(1)} %fusion.41), channel_id=1, source_target_pairs={{0,3},{1,0},{2,1},{3,2},{4,7},{5,4},{6,5},{7,6},{8,11},{9,8},{10,9... | collective-permute-start | bytes 350216 | tf_op jit(solution)/shard_map/ppermute | solution.py:106
  23.3 8.8 %collective-permute-start.3 = (bf16[96,2432]{1,0:T(8,128)(2,1)S(1)}, bf16[96,2432]{1,0:T(8,128)(2,1)S(1)}, u32[]{:S(2)}, u32[]{:S(2)}) collective-permute-start(bf16[96,2432]{1,0:T(8,128)(2,1)S(1)} %bitcast.372), channel_id=1, source_target_pairs={{0,8},{4,20},{8,0},{12,28},{16,24},{20,4},{24,16},{28,12},{1,9},{5... | collective-permute-start | bytes 1400840 | tf_op jit(solution)/shard_map/ppermute | solution.py:134
  33.3 14.6 %collective-permute-start.4 = (bf16[2,96,2432]{2,1,0:T(8,128)(2,1)S(1)}, bf16[2,96,2432]{2,1,0:T(8,128)(2,1)S(1)}, u32[]{:S(2)}, u32[]{:S(2)}) collective-permute-start(bf16[2,96,2432]{2,1,0:T(8,128)(2,1)S(1)} %shard_map.376.refs_0_), channel_id=1, source_target_pairs={{0,16},{4,12},{8,24},{12,4},{16,0},{20,28},{24,8},{28,20},{1,17},{... | collective-permute-start | bytes 2801672 | tf_op jit(solution)/shard_map/ppermute | solution.py:140
  40.2 11.0 %collective-permute-start.13 = (bf16[24,3968]{1,0:T(8,128)(2,1)S(1)}, bf16[24,3968]{1,0:T(8,128)(2,1)S(1)}, u32[]{:S(2)}, u32[]{:S(2)}) collective-permute-start(bf16[24,3968]{1,0:T(8,128)(2,1)S(1)} %pad_maximum_fusion.15), channel_id=1, source_target_pairs={{0,3},{1,0},{2,1},{3,2},{4,7},{5,4},{6,5},{7,6},{8,11},{9,8},{10,9... | collective-permute-start | bytes 571400 | tf_op jit(solution)/shard_map/ppermute | solution.py:106
  42.2 18.1 %collective-permute-start.12 = (bf16[24,3968]{1,0:T(8,128)(2,1)S(1)}, bf16[24,3968]{1,0:T(8,128)(2,1)S(1)}, u32[]{:S(2)}, u32[]{:S(2)}) collective-permute-start(bf16[24,3968]{1,0:T(8,128)(2,1)S(1)} %pad_maximum_fusion.15), channel_id=1, source_target_pairs={{0,2},{1,3},{2,0},{3,1},{4,6},{5,7},{6,4},{7,5},{8,10},{9,11},{10,... | collective-permute-start | bytes 571400 | tf_op jit(solution)/shard_map/ppermute | solution.py:106
  43.8 16.6 %collective-permute-start.11 = (bf16[24,3968]{1,0:T(8,128)(2,1)S(1)}, bf16[24,3968]{1,0:T(8,128)(2,1)S(1)}, u32[]{:S(2)}, u32[]{:S(2)}) collective-permute-start(bf16[24,3968]{1,0:T(8,128)(2,1)S(1)} %pad_maximum_fusion.15), channel_id=1, source_target_pairs={{0,1},{1,2},{2,3},{3,0},{4,5},{5,6},{6,7},{7,4},{8,9},{9,10},{10,1... | collective-permute-start | bytes 571400 | tf_op jit(solution)/shard_map/ppermute | solution.py:106
  61.7 122.5 %all-gather.5.cloned.1.call-start = ((), (), s32[]{:S(2)}) async-start(), calls=%async_computation.3 | async-start | bytes 1179648 | tf_op jit(solution)/shard_map/all_gather | solution.py:119
  61.8 3.9 collective-permute-start.5
  71.5 14.1 %collective-permute-start.8 = (bf16[96,768]{1,0:T(8,128)(2,1)}, bf16[96,768]{1,0:T(8,128)(2,1)S(1)}, u32[]{:S(2)}, u32[]{:S(2)}) collective-permute-start(bf16[96,768]{1,0:T(8,128)(2,1)} %convert_element_type.538), channel_id=1, source_target_pairs={{0,3},{1,0},{2,1},{3,2},{4,7},{5,4},{6,5},{7,6},{8,11},{9,8},{10,9... | collective-permute-start | bytes 442376 | tf_op jit(solution)/shard_map/ppermute | solution.py:106
  71.6 14.6 %collective-permute-start.7 = (bf16[96,768]{1,0:T(8,128)(2,1)}, bf16[96,768]{1,0:T(8,128)(2,1)S(1)}, u32[]{:S(2)}, u32[]{:S(2)}) collective-permute-start(bf16[96,768]{1,0:T(8,128)(2,1)} %convert_element_type.538), channel_id=1, source_target_pairs={{0,2},{1,3},{2,0},{3,1},{4,6},{5,7},{6,4},{7,5},{8,10},{9,11},{10,... | collective-permute-start | bytes 442376 | tf_op jit(solution)/shard_map/ppermute | solution.py:106
  72.5 13.8 %collective-permute-start.6 = (bf16[96,768]{1,0:T(8,128)(2,1)}, bf16[96,768]{1,0:T(8,128)(2,1)S(1)}, u32[]{:S(2)}, u32[]{:S(2)}) collective-permute-start(bf16[96,768]{1,0:T(8,128)(2,1)} %convert_element_type.538), channel_id=1, source_target_pairs={{0,1},{1,2},{2,3},{3,0},{4,5},{5,6},{6,7},{7,4},{8,9},{9,10},{10,1... | collective-permute-start | bytes 442376 | tf_op jit(solution)/shard_map/ppermute | solution.py:106
  86.4 21.2 %collective-permute-start.9 = (bf16[384,768]{1,0:T(8,128)(2,1)S(1)}, bf16[384,768]{1,0:T(8,128)(2,1)S(1)}, u32[]{:S(2)}, u32[]{:S(2)}) collective-permute-start(bf16[384,768]{1,0:T(8,128)(2,1)S(1)} %bitcast.368), channel_id=1, source_target_pairs={{0,8},{4,20},{8,0},{12,28},{16,24},{20,4},{24,16},{28,12},{1,9},{5... | collective-permute-start | bytes 1769480 | tf_op jit(solution)/shard_map/ppermute | solution.py:134
  108.5 16.3 %collective-permute-start.10 = (bf16[2,384,768]{2,1,0:T(8,128)(2,1)S(1)}, bf16[2,384,768]{2,1,0:T(8,128)(2,1)S(1)}, u32[]{:S(2)}, u32[]{:S(2)}) collective-permute-start(bf16[2,384,768]{2,1,0:T(8,128)(2,1)S(1)} %shard_map.381.refs_0_), channel_id=1, source_target_pairs={{0,16},{4,12},{8,24},{12,4},{16,0},{20,28},{24,8},{28,20},{1,17},{... | collective-permute-start | bytes 3538952 | tf_op jit(solution)/shard_map/ppermute | solution.py:140
  125.8 6.0 %collective-permute-start.14 = (bf16[2,2,384,768]{3,2,1,0:T(8,128)(2,1)S(1)}, bf16[2,2,384,768]{3,2,1,0:T(8,128)(2,1)}, u32[]{:S(2)}, u32[]{:S(2)}) collective-permute-start(bf16[2,2,384,768]{3,2,1,0:T(8,128)(2,1)S(1)} %shard_map.383.refs_0_), channel_id=1, source_target_pairs={{0,4},{4,0},{8,12},{12,8},{16,20},{20,16},{24,28},{28,24},{1,5},{5... | collective-permute-start | bytes 7077896 | tf_op jit(solution)/shard_map/ppermute | solution.py:147
  142.5 6.3 %collective-permute-start.16 = (bf16[128,128]{1,0:T(8,128)(2,1)S(1)}, bf16[128,128]{1,0:T(8,128)(2,1)S(1)}, u32[]{:S(2)}, u32[]{:S(2)}) collective-permute-start(bf16[128,128]{1,0:T(8,128)(2,1)S(1)} %slice.208), channel_id=1, source_target_pairs={{0,2},{1,3},{2,0},{3,1},{4,6},{5,7},{6,4},{7,5},{8,10},{9,11},{10,... | collective-permute-start | bytes 98312 | tf_op jit(solution)/shard_map/ppermute | solution.py:106
  144.9 5.7 %collective-permute-start.17 = (bf16[128,128]{1,0:T(8,128)(2,1)S(1)}, bf16[128,128]{1,0:T(8,128)(2,1)S(1)}, u32[]{:S(2)}, u32[]{:S(2)}) collective-permute-start(bf16[128,128]{1,0:T(8,128)(2,1)S(1)} %slice.208), channel_id=1, source_target_pairs={{0,1},{1,2},{2,3},{3,0},{4,5},{5,6},{6,7},{7,4},{8,9},{9,10},{10,1... | collective-permute-start | bytes 98312 | tf_op jit(solution)/shard_map/ppermute | solution.py:106
  145.7 5.0 %collective-permute-start.15 = (bf16[128,128]{1,0:T(8,128)(2,1)S(1)}, bf16[128,128]{1,0:T(8,128)(2,1)S(1)}, u32[]{:S(2)}, u32[]{:S(2)}) collective-permute-start(bf16[128,128]{1,0:T(8,128)(2,1)S(1)} %slice.208), channel_id=1, source_target_pairs={{0,3},{1,0},{2,1},{3,2},{4,7},{5,4},{6,5},{7,6},{8,11},{9,8},{10,9... | collective-permute-start | bytes 98312 | tf_op jit(solution)/shard_map/ppermute | solution.py:106
  194.3 12.6 %all-to-all-start = ((f32[32,1,128]{2,1,0:T(1,128)}), f32[32,1,128]{2,1,0:T(1,128)S(1)}, u32[]{:S(2)}, u32[]{:S(2)}) async-start(f32[32,1,128]{2,1,0:T(1,128)} %broadcast_in_dim.39), calls=%async_computation | async-start | bytes 32768 | tf_op jit(solution)/shard_map/all_to_all | solution.py:265
  222.1 3.0 collective-permute-start.18
  228.3 10.7 %collective-permute-start.19 = (bf16[2,512,256]{2,1,0:T(8,128)(2,1)}, bf16[2,512,256]{2,1,0:T(8,128)(2,1)}, u32[]{:S(2)}, u32[]{:S(2)}) collective-permute-start(bf16[2,512,256]{2,1,0:T(8,128)(2,1)} %pad_maximum_fusion.7), channel_id=1, source_target_pairs={{0,16},{4,12},{8,24},{12,4},{16,0},{20,28},{24,8},{28,20},{1,17},{... | collective-permute-start | bytes 1572872 | tf_op jit(solution)/shard_map/ppermute | solution.py:235
  240.4 23.7 %collective-permute-start.20 = (bf16[512,256]{1,0:T(8,128)(2,1)S(1)}, bf16[512,256]{1,0:T(8,128)(2,1)S(1)}, u32[]{:S(2)}, u32[]{:S(2)}) collective-permute-start(bf16[512,256]{1,0:T(8,128)(2,1)S(1)} %pad_maximum_fusion.10), channel_id=1, source_target_pairs={{0,8},{4,20},{8,0},{12,28},{16,24},{20,4},{24,16},{28,12},{1,9},{5... | collective-permute-start | bytes 786440 | tf_op jit(solution)/shard_map/ppermute | solution.py:243
  264.2 4.8 %collective-permute-start.23 = (bf16[128,256]{1,0:T(8,128)(2,1)S(1)}, bf16[128,256]{1,0:T(8,128)(2,1)S(1)}, u32[]{:S(2)}, u32[]{:S(2)}) collective-permute-start(bf16[128,256]{1,0:T(8,128)(2,1)S(1)} %pad_maximum_fusion.23), channel_id=1, source_target_pairs={{0,3},{1,0},{2,1},{3,2},{4,7},{5,4},{6,5},{7,6},{8,11},{9,8},{10,9... | collective-permute-start | bytes 196616 | tf_op jit(solution)/shard_map/ppermute | solution.py:258
  264.9 7.8 %collective-permute-start.22 = (bf16[128,256]{1,0:T(8,128)(2,1)S(1)}, bf16[128,256]{1,0:T(8,128)(2,1)S(1)}, u32[]{:S(2)}, u32[]{:S(2)}) collective-permute-start(bf16[128,256]{1,0:T(8,128)(2,1)S(1)} %pad_maximum_fusion.22), channel_id=1, source_target_pairs={{0,2},{1,3},{2,0},{3,1},{4,6},{5,7},{6,4},{7,5},{8,10},{9,11},{10,... | collective-permute-start | bytes 196616 | tf_op jit(solution)/shard_map/ppermute | solution.py:258
  266.3 6.3 %collective-permute-start.21 = (bf16[128,256]{1,0:T(8,128)(2,1)S(1)}, bf16[128,256]{1,0:T(8,128)(2,1)S(1)}, u32[]{:S(2)}, u32[]{:S(2)}) collective-permute-start(bf16[128,256]{1,0:T(8,128)(2,1)S(1)} %pad_maximum_fusion.21), channel_id=1, source_target_pairs={{0,1},{1,2},{2,3},{3,0},{4,5},{5,6},{6,7},{7,4},{8,9},{9,10},{10,1... | collective-permute-start | bytes 196616 | tf_op jit(solution)/shard_map/ppermute | solution.py:258
  292.9 13.5 %collective-permute-start.25 = (bf16[4,384,768]{2,1,0:T(8,128)(2,1)S(1)}, bf16[4,384,768]{2,1,0:T(8,128)(2,1)S(1)}, u32[]{:S(2)}, u32[]{:S(2)}) collective-permute-start(bf16[4,384,768]{2,1,0:T(8,128)(2,1)S(1)} %fusion.2), channel_id=1, source_target_pairs={{0,4},{4,0},{8,12},{12,8},{16,20},{20,16},{24,28},{28,24},{1,5},{5... | collective-permute-start | bytes 7077896 | tf_op jit(solution)/shard_map/ppermute | solution.py:215
  305.6 15.4 %collective-permute-start.24 = (bf16[4,96,3072]{2,1,0:T(8,128)(2,1)S(1)}, bf16[4,96,3072]{2,1,0:T(8,128)(2,1)}, u32[]{:S(2)}, u32[]{:S(2)}) collective-permute-start(bf16[4,96,3072]{2,1,0:T(8,128)(2,1)S(1)} %fusion.3), channel_id=1, source_target_pairs={{0,4},{4,0},{8,12},{12,8},{16,20},{20,16},{24,28},{28,24},{1,5},{5... | collective-permute-start | bytes 7077896 | tf_op jit(solution)/shard_map/ppermute | solution.py:215
  310.3 10.8 %collective-permute-start.26 = (bf16[4,96,768]{2,1,0:T(8,128)(2,1)S(1)}, bf16[4,96,768]{2,1,0:T(8,128)(2,1)}, u32[]{:S(2)}, u32[]{:S(2)}) collective-permute-start(bf16[4,96,768]{2,1,0:T(8,128)(2,1)S(1)} %fusion.16), channel_id=1, source_target_pairs={{0,4},{4,0},{8,12},{12,8},{16,20},{20,16},{24,28},{28,24},{1,5},{5... | collective-permute-start | bytes 1769480 | tf_op jit(solution)/shard_map/ppermute | solution.py:215
  312.3 8.8 %collective-permute-start.27 = (f32[4,96,128]{2,1,0:T(8,128)S(1)}, f32[4,96,128]{2,1,0:T(8,128)S(1)}, u32[]{:S(2)}, u32[]{:S(2)}) collective-permute-start(f32[4,96,128]{2,1,0:T(8,128)S(1)} %dynamic-slice_bitcast_fusion.1), channel_id=1, source_target_pairs={{0,4},{4,0},{8,12},{12,8},{16,20},{20,16},{24,28},{28,24},{1,5},{5... | collective-permute-start | bytes 589832 | tf_op jit(solution)/shard_map/ppermute | solution.py:215
  314.2 16.5 %collective-permute-start.29 = (bf16[2,384,768]{2,1,0:T(8,128)(2,1)}, bf16[2,384,768]{2,1,0:T(8,128)(2,1)}, u32[]{:S(2)}, u32[]{:S(2)}) collective-permute-start(bf16[2,384,768]{2,1,0:T(8,128)(2,1)} %pad_maximum_fusion.2), channel_id=1, source_target_pairs={{0,16},{4,12},{8,24},{12,4},{16,0},{20,28},{24,8},{28,20},{1,17},{... | collective-permute-start | bytes 3538952 | tf_op jit(solution)/shard_map/ppermute | solution.py:235
  329.0 38.8 %collective-permute-start.28 = (bf16[2,96,4096]{2,1,0:T(8,128)(2,1)}, bf16[2,96,4096]{2,1,0:T(8,128)(2,1)}, u32[]{:S(2)}, u32[]{:S(2)}) collective-permute-start(bf16[2,96,4096]{2,1,0:T(8,128)(2,1)} %pad_maximum_fusion.1), channel_id=1, source_target_pairs={{0,16},{4,12},{8,24},{12,4},{16,0},{20,28},{24,8},{28,20},{1,17},{... | collective-permute-start | bytes 4718600 | tf_op jit(solution)/shard_map/ppermute | solution.py:235
  332.3 16.3 %collective-permute-start.30 = (bf16[384,768]{1,0:T(8,128)(2,1)S(1)}, bf16[384,768]{1,0:T(8,128)(2,1)S(1)}, u32[]{:S(2)}, u32[]{:S(2)}) collective-permute-start(bf16[384,768]{1,0:T(8,128)(2,1)S(1)} %fusion.13), channel_id=1, source_target_pairs={{0,8},{4,20},{8,0},{12,28},{16,24},{20,4},{24,16},{28,12},{1,9},{5... | collective-permute-start | bytes 1769480 | tf_op jit(solution)/shard_map/ppermute | solution.py:243
  348.8 17.6 %collective-permute-start.31 = (bf16[96,768]{1,0:T(8,128)(2,1)S(1)}, bf16[96,768]{1,0:T(8,128)(2,1)S(1)}, u32[]{:S(2)}, u32[]{:S(2)}) collective-permute-start(bf16[96,768]{1,0:T(8,128)(2,1)S(1)} %get-tuple-element.392), channel_id=1, source_target_pairs={{0,1},{1,2},{2,3},{3,0},{4,5},{5,6},{6,7},{7,4},{8,9},{9,10},{10,1... | collective-permute-start | bytes 442376 | tf_op jit(solution)/shard_map/ppermute | solution.py:258
  348.9 17.5 %collective-permute-start.33 = (bf16[96,768]{1,0:T(8,128)(2,1)S(1)}, bf16[96,768]{1,0:T(8,128)(2,1)S(1)}, u32[]{:S(2)}, u32[]{:S(2)}) collective-permute-start(bf16[96,768]{1,0:T(8,128)(2,1)S(1)} %get-tuple-element.393), channel_id=1, source_target_pairs={{0,3},{1,0},{2,1},{3,2},{4,7},{5,4},{6,5},{7,6},{8,11},{9,8},{10,9... | collective-permute-start | bytes 442376 | tf_op jit(solution)/shard_map/ppermute | solution.py:258
  352.7 13.7 %collective-permute-start.32 = (bf16[96,768]{1,0:T(8,128)(2,1)S(1)}, bf16[96,768]{1,0:T(8,128)(2,1)S(1)}, u32[]{:S(2)}, u32[]{:S(2)}) collective-permute-start(bf16[96,768]{1,0:T(8,128)(2,1)S(1)} %get-tuple-element.394), channel_id=1, source_target_pairs={{0,2},{1,3},{2,0},{3,1},{4,6},{5,7},{6,4},{7,5},{8,10},{9,11},{10,... | collective-permute-start | bytes 442376 | tf_op jit(solution)/shard_map/ppermute | solution.py:258
  372.7 13.8 %collective-permute-start.34 = (bf16[96,4096]{1,0:T(8,128)(2,1)}, bf16[96,4096]{1,0:T(8,128)(2,1)}, u32[]{:S(2)}, u32[]{:S(2)}) collective-permute-start(bf16[96,4096]{1,0:T(8,128)(2,1)} %pad_maximum_fusion.3), channel_id=1, source_target_pairs={{0,8},{4,20},{8,0},{12,28},{16,24},{20,4},{24,16},{28,12},{1,9},{5... | collective-permute-start | bytes 2359304 | tf_op jit(solution)/shard_map/ppermute | solution.py:243
  386.4 14.3 %collective-permute-start.38 = (bf16[4,96,128]{2,1,0:T(8,128)(2,1)S(1)}, bf16[4,96,128]{2,1,0:T(8,128)(2,1)S(1)}, u32[]{:S(2)}, u32[]{:S(2)}) collective-permute-start(bf16[4,96,128]{2,1,0:T(8,128)(2,1)S(1)} %fusion.43), channel_id=1, source_target_pairs={{0,4},{4,0},{8,12},{12,8},{16,20},{20,16},{24,28},{28,24},{1,5},{5... | collective-permute-start | bytes 294920 | tf_op jit(solution)/shard_map/ppermute | solution.py:215
  396.8 13.0 %collective-permute-start.41 = (bf16[24,4096]{1,0:T(8,128)(2,1)S(1)}, bf16[24,4096]{1,0:T(8,128)(2,1)S(1)}, u32[]{:S(2)}, u32[]{:S(2)}) collective-permute-start(bf16[24,4096]{1,0:T(8,128)(2,1)S(1)} %pad_maximum_fusion.13), channel_id=1, source_target_pairs={{0,2},{1,3},{2,0},{3,1},{4,6},{5,7},{6,4},{7,5},{8,10},{9,11},{10,... | collective-permute-start | bytes 589832 | tf_op jit(solution)/shard_map/ppermute | solution.py:258
  400.6 3.0 collective-permute-start.35
  400.8 14.5 %collective-permute-start.42 = (bf16[24,4096]{1,0:T(8,128)(2,1)S(1)}, bf16[24,4096]{1,0:T(8,128)(2,1)S(1)}, u32[]{:S(2)}, u32[]{:S(2)}) collective-permute-start(bf16[24,4096]{1,0:T(8,128)(2,1)S(1)} %pad_maximum_fusion.14), channel_id=1, source_target_pairs={{0,3},{1,0},{2,1},{3,2},{4,7},{5,4},{6,5},{7,6},{8,11},{9,8},{10,9... | collective-permute-start | bytes 589832 | tf_op jit(solution)/shard_map/ppermute | solution.py:258
  402.2 13.1 %collective-permute-start.40 = (bf16[24,4096]{1,0:T(8,128)(2,1)S(1)}, bf16[24,4096]{1,0:T(8,128)(2,1)S(1)}, u32[]{:S(2)}, u32[]{:S(2)}) collective-permute-start(bf16[24,4096]{1,0:T(8,128)(2,1)S(1)} %pad_maximum_fusion.12), channel_id=1, source_target_pairs={{0,1},{1,2},{2,3},{3,0},{4,5},{5,6},{6,7},{7,4},{8,9},{9,10},{10,1... | collective-permute-start | bytes 589832 | tf_op jit(solution)/shard_map/ppermute | solution.py:258
  404.3 14.4 %collective-permute-start.39 = (bf16[2,96,2432]{2,1,0:T(8,128)(2,1)S(1)}, bf16[2,96,2432]{2,1,0:T(8,128)(2,1)S(1)}, u32[]{:S(2)}, u32[]{:S(2)}) collective-permute-start(bf16[2,96,2432]{2,1,0:T(8,128)(2,1)S(1)} %maximum_maximum_fusion), channel_id=1, source_target_pairs={{0,16},{4,12},{8,24},{12,4},{16,0},{20,28},{24,8},{28,20},{1,17},{... | collective-permute-start | bytes 2801672 | tf_op jit(solution)/shard_map/ppermute | solution.py:235
  419.0 8.6 %collective-permute-start.43 = (bf16[96,2432]{1,0:T(8,128)(2,1)S(1)}, bf16[96,2432]{1,0:T(8,128)(2,1)S(1)}, u32[]{:S(2)}, u32[]{:S(2)}) collective-permute-start(bf16[96,2432]{1,0:T(8,128)(2,1)S(1)} %pad_maximum_fusion.9), channel_id=1, source_target_pairs={{0,8},{4,20},{8,0},{12,28},{16,24},{20,4},{24,16},{28,12},{1,9},{5... | collective-permute-start | bytes 1400840 | tf_op jit(solution)/shard_map/ppermute | solution.py:243
  428.0 9.7 %collective-permute-start.45 = (bf16[24,2432]{1,0:T(8,128)(2,1)S(1)}, bf16[24,2432]{1,0:T(8,128)(2,1)}, u32[]{:S(2)}, u32[]{:S(2)}) collective-permute-start(bf16[24,2432]{1,0:T(8,128)(2,1)S(1)} %pad_maximum_fusion.18), channel_id=1, source_target_pairs={{0,2},{1,3},{2,0},{3,1},{4,6},{5,7},{6,4},{7,5},{8,10},{9,11},{10,... | collective-permute-start | bytes 350216 | tf_op jit(solution)/shard_map/ppermute | solution.py:258
  429.3 9.2 %collective-permute-start.46 = (bf16[24,2432]{1,0:T(8,128)(2,1)}, bf16[24,2432]{1,0:T(8,128)(2,1)}, u32[]{:S(2)}, u32[]{:S(2)}) collective-permute-start(bf16[24,2432]{1,0:T(8,128)(2,1)} %pad_maximum_fusion.19), channel_id=1, source_target_pairs={{0,3},{1,0},{2,1},{3,2},{4,7},{5,4},{6,5},{7,6},{8,11},{9,8},{10,9... | collective-permute-start | bytes 350216 | tf_op jit(solution)/shard_map/ppermute | solution.py:258
  432.4 7.0 %collective-permute-start.44 = (bf16[24,2432]{1,0:T(8,128)(2,1)}, bf16[24,2432]{1,0:T(8,128)(2,1)}, u32[]{:S(2)}, u32[]{:S(2)}) collective-permute-start(bf16[24,2432]{1,0:T(8,128)(2,1)} %pad_maximum_fusion.17), channel_id=1, source_target_pairs={{0,1},{1,2},{2,3},{3,0},{4,5},{5,6},{6,7},{7,4},{8,9},{9,10},{10,1... | collective-permute-start | bytes 350216 | tf_op jit(solution)/shard_map/ppermute | solution.py:258
  (79 other events, 652.5 us)
Sparse Core Ops, SparseCore 0:
  61.8 47.6 all-gather.2
  152.3 24.0 all-gather.4

commit v4 on v3

--- a/solution.py
+++ b/solution.py
@@ -2,6 +2,7 @@
 
 import jax
 import jax.numpy as jnp
+import numpy as np
 from jax import lax
 from jax.experimental import pallas as pl
 from jax.experimental.pallas import tpu as pltpu
@@ -218,21 +219,27 @@
     ]
 
 
-def scatter_pair(arrays, exact, *others):
+def chip_pairs(arrays, bit):
+    core = position()[1]
+    first = jnp.where(core == 0, 2 * bit, bit)
+    second = first + jnp.where(core == 0, 1, 2)
+    return [
+        jnp.stack([lax.dynamic_index_in_dim(a, i, 0, False) for i in (first, second)])
+        for a in arrays
+    ]
+
+
+def pair_send(arrays, exact):
     if not staged_mesh():
         return arrays
-    _, core, _, bit = position()
-
-    def two_at(bit):
-        first = jnp.where(core == 0, 2 * bit, bit)
-        second = first + jnp.where(core == 0, 1, 2)
-        return [
-            jnp.stack([lax.dynamic_index_in_dim(a, i, 0, False) for i in (first, second)])
-            for a in arrays
-        ]
-
-    send = packed(two_at(1 - bit), exact)
-    return joined(two_at(bit), exact, gate(lax.ppermute(send, "pb", SECOND_STEP), others))
+    return packed(chip_pairs(arrays, 1 - position()[3]), exact)
+
+
+def scatter_pair(arrays, send, exact, *others):
+    if not staged_mesh():
+        return arrays
+    moved = gate(lax.ppermute(send, "pb", SECOND_STEP), others)
+    return joined(chip_pairs(arrays, position()[3]), exact, moved)
 
 
 def scatter_line(arrays, exact):
@@ -247,15 +254,23 @@
     return [lax.psum_scatter(a, "pa", scatter_dimension=0, tiled=True) for a in arrays]
 
 
+def last_moves(arrays, exact):
+    depth = position()[0]
+    sends = [packed(blocks_at(arrays, (depth + k) % 4), exact) for k in (1, 2, 3)]
+    return [lax.ppermute(s, "pa", shift_pairs(k + 1)) for k, s in enumerate(sends)]
+
+
+def depth_blocks(arrays):
+    return [a.reshape((4, a.shape[0] // 4) + a.shape[1:]) for a in arrays]
+
+
 def scatter_total(arrays, exact):
     if not staged_mesh():
         return scatter_rest(arrays)
-    depth = position()[0]
-    arrays = [a.reshape((4, a.shape[0] // 4) + a.shape[1:]) for a in arrays]
-    total = blocks_at(arrays, depth)
-    for k in (1, 2, 3):
-        send = packed(blocks_at(arrays, (depth + k) % 4), exact)
-        total = joined(total, exact, lax.ppermute(send, "pa", shift_pairs(k)))
+    arrays = depth_blocks(arrays)
+    total = blocks_at(arrays, position()[0])
+    for moved in last_moves(arrays, exact):
+        total = joined(total, exact, moved)
     return total
 
 
@@ -290,8 +305,8 @@
 
 def gelu_with_slope(value):
     below = 0.5 + 0.5 * lax.erf(value * 0.7071067811865476)
-    density = 0.3989422804014327 * jnp.exp(-0.5 * value * value)
-    return value * below, below + value * density
+    bell = jnp.exp2(value * (value * -0.7213475204444817))
+    return value * below, below + value * (0.3989422804014327 * bell)
 
 
 def columns(array, low=0, high=None):
@@ -660,8 +675,9 @@
     return jnp.exp2(cosine * 14.426950408889634 - 14.426950408889634)
 
 
-def score_kernel(query_ref, passage_ref, member_ref, score_ref, sums_ref):
+def score_kernel(query_ref, passage_ref, member_ref, score_ref, sums_ref, terms_ref):
     terms = sharp(dot(query_ref[...], passage_ref[...], ACROSS)).astype(LOW)
+    terms_ref[...] = terms
     sums = dot(terms, member_ref[...])
     sums_ref[...] = sums
     lane = lax.broadcasted_iota(jnp.int32, sums.shape, 1)
@@ -678,10 +694,9 @@
     return jnp.where(lane < 64, high, rest)
 
 
-def score_query_kernel(query_ref, passage_ref, member_ref, grad_ref, sums_ref, out_ref):
-    ratio = score_ratio(grad_ref, sums_ref)
-    terms = sharp(dot(query_ref[...], passage_ref[...], ACROSS))
-    terms = (terms * dot(ratio, member_ref[...], ACROSS)).astype(LOW)
+def score_query_kernel(terms_ref, passage_ref, member_ref, grad_ref, sums_ref, out_ref):
+    spread = dot(score_ratio(grad_ref, sums_ref), member_ref[...], ACROSS)
+    terms = (terms_ref[...].astype(F32) * spread).astype(LOW)
     out_ref[...] = dot(terms, passage_ref[...])
 
 
@@ -696,7 +711,7 @@
     out_ref[...] += dot(terms, query_ref[...])
 
 
-SCORE_ROWS = 512
+SCORE_ROWS = 1024
 
 
 def score_call(kernel, inputs, in_specs, out_specs, out_shape, flops):
@@ -732,10 +747,11 @@
         score_kernel,
         (queries, passages, member),
         [rows, fixed, fixed],
-        [grads, rows],
+        [grads, rows, pl.BlockSpec((SCORE_ROWS, BIN), lambda i: (i, 0))],
         [
             jax.ShapeDtypeStruct((count // QLEN, 128), F32),
             jax.ShapeDtypeStruct((count, 128), F32),
+            jax.ShapeDtypeStruct((count, BIN), LOW),
         ],
         6 * count * BIN * 128,
     )
@@ -745,10 +761,55 @@
     rows, fixed, grads = score_specs()
     count = queries.shape[0]
     inputs = (queries, passages, member, grad_scores, sums)
-    in_specs = [rows, fixed, fixed, grads, rows]
+    left = pl.BlockSpec((SCORE_ROWS, queries.shape[1]), lambda i: (i, 0))
+    in_specs = [left, fixed, fixed, grads, rows]
     width, spec = (BIN, fixed) if kernel is score_passage_kernel else (count, rows)
     out = jax.ShapeDtypeStruct((width, 128), F32)
     return score_call(kernel, inputs, in_specs, spec, out, 6 * count * BIN * 128)
+
+
+def finish_kernel(scalars, *refs):
+    own, moved, sums, (first_ref, vector_ref, square_ref) = refs[:4], refs[4:7], refs[7:-3], refs[-3:]
+    rows = first_ref.shape[0]
+    here = pl.ds(pl.multiple_of(scalars[0] * rows, rows), rows)
+    square = jnp.zeros((1, 1), F32)
+    at = 0
+    for ref in own:
+        part = slice(at, at + ref.shape[1])
+        total = ref[here, :]
+        for more in moved:
+            total = total + more[:, part].astype(F32)
+        if at < 3 * D:
+            first_ref[:, part] = total
+        else:
+            vector_ref[...] = total
+        square = square + jnp.sum(total * total, keepdims=True)
+        at += ref.shape[1]
+    for ref in sums:
+        square = square + jnp.sum(ref[...] * ref[...], keepdims=True)
+    square_ref[...] = jnp.broadcast_to(square, square_ref.shape)
+
+
+def finish(arrays, sums):
+    kinds = (False,) * 4
+    if not staged_mesh():
+        *thirds, vector = scatter_rest(arrays)
+        square = sum(jnp.sum(a * a) for a in (*thirds, vector, *sums))
+        return jnp.concatenate(thirds, 1), vector, jnp.full((1, 128), square)
+    rows = arrays[0].shape[0] // 4
+    inputs = [*arrays, *last_moves(depth_blocks(arrays), kinds), *sums]
+    shapes = [(rows, 3 * D), (rows, 128), (1, 128)]
+    return pl.pallas_call(
+        finish_kernel,
+        grid_spec=pltpu.PrefetchScalarGridSpec(
+            num_scalar_prefetch=1,
+            grid=(1,),
+            in_specs=[pl.BlockSpec(a.shape, lambda i, s: (0, 0)) for a in inputs],
+            out_specs=[pl.BlockSpec(shape, lambda i, s: (0, 0)) for shape in shapes],
+        ),
+        out_shape=[jax.ShapeDtypeStruct(shape, F32) for shape in shapes],
+        compiler_params=pltpu.CompilerParams(vmem_limit_bytes=32 << 20),
+    )(scalars_of_position(), *inputs)
 
 
 def cross_grad(scores, partition, passage_ids, chosen_ids, query_total):
@@ -790,18 +851,6 @@
     vector_first,
     vector_second,
 ):
-    own_index = lax.axis_index(("pb", "pa"))
-    query_total = QPD * lax.axis_size(("pb", "pa"))
-    query_flat = query_tokens.reshape(QUERY_ROWS, D)
-    tokens = jnp.concatenate([passage_tokens[0], query_flat], 0)
-    query_tables = segment_tables(jnp.arange(QUERY_ROWS, dtype=jnp.int32) // QLEN, QUERY_ROWS)
-    own_lengths = lax.dynamic_index_in_dim(passage_lengths, own_index, 0, keepdims=False)
-    ends = jnp.cumsum(own_lengths)
-    places = jnp.arange(BIN, dtype=jnp.int32)
-    own_seg = jnp.sum((places[:, None] >= ends[None, :]).astype(jnp.int32), 1)
-    passage_tables = segment_tables(own_seg, ATTEND_TILE)
-    member = (own_seg[:, None] == jnp.arange(128, dtype=jnp.int32)[None, :] % 64).astype(LOW)
-
     vector_part = jnp.pad(vector_params.T, ((0, 0), (0, 116))).astype(LOW)
     first_part = jnp.concatenate([qkv_weight.astype(LOW), vector_part], 1)
     middle_part = jnp.concatenate([up_weight, out_weight, proj_weight], 1).astype(LOW)
@@ -809,10 +858,26 @@
     first_line = line_of(first_part, send_line(first_part))
     middle_moved = send_line(gate(middle_part, first_line))
     first_pair = gather_pair(first_line)
-    turned = transposed(tokens)
-    ready = gate((tokens, turned, query_tables, passage_tables, member), first_pair)
+    own_index = lax.axis_index(("pb", "pa"))
+    query_total = QPD * lax.axis_size(("pb", "pa"))
+    query_flat = query_tokens.reshape(QUERY_ROWS, D)
+    lengths, passages = gate((passage_lengths, passage_tokens[0]), first_pair)
+    tokens = jnp.concatenate([passages, query_flat], 0)
+    query_seg = np.arange(QUERY_ROWS, dtype=np.int32) // QLEN
+    query_tables = (
+        jnp.zeros((1, 2), jnp.int32),
+        jnp.asarray(np.broadcast_to(query_seg[:, None], (QUERY_ROWS, QUERY_ROWS))),
+        jnp.asarray(np.broadcast_to(query_seg[None, :], (8, QUERY_ROWS))),
+    )
+    own_lengths = lax.dynamic_index_in_dim(lengths, own_index, 0, keepdims=False)
+    upto = np.tril(np.ones((PPB, PPB), np.int32))
+    ends = jnp.sum(jnp.where(upto > 0, own_lengths[None, :], 0), 1)
+    places = jnp.arange(BIN, dtype=jnp.int32)
+    own_seg = jnp.sum((places[:, None] >= ends[None, :]).astype(jnp.int32), 1)
+    passage_tables = segment_tables(own_seg, ATTEND_TILE)
+    member = (own_seg[:, None] == jnp.arange(128, dtype=jnp.int32)[None, :] % 64).astype(LOW)
+    ready = tokens, passage_tables, member
     first_quad = gather_quad(first_pair, ready)
-    tokens, turned, query_tables, passage_tables, member = ready
     middle = gather_rest(line_of(middle_part, gate(middle_moved, first_quad)))
     qkv_matrix, vectors = gather_whole(first_quad, [(0, 2304), (2304, 2432)])
     vectors = vectors[:, :12].T.astype(F32)
@@ -824,10 +889,10 @@
     query_mixed = mix(query_flat)
     down_moved = send_line(gate(down_part, query_mixed))
     passage_mixed = mix(gate(passage_tokens[0], query_mixed))
+    down_line = line_of(down_part, gate(down_moved, passage_mixed))
     attended, query_log = attend_forward(
-        gate(query_mixed, passage_mixed), query_tables, QUERY_ROWS, 0, 6, BIN // QUERY_ROWS
-    )
-    down_line = line_of(down_part, gate(down_moved, attended))
+        gate(query_mixed, down_line), query_tables, QUERY_ROWS, 0, 6, BIN // QUERY_ROWS
+    )
     passage_state = attend_forward(
         gate(passage_mixed, down_line), passage_tables, ATTEND_TILE, 0, 3, 0, (attended,)
     )
@@ -883,13 +948,14 @@
     passage_unit = unit[:BIN]
 
     passage_ids = own_index * PPB + jnp.arange(PPB, dtype=jnp.int32)
-    scores, totals = score_forward(every_query, passage_unit, member)
+    scores, totals, score_terms = score_forward(every_query, passage_unit, member)
     scores = scores[:, :PPB]
-    partition = sum_everywhere(jnp.sum(jnp.exp(scores), 1))
+    turned = transposed(gate(tokens, scores))
+    partition = gate(sum_everywhere(jnp.sum(jnp.exp(scores), 1)), turned)
     grad_scores = cross_grad(scores, partition, passage_ids, positives, query_total)
     grad_scores = jnp.tile(jnp.pad(grad_scores, ((0, 0), (0, 64 - PPB))), (1, 2))
     grad_every = score_backward(
-        score_query_kernel, every_query, passage_unit, member, grad_scores, totals
+        score_query_kernel, score_terms, passage_unit, member, grad_scores, totals
     )
     whole, rounded = (True,), (False,)
     query_back = scatter_quad([grad_every], scatter_sends([grad_every], whole))
@@ -916,7 +982,7 @@
             flops=18 * D * D,
         )
 
-    query_back = scatter_pair(query_back, whole)
+    query_back = scatter_pair(query_back, pair_send(query_back, whole), whole)
     back = go_back(
         BACK_ROWS, 0, BIN // BACK_ROWS, (gate(grad_passage, query_back), 0), None
     )
@@ -926,7 +992,7 @@
     gproj, gtwo, ghid, gone, gatt, sums = back
 
     def terms(left, right):
-        return dot(left, right, (((0,), (0,)), ((), ())))
+        return dot(left, right, (((0,), (0,)), ((), ()))).astype(LOW)
 
     def attend_back(first, pairs, into, *others):
         mixed = gate(passage_mixed, *others)
@@ -938,9 +1004,10 @@
     down_sends = scatter_sends([down_terms], rounded)
     up_terms = terms(normed, gate(ghid, down_sends))
     down_back = scatter_quad([down_terms], down_sends, up_terms)
-    down_pair = scatter_pair(down_back, rounded)
-    rest = gate((gone, gproj), down_back)
-    out_terms, proj_terms = terms(attended, rest[0]), terms(rest[1], normed_out).T
+    down_send = pair_send(down_back, rounded)
+    down_pair = scatter_pair(down_back, down_send, rounded)
+    rest = gate((gone, gproj), down_send)
+    out_terms, proj_terms = terms(attended, rest[0]), dot(rest[1], normed_out, (((0,), (0,)), ((), ()))).T
     kinds = (False, False, True)
     middle_terms = [up_terms, out_terms, proj_terms]
     middle_sends = scatter_sends(middle_terms, kinds)
@@ -955,28 +1022,29 @@
         BIN // QUERY_ROWS,
     )
     middle_back = scatter_quad(middle_terms, middle_sends, query_grads)
-    middle_pair = scatter_pair(middle_back, kinds)
+    middle_send = pair_send(middle_back, kinds)
+    middle_pair = scatter_pair(middle_back, middle_send, kinds)
     down_line = scatter_line(down_pair, rounded)
-    grads = attend_back(0, 2, query_grads[:1], query_grads, down_pair, middle_back)
+    grads = attend_back(0, 2, query_grads[:1], query_grads, down_pair, middle_send)
     (down_sum,) = scatter_total(gate(down_line, grads), rounded)
     grads = attend_back(2, 2, grads, down_line)
     middle_line = scatter_line(gate(middle_pair, grads), kinds)
     grads = attend_back(4, 2, grads, middle_pair, down_sum)
     up_sum, out_sum, proj_sum = scatter_total(middle_line, kinds)
     mixed_grads = gate(grads[0], middle_line)
-    first_terms = [dot(turned, mixed_grads[third]) for third in range(3)]
+    first_terms = [dot(turned, mixed_grads[third]).astype(LOW) for third in range(3)]
     mixed_sums = grads[1] + query_grads[1]
     vector_grad = jnp.concatenate([mixed_sums[:2], sums[2:12]], 0)
     vector_terms = jnp.pad(vector_grad.T, ((0, 0), (0, 116)))
     kinds = (False,) * 4
     first_terms.append(vector_terms)
     first_back = scatter_quad(first_terms, scatter_sends(first_terms, kinds))
-    first_back = scatter_pair(first_back, kinds, up_sum)
-    *thirds, vector_sum = scatter_total(scatter_line(first_back, kinds), kinds)
-    qkv_sum = jnp.concatenate(thirds, 1)
+    first_back = scatter_pair(first_back, pair_send(first_back, kinds), kinds, up_sum, down_sum)
+    qkv_sum, vector_sum, square = finish(
+        scatter_line(first_back, kinds), (out_sum, up_sum, down_sum, proj_sum)
+    )
     reduced = (qkv_sum, out_sum, up_sum, down_sum, proj_sum, vector_sum[:, :12].T)
-    square = sum((jnp.sum(gradient * gradient) for gradient in reduced))
-    norm_value = jnp.sqrt(sum_everywhere(jnp.full((1, 128), square))[0, 0])
+    norm_value = jnp.sqrt(sum_everywhere(square)[0, 0])
     factor = jnp.minimum(1.0, clip_max / (norm_value + 1e-06))
     qkv_res = adam_update(qkv_weight, qkv_first, qkv_second, reduced[0], factor, learn_rate)
     out_res = adam_update(out_weight, out_first, out_second, reduced[1], factor, learn_rate)

time: 477 us -> 459 us (0.962)
  waiting for transfers between devices: 67.9 us -> 89.2 us
  Pallas kernels: 188 us -> 171 us
  blocking collectives: 11 us -> 0 us
  other arithmetic: 47.5 us -> 36.9 us
  starting transfers between devices: 59.3 us -> 68 us
  between operations: 24.6 us -> 17.3 us
    all_to_all x1 -> x0, blocking collectives: 11 us -> none  [sum_everywhere(): return jnp.sum(lax.all_to_all(copies, ('pb', 'pa'), 0, 0), 0)]
    pallas_call x7, Pallas kernels: 75.4 us -> 64.7 us  [attend_call(): pl.pallas_call(run, out_shape=[shape for shape, _ in outputs], grid_spec=...]
    ppermute x2, waiting for transfers between devices: 1.68 us -> 11.1 us  [gather_quad(): lax.ppermute(pair, 'pb', SECOND_STEP)]
    ppermute x16, waiting for transfers between devices: 21.2 us -> 28.4 us  [the longest x12 20.3 us: last_moves(): lax.ppermute(s, 'pa', shift_pairs(k + 1))]
    pallas_call x3, Pallas kernels: 25.2 us -> 19.3 us  [score_call(): pl.pallas_call(kernel, grid=(inputs[0].shape[0] // SCORE_ROWS,), in_specs...]
    unnamed x161 -> x140, local copies, waits for them, and re-layouts: 19.8 us -> 25 us
    add x16 -> x19, other arithmetic: 11.9 us -> 8.68 us  [joined(): total = total + moved[..., at:at + array.shape[-1]].astype(F32)]
  transfers between devices with their start and end apart: 50 -> 51, of which waited for: 21 -> 24; matrix products, arithmetic and copies ran while one was open for 14% -> 12% of each run, Pallas kernels for 32% -> 31%
where the time goes in v4:
time: 459 us; the launch traced here: 453 us
  Pallas kernels  171 us (37%)
  waiting for transfers between devices  89.2 us (19%)
  starting transfers between devices  68 us (15%)
  other arithmetic  36.9 us (8%)
  local copies, waits for them, and re-layouts  35.8 us (8%)
  matrix products  34.7 us (8%)
  between operations  17.3 us (4%)
    pallas_call x6, Pallas kernels, row_call(): pl.pallas_call(run, grid=(count,), in_specs=in_specs, out_specs=[rows_at(...  73.7 us
    pallas_call x7, Pallas kernels, attend_call(): pl.pallas_call(run, out_shape=[shape for shape, _ in outputs], grid_spec=...  64.7 us
    dot_general x9, matrix products, dot(): return lax.dot_general(left, right, dims, preferred_element_type=F32)  34.7 us
    unnamed x140, local copies, waits for them, and re-layouts  25 us
    ppermute x12, starting transfers between devices, send_line(): return [lax.ppermute(part, 'pa', shift_pairs(k)) for k in (1, 2, 3)]  22.5 us
    ppermute x12, waiting for transfers between devices, last_moves(): lax.ppermute(s, 'pa', shift_pairs(k + 1))  20.3 us
    ppermute x12, starting transfers between devices, last_moves(): lax.ppermute(s, 'pa', shift_pairs(k + 1))  19.4 us
    pallas_call x3, Pallas kernels, score_call(): pl.pallas_call(kernel, grid=(inputs[0].shape[0] // SCORE_ROWS,), in_specs...  19.3 us
  transfers between devices with their start and end apart: 51, of which 24 were waited for; matrix products, arithmetic and copies ran while one was open for 12% of the time, Pallas kernels for 31%

profile of v4, /device:TPU:0, one launch (start us, length us, event | category | flops | bytes accessed | tf_op | source)
XLA Modules:
  0.0 453.3 jit_solution(17347612487963575221)
XLA Ops:
  9.1 5.1 %collective-permute-start = (bf16[24,2432]{1,0:T(8,128)(2,1)S(1)}, bf16[24,2432]{1,0:T(8,128)(2,1)S(1)}, u32[]{:S(2)}, u32[]{:S(2)}) collective-permute-start(bf16[24,2432]{1,0:T(8,128)(2,1)S(1)} %fusion.44), channel_id=1, source_target_pairs={{0,3},{1,0},{2,1},{3,2},{4,7},{5,4},{6,5},{7,6},{8,11},{9,8},{10,9... | collective-permute-start | bytes 350216 | tf_op jit(solution)/shard_map/ppermute | solution.py:107
  17.8 6.5 %collective-permute-done.1 = bf16[24,2432]{1,0:T(8,128)(2,1)S(1)} collective-permute-done((bf16[24,2432]{1,0:T(8,128)(2,1)S(1)}, bf16[24,2432]{1,0:T(8,128)(2,1)S(1)}, u32[]{:S(2)}, u32[]{:S(2)}) %collective-permute-start.1) | collective-permute-done | bytes 116768 | tf_op jit(solution)/shard_map/ppermute | solution.py:107
  29.5 2.9 collective-permute-start.13
  40.6 7.5 %collective-permute-done.4.refs_1_ = bf16[2,96,2432]{2,1,0:T(8,128)(2,1)S(1)} collective-permute-done((bf16[2,96,2432]{2,1,0:T(8,128)(2,1)S(1)}, bf16[2,96,2432]{2,1,0:T(8,128)(2,1)S(1)}, u32[]{:S(2)}, u32[]{:S(2)}) %collective-permute-start.4) | collective-permute-done | bytes 933920 | tf_op jit(solution)/shard_map/ppermute | solution.py:141
  55.4 3.8 collective-permute-done.5.refs_1_
  62.2 3.1 fusion.1.refs_1_.refs_2_.refs_3_
  68.0 3.0 collective-permute-start.8
  71.0 7.3 %add_convert_fusion.refs_1_.refs_2_.refs_3_ = bf16[1024,2304]{1,0:T(8,128)(2,1)} fusion(bf16[1024,768]{1,0:T(8,128)(2,1)} %bitcast.365, bf16[768,2304]{1,0:T(8,128)(2,1)S(1)} %bitcast.340, f32[2304]{0:T(1024)S(1)} %pad_maximum_fusion.23), kind=kOutput, calls=%fused_computation | convolution fusion | flops 3628597248 | bytes 9839616 | tf_op jit(solution)/shard_map/dot_general | solution.py:288
  81.4 3.8 shard_map.396
  85.2 11.0 %shard_map.397 = (bf16[1152,768]{1,0:T(8,128)(2,1)S(1)}, f32[6,8,1024]{2,1,0:T(8,128)S(1)}) custom-call(s32[4,2]{1,0:T(4,128)S(1)} %pad_add_fusion.refs_0_, bf16[1024,2304]{1,0:T(8,128)(2,1)} %add_convert_fusion.refs_1_.refs_2_.refs_3_, bf16[1024,2304]{1,0:T(8,128)(2,1)} %add_convert_fusion.refs_1_.refs_2_.refs_3_, ...), custom_call_target="tpu_custom_call", output_to_operand_aliasing={{0}: (6, {})} | custom-call | flops 16106127360 | bytes 3145728 | tf_op jit(solution)/shard_map/pallas_call | solution.py:508
  96.2 5.9 %collective-permute-done.9.refs_1_ = bf16[384,768]{1,0:T(8,128)(2,1)S(1)} collective-permute-done((bf16[384,768]{1,0:T(8,128)(2,1)S(1)}, bf16[384,768]{1,0:T(8,128)(2,1)S(1)}, u32[]{:S(2)}, u32[]{:S(2)}) %collective-permute-start.9) | collective-permute-done | bytes 589856 | tf_op jit(solution)/shard_map/ppermute | solution.py:135
  104.6 11.0 %shard_map.399 = (bf16[1152,768]{1,0:T(8,128)(2,1)S(1)}, f32[6,8,1024]{2,1,0:T(8,128)S(1)}) custom-call(s32[4,2]{1,0:T(4,128)S(1)} %pad_add_fusion.refs_0_, bf16[1024,2304]{1,0:T(8,128)(2,1)} %add_convert_fusion.refs_1_.refs_2_.refs_3_, bf16[1024,2304]{1,0:T(8,128)(2,1)} %add_convert_fusion.refs_1_.refs_2_.refs_3_, ...), custom_call_target="tpu_custom_call", output_to_operand_aliasing={{0}: (6, {}), {1}: (7, {})} | custom-call | flops 16106127360 | bytes 3145728 | tf_op jit(solution)/shard_map/pallas_call | solution.py:508
  115.6 3.6 collective-permute-done.10.refs_1_
  120.4 5.8 %shard_map.401 = (f32[1152,768]{1,0:T(8,128)}, bf16[1152,768]{1,0:T(8,128)(2,1)}, bf16[1152,3072]{1,0:T(8,128)(2,1)}, bf16[1152,3072]{1,0:T(8,128)(2,1)}) custom-call(bf16[1152,768]{1,0:T(8,128)(2,1)} %pad_maximum_fusion.refs_0_.x_ref, bf16[1152,768]{1,0:T(8,128)(2,1)} %copy-done.5, ...), custom_call_target="tpu_custom_call" | custom-call | flops 754974720 | bytes 14782464 | tf_op jit(solution)/shard_map/pallas_call | solution.py:362
  126.1 2.9 shard_map.402
  131.3 4.8 %shard_map.403 = (f32[1152,768]{1,0:T(8,128)}, bf16[1152,768]{1,0:T(8,128)(2,1)}, f32[1152,128]{1,0:T(8,128)}, bf16[1152,128]{1,0:T(8,128)(2,1)}) custom-call(bf16[1152,3072]{1,0:T(8,128)(2,1)} %get-tuple-element.155.refs_0_.refs_7_, f32[1152,768]{1,0:T(8,128)} %get-tuple-element.153.refs_1_.refs_5_, bf16[3072,768]{1,0:T(8,128)(2,1)} %bitcast.333, ...), custom_call_target="tpu_custom_call" | custom-call | flops 603979776 | bytes 12718080 | tf_op jit(solution)/shard_map/pallas_call | solution.py:362
  136.8 4.8 %collective-permute-start.15 = (bf16[128,128]{1,0:T(8,128)(2,1)S(1)}, bf16[128,128]{1,0:T(8,128)(2,1)S(1)}, u32[]{:S(2)}, u32[]{:S(2)}) collective-permute-start(bf16[128,128]{1,0:T(8,128)(2,1)S(1)} %slice.164), channel_id=1, source_target_pairs={{0,3},{1,0},{2,1},{3,2},{4,7},{5,4},{6,5},{7,6},{8,11},{9,8},{10,9... | collective-permute-start | bytes 98312 | tf_op jit(solution)/shard_map/ppermute | solution.py:107
  143.3 3.5 collective-permute-done.16
  148.8 17.5 %shard_map.404 = (f32[1152,768]{1,0:T(8,128)}, bf16[1152,768]{1,0:T(8,128)(2,1)}, bf16[1152,3072]{1,0:T(8,128)(2,1)}, bf16[1152,3072]{1,0:T(8,128)(2,1)}) custom-call(bf16[1152,768]{1,0:T(8,128)(2,1)} %pad_maximum_fusion.refs_0_.x_ref, bf16[1152,768]{1,0:T(8,128)(2,1)} %copy-done.5, ...), custom_call_target="tpu_custom_call", output_to_operand_aliasing={{0}: (5, {}), {1}: (6, {}), {2}: (7, {}), {3}: (8, {})} | custom-call | flops 6039797760 | bytes 32673792 | tf_op jit(solution)/shard_map/pallas_call | solution.py:362
  166.3 12.9 %shard_map.405 = (f32[1152,768]{1,0:T(8,128)}, bf16[1152,768]{1,0:T(8,128)(2,1)}, f32[1152,128]{1,0:T(8,128)}, bf16[1152,128]{1,0:T(8,128)(2,1)}) custom-call(bf16[1152,3072]{1,0:T(8,128)(2,1)} %get-tuple-element.157.refs_0_, ...), custom_call_target="tpu_custom_call", output_to_operand_aliasing={{0}: (5, {}), {1}: (6, {}), {2}: (7, {}), {3}: (8, {})} | custom-call | flops 4831838208 | bytes 25792512 | tf_op jit(solution)/shard_map/pallas_call | solution.py:362
  181.4 5.6 %shard_map.406 = (f32[128,128]{1,0:T(8,128)S(1)}, f32[4096,128]{1,0:T(8,128)S(1)}, bf16[4096,1024]{1,0:T(8,128)(2,1)S(1)}) custom-call(bf16[4096,128]{1,0:T(8,128)(2,1)S(1)} %copy-done.19, bf16[1024,128]{1,0:T(8,128)(2,1)S(1)} %slice.165.passage_ref, bf16[1024,128]{1,0:T(8,128)(2,1)S(1)} %compare_convert_fusion.member_ref), custom_call_target="tpu_custom_call" | custom-call | flops 3221225472 | bytes 4194304 | tf_op jit(solution)/shard_map/pallas_call | solution.py:718
  187.0 3.3 copy-done.3
  192.4 3.7 all-to-all-start
  196.1 5.0 %shard_map.407 = bf16[768,1152]{1,0:T(8,128)(2,1)} custom-call(bf16[1152,768]{1,0:T(8,128)(2,1)} %pad_maximum_fusion.refs_0_.x_ref), custom_call_target="tpu_custom_call" | custom-call | tf_op jit(solution)/shard_map/pallas_call | solution.py:322
  203.6 3.4 copy-done.4
  208.6 5.5 %shard_map.408 = f32[4096,128]{1,0:T(8,128)S(1)} custom-call(bf16[4096,1024]{1,0:T(8,128)(2,1)S(1)} %copy-done.4, bf16[1024,128]{1,0:T(8,128)(2,1)S(1)} %slice.165.passage_ref, bf16[1024,128]{1,0:T(8,128)(2,1)S(1)} %compare_convert_fusion.member_ref, f32[128,128]{1,0:T(8,128)S(1)} %copy.207.grad_ref, f32[4096,128]{1,0:T(8,128)S(1)} %copy-done.10), custom_call_target="tpu_custom_call" | custom-call | flops 3221225472 | bytes 4194304 | tf_op jit(solution)/shard_map/pallas_call | solution.py:718
  215.1 3.0 collective-permute-done.18
  222.5 8.3 %shard_map.409.refs_0_ = f32[1024,128]{1,0:T(8,128)S(1)} custom-call(bf16[4096,128]{1,0:T(8,128)(2,1)S(1)} %copy-done.20, bf16[1024,128]{1,0:T(8,128)(2,1)S(1)} %slice.165.passage_ref, bf16[1024,128]{1,0:T(8,128)(2,1)S(1)} %compare_convert_fusion.member_ref, f32[128,128]{1,0:T(8,128)S(1)} %copy.207.grad_ref, f32[4096,128]{1,0:T(8,128)S(1)} %copy-done.11), custom_call_target="tpu_custom_call" | custom-call | flops 3221225472 | bytes 4194304 | tf_op jit(solution)/shard_map/pallas_call | solution.py:718
  233.5 23.2 %shard_map.410 = (bf16[1152,128]{1,0:T(8,128)(2,1)}, bf16[1152,768]{1,0:T(8,128)(2,1)}, bf16[1152,3072]{1,0:T(8,128)(2,1)}, bf16[1152,768]{1,0:T(8,128)(2,1)}, b...) custom-call(f32[1024,128]{1,0:T(8,128)} %copy-done.21, f32[1152,128]{1,0:T(8,128)} %get-tuple-element.168.refs_1_, ...), custom_call_target="tpu_custom_call" | custom-call | flops 10871635968 | bytes 47943680 | tf_op jit(solution)/shard_map/pallas_call | solution.py:362
  268.7 9.7 %shard_map.411 = (bf16[1152,128]{1,0:T(8,128)(2,1)}, bf16[1152,768]{1,0:T(8,128)(2,1)}, bf16[1152,3072]{1,0:T(8,128)(2,1)}, bf16[1152,768]{1,0:T(8,128)(2,1)}, b...) custom-call(f32[128,128]{1,0:T(8,128)} %fusion.58.refs_0_, ...), custom_call_target="tpu_custom_call", output_to_operand_aliasing={{0}: (10, {}), {1}: (11, {}), {2}: (12, {}), {3}: (13, {}),... | custom-call | flops 1358954496 | bytes 26152960 | tf_op jit(solution)/shard_map/pallas_call | solution.py:362
  278.4 8.6 %convolution_convert_fusion.1 = bf16[3072,768]{1,0:T(8,128)(2,1)S(1)} fusion(bf16[1152,3072]{1,0:T(8,128)(2,1)S(1)} %bitcast.352, bf16[1152,768]{1,0:T(8,128)(2,1)} %get-tuple-element.179), kind=kOutput, calls=%fused_computation.2 | convolution fusion | flops 5438177280 | bytes 13565952 | tf_op jit(solution)/shard_map/dot_general | solution.py:288
  288.4 6.7 %convolution_convert_fusion = bf16[768,3072]{1,0:T(8,128)(2,1)S(1)} fusion(bf16[1152,768]{1,0:T(8,128)(2,1)S(1)} %copy-done.29, bf16[1152,3072]{1,0:T(8,128)(2,1)S(1)} %copy-done.23), kind=kOutput, calls=%fused_computation.1 | convolution fusion | flops 5438177280 | bytes 13565952 | tf_op jit(solution)/shard_map/dot_general | solution.py:288
  304.5 5.2 %shard_map.412 = (bf16[3,1152,768]{2,1,0:T(8,128)(2,1)}, f32[16,768]{1,0:T(8,128)S(1)}) custom-call(s32[1,2]{1,0:T(1,128)S(1)} %broadcast_11_refs_0_.2.refs_0_, bf16[128,2304]{1,0:T(8,128)(2,1)S(1)} %copy-done.18, bf16[128,2304]{1,0:T(8,128)(2,1)S(1)} %copy-done.18, bf16[128,2304]{1,0:T(8,128)(2,1)S(1)} %copy-done.18, bf16[1152,768]{1,0:T(8,128)(2,1)S(1)} %copy-done.12, ...), custom_call_target="tpu_custom_call" | custom-call | flops 1006632960 | bytes 786432 | tf_op jit(solution)/shard_map/pallas_call | solution.py:508
  315.5 4.5 collective-permute-done.29
  322.6 11.1 %shard_map.413 = (bf16[3,1152,768]{2,1,0:T(8,128)(2,1)}, f32[16,768]{1,0:T(8,128)S(1)}) custom-call(s32[4,2]{1,0:T(4,128)S(1)} %pad_add_fusion.refs_0_, bf16[1024,2304]{1,0:T(8,128)(2,1)} %add_convert_fusion.refs_1_.refs_2_.refs_3_, bf16[1024,2304]{1,0:T(8,128)(2,1)} %add_convert_fusion.refs_1_.refs_2_.refs_3_, ...), custom_call_target="tpu_custom_call", output_to_operand_aliasing={{0}: (8, {})} | custom-call | flops 21474836480 | bytes 2097152 | tf_op jit(solution)/shard_map/pallas_call | solution.py:508
  333.7 4.4 collective-permute-done.30
  342.1 11.4 %shard_map.414 = (bf16[3,1152,768]{2,1,0:T(8,128)(2,1)}, f32[16,768]{1,0:T(8,128)S(1)}) custom-call(s32[4,2]{1,0:T(4,128)S(1)} %pad_add_fusion.refs_0_, bf16[1024,2304]{1,0:T(8,128)(2,1)} %add_convert_fusion.refs_1_.refs_2_.refs_3_, bf16[1024,2304]{1,0:T(8,128)(2,1)} %add_convert_fusion.refs_1_.refs_2_.refs_3_, ...), custom_call_target="tpu_custom_call", output_to_operand_aliasing={{0}: (8, {}), {1}: (9, {})} | custom-call | flops 21474836480 | bytes 2097152 | tf_op jit(solution)/shard_map/pallas_call | solution.py:508
  355.3 2.8 collective-permute-start.34
  358.2 11.2 %shard_map.415 = (bf16[3,1152,768]{2,1,0:T(8,128)(2,1)}, f32[16,768]{1,0:T(8,128)S(1)}) custom-call(s32[4,2]{1,0:T(4,128)S(1)} %pad_add_fusion.refs_0_, bf16[1024,2304]{1,0:T(8,128)(2,1)} %add_convert_fusion.refs_1_.refs_2_.refs_3_, bf16[1024,2304]{1,0:T(8,128)(2,1)} %add_convert_fusion.refs_1_.refs_2_.refs_3_, ...), custom_call_target="tpu_custom_call", output_to_operand_aliasing={{0}: (8, {}), {1}: (9, {})} | custom-call | flops 21474836480 | bytes 2097152 | tf_op jit(solution)/shard_map/pallas_call | solution.py:508
  375.0 3.3 fusion.17
  381.8 4.2 collective-permute-start.40
  392.6 7.8 %collective-permute-done.41 = bf16[24,4096]{1,0:T(8,128)(2,1)S(1)} collective-permute-done((bf16[24,4096]{1,0:T(8,128)(2,1)S(1)}, bf16[24,4096]{1,0:T(8,128)(2,1)S(1)}, u32[]{:S(2)}, u32[]{:S(2)}) %collective-permute-start.41) | collective-permute-done | bytes 196640 | tf_op jit(solution)/shard_map/ppermute | solution.py:260
  400.7 3.6 collective-permute-done.39
  406.1 7.1 %collective-permute-done.43 = bf16[96,2432]{1,0:T(8,128)(2,1)S(1)} collective-permute-done((bf16[96,2432]{1,0:T(8,128)(2,1)S(1)}, bf16[96,2432]{1,0:T(8,128)(2,1)S(1)}, u32[]{:S(2)}, u32[]{:S(2)}) %collective-permute-start.43) | collective-permute-done | bytes 466976 | tf_op jit(solution)/shard_map/ppermute | solution.py:250
  416.9 2.9 collective-permute-done.46.refs_6_
  419.8 6.3 %collective-permute-done.45.refs_5_ = bf16[24,2432]{1,0:T(8,128)(2,1)S(1)} collective-permute-done((bf16[24,2432]{1,0:T(8,128)(2,1)S(1)}, bf16[24,2432]{1,0:T(8,128)(2,1)S(1)}, u32[]{:S(2)}, u32[]{:S(2)}) %collective-permute-start.45) | collective-permute-done | bytes 116768 | tf_op jit(solution)/shard_map/ppermute | solution.py:260
  427.5 3.7 all-to-all-start.1
  431.5 6.8 %all-to-all-done.1 = f32[32,1,128]{2,1,0:T(1,128)S(1)} async-done(((f32[32,1,128]{2,1,0:T(1,128)}), f32[32,1,128]{2,1,0:T(1,128)S(1)}, u32[]{:S(2)}, u32[]{:S(2)}) %all-to-all-start.1) | async-done | bytes 16416 | tf_op jit(solution)/shard_map/all_to_all | solution.py:280
  (387 shorter events, 127.4 us)
Async XLA Ops:
  7.2 113.1 %all-gather.3.cloned.1.call-start = ((), (), s32[]{:S(2)}) async-start(), calls=%async_computation.2 | async-start | bytes 6856704 | tf_op jit(solution)/shard_map/all_gather | solution.py:120
  9.1 8.7 %collective-permute-start = (bf16[24,2432]{1,0:T(8,128)(2,1)S(1)}, bf16[24,2432]{1,0:T(8,128)(2,1)S(1)}, u32[]{:S(2)}, u32[]{:S(2)}) collective-permute-start(bf16[24,2432]{1,0:T(8,128)(2,1)S(1)} %fusion.44), channel_id=1, source_target_pairs={{0,3},{1,0},{2,1},{3,2},{4,7},{5,4},{6,5},{7,6},{8,11},{9,8},{10,9... | collective-permute-start | bytes 350216 | tf_op jit(solution)/shard_map/ppermute | solution.py:107
  14.2 10.1 %collective-permute-start.1 = (bf16[24,2432]{1,0:T(8,128)(2,1)S(1)}, bf16[24,2432]{1,0:T(8,128)(2,1)S(1)}, u32[]{:S(2)}, u32[]{:S(2)}) collective-permute-start(bf16[24,2432]{1,0:T(8,128)(2,1)S(1)} %fusion.44), channel_id=1, source_target_pairs={{0,2},{1,3},{2,0},{3,1},{4,6},{5,7},{6,4},{7,5},{8,10},{9,11},{10,... | collective-permute-start | bytes 350216 | tf_op jit(solution)/shard_map/ppermute | solution.py:107
  14.2 10.1 %collective-permute-start.2 = (bf16[24,2432]{1,0:T(8,128)(2,1)S(1)}, bf16[24,2432]{1,0:T(8,128)(2,1)S(1)}, u32[]{:S(2)}, u32[]{:S(2)}) collective-permute-start(bf16[24,2432]{1,0:T(8,128)(2,1)S(1)} %fusion.44), channel_id=1, source_target_pairs={{0,1},{1,2},{2,3},{3,0},{4,5},{5,6},{6,7},{7,4},{8,9},{9,10},{10,1... | collective-permute-start | bytes 350216 | tf_op jit(solution)/shard_map/ppermute | solution.py:107
  24.7 8.6 %collective-permute-start.3 = (bf16[96,2432]{1,0:T(8,128)(2,1)S(1)}, bf16[96,2432]{1,0:T(8,128)(2,1)S(1)}, u32[]{:S(2)}, u32[]{:S(2)}) collective-permute-start(bf16[96,2432]{1,0:T(8,128)(2,1)S(1)} %bitcast.343), channel_id=1, source_target_pairs={{0,8},{4,20},{8,0},{12,28},{16,24},{20,4},{24,16},{28,12},{1,9},{5... | collective-permute-start | bytes 1400840 | tf_op jit(solution)/shard_map/ppermute | solution.py:135
  27.1 24.5 %collective-permute-start.11 = (bf16[24,3968]{1,0:T(8,128)(2,1)}, bf16[24,3968]{1,0:T(8,128)(2,1)}, u32[]{:S(2)}, u32[]{:S(2)}) collective-permute-start(bf16[24,3968]{1,0:T(8,128)(2,1)} %pad_maximum_fusion.14), channel_id=1, source_target_pairs={{0,1},{1,2},{2,3},{3,0},{4,5},{5,6},{6,7},{7,4},{8,9},{9,10},{10,1... | collective-permute-start | bytes 571400 | tf_op jit(solution)/shard_map/ppermute | solution.py:107
  27.6 24.0 %collective-permute-start.12 = (bf16[24,3968]{1,0:T(8,128)(2,1)}, bf16[24,3968]{1,0:T(8,128)(2,1)}, u32[]{:S(2)}, u32[]{:S(2)}) collective-permute-start(bf16[24,3968]{1,0:T(8,128)(2,1)} %pad_maximum_fusion.14), channel_id=1, source_target_pairs={{0,2},{1,3},{2,0},{3,1},{4,6},{5,7},{6,4},{7,5},{8,10},{9,11},{10,... | collective-permute-start | bytes 571400 | tf_op jit(solution)/shard_map/ppermute | solution.py:107
  29.5 22.1 %collective-permute-start.13 = (bf16[24,3968]{1,0:T(8,128)(2,1)}, bf16[24,3968]{1,0:T(8,128)(2,1)}, u32[]{:S(2)}, u32[]{:S(2)}) collective-permute-start(bf16[24,3968]{1,0:T(8,128)(2,1)} %pad_maximum_fusion.14), channel_id=1, source_target_pairs={{0,3},{1,0},{2,1},{3,2},{4,7},{5,4},{6,5},{7,6},{8,11},{9,8},{10,9... | collective-permute-start | bytes 571400 | tf_op jit(solution)/shard_map/ppermute | solution.py:107
  34.4 13.6 %collective-permute-start.4 = (bf16[2,96,2432]{2,1,0:T(8,128)(2,1)S(1)}, bf16[2,96,2432]{2,1,0:T(8,128)(2,1)S(1)}, u32[]{:S(2)}, u32[]{:S(2)}) collective-permute-start(bf16[2,96,2432]{2,1,0:T(8,128)(2,1)S(1)} %shard_map.393.refs_0_), channel_id=1, source_target_pairs={{0,16},{4,12},{8,24},{12,4},{16,0},{20,28},{24,8},{28,20},{1,17},{... | collective-permute-start | bytes 2801672 | tf_op jit(solution)/shard_map/ppermute | solution.py:141
  55.2 124.9 %all-gather.5.cloned.1.call-start = ((), (), s32[]{:S(2)}) async-start(), calls=%async_computation.3 | async-start | bytes 1179648 | tf_op jit(solution)/shard_map/all_gather | solution.py:120
  55.3 3.9 collective-permute-start.5
  65.3 13.0 %collective-permute-start.6 = (bf16[96,768]{1,0:T(8,128)(2,1)S(1)}, bf16[96,768]{1,0:T(8,128)(2,1)S(1)}, u32[]{:S(2)}, u32[]{:S(2)}) collective-permute-start(bf16[96,768]{1,0:T(8,128)(2,1)S(1)} %convert_element_type.502), channel_id=1, source_target_pairs={{0,1},{1,2},{2,3},{3,0},{4,5},{5,6},{6,7},{7,4},{8,9},{9,10},{10,1... | collective-permute-start | bytes 442376 | tf_op jit(solution)/shard_map/ppermute | solution.py:107
  66.0 13.5 %collective-permute-start.7 = (bf16[96,768]{1,0:T(8,128)(2,1)S(1)}, bf16[96,768]{1,0:T(8,128)(2,1)S(1)}, u32[]{:S(2)}, u32[]{:S(2)}) collective-permute-start(bf16[96,768]{1,0:T(8,128)(2,1)S(1)} %convert_element_type.502), channel_id=1, source_target_pairs={{0,2},{1,3},{2,0},{3,1},{4,6},{5,7},{6,4},{7,5},{8,10},{9,11},{10,... | collective-permute-start | bytes 442376 | tf_op jit(solution)/shard_map/ppermute | solution.py:107
  68.0 11.6 %collective-permute-start.8 = (bf16[96,768]{1,0:T(8,128)(2,1)S(1)}, bf16[96,768]{1,0:T(8,128)(2,1)S(1)}, u32[]{:S(2)}, u32[]{:S(2)}) collective-permute-start(bf16[96,768]{1,0:T(8,128)(2,1)S(1)} %convert_element_type.502), channel_id=1, source_target_pairs={{0,3},{1,0},{2,1},{3,2},{4,7},{5,4},{6,5},{7,6},{8,11},{9,8},{10,9... | collective-permute-start | bytes 442376 | tf_op jit(solution)/shard_map/ppermute | solution.py:107
  79.7 22.4 %collective-permute-start.9 = (bf16[384,768]{1,0:T(8,128)(2,1)S(1)}, bf16[384,768]{1,0:T(8,128)(2,1)S(1)}, u32[]{:S(2)}, u32[]{:S(2)}) collective-permute-start(bf16[384,768]{1,0:T(8,128)(2,1)S(1)} %bitcast.341), channel_id=1, source_target_pairs={{0,8},{4,20},{8,0},{12,28},{16,24},{20,4},{24,16},{28,12},{1,9},{5... | collective-permute-start | bytes 1769480 | tf_op jit(solution)/shard_map/ppermute | solution.py:135
  102.9 16.3 %collective-permute-start.10 = (bf16[2,384,768]{2,1,0:T(8,128)(2,1)S(1)}, bf16[2,384,768]{2,1,0:T(8,128)(2,1)S(1)}, u32[]{:S(2)}, u32[]{:S(2)}) collective-permute-start(bf16[2,384,768]{2,1,0:T(8,128)(2,1)S(1)} %shard_map.398.refs_0_), channel_id=1, source_target_pairs={{0,16},{4,12},{8,24},{12,4},{16,0},{20,28},{24,8},{28,20},{1,17},{... | collective-permute-start | bytes 3538952 | tf_op jit(solution)/shard_map/ppermute | solution.py:141
  120.3 5.9 %collective-permute-start.14 = (bf16[2,2,384,768]{3,2,1,0:T(8,128)(2,1)S(1)}, bf16[2,2,384,768]{3,2,1,0:T(8,128)(2,1)}, u32[]{:S(2)}, u32[]{:S(2)}) collective-permute-start(bf16[2,2,384,768]{3,2,1,0:T(8,128)(2,1)S(1)} %shard_map.400.refs_0_), channel_id=1, source_target_pairs={{0,4},{4,0},{8,12},{12,8},{16,20},{20,16},{24,28},{28,24},{1,5},{5... | collective-permute-start | bytes 7077896 | tf_op jit(solution)/shard_map/ppermute | solution.py:148
  136.8 6.5 %collective-permute-start.15 = (bf16[128,128]{1,0:T(8,128)(2,1)S(1)}, bf16[128,128]{1,0:T(8,128)(2,1)S(1)}, u32[]{:S(2)}, u32[]{:S(2)}) collective-permute-start(bf16[128,128]{1,0:T(8,128)(2,1)S(1)} %slice.164), channel_id=1, source_target_pairs={{0,3},{1,0},{2,1},{3,2},{4,7},{5,4},{6,5},{7,6},{8,11},{9,8},{10,9... | collective-permute-start | bytes 98312 | tf_op jit(solution)/shard_map/ppermute | solution.py:107
  141.6 5.2 %collective-permute-start.16 = (bf16[128,128]{1,0:T(8,128)(2,1)S(1)}, bf16[128,128]{1,0:T(8,128)(2,1)S(1)}, u32[]{:S(2)}, u32[]{:S(2)}) collective-permute-start(bf16[128,128]{1,0:T(8,128)(2,1)S(1)} %slice.164), channel_id=1, source_target_pairs={{0,2},{1,3},{2,0},{3,1},{4,6},{5,7},{6,4},{7,5},{8,10},{9,11},{10,... | collective-permute-start | bytes 98312 | tf_op jit(solution)/shard_map/ppermute | solution.py:107
  141.6 5.7 %collective-permute-start.17 = (bf16[128,128]{1,0:T(8,128)(2,1)S(1)}, bf16[128,128]{1,0:T(8,128)(2,1)S(1)}, u32[]{:S(2)}, u32[]{:S(2)}) collective-permute-start(bf16[128,128]{1,0:T(8,128)(2,1)S(1)} %slice.164), channel_id=1, source_target_pairs={{0,1},{1,2},{2,3},{3,0},{4,5},{5,6},{6,7},{7,4},{8,9},{9,10},{10,1... | collective-permute-start | bytes 98312 | tf_op jit(solution)/shard_map/ppermute | solution.py:107
  192.4 10.8 %all-to-all-start = ((f32[32,1,128]{2,1,0:T(1,128)}), f32[32,1,128]{2,1,0:T(1,128)S(1)}, u32[]{:S(2)}, u32[]{:S(2)}) async-start(f32[32,1,128]{2,1,0:T(1,128)} %broadcast_in_dim.46), calls=%async_computation | async-start | bytes 32768 | tf_op jit(solution)/shard_map/all_to_all | solution.py:280
  220.6 11.0 %collective-permute-start.19 = (bf16[2,512,256]{2,1,0:T(8,128)(2,1)}, bf16[2,512,256]{2,1,0:T(8,128)(2,1)}, u32[]{:S(2)}, u32[]{:S(2)}) collective-permute-start(bf16[2,512,256]{2,1,0:T(8,128)(2,1)} %pad_maximum_fusion.7), channel_id=1, source_target_pairs={{0,16},{4,12},{8,24},{12,4},{16,0},{20,28},{24,8},{28,20},{1,17},{... | collective-permute-start | bytes 1572872 | tf_op jit(solution)/shard_map/ppermute | solution.py:241
  232.8 23.8 %collective-permute-start.20 = (bf16[512,256]{1,0:T(8,128)(2,1)S(1)}, bf16[512,256]{1,0:T(8,128)(2,1)S(1)}, u32[]{:S(2)}, u32[]{:S(2)}) collective-permute-start(bf16[512,256]{1,0:T(8,128)(2,1)S(1)} %pad_maximum_fusion.10), channel_id=1, source_target_pairs={{0,8},{4,20},{8,0},{12,28},{16,24},{20,4},{24,16},{28,12},{1,9},{5... | collective-permute-start | bytes 786440 | tf_op jit(solution)/shard_map/ppermute | solution.py:250
  257.4 6.6 %collective-permute-start.21 = (bf16[128,256]{1,0:T(8,128)(2,1)}, bf16[128,256]{1,0:T(8,128)(2,1)S(1)}, u32[]{:S(2)}, u32[]{:S(2)}) collective-permute-start(bf16[128,256]{1,0:T(8,128)(2,1)} %pad_maximum_fusion.20), channel_id=1, source_target_pairs={{0,1},{1,2},{2,3},{3,0},{4,5},{5,6},{6,7},{7,4},{8,9},{9,10},{10,1... | collective-permute-start | bytes 196616 | tf_op jit(solution)/shard_map/ppermute | solution.py:260
  259.4 7.3 %collective-permute-start.22 = (bf16[128,256]{1,0:T(8,128)(2,1)}, bf16[128,256]{1,0:T(8,128)(2,1)}, u32[]{:S(2)}, u32[]{:S(2)}) collective-permute-start(bf16[128,256]{1,0:T(8,128)(2,1)} %pad_maximum_fusion.21), channel_id=1, source_target_pairs={{0,2},{1,3},{2,0},{3,1},{4,6},{5,7},{6,4},{7,5},{8,10},{9,11},{10,... | collective-permute-start | bytes 196616 | tf_op jit(solution)/shard_map/ppermute | solution.py:260
  262.5 4.7 %collective-permute-start.23 = (bf16[128,256]{1,0:T(8,128)(2,1)}, bf16[128,256]{1,0:T(8,128)(2,1)}, u32[]{:S(2)}, u32[]{:S(2)}) collective-permute-start(bf16[128,256]{1,0:T(8,128)(2,1)} %pad_maximum_fusion.22), channel_id=1, source_target_pairs={{0,3},{1,0},{2,1},{3,2},{4,7},{5,4},{6,5},{7,6},{8,11},{9,8},{10,9... | collective-permute-start | bytes 196616 | tf_op jit(solution)/shard_map/ppermute | solution.py:260
  287.1 9.4 %collective-permute-start.25 = (bf16[4,384,768]{2,1,0:T(8,128)(2,1)S(1)}, bf16[4,384,768]{2,1,0:T(8,128)(2,1)S(1)}, u32[]{:S(2)}, u32[]{:S(2)}) collective-permute-start(bf16[4,384,768]{2,1,0:T(8,128)(2,1)S(1)} %dynamic-slice_bitcast_fusion.1), channel_id=1, source_target_pairs={{0,4},{4,0},{8,12},{12,8},{16,20},{20,16},{24,28},{28,24},{1,5},{5... | collective-permute-start | bytes 7077896 | tf_op jit(solution)/shard_map/ppermute | solution.py:216
  295.3 14.6 %collective-permute-start.24 = (bf16[4,96,3072]{2,1,0:T(8,128)(2,1)S(1)}, bf16[4,96,3072]{2,1,0:T(8,128)(2,1)}, u32[]{:S(2)}, u32[]{:S(2)}) collective-permute-start(bf16[4,96,3072]{2,1,0:T(8,128)(2,1)S(1)} %dynamic-slice_bitcast_fusion), channel_id=1, source_target_pairs={{0,4},{4,0},{8,12},{12,8},{16,20},{20,16},{24,28},{28,24},{1,5},{5... | collective-permute-start | bytes 7077896 | tf_op jit(solution)/shard_map/ppermute | solution.py:216
  302.2 7.7 %collective-permute-start.26 = (bf16[4,96,768]{2,1,0:T(8,128)(2,1)}, bf16[4,96,768]{2,1,0:T(8,128)(2,1)}, u32[]{:S(2)}, u32[]{:S(2)}) collective-permute-start(bf16[4,96,768]{2,1,0:T(8,128)(2,1)} %dynamic-slice_bitcast_fusion.6), channel_id=1, source_target_pairs={{0,4},{4,0},{8,12},{12,8},{16,20},{20,16},{24,28},{28,24},{1,5},{5... | collective-permute-start | bytes 1769480 | tf_op jit(solution)/shard_map/ppermute | solution.py:216
  302.9 7.0 %collective-permute-start.27 = (f32[4,96,128]{2,1,0:T(8,128)S(1)}, f32[4,96,128]{2,1,0:T(8,128)S(1)}, u32[]{:S(2)}, u32[]{:S(2)}) collective-permute-start(f32[4,96,128]{2,1,0:T(8,128)S(1)} %dynamic-slice_bitcast_fusion.7), channel_id=1, source_target_pairs={{0,4},{4,0},{8,12},{12,8},{16,20},{20,16},{24,28},{28,24},{1,5},{5... | collective-permute-start | bytes 589832 | tf_op jit(solution)/shard_map/ppermute | solution.py:216
  303.5 16.5 %collective-permute-start.29 = (bf16[2,384,768]{2,1,0:T(8,128)(2,1)}, bf16[2,384,768]{2,1,0:T(8,128)(2,1)}, u32[]{:S(2)}, u32[]{:S(2)}) collective-permute-start(bf16[2,384,768]{2,1,0:T(8,128)(2,1)} %pad_maximum_fusion.2), channel_id=1, source_target_pairs={{0,16},{4,12},{8,24},{12,4},{16,0},{20,28},{24,8},{28,20},{1,17},{... | collective-permute-start | bytes 3538952 | tf_op jit(solution)/shard_map/ppermute | solution.py:241
  314.2 39.5 %collective-permute-start.28 = (bf16[2,96,4096]{2,1,0:T(8,128)(2,1)S(1)}, bf16[2,96,4096]{2,1,0:T(8,128)(2,1)S(1)}, u32[]{:S(2)}, u32[]{:S(2)}) collective-permute-start(bf16[2,96,4096]{2,1,0:T(8,128)(2,1)S(1)} %pad_maximum_fusion.1), channel_id=1, source_target_pairs={{0,16},{4,12},{8,24},{12,4},{16,0},{20,28},{24,8},{28,20},{1,17},{... | collective-permute-start | bytes 4718600 | tf_op jit(solution)/shard_map/ppermute | solution.py:241
  321.8 16.3 %collective-permute-start.30 = (bf16[384,768]{1,0:T(8,128)(2,1)S(1)}, bf16[384,768]{1,0:T(8,128)(2,1)S(1)}, u32[]{:S(2)}, u32[]{:S(2)}) collective-permute-start(bf16[384,768]{1,0:T(8,128)(2,1)S(1)} %fusion.20), channel_id=1, source_target_pairs={{0,8},{4,20},{8,0},{12,28},{16,24},{20,4},{24,16},{28,12},{1,9},{5... | collective-permute-start | bytes 1769480 | tf_op jit(solution)/shard_map/ppermute | solution.py:250
  338.3 15.3 %collective-permute-start.31 = (bf16[96,768]{1,0:T(8,128)(2,1)S(1)}, bf16[96,768]{1,0:T(8,128)(2,1)S(1)}, u32[]{:S(2)}, u32[]{:S(2)}) collective-permute-start(bf16[96,768]{1,0:T(8,128)(2,1)S(1)} %get-tuple-element.380), channel_id=1, source_target_pairs={{0,1},{1,2},{2,3},{3,0},{4,5},{5,6},{6,7},{7,4},{8,9},{9,10},{10,1... | collective-permute-start | bytes 442376 | tf_op jit(solution)/shard_map/ppermute | solution.py:260
  339.3 14.3 %collective-permute-start.32 = (bf16[96,768]{1,0:T(8,128)(2,1)S(1)}, bf16[96,768]{1,0:T(8,128)(2,1)S(1)}, u32[]{:S(2)}, u32[]{:S(2)}) collective-permute-start(bf16[96,768]{1,0:T(8,128)(2,1)S(1)} %get-tuple-element.382), channel_id=1, source_target_pairs={{0,2},{1,3},{2,0},{3,1},{4,6},{5,7},{6,4},{7,5},{8,10},{9,11},{10,... | collective-permute-start | bytes 442376 | tf_op jit(solution)/shard_map/ppermute | solution.py:260
  341.9 11.7 %collective-permute-start.33 = (bf16[96,768]{1,0:T(8,128)(2,1)S(1)}, bf16[96,768]{1,0:T(8,128)(2,1)S(1)}, u32[]{:S(2)}, u32[]{:S(2)}) collective-permute-start(bf16[96,768]{1,0:T(8,128)(2,1)S(1)} %get-tuple-element.381), channel_id=1, source_target_pairs={{0,3},{1,0},{2,1},{3,2},{4,7},{5,4},{6,5},{7,6},{8,11},{9,8},{10,9... | collective-permute-start | bytes 442376 | tf_op jit(solution)/shard_map/ppermute | solution.py:260
  355.3 16.2 %collective-permute-start.34 = (bf16[96,4096]{1,0:T(8,128)(2,1)}, bf16[96,4096]{1,0:T(8,128)(2,1)}, u32[]{:S(2)}, u32[]{:S(2)}) collective-permute-start(bf16[96,4096]{1,0:T(8,128)(2,1)} %pad_maximum_fusion.3), channel_id=1, source_target_pairs={{0,8},{4,20},{8,0},{12,28},{16,24},{20,4},{24,16},{28,12},{1,9},{5... | collective-permute-start | bytes 2359304 | tf_op jit(solution)/shard_map/ppermute | solution.py:250
  371.5 15.5 %collective-permute-start.38 = (bf16[4,96,128]{2,1,0:T(8,128)(2,1)S(1)}, bf16[4,96,128]{2,1,0:T(8,128)(2,1)S(1)}, u32[]{:S(2)}, u32[]{:S(2)}) collective-permute-start(bf16[4,96,128]{2,1,0:T(8,128)(2,1)S(1)} %fusion.46), channel_id=1, source_target_pairs={{0,4},{4,0},{8,12},{12,8},{16,20},{20,16},{24,28},{28,24},{1,5},{5... | collective-permute-start | bytes 294920 | tf_op jit(solution)/shard_map/ppermute | solution.py:216
  381.8 10.8 %collective-permute-start.40 = (bf16[24,4096]{1,0:T(8,128)(2,1)S(1)}, bf16[24,4096]{1,0:T(8,128)(2,1)S(1)}, u32[]{:S(2)}, u32[]{:S(2)}) collective-permute-start(bf16[24,4096]{1,0:T(8,128)(2,1)S(1)} %pad_maximum_fusion.11), channel_id=1, source_target_pairs={{0,1},{1,2},{2,3},{3,0},{4,5},{5,6},{6,7},{7,4},{8,9},{9,10},{10,1... | collective-permute-start | bytes 589832 | tf_op jit(solution)/shard_map/ppermute | solution.py:260
  386.3 3.6 collective-permute-start.36
  387.0 13.4 %collective-permute-start.41 = (bf16[24,4096]{1,0:T(8,128)(2,1)S(1)}, bf16[24,4096]{1,0:T(8,128)(2,1)S(1)}, u32[]{:S(2)}, u32[]{:S(2)}) collective-permute-start(bf16[24,4096]{1,0:T(8,128)(2,1)S(1)} %pad_maximum_fusion.12), channel_id=1, source_target_pairs={{0,2},{1,3},{2,0},{3,1},{4,6},{5,7},{6,4},{7,5},{8,10},{9,11},{10,... | collective-permute-start | bytes 589832 | tf_op jit(solution)/shard_map/ppermute | solution.py:260
  388.1 12.3 %collective-permute-start.42 = (bf16[24,4096]{1,0:T(8,128)(2,1)S(1)}, bf16[24,4096]{1,0:T(8,128)(2,1)S(1)}, u32[]{:S(2)}, u32[]{:S(2)}) collective-permute-start(bf16[24,4096]{1,0:T(8,128)(2,1)S(1)} %pad_maximum_fusion.13), channel_id=1, source_target_pairs={{0,3},{1,0},{2,1},{3,2},{4,7},{5,4},{6,5},{7,6},{8,11},{9,8},{10,9... | collective-permute-start | bytes 589832 | tf_op jit(solution)/shard_map/ppermute | solution.py:260
  390.6 13.6 %collective-permute-start.39 = (bf16[2,96,2432]{2,1,0:T(8,128)(2,1)S(1)}, bf16[2,96,2432]{2,1,0:T(8,128)(2,1)S(1)}, u32[]{:S(2)}, u32[]{:S(2)}) collective-permute-start(bf16[2,96,2432]{2,1,0:T(8,128)(2,1)S(1)} %maximum_maximum_fusion), channel_id=1, source_target_pairs={{0,16},{4,12},{8,24},{12,4},{16,0},{20,28},{24,8},{28,20},{1,17},{... | collective-permute-start | bytes 2801672 | tf_op jit(solution)/shard_map/ppermute | solution.py:241
  404.6 8.6 %collective-permute-start.43 = (bf16[96,2432]{1,0:T(8,128)(2,1)S(1)}, bf16[96,2432]{1,0:T(8,128)(2,1)S(1)}, u32[]{:S(2)}, u32[]{:S(2)}) collective-permute-start(bf16[96,2432]{1,0:T(8,128)(2,1)S(1)} %pad_maximum_fusion.9), channel_id=1, source_target_pairs={{0,8},{4,20},{8,0},{12,28},{16,24},{20,4},{24,16},{28,12},{1,9},{5... | collective-permute-start | bytes 1400840 | tf_op jit(solution)/shard_map/ppermute | solution.py:250
  413.6 6.2 %collective-permute-start.46 = (bf16[24,2432]{1,0:T(8,128)(2,1)S(1)}, bf16[24,2432]{1,0:T(8,128)(2,1)S(1)}, u32[]{:S(2)}, u32[]{:S(2)}) collective-permute-start(bf16[24,2432]{1,0:T(8,128)(2,1)S(1)} %pad_maximum_fusion.18), channel_id=1, source_target_pairs={{0,3},{1,0},{2,1},{3,2},{4,7},{5,4},{6,5},{7,6},{8,11},{9,8},{10,9... | collective-permute-start | bytes 350216 | tf_op jit(solution)/shard_map/ppermute | solution.py:260
  416.2 9.9 %collective-permute-start.45 = (bf16[24,2432]{1,0:T(8,128)(2,1)S(1)}, bf16[24,2432]{1,0:T(8,128)(2,1)S(1)}, u32[]{:S(2)}, u32[]{:S(2)}) collective-permute-start(bf16[24,2432]{1,0:T(8,128)(2,1)S(1)} %pad_maximum_fusion.17), channel_id=1, source_target_pairs={{0,2},{1,3},{2,0},{3,1},{4,6},{5,7},{6,4},{7,5},{8,10},{9,11},{10,... | collective-permute-start | bytes 350216 | tf_op jit(solution)/shard_map/ppermute | solution.py:260
  416.4 9.7 %collective-permute-start.44 = (bf16[24,2432]{1,0:T(8,128)(2,1)S(1)}, bf16[24,2432]{1,0:T(8,128)(2,1)S(1)}, u32[]{:S(2)}, u32[]{:S(2)}) collective-permute-start(bf16[24,2432]{1,0:T(8,128)(2,1)S(1)} %pad_maximum_fusion.16), channel_id=1, source_target_pairs={{0,1},{1,2},{2,3},{3,0},{4,5},{5,6},{6,7},{7,4},{8,9},{9,10},{10,1... | collective-permute-start | bytes 350216 | tf_op jit(solution)/shard_map/ppermute | solution.py:260
  427.5 10.8 %all-to-all-start.1 = ((f32[32,1,128]{2,1,0:T(1,128)}), f32[32,1,128]{2,1,0:T(1,128)S(1)}, u32[]{:S(2)}, u32[]{:S(2)}) async-start(f32[32,1,128]{2,1,0:T(1,128)} %broadcast_in_dim.48), calls=%async_computation.1 | async-start | bytes 32768 | tf_op jit(solution)/shard_map/all_to_all | solution.py:280
  (68 other events, 608.3 us)
Sparse Core Ops, SparseCore 0:
  55.4 52.1 all-gather.2
  148.9 22.1 all-gather.4

commit v5 on v4

--- a/solution.py
+++ b/solution.py
@@ -173,6 +173,8 @@
 
 
 def packed(arrays, exact):
+    if exact == (None,):
+        return arrays[0]
     pieces = []
     for array, whole in zip(arrays, exact):
         pieces += split_low(array) if whole else [array.astype(LOW)]
@@ -204,7 +206,7 @@
     if not staged_mesh():
         return arrays
     sends = [core_blocks(array, True) for array in arrays]
-    return [a if whole else a.astype(LOW) for a, whole in zip(sends, exact)]
+    return [a.astype(LOW) if whole is False else a for a, whole in zip(sends, exact)]
 
 
 def scatter_quad(arrays, sends, *others):
@@ -274,10 +276,10 @@
     return total
 
 
-def sum_everywhere(value):
+def everywhere(value):
     count = lax.axis_size(("pb", "pa"))
     copies = jnp.broadcast_to(value[None], (count,) + value.shape)
-    return jnp.sum(lax.all_to_all(copies, ("pb", "pa"), 0, 0), 0)
+    return lax.all_to_all(copies, ("pb", "pa"), 0, 0)
 
 
 ACROSS = (((1,), (1,)), ((), ()))
@@ -374,28 +376,37 @@
     )(*arguments)
 
 
+def row_parts(ref):
+    return [slice(at, at + 128) for at in range(0, ref.shape[0], 128)]
+
+
 def widen_kernel(x_ref, att_ref, out_w, up_w, vec, resid_ref, low_ref, act_ref, slope_ref):
-    resid = x_ref[...].astype(F32) + dot(att_ref[...], out_w[...]) + vec[2:3]
-    resid_ref[...] = resid
-    low = (standard(resid)[0] * vec[3:4] + vec[4:5]).astype(LOW)
-    low_ref[...] = low
+    lows = []
+    for part in row_parts(x_ref):
+        resid = x_ref[part, :].astype(F32) + dot(att_ref[part, :], out_w[...]) + vec[2:3]
+        resid_ref[part, :] = resid
+        lows.append((standard(resid)[0] * vec[3:4] + vec[4:5]).astype(LOW))
+        low_ref[part, :] = lows[-1]
     for row in range(4):
-        part = slice(row * D, row * D + D)
-        value, slope = gelu_with_slope(dot(low, up_w[:, part]) + vec[5 + row : 6 + row])
-        act_ref[:, part] = value.astype(LOW)
-        slope_ref[:, part] = slope.astype(LOW)
+        cols = slice(row * D, row * D + D)
+        for part, low in zip(row_parts(x_ref), lows):
+            value, slope = gelu_with_slope(dot(low, up_w[:, cols]) + vec[5 + row : 6 + row])
+            act_ref[part, cols] = value.astype(LOW)
+            slope_ref[part, cols] = slope.astype(LOW)
 
 
 def narrow_kernel(act_ref, resid_ref, down_w, proj_w, vec, two_ref, low_ref, proj_ref, unit_ref):
-    normed = standard(resid_ref[...])[0] * vec[3:4] + vec[4:5]
-    two = normed + dot(act_ref[...], down_w[...]) + vec[9:10]
-    two_ref[...] = two
-    low = (standard(two)[0] * vec[10:11] + vec[11:12]).astype(LOW)
-    low_ref[...] = low
-    projected = dot(low, proj_w[...])
-    proj_ref[...] = projected
-    square = jnp.sum(projected * projected, -1, keepdims=True) + 1e-06
-    unit_ref[...] = (projected * lax.rsqrt(square)).astype(LOW)
+    branches = [dot(act_ref[part, :], down_w[...]) for part in row_parts(act_ref)]
+    for part, branch in zip(row_parts(act_ref), branches):
+        normed = standard(resid_ref[part, :])[0] * vec[3:4] + vec[4:5]
+        two = normed + branch + vec[9:10]
+        two_ref[part, :] = two
+        low = (standard(two)[0] * vec[10:11] + vec[11:12]).astype(LOW)
+        low_ref[part, :] = low
+        projected = dot(low, proj_w[...])
+        proj_ref[part, :] = projected
+        square = jnp.sum(projected * projected, -1, keepdims=True) + 1e-06
+        unit_ref[part, :] = (projected * lax.rsqrt(square)).astype(LOW)
 
 
 def back_kernel(
@@ -817,14 +828,36 @@
     return (jnp.exp(scores) / partition[:, None] - onehot) / query_total
 
 
-def adam_update(weight, moment_one, moment_two, gradient, factor, rate):
-    clipped = gradient * factor
-    new_one = beta_one * moment_one + (1.0 - beta_one) * clipped
-    new_two = beta_two * moment_two + (1.0 - beta_two) * clipped * clipped
-    direction = (
-        new_one / (1.0 - beta_one**STEP) / (jnp.sqrt(new_two / (1.0 - beta_two**STEP)) + adam_eps)
-    )
-    return (weight - rate * (direction + decay_rate * weight), new_one, new_two)
+def adam_kernel(square_ref, *refs):
+    count = 6
+    given, (norm_ref, *results) = refs[: 4 * count], refs[4 * count :]
+    norm = jnp.sqrt(jnp.sum(square_ref[...], 0, keepdims=True)[:, 0:1])
+    norm_ref[...] = jnp.broadcast_to(norm, norm_ref.shape)
+    factor = jnp.minimum(1.0, clip_max / (norm + 1e-06))
+    for number in range(count):
+        weight, first, second, gradient = (r[...] for r in given[4 * number : 4 * number + 4])
+        rate = vector_rate if number == count - 1 else learn_rate
+        clipped = gradient * factor
+        new_first = beta_one * first + (1.0 - beta_one) * clipped
+        new_second = beta_two * second + (1.0 - beta_two) * clipped * clipped
+        spread = jnp.sqrt(new_second / (1.0 - beta_two**STEP)) + adam_eps
+        direction = new_first / (1.0 - beta_one**STEP) / spread
+        results[3 * number][...] = weight - rate * (direction + decay_rate * weight)
+        results[3 * number + 1][...] = new_first
+        results[3 * number + 2][...] = new_second
+
+
+def adam_updates(squares, groups):
+    inputs = [squares] + [array for group in groups for array in group]
+    shapes = [(1, 128)] + [group[0].shape for group in groups for _ in range(3)]
+    return pl.pallas_call(
+        adam_kernel,
+        grid=(1,),
+        in_specs=[pl.BlockSpec(a.shape, lambda i: (0, 0)) for a in inputs],
+        out_specs=[pl.BlockSpec(shape, lambda i: (0, 0)) for shape in shapes],
+        out_shape=[jax.ShapeDtypeStruct(shape, F32) for shape in shapes],
+        compiler_params=pltpu.CompilerParams(vmem_limit_bytes=58 << 20),
+    )(*inputs)
 
 
 def body(
@@ -945,19 +978,19 @@
     narrower = narrow(FEED_ROWS, 0, BIN // FEED_ROWS, wider, narrower)
     resid, normed, active, slope = wider
     two, normed_out, projected, unit = narrower
-    passage_unit = unit[:BIN]
+    passage_unit = unit
 
     passage_ids = own_index * PPB + jnp.arange(PPB, dtype=jnp.int32)
     scores, totals, score_terms = score_forward(every_query, passage_unit, member)
     scores = scores[:, :PPB]
     turned = transposed(gate(tokens, scores))
-    partition = gate(sum_everywhere(jnp.sum(jnp.exp(scores), 1)), turned)
+    partition = gate(jnp.sum(everywhere(jnp.sum(jnp.exp(scores), 1)), 0), turned)
     grad_scores = cross_grad(scores, partition, passage_ids, positives, query_total)
     grad_scores = jnp.tile(jnp.pad(grad_scores, ((0, 0), (0, 64 - PPB))), (1, 2))
     grad_every = score_backward(
         score_query_kernel, score_terms, passage_unit, member, grad_scores, totals
     )
-    whole, rounded = (True,), (False,)
+    whole, rounded = (None,), (False,)
     query_back = scatter_quad([grad_every], scatter_sends([grad_every], whole))
     grad_passage = score_backward(
         score_passage_kernel,
@@ -1043,38 +1076,16 @@
     qkv_sum, vector_sum, square = finish(
         scatter_line(first_back, kinds), (out_sum, up_sum, down_sum, proj_sum)
     )
-    reduced = (qkv_sum, out_sum, up_sum, down_sum, proj_sum, vector_sum[:, :12].T)
-    norm_value = jnp.sqrt(sum_everywhere(square)[0, 0])
-    factor = jnp.minimum(1.0, clip_max / (norm_value + 1e-06))
-    qkv_res = adam_update(qkv_weight, qkv_first, qkv_second, reduced[0], factor, learn_rate)
-    out_res = adam_update(out_weight, out_first, out_second, reduced[1], factor, learn_rate)
-    up_res = adam_update(up_weight, up_first, up_second, reduced[2], factor, learn_rate)
-    down_res = adam_update(down_weight, down_first, down_second, reduced[3], factor, learn_rate)
-    proj_res = adam_update(proj_weight, proj_first, proj_second, reduced[4], factor, learn_rate)
-    vector_res = adam_update(
-        vector_params, vector_first, vector_second, reduced[5], factor, vector_rate
-    )
-    return (
-        norm_value,
-        qkv_res[0],
-        qkv_res[1],
-        qkv_res[2],
-        out_res[0],
-        out_res[1],
-        out_res[2],
-        up_res[0],
-        up_res[1],
-        up_res[2],
-        down_res[0],
-        down_res[1],
-        down_res[2],
-        proj_res[0],
-        proj_res[1],
-        proj_res[2],
-        vector_res[0],
-        vector_res[1],
-        vector_res[2],
-    )
+    groups = (
+        (qkv_weight, qkv_first, qkv_second, qkv_sum),
+        (out_weight, out_first, out_second, out_sum),
+        (up_weight, up_first, up_second, up_sum),
+        (down_weight, down_first, down_second, down_sum),
+        (proj_weight, proj_first, proj_second, proj_sum),
+        (vector_params, vector_first, vector_second, vector_sum[:, :12].T),
+    )
+    norm, *results = adam_updates(everywhere(square)[:, 0], groups)
+    return (norm[0, 0], *results)
 
 
 def solution(mesh):

time: 459 us -> 455 us (level)
  other arithmetic: 36.9 us -> 27.9 us
    unnamed x140 -> x112, local copies, waits for them, and re-layouts: 25 us -> 27.9 us
  transfers between devices with their start and end apart: 51 -> 51, of which waited for: 24 -> 25; matrix products, arithmetic and copies ran while one was open for 12% -> 11% of each run, Pallas kernels for 31% -> 31%
where the time goes in v5:
time: 455 us; the launch traced here: 450 us
  Pallas kernels  175 us (38%)
  waiting for transfers between devices  87.3 us (19%)
  starting transfers between devices  70.2 us (15%)
  local copies, waits for them, and re-layouts  38.6 us (8%)
  matrix products  35.7 us (8%)
  other arithmetic  27.9 us (6%)
  between operations  15.9 us (3%)
    pallas_call x6, Pallas kernels, row_call(): pl.pallas_call(run, grid=(count,), in_specs=in_specs, out_specs=[rows_at(...  71.2 us
    pallas_call x7, Pallas kernels, attend_call(): pl.pallas_call(run, out_shape=[shape for shape, _ in outputs], grid_spec=...  66.1 us
    dot_general x9, matrix products, dot(): return lax.dot_general(left, right, dims, preferred_element_type=F32)  35.7 us
    unnamed x112, local copies, waits for them, and re-layouts  27.9 us
    ppermute x12, starting transfers between devices, send_line(): return [lax.ppermute(part, 'pa', shift_pairs(k)) for k in (1, 2, 3)]  23.7 us
    ppermute x12, waiting for transfers between devices, last_moves(): lax.ppermute(s, 'pa', shift_pairs(k + 1))  23.5 us
    pallas_call x3, Pallas kernels, score_call(): pl.pallas_call(kernel, grid=(inputs[0].shape[0] // SCORE_ROWS,), in_specs...  19.3 us
    ppermute x12, starting transfers between devices, last_moves(): lax.ppermute(s, 'pa', shift_pairs(k + 1))  18 us
  transfers between devices with their start and end apart: 51, of which 25 were waited for; matrix products, arithmetic and copies ran while one was open for 11% of the time, Pallas kernels for 31%

profile of v5, /device:TPU:0, one launch (start us, length us, event | category | flops | bytes accessed | tf_op | source)
XLA Modules:
  0.0 450.1 jit_solution(17342040339092034252)
XLA Ops:
  9.1 4.1 collective-permute-start.1
  17.0 5.2 %collective-permute-done.1 = bf16[24,2432]{1,0:T(8,128)(2,1)S(1)} collective-permute-done((bf16[24,2432]{1,0:T(8,128)(2,1)S(1)}, bf16[24,2432]{1,0:T(8,128)(2,1)S(1)}, u32[]{:S(2)}, u32[]{:S(2)}) %collective-permute-start.1) | collective-permute-done | bytes 116768 | tf_op jit(solution)/shard_map/ppermute | solution.py:107
  39.3 7.5 %collective-permute-done.4.refs_1_ = bf16[2,96,2432]{2,1,0:T(8,128)(2,1)S(1)} collective-permute-done((bf16[2,96,2432]{2,1,0:T(8,128)(2,1)S(1)}, bf16[2,96,2432]{2,1,0:T(8,128)(2,1)S(1)}, u32[]{:S(2)}, u32[]{:S(2)}) %collective-permute-start.4) | collective-permute-done | bytes 933920 | tf_op jit(solution)/shard_map/ppermute | solution.py:141
  54.9 3.8 collective-permute-done.5.refs_1_
  61.8 3.2 fusion.1.refs_1_.refs_2_.refs_3_
  70.7 7.3 %add_convert_fusion.refs_1_.refs_2_.refs_3_ = bf16[1024,2304]{1,0:T(8,128)(2,1)} fusion(bf16[1024,768]{1,0:T(8,128)(2,1)} %bitcast.345, bf16[768,2304]{1,0:T(8,128)(2,1)S(1)} %bitcast.322, f32[2304]{0:T(1024)S(1)} %pad_maximum_fusion.18), kind=kOutput, calls=%fused_computation | convolution fusion | flops 3628597248 | bytes 9839616 | tf_op jit(solution)/shard_map/dot_general | solution.py:290
  78.0 4.2 collective-permute-done.7
  84.0 3.8 shard_map.396
  87.7 11.3 %shard_map.397 = (bf16[1152,768]{1,0:T(8,128)(2,1)S(1)}, f32[6,8,1024]{2,1,0:T(8,128)S(1)}) custom-call(s32[4,2]{1,0:T(4,128)S(1)} %pad_add_fusion.refs_0_, bf16[1024,2304]{1,0:T(8,128)(2,1)} %add_convert_fusion.refs_1_.refs_2_.refs_3_, bf16[1024,2304]{1,0:T(8,128)(2,1)} %add_convert_fusion.refs_1_.refs_2_.refs_3_, ...), custom_call_target="tpu_custom_call", output_to_operand_aliasing={{0}: (6, {})} | custom-call | flops 16106127360 | bytes 3145728 | tf_op jit(solution)/shard_map/pallas_call | solution.py:519
  99.1 5.8 %collective-permute-done.9.refs_1_ = bf16[384,768]{1,0:T(8,128)(2,1)S(1)} collective-permute-done((bf16[384,768]{1,0:T(8,128)(2,1)S(1)}, bf16[384,768]{1,0:T(8,128)(2,1)S(1)}, u32[]{:S(2)}, u32[]{:S(2)}) %collective-permute-start.9) | collective-permute-done | bytes 589856 | tf_op jit(solution)/shard_map/ppermute | solution.py:135
  107.3 11.3 %shard_map.399 = (bf16[1152,768]{1,0:T(8,128)(2,1)S(1)}, f32[6,8,1024]{2,1,0:T(8,128)S(1)}) custom-call(s32[4,2]{1,0:T(4,128)S(1)} %pad_add_fusion.refs_0_, bf16[1024,2304]{1,0:T(8,128)(2,1)} %add_convert_fusion.refs_1_.refs_2_.refs_3_, bf16[1024,2304]{1,0:T(8,128)(2,1)} %add_convert_fusion.refs_1_.refs_2_.refs_3_, ...), custom_call_target="tpu_custom_call", output_to_operand_aliasing={{0}: (6, {}), {1}: (7, {})} | custom-call | flops 16106127360 | bytes 3145728 | tf_op jit(solution)/shard_map/pallas_call | solution.py:519
  118.6 3.4 collective-permute-done.10.refs_1_
  123.1 5.8 %shard_map.401 = (f32[1152,768]{1,0:T(8,128)}, bf16[1152,768]{1,0:T(8,128)(2,1)}, bf16[1152,3072]{1,0:T(8,128)(2,1)}, bf16[1152,3072]{1,0:T(8,128)(2,1)}) custom-call(bf16[1152,768]{1,0:T(8,128)(2,1)} %pad_maximum_fusion.refs_0_.x_ref, bf16[1152,768]{1,0:T(8,128)(2,1)} %copy-done.5, ...), custom_call_target="tpu_custom_call" | custom-call | flops 754974720 | bytes 14782464 | tf_op jit(solution)/shard_map/pallas_call | solution.py:364
  134.1 4.8 %shard_map.403 = (f32[1152,768]{1,0:T(8,128)}, bf16[1152,768]{1,0:T(8,128)(2,1)}, f32[1152,128]{1,0:T(8,128)}, bf16[1152,128]{1,0:T(8,128)(2,1)}) custom-call(bf16[1152,3072]{1,0:T(8,128)(2,1)} %get-tuple-element.174.refs_0_.refs_7_, f32[1152,768]{1,0:T(8,128)} %get-tuple-element.172.refs_1_.refs_5_, bf16[3072,768]{1,0:T(8,128)(2,1)} %bitcast.315, ...), custom_call_target="tpu_custom_call" | custom-call | flops 603979776 | bytes 12718080 | tf_op jit(solution)/shard_map/pallas_call | solution.py:364
  140.3 3.8 collective-permute-start.15
  147.5 15.9 %shard_map.404 = (f32[1152,768]{1,0:T(8,128)}, bf16[1152,768]{1,0:T(8,128)(2,1)}, bf16[1152,3072]{1,0:T(8,128)(2,1)}, bf16[1152,3072]{1,0:T(8,128)(2,1)}) custom-call(bf16[1152,768]{1,0:T(8,128)(2,1)} %pad_maximum_fusion.refs_0_.x_ref, bf16[1152,768]{1,0:T(8,128)(2,1)} %copy-done.5, ...), custom_call_target="tpu_custom_call", output_to_operand_aliasing={{0}: (5, {}), {1}: (6, {}), {2}: (7, {}), {3}: (8, {})} | custom-call | flops 6039797760 | bytes 32673792 | tf_op jit(solution)/shard_map/pallas_call | solution.py:364
  163.4 12.2 %shard_map.405 = (f32[1152,768]{1,0:T(8,128)}, bf16[1152,768]{1,0:T(8,128)(2,1)}, f32[1152,128]{1,0:T(8,128)}, bf16[1152,128]{1,0:T(8,128)(2,1)}) custom-call(bf16[1152,3072]{1,0:T(8,128)(2,1)} %get-tuple-element.176.refs_0_, ...), custom_call_target="tpu_custom_call", output_to_operand_aliasing={{0}: (5, {}), {1}: (6, {}), {2}: (7, {}), {3}: (8, {})} | custom-call | flops 4831838208 | bytes 25792512 | tf_op jit(solution)/shard_map/pallas_call | solution.py:364
  177.8 5.6 %shard_map.406 = (f32[128,128]{1,0:T(8,128)S(1)}, f32[4096,128]{1,0:T(8,128)S(1)}, bf16[4096,1024]{1,0:T(8,128)(2,1)S(1)}) custom-call(bf16[4096,128]{1,0:T(8,128)(2,1)S(1)} %copy-done.26, bf16[1152,128]{1,0:T(8,128)(2,1)S(1)} %copy-done.15, bf16[1024,128]{1,0:T(8,128)(2,1)S(1)} %compare_convert_fusion.member_ref), custom_call_target="tpu_custom_call" | custom-call | flops 3221225472 | bytes 4194304 | tf_op jit(solution)/shard_map/pallas_call | solution.py:729
  183.4 3.3 copy-done.3
  188.7 6.7 %all-to-all-start = ((f32[32,1,128]{2,1,0:T(1,128)}), f32[32,1,128]{2,1,0:T(1,128)S(1)}, u32[]{:S(2)}, u32[]{:S(2)}) async-start(f32[32,1,128]{2,1,0:T(1,128)} %broadcast_in_dim.46), calls=%async_computation | async-start | bytes 32768 | tf_op jit(solution)/shard_map/all_to_all | solution.py:282
  195.5 5.0 %shard_map.407 = bf16[768,1152]{1,0:T(8,128)(2,1)} custom-call(bf16[1152,768]{1,0:T(8,128)(2,1)} %pad_maximum_fusion.refs_0_.x_ref), custom_call_target="tpu_custom_call" | custom-call | tf_op jit(solution)/shard_map/pallas_call | solution.py:324
  202.9 3.4 copy-done.4
  207.9 5.5 %shard_map.408 = f32[4096,128]{1,0:T(8,128)S(1)} custom-call(bf16[4096,1024]{1,0:T(8,128)(2,1)S(1)} %copy-done.4, bf16[1152,128]{1,0:T(8,128)(2,1)S(1)} %copy-done.16, bf16[1024,128]{1,0:T(8,128)(2,1)S(1)} %compare_convert_fusion.member_ref, f32[128,128]{1,0:T(8,128)S(1)} %copy.197.grad_ref, f32[4096,128]{1,0:T(8,128)S(1)} %copy-done.12), custom_call_target="tpu_custom_call" | custom-call | flops 3221225472 | bytes 4194304 | tf_op jit(solution)/shard_map/pallas_call | solution.py:729
  214.4 3.0 collective-permute-done.18
  222.3 8.3 %shard_map.409.refs_0_ = f32[1024,128]{1,0:T(8,128)S(1)} custom-call(bf16[4096,128]{1,0:T(8,128)(2,1)S(1)} %copy-done.27, bf16[1152,128]{1,0:T(8,128)(2,1)S(1)} %copy-done.16, bf16[1024,128]{1,0:T(8,128)(2,1)S(1)} %compare_convert_fusion.member_ref, f32[128,128]{1,0:T(8,128)S(1)} %copy.197.grad_ref, f32[4096,128]{1,0:T(8,128)S(1)} %copy-done.13), custom_call_target="tpu_custom_call" | custom-call | flops 3221225472 | bytes 4194304 | tf_op jit(solution)/shard_map/pallas_call | solution.py:729
  233.3 23.1 %shard_map.410 = (bf16[1152,128]{1,0:T(8,128)(2,1)}, bf16[1152,768]{1,0:T(8,128)(2,1)}, bf16[1152,3072]{1,0:T(8,128)(2,1)}, bf16[1152,768]{1,0:T(8,128)(2,1)}, b...) custom-call(f32[1024,128]{1,0:T(8,128)} %copy-done.28, f32[1152,128]{1,0:T(8,128)} %get-tuple-element.187.refs_1_, ...), custom_call_target="tpu_custom_call" | custom-call | flops 10871635968 | bytes 47943680 | tf_op jit(solution)/shard_map/pallas_call | solution.py:364
  263.4 3.0 collective-permute-done.22
  267.1 9.5 %shard_map.411 = (bf16[1152,128]{1,0:T(8,128)(2,1)}, bf16[1152,768]{1,0:T(8,128)(2,1)}, bf16[1152,3072]{1,0:T(8,128)(2,1)}, bf16[1152,768]{1,0:T(8,128)(2,1)}, b...) custom-call(f32[128,128]{1,0:T(8,128)} %fusion.44.refs_0_, ...), custom_call_target="tpu_custom_call", output_to_operand_aliasing={{0}: (10, {}), {1}: (11, {}), {2}: (12, {}), {3}: (13, {}),... | custom-call | flops 1358954496 | bytes 26152960 | tf_op jit(solution)/shard_map/pallas_call | solution.py:364
  276.6 9.5 %convolution_convert_fusion.1 = bf16[3072,768]{1,0:T(8,128)(2,1)S(1)} fusion(bf16[1152,3072]{1,0:T(8,128)(2,1)} %get-tuple-element.176.refs_0_, bf16[1152,768]{1,0:T(8,128)(2,1)} %get-tuple-element.198), kind=kOutput, calls=%fused_computation.2 | convolution fusion | flops 5438177280 | bytes 13565952 | tf_op jit(solution)/shard_map/dot_general | solution.py:290
  287.6 6.7 %convolution_convert_fusion = bf16[768,3072]{1,0:T(8,128)(2,1)S(1)} fusion(bf16[1152,768]{1,0:T(8,128)(2,1)S(1)} %copy-done.35, bf16[1152,3072]{1,0:T(8,128)(2,1)S(1)} %copy-done.30), kind=kOutput, calls=%fused_computation.1 | convolution fusion | flops 5438177280 | bytes 13565952 | tf_op jit(solution)/shard_map/dot_general | solution.py:290
  303.9 5.3 %shard_map.412 = (bf16[3,1152,768]{2,1,0:T(8,128)(2,1)}, f32[16,768]{1,0:T(8,128)S(1)}) custom-call(s32[1,2]{1,0:T(1,128)S(1)} %broadcast_11_refs_0_.2.refs_0_, bf16[128,2304]{1,0:T(8,128)(2,1)S(1)} %copy-done.23, bf16[128,2304]{1,0:T(8,128)(2,1)S(1)} %copy-done.23, bf16[128,2304]{1,0:T(8,128)(2,1)S(1)} %copy-done.23, bf16[1152,768]{1,0:T(8,128)(2,1)S(1)} %copy-done.14, ...), custom_call_target="tpu_custom_call" | custom-call | flops 1006632960 | bytes 786432 | tf_op jit(solution)/shard_map/pallas_call | solution.py:519
  309.4 3.2 convert_add_fusion.1
  314.7 4.6 %collective-permute-done.29 = bf16[2,384,768]{2,1,0:T(8,128)(2,1)} collective-permute-done((bf16[2,384,768]{2,1,0:T(8,128)(2,1)S(1)}, bf16[2,384,768]{2,1,0:T(8,128)(2,1)}, u32[]{:S(2)}, u32[]{:S(2)}) %collective-permute-start.29) | collective-permute-done | bytes 1179680 | tf_op jit(solution)/shard_map/ppermute | solution.py:243
  322.0 11.3 %shard_map.413 = (bf16[3,1152,768]{2,1,0:T(8,128)(2,1)}, f32[16,768]{1,0:T(8,128)S(1)}) custom-call(s32[4,2]{1,0:T(4,128)S(1)} %pad_add_fusion.refs_0_, bf16[1024,2304]{1,0:T(8,128)(2,1)} %add_convert_fusion.refs_1_.refs_2_.refs_3_, bf16[1024,2304]{1,0:T(8,128)(2,1)} %add_convert_fusion.refs_1_.refs_2_.refs_3_, ...), custom_call_target="tpu_custom_call", output_to_operand_aliasing={{0}: (8, {})} | custom-call | flops 21474836480 | bytes 2097152 | tf_op jit(solution)/shard_map/pallas_call | solution.py:519
  333.3 4.1 collective-permute-done.30
  337.7 3.8 collective-permute-start.33
  341.5 11.7 %shard_map.414 = (bf16[3,1152,768]{2,1,0:T(8,128)(2,1)}, f32[16,768]{1,0:T(8,128)S(1)}) custom-call(s32[4,2]{1,0:T(4,128)S(1)} %pad_add_fusion.refs_0_, bf16[1024,2304]{1,0:T(8,128)(2,1)} %add_convert_fusion.refs_1_.refs_2_.refs_3_, bf16[1024,2304]{1,0:T(8,128)(2,1)} %add_convert_fusion.refs_1_.refs_2_.refs_3_, ...), custom_call_target="tpu_custom_call", output_to_operand_aliasing={{0}: (8, {}), {1}: (9, {})} | custom-call | flops 21474836480 | bytes 2097152 | tf_op jit(solution)/shard_map/pallas_call | solution.py:519
  355.2 3.0 collective-permute-start.34
  358.2 11.6 %shard_map.415 = (bf16[3,1152,768]{2,1,0:T(8,128)(2,1)}, f32[16,768]{1,0:T(8,128)S(1)}) custom-call(s32[4,2]{1,0:T(4,128)S(1)} %pad_add_fusion.refs_0_, bf16[1024,2304]{1,0:T(8,128)(2,1)} %add_convert_fusion.refs_1_.refs_2_.refs_3_, bf16[1024,2304]{1,0:T(8,128)(2,1)} %add_convert_fusion.refs_1_.refs_2_.refs_3_, ...), custom_call_target="tpu_custom_call", output_to_operand_aliasing={{0}: (8, {}), {1}: (9, {})} | custom-call | flops 21474836480 | bytes 2097152 | tf_op jit(solution)/shard_map/pallas_call | solution.py:519
  375.9 3.3 fusion.17
  382.8 4.5 collective-permute-start.41
  392.2 4.3 collective-permute-done.41
  396.5 7.2 %collective-permute-done.42 = bf16[24,4096]{1,0:T(8,128)(2,1)S(1)} collective-permute-done((bf16[24,4096]{1,0:T(8,128)(2,1)S(1)}, bf16[24,4096]{1,0:T(8,128)(2,1)S(1)}, u32[]{:S(2)}, u32[]{:S(2)}) %collective-permute-start.42) | collective-permute-done | bytes 196640 | tf_op jit(solution)/shard_map/ppermute | solution.py:262
  407.0 7.3 %collective-permute-done.43 = bf16[96,2432]{1,0:T(8,128)(2,1)S(1)} collective-permute-done((bf16[96,2432]{1,0:T(8,128)(2,1)S(1)}, bf16[96,2432]{1,0:T(8,128)(2,1)S(1)}, u32[]{:S(2)}, u32[]{:S(2)}) %collective-permute-start.43) | collective-permute-done | bytes 466976 | tf_op jit(solution)/shard_map/ppermute | solution.py:252
  418.7 4.0 collective-permute-done.44.refs_4_
  427.3 3.8 all-to-all-start.1
  431.8 6.4 %all-to-all-done.1 = f32[32,1,128]{2,1,0:T(1,128)S(1)} async-done(((f32[32,1,128]{2,1,0:T(1,128)}), f32[32,1,128]{2,1,0:T(1,128)S(1)}, u32[]{:S(2)}, u32[]{:S(2)}) %all-to-all-start.1) | async-done | bytes 16416 | tf_op jit(solution)/shard_map/all_to_all | solution.py:282
  438.8 4.2 shard_map.417
  (348 shorter events, 125.0 us)
Async XLA Ops:
  7.2 115.9 %all-gather.3.cloned.1.call-start = ((), (), s32[]{:S(2)}) async-start(), calls=%async_computation.2 | async-start | bytes 6856704 | tf_op jit(solution)/shard_map/all_gather | solution.py:120
  9.1 13.2 %collective-permute-start.1 = (bf16[24,2432]{1,0:T(8,128)(2,1)S(1)}, bf16[24,2432]{1,0:T(8,128)(2,1)S(1)}, u32[]{:S(2)}, u32[]{:S(2)}) collective-permute-start(bf16[24,2432]{1,0:T(8,128)(2,1)S(1)} %fusion.37), channel_id=1, source_target_pairs={{0,2},{1,3},{2,0},{3,1},{4,6},{5,7},{6,4},{7,5},{8,10},{9,11},{10,... | collective-permute-start | bytes 350216 | tf_op jit(solution)/shard_map/ppermute | solution.py:107
  13.2 9.1 %collective-permute-start.2 = (bf16[24,2432]{1,0:T(8,128)(2,1)S(1)}, bf16[24,2432]{1,0:T(8,128)(2,1)S(1)}, u32[]{:S(2)}, u32[]{:S(2)}) collective-permute-start(bf16[24,2432]{1,0:T(8,128)(2,1)S(1)} %fusion.37), channel_id=1, source_target_pairs={{0,1},{1,2},{2,3},{3,0},{4,5},{5,6},{6,7},{7,4},{8,9},{9,10},{10,1... | collective-permute-start | bytes 350216 | tf_op jit(solution)/shard_map/ppermute | solution.py:107
  14.8 8.2 %collective-permute-start = (bf16[24,2432]{1,0:T(8,128)(2,1)S(1)}, bf16[24,2432]{1,0:T(8,128)(2,1)S(1)}, u32[]{:S(2)}, u32[]{:S(2)}) collective-permute-start(bf16[24,2432]{1,0:T(8,128)(2,1)S(1)} %fusion.37), channel_id=1, source_target_pairs={{0,3},{1,0},{2,1},{3,2},{4,7},{5,4},{6,5},{7,6},{8,11},{9,8},{10,9... | collective-permute-start | bytes 350216 | tf_op jit(solution)/shard_map/ppermute | solution.py:107
  23.3 8.6 %collective-permute-start.3 = (bf16[96,2432]{1,0:T(8,128)(2,1)S(1)}, bf16[96,2432]{1,0:T(8,128)(2,1)S(1)}, u32[]{:S(2)}, u32[]{:S(2)}) collective-permute-start(bf16[96,2432]{1,0:T(8,128)(2,1)S(1)} %bitcast.325), channel_id=1, source_target_pairs={{0,8},{4,20},{8,0},{12,28},{16,24},{20,4},{24,16},{28,12},{1,9},{5... | collective-permute-start | bytes 1400840 | tf_op jit(solution)/shard_map/ppermute | solution.py:135
  25.8 25.3 %collective-permute-start.13 = (bf16[24,3968]{1,0:T(8,128)(2,1)}, bf16[24,3968]{1,0:T(8,128)(2,1)}, u32[]{:S(2)}, u32[]{:S(2)}) collective-permute-start(bf16[24,3968]{1,0:T(8,128)(2,1)} %pad_maximum_fusion.12), channel_id=1, source_target_pairs={{0,3},{1,0},{2,1},{3,2},{4,7},{5,4},{6,5},{7,6},{8,11},{9,8},{10,9... | collective-permute-start | bytes 571400 | tf_op jit(solution)/shard_map/ppermute | solution.py:107
  27.8 23.4 %collective-permute-start.12 = (bf16[24,3968]{1,0:T(8,128)(2,1)}, bf16[24,3968]{1,0:T(8,128)(2,1)}, u32[]{:S(2)}, u32[]{:S(2)}) collective-permute-start(bf16[24,3968]{1,0:T(8,128)(2,1)} %pad_maximum_fusion.12), channel_id=1, source_target_pairs={{0,2},{1,3},{2,0},{3,1},{4,6},{5,7},{6,4},{7,5},{8,10},{9,11},{10,... | collective-permute-start | bytes 571400 | tf_op jit(solution)/shard_map/ppermute | solution.py:107
  29.3 21.9 %collective-permute-start.11 = (bf16[24,3968]{1,0:T(8,128)(2,1)}, bf16[24,3968]{1,0:T(8,128)(2,1)}, u32[]{:S(2)}, u32[]{:S(2)}) collective-permute-start(bf16[24,3968]{1,0:T(8,128)(2,1)} %pad_maximum_fusion.12), channel_id=1, source_target_pairs={{0,1},{1,2},{2,3},{3,0},{4,5},{5,6},{6,7},{7,4},{8,9},{9,10},{10,1... | collective-permute-start | bytes 571400 | tf_op jit(solution)/shard_map/ppermute | solution.py:107
  33.1 13.6 %collective-permute-start.4 = (bf16[2,96,2432]{2,1,0:T(8,128)(2,1)S(1)}, bf16[2,96,2432]{2,1,0:T(8,128)(2,1)S(1)}, u32[]{:S(2)}, u32[]{:S(2)}) collective-permute-start(bf16[2,96,2432]{2,1,0:T(8,128)(2,1)S(1)} %shard_map.393.refs_0_), channel_id=1, source_target_pairs={{0,16},{4,12},{8,24},{12,4},{16,0},{20,28},{24,8},{28,20},{1,17},{... | collective-permute-start | bytes 2801672 | tf_op jit(solution)/shard_map/ppermute | solution.py:141
  54.8 120.8 %all-gather.5.cloned.1.call-start = ((), (), s32[]{:S(2)}) async-start(), calls=%async_computation.3 | async-start | bytes 1179648 | tf_op jit(solution)/shard_map/all_gather | solution.py:120
  54.8 3.9 collective-permute-start.5
  65.0 13.0 %collective-permute-start.8 = (bf16[96,768]{1,0:T(8,128)(2,1)S(1)}, bf16[96,768]{1,0:T(8,128)(2,1)S(1)}, u32[]{:S(2)}, u32[]{:S(2)}) collective-permute-start(bf16[96,768]{1,0:T(8,128)(2,1)S(1)} %convert_element_type.442), channel_id=1, source_target_pairs={{0,3},{1,0},{2,1},{3,2},{4,7},{5,4},{6,5},{7,6},{8,11},{9,8},{10,9... | collective-permute-start | bytes 442376 | tf_op jit(solution)/shard_map/ppermute | solution.py:107
  66.7 15.4 %collective-permute-start.7 = (bf16[96,768]{1,0:T(8,128)(2,1)S(1)}, bf16[96,768]{1,0:T(8,128)(2,1)S(1)}, u32[]{:S(2)}, u32[]{:S(2)}) collective-permute-start(bf16[96,768]{1,0:T(8,128)(2,1)S(1)} %convert_element_type.442), channel_id=1, source_target_pairs={{0,2},{1,3},{2,0},{3,1},{4,6},{5,7},{6,4},{7,5},{8,10},{9,11},{10,... | collective-permute-start | bytes 442376 | tf_op jit(solution)/shard_map/ppermute | solution.py:107
  68.6 13.6 %collective-permute-start.6 = (bf16[96,768]{1,0:T(8,128)(2,1)S(1)}, bf16[96,768]{1,0:T(8,128)(2,1)S(1)}, u32[]{:S(2)}, u32[]{:S(2)}) collective-permute-start(bf16[96,768]{1,0:T(8,128)(2,1)S(1)} %convert_element_type.442), channel_id=1, source_target_pairs={{0,1},{1,2},{2,3},{3,0},{4,5},{5,6},{6,7},{7,4},{8,9},{9,10},{10,1... | collective-permute-start | bytes 442376 | tf_op jit(solution)/shard_map/ppermute | solution.py:107
  82.3 22.6 %collective-permute-start.9 = (bf16[384,768]{1,0:T(8,128)(2,1)S(1)}, bf16[384,768]{1,0:T(8,128)(2,1)S(1)}, u32[]{:S(2)}, u32[]{:S(2)}) collective-permute-start(bf16[384,768]{1,0:T(8,128)(2,1)S(1)} %bitcast.323), channel_id=1, source_target_pairs={{0,8},{4,20},{8,0},{12,28},{16,24},{20,4},{24,16},{28,12},{1,9},{5... | collective-permute-start | bytes 1769480 | tf_op jit(solution)/shard_map/ppermute | solution.py:135
  105.7 16.3 %collective-permute-start.10 = (bf16[2,384,768]{2,1,0:T(8,128)(2,1)S(1)}, bf16[2,384,768]{2,1,0:T(8,128)(2,1)S(1)}, u32[]{:S(2)}, u32[]{:S(2)}) collective-permute-start(bf16[2,384,768]{2,1,0:T(8,128)(2,1)S(1)} %shard_map.398.refs_0_), channel_id=1, source_target_pairs={{0,16},{4,12},{8,24},{12,4},{16,0},{20,28},{24,8},{28,20},{1,17},{... | collective-permute-start | bytes 3538952 | tf_op jit(solution)/shard_map/ppermute | solution.py:141
  123.0 5.9 %collective-permute-start.14 = (bf16[2,2,384,768]{3,2,1,0:T(8,128)(2,1)S(1)}, bf16[2,2,384,768]{3,2,1,0:T(8,128)(2,1)}, u32[]{:S(2)}, u32[]{:S(2)}) collective-permute-start(bf16[2,2,384,768]{3,2,1,0:T(8,128)(2,1)S(1)} %shard_map.400.refs_0_), channel_id=1, source_target_pairs={{0,4},{4,0},{8,12},{12,8},{16,20},{20,16},{24,28},{28,24},{1,5},{5... | collective-permute-start | bytes 7077896 | tf_op jit(solution)/shard_map/ppermute | solution.py:148
  139.6 4.9 %collective-permute-start.16 = (bf16[128,128]{1,0:T(8,128)(2,1)S(1)}, bf16[128,128]{1,0:T(8,128)(2,1)S(1)}, u32[]{:S(2)}, u32[]{:S(2)}) collective-permute-start(bf16[128,128]{1,0:T(8,128)(2,1)S(1)} %slice.131), channel_id=1, source_target_pairs={{0,2},{1,3},{2,0},{3,1},{4,6},{5,7},{6,4},{7,5},{8,10},{9,11},{10,... | collective-permute-start | bytes 98312 | tf_op jit(solution)/shard_map/ppermute | solution.py:107
  140.3 5.7 %collective-permute-start.17 = (bf16[128,128]{1,0:T(8,128)(2,1)S(1)}, bf16[128,128]{1,0:T(8,128)(2,1)S(1)}, u32[]{:S(2)}, u32[]{:S(2)}) collective-permute-start(bf16[128,128]{1,0:T(8,128)(2,1)S(1)} %slice.131), channel_id=1, source_target_pairs={{0,1},{1,2},{2,3},{3,0},{4,5},{5,6},{6,7},{7,4},{8,9},{9,10},{10,1... | collective-permute-start | bytes 98312 | tf_op jit(solution)/shard_map/ppermute | solution.py:107
  140.3 5.7 %collective-permute-start.15 = (bf16[128,128]{1,0:T(8,128)(2,1)S(1)}, bf16[128,128]{1,0:T(8,128)(2,1)S(1)}, u32[]{:S(2)}, u32[]{:S(2)}) collective-permute-start(bf16[128,128]{1,0:T(8,128)(2,1)S(1)} %slice.131), channel_id=1, source_target_pairs={{0,3},{1,0},{2,1},{3,2},{4,7},{5,4},{6,5},{7,6},{8,11},{9,8},{10,9... | collective-permute-start | bytes 98312 | tf_op jit(solution)/shard_map/ppermute | solution.py:107
  188.7 13.8 %all-to-all-start = ((f32[32,1,128]{2,1,0:T(1,128)}), f32[32,1,128]{2,1,0:T(1,128)S(1)}, u32[]{:S(2)}, u32[]{:S(2)}) async-start(f32[32,1,128]{2,1,0:T(1,128)} %broadcast_in_dim.46), calls=%async_computation | async-start | bytes 32768 | tf_op jit(solution)/shard_map/all_to_all | solution.py:282
  220.5 11.0 %collective-permute-start.19 = (f32[2,512,128]{2,1,0:T(8,128)}, f32[2,512,128]{2,1,0:T(8,128)}, u32[]{:S(2)}, u32[]{:S(2)}) collective-permute-start(f32[2,512,128]{2,1,0:T(8,128)} %pad_maximum_fusion.6), channel_id=1, source_target_pairs={{0,16},{4,12},{8,24},{12,4},{16,0},{20,28},{24,8},{28,20},{1,17},{... | collective-permute-start | bytes 1572872 | tf_op jit(solution)/shard_map/ppermute | solution.py:243
  232.6 23.8 %collective-permute-start.20 = (f32[512,128]{1,0:T(8,128)S(1)}, f32[512,128]{1,0:T(8,128)S(1)}, u32[]{:S(2)}, u32[]{:S(2)}) collective-permute-start(f32[512,128]{1,0:T(8,128)S(1)} %dynamic-slice_bitcast_fusion.7), channel_id=1, source_target_pairs={{0,8},{4,20},{8,0},{12,28},{16,24},{20,4},{24,16},{28,12},{1,9},{5... | collective-permute-start | bytes 786440 | tf_op jit(solution)/shard_map/ppermute | solution.py:252
  256.5 6.9 %collective-permute-start.21 = (f32[128,128]{1,0:T(8,128)S(1)}, f32[128,128]{1,0:T(8,128)S(1)}, u32[]{:S(2)}, u32[]{:S(2)}) collective-permute-start(f32[128,128]{1,0:T(8,128)S(1)} %get-tuple-element.330), channel_id=1, source_target_pairs={{0,1},{1,2},{2,3},{3,0},{4,5},{5,6},{6,7},{7,4},{8,9},{9,10},{10,1... | collective-permute-start | bytes 196616 | tf_op jit(solution)/shard_map/ppermute | solution.py:262
  258.0 5.4 %collective-permute-start.23 = (f32[128,128]{1,0:T(8,128)S(1)}, f32[128,128]{1,0:T(8,128)S(1)}, u32[]{:S(2)}, u32[]{:S(2)}) collective-permute-start(f32[128,128]{1,0:T(8,128)S(1)} %get-tuple-element.331), channel_id=1, source_target_pairs={{0,3},{1,0},{2,1},{3,2},{4,7},{5,4},{6,5},{7,6},{8,11},{9,8},{10,9... | collective-permute-start | bytes 196616 | tf_op jit(solution)/shard_map/ppermute | solution.py:262
  260.4 6.0 %collective-permute-start.22 = (f32[128,128]{1,0:T(8,128)S(1)}, f32[128,128]{1,0:T(8,128)S(1)}, u32[]{:S(2)}, u32[]{:S(2)}) collective-permute-start(f32[128,128]{1,0:T(8,128)S(1)} %get-tuple-element.332), channel_id=1, source_target_pairs={{0,2},{1,3},{2,0},{3,1},{4,6},{5,7},{6,4},{7,5},{8,10},{9,11},{10,... | collective-permute-start | bytes 196616 | tf_op jit(solution)/shard_map/ppermute | solution.py:262
  286.3 10.2 %collective-permute-start.25 = (bf16[4,384,768]{2,1,0:T(8,128)(2,1)S(1)}, bf16[4,384,768]{2,1,0:T(8,128)(2,1)S(1)}, u32[]{:S(2)}, u32[]{:S(2)}) collective-permute-start(bf16[4,384,768]{2,1,0:T(8,128)(2,1)S(1)} %dynamic-slice_bitcast_fusion.1), channel_id=1, source_target_pairs={{0,4},{4,0},{8,12},{12,8},{16,20},{20,16},{24,28},{28,24},{1,5},{5... | collective-permute-start | bytes 7077896 | tf_op jit(solution)/shard_map/ppermute | solution.py:218
  296.5 12.9 %collective-permute-start.24 = (bf16[4,96,3072]{2,1,0:T(8,128)(2,1)S(1)}, bf16[4,96,3072]{2,1,0:T(8,128)(2,1)}, u32[]{:S(2)}, u32[]{:S(2)}) collective-permute-start(bf16[4,96,3072]{2,1,0:T(8,128)(2,1)S(1)} %dynamic-slice_bitcast_fusion), channel_id=1, source_target_pairs={{0,4},{4,0},{8,12},{12,8},{16,20},{20,16},{24,28},{28,24},{1,5},{5... | collective-permute-start | bytes 7077896 | tf_op jit(solution)/shard_map/ppermute | solution.py:218
  301.7 7.6 %collective-permute-start.26 = (bf16[4,96,768]{2,1,0:T(8,128)(2,1)}, bf16[4,96,768]{2,1,0:T(8,128)(2,1)S(1)}, u32[]{:S(2)}, u32[]{:S(2)}) collective-permute-start(bf16[4,96,768]{2,1,0:T(8,128)(2,1)} %dynamic-slice_bitcast_fusion.6), channel_id=1, source_target_pairs={{0,4},{4,0},{8,12},{12,8},{16,20},{20,16},{24,28},{28,24},{1,5},{5... | collective-permute-start | bytes 1769480 | tf_op jit(solution)/shard_map/ppermute | solution.py:218
  302.9 6.4 %collective-permute-start.27 = (f32[4,96,128]{2,1,0:T(8,128)S(1)}, f32[4,96,128]{2,1,0:T(8,128)S(1)}, u32[]{:S(2)}, u32[]{:S(2)}) collective-permute-start(f32[4,96,128]{2,1,0:T(8,128)S(1)} %dynamic-slice_bitcast_fusion.8), channel_id=1, source_target_pairs={{0,4},{4,0},{8,12},{12,8},{16,20},{20,16},{24,28},{28,24},{1,5},{5... | collective-permute-start | bytes 589832 | tf_op jit(solution)/shard_map/ppermute | solution.py:218
  303.0 16.4 %collective-permute-start.29 = (bf16[2,384,768]{2,1,0:T(8,128)(2,1)S(1)}, bf16[2,384,768]{2,1,0:T(8,128)(2,1)}, u32[]{:S(2)}, u32[]{:S(2)}) collective-permute-start(bf16[2,384,768]{2,1,0:T(8,128)(2,1)S(1)} %pad_maximum_fusion.2), channel_id=1, source_target_pairs={{0,16},{4,12},{8,24},{12,4},{16,0},{20,28},{24,8},{28,20},{1,17},{... | collective-permute-start | bytes 3538952 | tf_op jit(solution)/shard_map/ppermute | solution.py:243
  313.2 40.1 %collective-permute-start.28 = (bf16[2,96,4096]{2,1,0:T(8,128)(2,1)S(1)}, bf16[2,96,4096]{2,1,0:T(8,128)(2,1)S(1)}, u32[]{:S(2)}, u32[]{:S(2)}) collective-permute-start(bf16[2,96,4096]{2,1,0:T(8,128)(2,1)S(1)} %pad_maximum_fusion.1), channel_id=1, source_target_pairs={{0,16},{4,12},{8,24},{12,4},{16,0},{20,28},{24,8},{28,20},{1,17},{... | collective-permute-start | bytes 4718600 | tf_op jit(solution)/shard_map/ppermute | solution.py:243
  321.1 16.3 %collective-permute-start.30 = (bf16[384,768]{1,0:T(8,128)(2,1)S(1)}, bf16[384,768]{1,0:T(8,128)(2,1)S(1)}, u32[]{:S(2)}, u32[]{:S(2)}) collective-permute-start(bf16[384,768]{1,0:T(8,128)(2,1)S(1)} %fusion.20), channel_id=1, source_target_pairs={{0,8},{4,20},{8,0},{12,28},{16,24},{20,4},{24,16},{28,12},{1,9},{5... | collective-permute-start | bytes 1769480 | tf_op jit(solution)/shard_map/ppermute | solution.py:252
  337.6 15.6 %collective-permute-start.31 = (bf16[96,768]{1,0:T(8,128)(2,1)S(1)}, bf16[96,768]{1,0:T(8,128)(2,1)S(1)}, u32[]{:S(2)}, u32[]{:S(2)}) collective-permute-start(bf16[96,768]{1,0:T(8,128)(2,1)S(1)} %get-tuple-element.286), channel_id=1, source_target_pairs={{0,1},{1,2},{2,3},{3,0},{4,5},{5,6},{6,7},{7,4},{8,9},{9,10},{10,1... | collective-permute-start | bytes 442376 | tf_op jit(solution)/shard_map/ppermute | solution.py:262
  337.7 15.5 %collective-permute-start.33 = (bf16[96,768]{1,0:T(8,128)(2,1)S(1)}, bf16[96,768]{1,0:T(8,128)(2,1)S(1)}, u32[]{:S(2)}, u32[]{:S(2)}) collective-permute-start(bf16[96,768]{1,0:T(8,128)(2,1)S(1)} %get-tuple-element.287), channel_id=1, source_target_pairs={{0,3},{1,0},{2,1},{3,2},{4,7},{5,4},{6,5},{7,6},{8,11},{9,8},{10,9... | collective-permute-start | bytes 442376 | tf_op jit(solution)/shard_map/ppermute | solution.py:262
  341.5 11.7 %collective-permute-start.32 = (bf16[96,768]{1,0:T(8,128)(2,1)S(1)}, bf16[96,768]{1,0:T(8,128)(2,1)S(1)}, u32[]{:S(2)}, u32[]{:S(2)}) collective-permute-start(bf16[96,768]{1,0:T(8,128)(2,1)S(1)} %get-tuple-element.288), channel_id=1, source_target_pairs={{0,2},{1,3},{2,0},{3,1},{4,6},{5,7},{6,4},{7,5},{8,10},{9,11},{10,... | collective-permute-start | bytes 442376 | tf_op jit(solution)/shard_map/ppermute | solution.py:262
  355.2 17.4 %collective-permute-start.34 = (bf16[96,4096]{1,0:T(8,128)(2,1)}, bf16[96,4096]{1,0:T(8,128)(2,1)}, u32[]{:S(2)}, u32[]{:S(2)}) collective-permute-start(bf16[96,4096]{1,0:T(8,128)(2,1)} %pad_maximum_fusion.3), channel_id=1, source_target_pairs={{0,8},{4,20},{8,0},{12,28},{16,24},{20,4},{24,16},{28,12},{1,9},{5... | collective-permute-start | bytes 2359304 | tf_op jit(solution)/shard_map/ppermute | solution.py:252
  371.8 16.4 %collective-permute-start.38 = (bf16[4,96,128]{2,1,0:T(8,128)(2,1)S(1)}, bf16[4,96,128]{2,1,0:T(8,128)(2,1)S(1)}, u32[]{:S(2)}, u32[]{:S(2)}) collective-permute-start(bf16[4,96,128]{2,1,0:T(8,128)(2,1)S(1)} %fusion.39), channel_id=1, source_target_pairs={{0,4},{4,0},{8,12},{12,8},{16,20},{20,16},{24,28},{28,24},{1,5},{5... | collective-permute-start | bytes 294920 | tf_op jit(solution)/shard_map/ppermute | solution.py:218
  382.8 13.8 %collective-permute-start.41 = (bf16[24,4096]{1,0:T(8,128)(2,1)S(1)}, bf16[24,4096]{1,0:T(8,128)(2,1)S(1)}, u32[]{:S(2)}, u32[]{:S(2)}) collective-permute-start(bf16[24,4096]{1,0:T(8,128)(2,1)S(1)} %pad_maximum_fusion.10), channel_id=1, source_target_pairs={{0,2},{1,3},{2,0},{3,1},{4,6},{5,7},{6,4},{7,5},{8,10},{9,11},{10,... | collective-permute-start | bytes 589832 | tf_op jit(solution)/shard_map/ppermute | solution.py:262
  388.0 3.0 collective-permute-start.36
  388.2 15.5 %collective-permute-start.42 = (bf16[24,4096]{1,0:T(8,128)(2,1)S(1)}, bf16[24,4096]{1,0:T(8,128)(2,1)S(1)}, u32[]{:S(2)}, u32[]{:S(2)}) collective-permute-start(bf16[24,4096]{1,0:T(8,128)(2,1)S(1)} %pad_maximum_fusion.11), channel_id=1, source_target_pairs={{0,3},{1,0},{2,1},{3,2},{4,7},{5,4},{6,5},{7,6},{8,11},{9,8},{10,9... | collective-permute-start | bytes 589832 | tf_op jit(solution)/shard_map/ppermute | solution.py:262
  389.3 14.4 %collective-permute-start.40 = (bf16[24,4096]{1,0:T(8,128)(2,1)S(1)}, bf16[24,4096]{1,0:T(8,128)(2,1)S(1)}, u32[]{:S(2)}, u32[]{:S(2)}) collective-permute-start(bf16[24,4096]{1,0:T(8,128)(2,1)S(1)} %pad_maximum_fusion.9), channel_id=1, source_target_pairs={{0,1},{1,2},{2,3},{3,0},{4,5},{5,6},{6,7},{7,4},{8,9},{9,10},{10,1... | collective-permute-start | bytes 589832 | tf_op jit(solution)/shard_map/ppermute | solution.py:262
  391.7 13.6 %collective-permute-start.39 = (bf16[2,96,2432]{2,1,0:T(8,128)(2,1)S(1)}, bf16[2,96,2432]{2,1,0:T(8,128)(2,1)S(1)}, u32[]{:S(2)}, u32[]{:S(2)}) collective-permute-start(bf16[2,96,2432]{2,1,0:T(8,128)(2,1)S(1)} %maximum_maximum_fusion), channel_id=1, source_target_pairs={{0,16},{4,12},{8,24},{12,4},{16,0},{20,28},{24,8},{28,20},{1,17},{... | collective-permute-start | bytes 2801672 | tf_op jit(solution)/shard_map/ppermute | solution.py:243
  405.7 8.6 %collective-permute-start.43 = (bf16[96,2432]{1,0:T(8,128)(2,1)S(1)}, bf16[96,2432]{1,0:T(8,128)(2,1)S(1)}, u32[]{:S(2)}, u32[]{:S(2)}) collective-permute-start(bf16[96,2432]{1,0:T(8,128)(2,1)S(1)} %pad_maximum_fusion.8), channel_id=1, source_target_pairs={{0,8},{4,20},{8,0},{12,28},{16,24},{20,4},{24,16},{28,12},{1,9},{5... | collective-permute-start | bytes 1400840 | tf_op jit(solution)/shard_map/ppermute | solution.py:252
  414.6 8.0 %collective-permute-start.44 = (bf16[24,2432]{1,0:T(8,128)(2,1)S(1)}, bf16[24,2432]{1,0:T(8,128)(2,1)S(1)}, u32[]{:S(2)}, u32[]{:S(2)}) collective-permute-start(bf16[24,2432]{1,0:T(8,128)(2,1)S(1)} %pad_maximum_fusion.14), channel_id=1, source_target_pairs={{0,1},{1,2},{2,3},{3,0},{4,5},{5,6},{6,7},{7,4},{8,9},{9,10},{10,1... | collective-permute-start | bytes 350216 | tf_op jit(solution)/shard_map/ppermute | solution.py:262
  414.7 10.5 %collective-permute-start.45 = (bf16[24,2432]{1,0:T(8,128)(2,1)S(1)}, bf16[24,2432]{1,0:T(8,128)(2,1)S(1)}, u32[]{:S(2)}, u32[]{:S(2)}) collective-permute-start(bf16[24,2432]{1,0:T(8,128)(2,1)S(1)} %pad_maximum_fusion.15), channel_id=1, source_target_pairs={{0,2},{1,3},{2,0},{3,1},{4,6},{5,7},{6,4},{7,5},{8,10},{9,11},{10,... | collective-permute-start | bytes 350216 | tf_op jit(solution)/shard_map/ppermute | solution.py:262
  417.7 7.5 %collective-permute-start.46 = (bf16[24,2432]{1,0:T(8,128)(2,1)S(1)}, bf16[24,2432]{1,0:T(8,128)(2,1)S(1)}, u32[]{:S(2)}, u32[]{:S(2)}) collective-permute-start(bf16[24,2432]{1,0:T(8,128)(2,1)S(1)} %pad_maximum_fusion.16), channel_id=1, source_target_pairs={{0,3},{1,0},{2,1},{3,2},{4,7},{5,4},{6,5},{7,6},{8,11},{9,8},{10,9... | collective-permute-start | bytes 350216 | tf_op jit(solution)/shard_map/ppermute | solution.py:262
  427.3 10.9 %all-to-all-start.1 = ((f32[32,1,128]{2,1,0:T(1,128)}), f32[32,1,128]{2,1,0:T(1,128)S(1)}, u32[]{:S(2)}, u32[]{:S(2)}) async-start(f32[32,1,128]{2,1,0:T(1,128)} %broadcast_in_dim.48), calls=%async_computation.1 | async-start | bytes 32768 | tf_op jit(solution)/shard_map/all_to_all | solution.py:282
  (57 other events, 413.4 us)
Sparse Core Ops, SparseCore 0:
  54.9 52.2 all-gather.2
  147.7 25.0 all-gather.4

commit v6 on v5

--- a/solution.py
+++ b/solution.py
@@ -911,7 +911,9 @@
     member = (own_seg[:, None] == jnp.arange(128, dtype=jnp.int32)[None, :] % 64).astype(LOW)
     ready = tokens, passage_tables, member
     first_quad = gather_quad(first_pair, ready)
-    middle = gather_rest(line_of(middle_part, gate(middle_moved, first_quad)))
+    middle_line = line_of(middle_part, gate(middle_moved, first_quad))
+    middle = gather_rest(middle_line)
+    down_moved = send_line(gate(down_part, middle_line))
     qkv_matrix, vectors = gather_whole(first_quad, [(0, 2304), (2304, 2432)])
     vectors = vectors[:, :12].T.astype(F32)
     bias_qkv = jnp.concatenate([vectors[0], jnp.zeros_like(vectors[0]), vectors[1]])
@@ -920,7 +922,6 @@
         return (dot(rows, qkv_matrix) + bias_qkv).astype(LOW)
 
     query_mixed = mix(query_flat)
-    down_moved = send_line(gate(down_part, query_mixed))
     passage_mixed = mix(gate(passage_tokens[0], query_mixed))
     down_line = line_of(down_part, gate(down_moved, passage_mixed))
     attended, query_log = attend_forward(

time: 455 us -> 447 us (0.982)
  waiting for transfers between devices: 87.3 us -> 73.4 us
  Pallas kernels: 175 us -> 183 us
    pallas_call x7, Pallas kernels: 66.1 us -> 74.5 us  [attend_call(): pl.pallas_call(run, out_shape=[shape for shape, _ in outputs], grid_spec=...]
    ppermute x2, waiting for transfers between devices: 6.47 us -> 0.67 us  [gather_pair(): return in_order(line, gate(lax.ppermute(line, 'pb', FIRST_STEP), others), 2)]
  transfers between devices with their start and end apart: 51 -> 51, of which waited for: 25 -> 21; matrix products, arithmetic and copies ran while one was open for 11% -> 11% of each run, Pallas kernels for 31% -> 34%
where the time goes in v6:
time: 447 us; the launch traced here: 443 us
  Pallas kernels  183 us (41%)
  waiting for transfers between devices  73.4 us (16%)
  starting transfers between devices  67.6 us (15%)
  local copies, waits for them, and re-layouts  38.8 us (9%)
  matrix products  35.8 us (8%)
  other arithmetic  28 us (6%)
  between operations  15.9 us (4%)
    pallas_call x7, Pallas kernels, attend_call(): pl.pallas_call(run, out_shape=[shape for shape, _ in outputs], grid_spec=...  74.5 us
    pallas_call x6, Pallas kernels, row_call(): pl.pallas_call(run, grid=(count,), in_specs=in_specs, out_specs=[rows_at(...  71.3 us
    dot_general x9, matrix products, dot(): return lax.dot_general(left, right, dims, preferred_element_type=F32)  35.8 us
    unnamed x112, local copies, waits for them, and re-layouts  28.2 us
    ppermute x12, starting transfers between devices, send_line(): return [lax.ppermute(part, 'pa', shift_pairs(k)) for k in (1, 2, 3)]  24.9 us
    ppermute x12, waiting for transfers between devices, last_moves(): lax.ppermute(s, 'pa', shift_pairs(k + 1))  22.5 us
    pallas_call x3, Pallas kernels, score_call(): pl.pallas_call(kernel, grid=(inputs[0].shape[0] // SCORE_ROWS,), in_specs...  19.3 us
    ppermute x12, starting transfers between devices, last_moves(): lax.ppermute(s, 'pa', shift_pairs(k + 1))  17.8 us
  transfers between devices with their start and end apart: 51, of which 21 were waited for; matrix products, arithmetic and copies ran while one was open for 11% of the time, Pallas kernels for 34%

profile of v6, /device:TPU:0, one launch (start us, length us, event | category | flops | bytes accessed | tf_op | source)
XLA Modules:
  0.0 442.5 jit_solution(3904163069102245339)
XLA Ops:
  9.1 4.1 collective-permute-start.1
  17.0 5.2 %collective-permute-done.1 = bf16[24,2432]{1,0:T(8,128)(2,1)S(1)} collective-permute-done((bf16[24,2432]{1,0:T(8,128)(2,1)S(1)}, bf16[24,2432]{1,0:T(8,128)(2,1)S(1)}, u32[]{:S(2)}, u32[]{:S(2)}) %collective-permute-start.1) | collective-permute-done | bytes 116768 | tf_op jit(solution)/shard_map/ppermute | solution.py:107
  36.3 2.7 pad_maximum_fusion.refs_0_.x_ref
  39.3 7.5 %collective-permute-done.4.refs_1_ = bf16[2,96,2432]{2,1,0:T(8,128)(2,1)S(1)} collective-permute-done((bf16[2,96,2432]{2,1,0:T(8,128)(2,1)S(1)}, bf16[2,96,2432]{2,1,0:T(8,128)(2,1)S(1)}, u32[]{:S(2)}, u32[]{:S(2)}) %collective-permute-start.4) | collective-permute-done | bytes 933920 | tf_op jit(solution)/shard_map/ppermute | solution.py:141
  63.8 3.0 fusion.1.refs_1_.refs_2_.refs_3_
  67.1 7.5 %add_convert_fusion.refs_1_.refs_2_.refs_3_ = bf16[1024,2304]{1,0:T(8,128)(2,1)} fusion(bf16[1024,768]{1,0:T(8,128)(2,1)} %bitcast.345, bf16[768,2304]{1,0:T(8,128)(2,1)S(1)} %bitcast.322, f32[2304]{0:T(1024)S(1)} %pad_maximum_fusion.18), kind=kOutput, calls=%fused_computation | convolution fusion | flops 3628597248 | bytes 9839616 | tf_op jit(solution)/shard_map/dot_general | solution.py:290
  76.5 3.8 shard_map.396
  80.3 12.8 %shard_map.397 = (bf16[1152,768]{1,0:T(8,128)(2,1)S(1)}, f32[6,8,1024]{2,1,0:T(8,128)S(1)}) custom-call(s32[4,2]{1,0:T(4,128)S(1)} %pad_add_fusion.refs_0_, bf16[1024,2304]{1,0:T(8,128)(2,1)} %add_convert_fusion.refs_1_.refs_2_.refs_3_, bf16[1024,2304]{1,0:T(8,128)(2,1)} %add_convert_fusion.refs_1_.refs_2_.refs_3_, ...), custom_call_target="tpu_custom_call", output_to_operand_aliasing={{0}: (6, {})} | custom-call | flops 16106127360 | bytes 3145728 | tf_op jit(solution)/shard_map/pallas_call | solution.py:519
  94.0 12.7 %shard_map.399 = (bf16[1152,768]{1,0:T(8,128)(2,1)S(1)}, f32[6,8,1024]{2,1,0:T(8,128)S(1)}) custom-call(s32[4,2]{1,0:T(4,128)S(1)} %pad_add_fusion.refs_0_, bf16[1024,2304]{1,0:T(8,128)(2,1)} %add_convert_fusion.refs_1_.refs_2_.refs_3_, bf16[1024,2304]{1,0:T(8,128)(2,1)} %add_convert_fusion.refs_1_.refs_2_.refs_3_, ...), custom_call_target="tpu_custom_call", output_to_operand_aliasing={{0}: (6, {}), {1}: (7, {})} | custom-call | flops 16106127360 | bytes 3145728 | tf_op jit(solution)/shard_map/pallas_call | solution.py:519
  106.8 5.8 %collective-permute-done.13.refs_1_ = bf16[2,384,768]{2,1,0:T(8,128)(2,1)S(1)} collective-permute-done((bf16[2,384,768]{2,1,0:T(8,128)(2,1)S(1)}, bf16[2,384,768]{2,1,0:T(8,128)(2,1)S(1)}, u32[]{:S(2)}, u32[]{:S(2)}) %collective-permute-start.13) | collective-permute-done | bytes 1179680 | tf_op jit(solution)/shard_map/ppermute | solution.py:141
  114.9 5.8 %shard_map.401 = (f32[1152,768]{1,0:T(8,128)}, bf16[1152,768]{1,0:T(8,128)(2,1)}, bf16[1152,3072]{1,0:T(8,128)(2,1)}, bf16[1152,3072]{1,0:T(8,128)(2,1)}) custom-call(bf16[1152,768]{1,0:T(8,128)(2,1)} %pad_maximum_fusion.refs_0_.x_ref, bf16[1152,768]{1,0:T(8,128)(2,1)} %copy-done.5, ...), custom_call_target="tpu_custom_call" | custom-call | flops 754974720 | bytes 14782464 | tf_op jit(solution)/shard_map/pallas_call | solution.py:364
  120.7 2.7 shard_map.402
  125.6 4.8 %shard_map.403 = (f32[1152,768]{1,0:T(8,128)}, bf16[1152,768]{1,0:T(8,128)(2,1)}, f32[1152,128]{1,0:T(8,128)}, bf16[1152,128]{1,0:T(8,128)(2,1)}) custom-call(bf16[1152,3072]{1,0:T(8,128)(2,1)} %get-tuple-element.174.refs_0_.refs_7_, f32[1152,768]{1,0:T(8,128)} %get-tuple-element.172.refs_1_.refs_5_, bf16[3072,768]{1,0:T(8,128)(2,1)} %bitcast.315, ...), custom_call_target="tpu_custom_call" | custom-call | flops 603979776 | bytes 12718080 | tf_op jit(solution)/shard_map/pallas_call | solution.py:364
  134.0 2.8 collective-permute-start.15
  140.2 15.9 %shard_map.404 = (f32[1152,768]{1,0:T(8,128)}, bf16[1152,768]{1,0:T(8,128)(2,1)}, bf16[1152,3072]{1,0:T(8,128)(2,1)}, bf16[1152,3072]{1,0:T(8,128)(2,1)}) custom-call(bf16[1152,768]{1,0:T(8,128)(2,1)} %pad_maximum_fusion.refs_0_.x_ref, bf16[1152,768]{1,0:T(8,128)(2,1)} %copy-done.5, ...), custom_call_target="tpu_custom_call", output_to_operand_aliasing={{0}: (5, {}), {1}: (6, {}), {2}: (7, {}), {3}: (8, {})} | custom-call | flops 6039797760 | bytes 32673792 | tf_op jit(solution)/shard_map/pallas_call | solution.py:364
  156.0 12.3 %shard_map.405 = (f32[1152,768]{1,0:T(8,128)}, bf16[1152,768]{1,0:T(8,128)(2,1)}, f32[1152,128]{1,0:T(8,128)}, bf16[1152,128]{1,0:T(8,128)(2,1)}) custom-call(bf16[1152,3072]{1,0:T(8,128)(2,1)} %get-tuple-element.176.refs_0_, ...), custom_call_target="tpu_custom_call", output_to_operand_aliasing={{0}: (5, {}), {1}: (6, {}), {2}: (7, {}), {3}: (8, {})} | custom-call | flops 4831838208 | bytes 25792512 | tf_op jit(solution)/shard_map/pallas_call | solution.py:364
  170.5 5.6 %shard_map.406 = (f32[128,128]{1,0:T(8,128)S(1)}, f32[4096,128]{1,0:T(8,128)S(1)}, bf16[4096,1024]{1,0:T(8,128)(2,1)S(1)}) custom-call(bf16[4096,128]{1,0:T(8,128)(2,1)S(1)} %copy-done.26, bf16[1152,128]{1,0:T(8,128)(2,1)S(1)} %copy-done.15, bf16[1024,128]{1,0:T(8,128)(2,1)S(1)} %compare_convert_fusion.member_ref), custom_call_target="tpu_custom_call" | custom-call | flops 3221225472 | bytes 4194304 | tf_op jit(solution)/shard_map/pallas_call | solution.py:729
  176.1 3.3 copy-done.3
  181.4 6.5 %all-to-all-start = ((f32[32,1,128]{2,1,0:T(1,128)}), f32[32,1,128]{2,1,0:T(1,128)S(1)}, u32[]{:S(2)}, u32[]{:S(2)}) async-start(f32[32,1,128]{2,1,0:T(1,128)} %broadcast_in_dim.46), calls=%async_computation | async-start | bytes 32768 | tf_op jit(solution)/shard_map/all_to_all | solution.py:282
  188.0 5.0 %shard_map.407 = bf16[768,1152]{1,0:T(8,128)(2,1)} custom-call(bf16[1152,768]{1,0:T(8,128)(2,1)} %pad_maximum_fusion.refs_0_.x_ref), custom_call_target="tpu_custom_call" | custom-call | tf_op jit(solution)/shard_map/pallas_call | solution.py:324
  195.4 3.4 copy-done.4
  200.4 5.5 %shard_map.408 = f32[4096,128]{1,0:T(8,128)S(1)} custom-call(bf16[4096,1024]{1,0:T(8,128)(2,1)S(1)} %copy-done.4, bf16[1152,128]{1,0:T(8,128)(2,1)S(1)} %copy-done.16, bf16[1024,128]{1,0:T(8,128)(2,1)S(1)} %compare_convert_fusion.member_ref, f32[128,128]{1,0:T(8,128)S(1)} %copy.197.grad_ref, f32[4096,128]{1,0:T(8,128)S(1)} %copy-done.12), custom_call_target="tpu_custom_call" | custom-call | flops 3221225472 | bytes 4194304 | tf_op jit(solution)/shard_map/pallas_call | solution.py:729
  206.9 3.0 collective-permute-done.18
  214.8 8.3 %shard_map.409.refs_0_ = f32[1024,128]{1,0:T(8,128)S(1)} custom-call(bf16[4096,128]{1,0:T(8,128)(2,1)S(1)} %copy-done.27, bf16[1152,128]{1,0:T(8,128)(2,1)S(1)} %copy-done.16, bf16[1024,128]{1,0:T(8,128)(2,1)S(1)} %compare_convert_fusion.member_ref, f32[128,128]{1,0:T(8,128)S(1)} %copy.197.grad_ref, f32[4096,128]{1,0:T(8,128)S(1)} %copy-done.13), custom_call_target="tpu_custom_call" | custom-call | flops 3221225472 | bytes 4194304 | tf_op jit(solution)/shard_map/pallas_call | solution.py:729
  225.8 23.1 %shard_map.410 = (bf16[1152,128]{1,0:T(8,128)(2,1)}, bf16[1152,768]{1,0:T(8,128)(2,1)}, bf16[1152,3072]{1,0:T(8,128)(2,1)}, bf16[1152,768]{1,0:T(8,128)(2,1)}, b...) custom-call(f32[1024,128]{1,0:T(8,128)} %copy-done.28, f32[1152,128]{1,0:T(8,128)} %get-tuple-element.187.refs_1_, ...), custom_call_target="tpu_custom_call" | custom-call | flops 10871635968 | bytes 47943680 | tf_op jit(solution)/shard_map/pallas_call | solution.py:364
  253.5 2.4 collective-permute-done.21
  255.9 3.0 collective-permute-done.22
  259.6 9.5 %shard_map.411 = (bf16[1152,128]{1,0:T(8,128)(2,1)}, bf16[1152,768]{1,0:T(8,128)(2,1)}, bf16[1152,3072]{1,0:T(8,128)(2,1)}, bf16[1152,768]{1,0:T(8,128)(2,1)}, b...) custom-call(f32[128,128]{1,0:T(8,128)} %fusion.44.refs_0_, ...), custom_call_target="tpu_custom_call", output_to_operand_aliasing={{0}: (10, {}), {1}: (11, {}), {2}: (12, {}), {3}: (13, {}),... | custom-call | flops 1358954496 | bytes 26152960 | tf_op jit(solution)/shard_map/pallas_call | solution.py:364
  269.1 9.5 %convolution_convert_fusion.1 = bf16[3072,768]{1,0:T(8,128)(2,1)S(1)} fusion(bf16[1152,3072]{1,0:T(8,128)(2,1)} %get-tuple-element.176.refs_0_, bf16[1152,768]{1,0:T(8,128)(2,1)} %get-tuple-element.198), kind=kOutput, calls=%fused_computation.2 | convolution fusion | flops 5438177280 | bytes 13565952 | tf_op jit(solution)/shard_map/dot_general | solution.py:290
  280.1 6.7 %convolution_convert_fusion = bf16[768,3072]{1,0:T(8,128)(2,1)S(1)} fusion(bf16[1152,768]{1,0:T(8,128)(2,1)S(1)} %copy-done.35, bf16[1152,3072]{1,0:T(8,128)(2,1)S(1)} %copy-done.30), kind=kOutput, calls=%fused_computation.1 | convolution fusion | flops 5438177280 | bytes 13565952 | tf_op jit(solution)/shard_map/dot_general | solution.py:290
  296.4 5.3 %shard_map.412 = (bf16[3,1152,768]{2,1,0:T(8,128)(2,1)}, f32[16,768]{1,0:T(8,128)S(1)}) custom-call(s32[1,2]{1,0:T(1,128)S(1)} %broadcast_11_refs_0_.2.refs_0_, bf16[128,2304]{1,0:T(8,128)(2,1)S(1)} %copy-done.23, bf16[128,2304]{1,0:T(8,128)(2,1)S(1)} %copy-done.23, bf16[128,2304]{1,0:T(8,128)(2,1)S(1)} %copy-done.23, bf16[1152,768]{1,0:T(8,128)(2,1)S(1)} %copy-done.14, ...), custom_call_target="tpu_custom_call" | custom-call | flops 1006632960 | bytes 786432 | tf_op jit(solution)/shard_map/pallas_call | solution.py:519
  301.9 3.2 convert_add_fusion.1
  307.3 4.6 %collective-permute-done.29 = bf16[2,384,768]{2,1,0:T(8,128)(2,1)} collective-permute-done((bf16[2,384,768]{2,1,0:T(8,128)(2,1)S(1)}, bf16[2,384,768]{2,1,0:T(8,128)(2,1)}, u32[]{:S(2)}, u32[]{:S(2)}) %collective-permute-start.29) | collective-permute-done | bytes 1179680 | tf_op jit(solution)/shard_map/ppermute | solution.py:243
  314.6 13.1 %shard_map.413 = (bf16[3,1152,768]{2,1,0:T(8,128)(2,1)}, f32[16,768]{1,0:T(8,128)S(1)}) custom-call(s32[4,2]{1,0:T(4,128)S(1)} %pad_add_fusion.refs_0_, bf16[1024,2304]{1,0:T(8,128)(2,1)} %add_convert_fusion.refs_1_.refs_2_.refs_3_, bf16[1024,2304]{1,0:T(8,128)(2,1)} %add_convert_fusion.refs_1_.refs_2_.refs_3_, ...), custom_call_target="tpu_custom_call", output_to_operand_aliasing={{0}: (8, {})} | custom-call | flops 21474836480 | bytes 2097152 | tf_op jit(solution)/shard_map/pallas_call | solution.py:519
  330.2 3.8 collective-permute-start.33
  334.0 13.5 %shard_map.414 = (bf16[3,1152,768]{2,1,0:T(8,128)(2,1)}, f32[16,768]{1,0:T(8,128)S(1)}) custom-call(s32[4,2]{1,0:T(4,128)S(1)} %pad_add_fusion.refs_0_, bf16[1024,2304]{1,0:T(8,128)(2,1)} %add_convert_fusion.refs_1_.refs_2_.refs_3_, bf16[1024,2304]{1,0:T(8,128)(2,1)} %add_convert_fusion.refs_1_.refs_2_.refs_3_, ...), custom_call_target="tpu_custom_call", output_to_operand_aliasing={{0}: (8, {}), {1}: (9, {})} | custom-call | flops 21474836480 | bytes 2097152 | tf_op jit(solution)/shard_map/pallas_call | solution.py:519
  349.5 13.4 %shard_map.415 = (bf16[3,1152,768]{2,1,0:T(8,128)(2,1)}, f32[16,768]{1,0:T(8,128)S(1)}) custom-call(s32[4,2]{1,0:T(4,128)S(1)} %pad_add_fusion.refs_0_, bf16[1024,2304]{1,0:T(8,128)(2,1)} %add_convert_fusion.refs_1_.refs_2_.refs_3_, bf16[1024,2304]{1,0:T(8,128)(2,1)} %add_convert_fusion.refs_1_.refs_2_.refs_3_, ...), custom_call_target="tpu_custom_call", output_to_operand_aliasing={{0}: (8, {}), {1}: (9, {})} | custom-call | flops 21474836480 | bytes 2097152 | tf_op jit(solution)/shard_map/pallas_call | solution.py:519
  368.4 3.3 fusion.17
  375.3 4.2 collective-permute-start.41
  385.1 2.9 collective-permute-done.41
  388.0 7.6 %collective-permute-done.42 = bf16[24,4096]{1,0:T(8,128)(2,1)S(1)} collective-permute-done((bf16[24,4096]{1,0:T(8,128)(2,1)S(1)}, bf16[24,4096]{1,0:T(8,128)(2,1)S(1)}, u32[]{:S(2)}, u32[]{:S(2)}) %collective-permute-start.42) | collective-permute-done | bytes 196640 | tf_op jit(solution)/shard_map/ppermute | solution.py:262
  399.2 7.3 %collective-permute-done.43 = bf16[96,2432]{1,0:T(8,128)(2,1)S(1)} collective-permute-done((bf16[96,2432]{1,0:T(8,128)(2,1)S(1)}, bf16[96,2432]{1,0:T(8,128)(2,1)S(1)}, u32[]{:S(2)}, u32[]{:S(2)}) %collective-permute-start.43) | collective-permute-done | bytes 466976 | tf_op jit(solution)/shard_map/ppermute | solution.py:252
  406.9 2.9 collective-permute-start.45
  410.9 3.9 collective-permute-done.44.refs_4_
  414.8 2.6 collective-permute-done.45.refs_5_
  419.5 4.0 all-to-all-start.1
  424.3 6.4 %all-to-all-done.1 = f32[32,1,128]{2,1,0:T(1,128)S(1)} async-done(((f32[32,1,128]{2,1,0:T(1,128)}), f32[32,1,128]{2,1,0:T(1,128)S(1)}, u32[]{:S(2)}, u32[]{:S(2)}) %all-to-all-start.1) | async-done | bytes 16416 | tf_op jit(solution)/shard_map/all_to_all | solution.py:282
  431.3 4.2 shard_map.417
  (348 shorter events, 116.4 us)
Async XLA Ops:
  7.2 107.6 %all-gather.3.cloned.1.call-start = ((), (), s32[]{:S(2)}) async-start(), calls=%async_computation.2 | async-start | bytes 6856704 | tf_op jit(solution)/shard_map/all_gather | solution.py:120
  9.1 13.2 %collective-permute-start.1 = (bf16[24,2432]{1,0:T(8,128)(2,1)S(1)}, bf16[24,2432]{1,0:T(8,128)(2,1)S(1)}, u32[]{:S(2)}, u32[]{:S(2)}) collective-permute-start(bf16[24,2432]{1,0:T(8,128)(2,1)S(1)} %fusion.37), channel_id=1, source_target_pairs={{0,2},{1,3},{2,0},{3,1},{4,6},{5,7},{6,4},{7,5},{8,10},{9,11},{10,... | collective-permute-start | bytes 350216 | tf_op jit(solution)/shard_map/ppermute | solution.py:107
  13.2 9.1 %collective-permute-start.2 = (bf16[24,2432]{1,0:T(8,128)(2,1)S(1)}, bf16[24,2432]{1,0:T(8,128)(2,1)S(1)}, u32[]{:S(2)}, u32[]{:S(2)}) collective-permute-start(bf16[24,2432]{1,0:T(8,128)(2,1)S(1)} %fusion.37), channel_id=1, source_target_pairs={{0,1},{1,2},{2,3},{3,0},{4,5},{5,6},{6,7},{7,4},{8,9},{9,10},{10,1... | collective-permute-start | bytes 350216 | tf_op jit(solution)/shard_map/ppermute | solution.py:107
  14.8 8.2 %collective-permute-start = (bf16[24,2432]{1,0:T(8,128)(2,1)S(1)}, bf16[24,2432]{1,0:T(8,128)(2,1)S(1)}, u32[]{:S(2)}, u32[]{:S(2)}) collective-permute-start(bf16[24,2432]{1,0:T(8,128)(2,1)S(1)} %fusion.37), channel_id=1, source_target_pairs={{0,3},{1,0},{2,1},{3,2},{4,7},{5,4},{6,5},{7,6},{8,11},{9,8},{10,9... | collective-permute-start | bytes 350216 | tf_op jit(solution)/shard_map/ppermute | solution.py:107
  23.3 8.6 %collective-permute-start.3 = (bf16[96,2432]{1,0:T(8,128)(2,1)S(1)}, bf16[96,2432]{1,0:T(8,128)(2,1)S(1)}, u32[]{:S(2)}, u32[]{:S(2)}) collective-permute-start(bf16[96,2432]{1,0:T(8,128)(2,1)S(1)} %bitcast.325), channel_id=1, source_target_pairs={{0,8},{4,20},{8,0},{12,28},{16,24},{20,4},{24,16},{28,12},{1,9},{5... | collective-permute-start | bytes 1400840 | tf_op jit(solution)/shard_map/ppermute | solution.py:135
  25.8 25.3 %collective-permute-start.8 = (bf16[24,3968]{1,0:T(8,128)(2,1)}, bf16[24,3968]{1,0:T(8,128)(2,1)}, u32[]{:S(2)}, u32[]{:S(2)}) collective-permute-start(bf16[24,3968]{1,0:T(8,128)(2,1)} %pad_maximum_fusion.12), channel_id=1, source_target_pairs={{0,3},{1,0},{2,1},{3,2},{4,7},{5,4},{6,5},{7,6},{8,11},{9,8},{10,9... | collective-permute-start | bytes 571400 | tf_op jit(solution)/shard_map/ppermute | solution.py:107
  27.8 23.4 %collective-permute-start.7 = (bf16[24,3968]{1,0:T(8,128)(2,1)}, bf16[24,3968]{1,0:T(8,128)(2,1)}, u32[]{:S(2)}, u32[]{:S(2)}) collective-permute-start(bf16[24,3968]{1,0:T(8,128)(2,1)} %pad_maximum_fusion.12), channel_id=1, source_target_pairs={{0,2},{1,3},{2,0},{3,1},{4,6},{5,7},{6,4},{7,5},{8,10},{9,11},{10,... | collective-permute-start | bytes 571400 | tf_op jit(solution)/shard_map/ppermute | solution.py:107
  29.3 21.9 %collective-permute-start.6 = (bf16[24,3968]{1,0:T(8,128)(2,1)}, bf16[24,3968]{1,0:T(8,128)(2,1)}, u32[]{:S(2)}, u32[]{:S(2)}) collective-permute-start(bf16[24,3968]{1,0:T(8,128)(2,1)} %pad_maximum_fusion.12), channel_id=1, source_target_pairs={{0,1},{1,2},{2,3},{3,0},{4,5},{5,6},{6,7},{7,4},{8,9},{9,10},{10,1... | collective-permute-start | bytes 571400 | tf_op jit(solution)/shard_map/ppermute | solution.py:107
  33.1 13.6 %collective-permute-start.4 = (bf16[2,96,2432]{2,1,0:T(8,128)(2,1)S(1)}, bf16[2,96,2432]{2,1,0:T(8,128)(2,1)S(1)}, u32[]{:S(2)}, u32[]{:S(2)}) collective-permute-start(bf16[2,96,2432]{2,1,0:T(8,128)(2,1)S(1)} %shard_map.393.refs_0_), channel_id=1, source_target_pairs={{0,16},{4,12},{8,24},{12,4},{16,0},{20,28},{24,8},{28,20},{1,17},{... | collective-permute-start | bytes 2801672 | tf_op jit(solution)/shard_map/ppermute | solution.py:141
  54.8 113.5 %all-gather.5.cloned.1.call-start = ((), (), s32[]{:S(2)}) async-start(), calls=%async_computation.3 | async-start | bytes 1179648 | tf_op jit(solution)/shard_map/all_gather | solution.py:120
  54.8 5.9 %collective-permute-start.5 = (bf16[2,2,96,2432]{3,2,1,0:T(8,128)(2,1)S(1)}, bf16[2,2,96,2432]{3,2,1,0:T(8,128)(2,1)S(1)}, u32[]{:S(2)}, u32[]{:S(2)}) collective-permute-start(bf16[2,2,96,2432]{3,2,1,0:T(8,128)(2,1)S(1)} %shard_map.394.refs_0_), channel_id=1, source_target_pairs={{0,4},{4,0},{8,12},{12,8},{16,20},{20,16},{24,28},{28,24},{1,5},{5... | collective-permute-start | bytes 5603336 | tf_op jit(solution)/shard_map/ppermute | solution.py:148
  54.9 19.6 %collective-permute-start.11 = (bf16[96,768]{1,0:T(8,128)(2,1)S(1)}, bf16[96,768]{1,0:T(8,128)(2,1)S(1)}, u32[]{:S(2)}, u32[]{:S(2)}) collective-permute-start(bf16[96,768]{1,0:T(8,128)(2,1)S(1)} %convert_element_type.442), channel_id=1, source_target_pairs={{0,3},{1,0},{2,1},{3,2},{4,7},{5,4},{6,5},{7,6},{8,11},{9,8},{10,9... | collective-permute-start | bytes 442376 | tf_op jit(solution)/shard_map/ppermute | solution.py:107
  57.0 17.6 %collective-permute-start.10 = (bf16[96,768]{1,0:T(8,128)(2,1)S(1)}, bf16[96,768]{1,0:T(8,128)(2,1)S(1)}, u32[]{:S(2)}, u32[]{:S(2)}) collective-permute-start(bf16[96,768]{1,0:T(8,128)(2,1)S(1)} %convert_element_type.442), channel_id=1, source_target_pairs={{0,2},{1,3},{2,0},{3,1},{4,6},{5,7},{6,4},{7,5},{8,10},{9,11},{10,... | collective-permute-start | bytes 442376 | tf_op jit(solution)/shard_map/ppermute | solution.py:107
  58.6 16.0 %collective-permute-start.9 = (bf16[96,768]{1,0:T(8,128)(2,1)S(1)}, bf16[96,768]{1,0:T(8,128)(2,1)S(1)}, u32[]{:S(2)}, u32[]{:S(2)}) collective-permute-start(bf16[96,768]{1,0:T(8,128)(2,1)S(1)} %convert_element_type.442), channel_id=1, source_target_pairs={{0,1},{1,2},{2,3},{3,0},{4,5},{5,6},{6,7},{7,4},{8,9},{9,10},{10,1... | collective-permute-start | bytes 442376 | tf_op jit(solution)/shard_map/ppermute | solution.py:107
  74.8 18.3 %collective-permute-start.12 = (bf16[384,768]{1,0:T(8,128)(2,1)S(1)}, bf16[384,768]{1,0:T(8,128)(2,1)S(1)}, u32[]{:S(2)}, u32[]{:S(2)}) collective-permute-start(bf16[384,768]{1,0:T(8,128)(2,1)S(1)} %bitcast.323), channel_id=1, source_target_pairs={{0,8},{4,20},{8,0},{12,28},{16,24},{20,4},{24,16},{28,12},{1,9},{5... | collective-permute-start | bytes 1769480 | tf_op jit(solution)/shard_map/ppermute | solution.py:135
  93.9 18.6 %collective-permute-start.13 = (bf16[2,384,768]{2,1,0:T(8,128)(2,1)S(1)}, bf16[2,384,768]{2,1,0:T(8,128)(2,1)S(1)}, u32[]{:S(2)}, u32[]{:S(2)}) collective-permute-start(bf16[2,384,768]{2,1,0:T(8,128)(2,1)S(1)} %shard_map.398.refs_0_), channel_id=1, source_target_pairs={{0,16},{4,12},{8,24},{12,4},{16,0},{20,28},{24,8},{28,20},{1,17},{... | collective-permute-start | bytes 3538952 | tf_op jit(solution)/shard_map/ppermute | solution.py:141
  113.8 6.8 %collective-permute-start.14 = (bf16[2,2,384,768]{3,2,1,0:T(8,128)(2,1)S(1)}, bf16[2,2,384,768]{3,2,1,0:T(8,128)(2,1)}, u32[]{:S(2)}, u32[]{:S(2)}) collective-permute-start(bf16[2,2,384,768]{3,2,1,0:T(8,128)(2,1)S(1)} %shard_map.400.refs_0_), channel_id=1, source_target_pairs={{0,4},{4,0},{8,12},{12,8},{16,20},{20,16},{24,28},{28,24},{1,5},{5... | collective-permute-start | bytes 7077896 | tf_op jit(solution)/shard_map/ppermute | solution.py:148
  131.1 5.7 %collective-permute-start.16 = (bf16[128,128]{1,0:T(8,128)(2,1)S(1)}, bf16[128,128]{1,0:T(8,128)(2,1)S(1)}, u32[]{:S(2)}, u32[]{:S(2)}) collective-permute-start(bf16[128,128]{1,0:T(8,128)(2,1)S(1)} %slice.131), channel_id=1, source_target_pairs={{0,2},{1,3},{2,0},{3,1},{4,6},{5,7},{6,4},{7,5},{8,10},{9,11},{10,... | collective-permute-start | bytes 98312 | tf_op jit(solution)/shard_map/ppermute | solution.py:107
  133.0 5.7 %collective-permute-start.17 = (bf16[128,128]{1,0:T(8,128)(2,1)S(1)}, bf16[128,128]{1,0:T(8,128)(2,1)S(1)}, u32[]{:S(2)}, u32[]{:S(2)}) collective-permute-start(bf16[128,128]{1,0:T(8,128)(2,1)S(1)} %slice.131), channel_id=1, source_target_pairs={{0,1},{1,2},{2,3},{3,0},{4,5},{5,6},{6,7},{7,4},{8,9},{9,10},{10,1... | collective-permute-start | bytes 98312 | tf_op jit(solution)/shard_map/ppermute | solution.py:107
  134.0 4.7 %collective-permute-start.15 = (bf16[128,128]{1,0:T(8,128)(2,1)S(1)}, bf16[128,128]{1,0:T(8,128)(2,1)S(1)}, u32[]{:S(2)}, u32[]{:S(2)}) collective-permute-start(bf16[128,128]{1,0:T(8,128)(2,1)S(1)} %slice.131), channel_id=1, source_target_pairs={{0,3},{1,0},{2,1},{3,2},{4,7},{5,4},{6,5},{7,6},{8,11},{9,8},{10,9... | collective-permute-start | bytes 98312 | tf_op jit(solution)/shard_map/ppermute | solution.py:107
  181.4 13.7 %all-to-all-start = ((f32[32,1,128]{2,1,0:T(1,128)}), f32[32,1,128]{2,1,0:T(1,128)S(1)}, u32[]{:S(2)}, u32[]{:S(2)}) async-start(f32[32,1,128]{2,1,0:T(1,128)} %broadcast_in_dim.46), calls=%async_computation | async-start | bytes 32768 | tf_op jit(solution)/shard_map/all_to_all | solution.py:282
  213.0 11.0 %collective-permute-start.19 = (f32[2,512,128]{2,1,0:T(8,128)}, f32[2,512,128]{2,1,0:T(8,128)}, u32[]{:S(2)}, u32[]{:S(2)}) collective-permute-start(f32[2,512,128]{2,1,0:T(8,128)} %pad_maximum_fusion.6), channel_id=1, source_target_pairs={{0,16},{4,12},{8,24},{12,4},{16,0},{20,28},{24,8},{28,20},{1,17},{... | collective-permute-start | bytes 1572872 | tf_op jit(solution)/shard_map/ppermute | solution.py:243
  225.1 23.8 %collective-permute-start.20 = (f32[512,128]{1,0:T(8,128)S(1)}, f32[512,128]{1,0:T(8,128)S(1)}, u32[]{:S(2)}, u32[]{:S(2)}) collective-permute-start(f32[512,128]{1,0:T(8,128)S(1)} %dynamic-slice_bitcast_fusion.7), channel_id=1, source_target_pairs={{0,8},{4,20},{8,0},{12,28},{16,24},{20,4},{24,16},{28,12},{1,9},{5... | collective-permute-start | bytes 786440 | tf_op jit(solution)/shard_map/ppermute | solution.py:252
  249.0 6.9 %collective-permute-start.21 = (f32[128,128]{1,0:T(8,128)S(1)}, f32[128,128]{1,0:T(8,128)S(1)}, u32[]{:S(2)}, u32[]{:S(2)}) collective-permute-start(f32[128,128]{1,0:T(8,128)S(1)} %get-tuple-element.330), channel_id=1, source_target_pairs={{0,1},{1,2},{2,3},{3,0},{4,5},{5,6},{6,7},{7,4},{8,9},{9,10},{10,1... | collective-permute-start | bytes 196616 | tf_op jit(solution)/shard_map/ppermute | solution.py:262
  250.6 5.4 %collective-permute-start.23 = (f32[128,128]{1,0:T(8,128)S(1)}, f32[128,128]{1,0:T(8,128)S(1)}, u32[]{:S(2)}, u32[]{:S(2)}) collective-permute-start(f32[128,128]{1,0:T(8,128)S(1)} %get-tuple-element.331), channel_id=1, source_target_pairs={{0,3},{1,0},{2,1},{3,2},{4,7},{5,4},{6,5},{7,6},{8,11},{9,8},{10,9... | collective-permute-start | bytes 196616 | tf_op jit(solution)/shard_map/ppermute | solution.py:262
  252.9 6.0 %collective-permute-start.22 = (f32[128,128]{1,0:T(8,128)S(1)}, f32[128,128]{1,0:T(8,128)S(1)}, u32[]{:S(2)}, u32[]{:S(2)}) collective-permute-start(f32[128,128]{1,0:T(8,128)S(1)} %get-tuple-element.332), channel_id=1, source_target_pairs={{0,2},{1,3},{2,0},{3,1},{4,6},{5,7},{6,4},{7,5},{8,10},{9,11},{10,... | collective-permute-start | bytes 196616 | tf_op jit(solution)/shard_map/ppermute | solution.py:262
  278.8 10.2 %collective-permute-start.25 = (bf16[4,384,768]{2,1,0:T(8,128)(2,1)S(1)}, bf16[4,384,768]{2,1,0:T(8,128)(2,1)S(1)}, u32[]{:S(2)}, u32[]{:S(2)}) collective-permute-start(bf16[4,384,768]{2,1,0:T(8,128)(2,1)S(1)} %dynamic-slice_bitcast_fusion.1), channel_id=1, source_target_pairs={{0,4},{4,0},{8,12},{12,8},{16,20},{20,16},{24,28},{28,24},{1,5},{5... | collective-permute-start | bytes 7077896 | tf_op jit(solution)/shard_map/ppermute | solution.py:218
  289.0 12.9 %collective-permute-start.24 = (bf16[4,96,3072]{2,1,0:T(8,128)(2,1)S(1)}, bf16[4,96,3072]{2,1,0:T(8,128)(2,1)}, u32[]{:S(2)}, u32[]{:S(2)}) collective-permute-start(bf16[4,96,3072]{2,1,0:T(8,128)(2,1)S(1)} %dynamic-slice_bitcast_fusion), channel_id=1, source_target_pairs={{0,4},{4,0},{8,12},{12,8},{16,20},{20,16},{24,28},{28,24},{1,5},{5... | collective-permute-start | bytes 7077896 | tf_op jit(solution)/shard_map/ppermute | solution.py:218
  294.2 7.6 %collective-permute-start.26 = (bf16[4,96,768]{2,1,0:T(8,128)(2,1)}, bf16[4,96,768]{2,1,0:T(8,128)(2,1)S(1)}, u32[]{:S(2)}, u32[]{:S(2)}) collective-permute-start(bf16[4,96,768]{2,1,0:T(8,128)(2,1)} %dynamic-slice_bitcast_fusion.6), channel_id=1, source_target_pairs={{0,4},{4,0},{8,12},{12,8},{16,20},{20,16},{24,28},{28,24},{1,5},{5... | collective-permute-start | bytes 1769480 | tf_op jit(solution)/shard_map/ppermute | solution.py:218
  295.4 6.4 %collective-permute-start.27 = (f32[4,96,128]{2,1,0:T(8,128)S(1)}, f32[4,96,128]{2,1,0:T(8,128)S(1)}, u32[]{:S(2)}, u32[]{:S(2)}) collective-permute-start(f32[4,96,128]{2,1,0:T(8,128)S(1)} %dynamic-slice_bitcast_fusion.8), channel_id=1, source_target_pairs={{0,4},{4,0},{8,12},{12,8},{16,20},{20,16},{24,28},{28,24},{1,5},{5... | collective-permute-start | bytes 589832 | tf_op jit(solution)/shard_map/ppermute | solution.py:218
  295.5 16.4 %collective-permute-start.29 = (bf16[2,384,768]{2,1,0:T(8,128)(2,1)S(1)}, bf16[2,384,768]{2,1,0:T(8,128)(2,1)}, u32[]{:S(2)}, u32[]{:S(2)}) collective-permute-start(bf16[2,384,768]{2,1,0:T(8,128)(2,1)S(1)} %pad_maximum_fusion.2), channel_id=1, source_target_pairs={{0,16},{4,12},{8,24},{12,4},{16,0},{20,28},{24,8},{28,20},{1,17},{... | collective-permute-start | bytes 3538952 | tf_op jit(solution)/shard_map/ppermute | solution.py:243
  305.7 42.0 %collective-permute-start.28 = (bf16[2,96,4096]{2,1,0:T(8,128)(2,1)S(1)}, bf16[2,96,4096]{2,1,0:T(8,128)(2,1)S(1)}, u32[]{:S(2)}, u32[]{:S(2)}) collective-permute-start(bf16[2,96,4096]{2,1,0:T(8,128)(2,1)S(1)} %pad_maximum_fusion.1), channel_id=1, source_target_pairs={{0,16},{4,12},{8,24},{12,4},{16,0},{20,28},{24,8},{28,20},{1,17},{... | collective-permute-start | bytes 4718600 | tf_op jit(solution)/shard_map/ppermute | solution.py:243
  313.7 16.3 %collective-permute-start.30 = (bf16[384,768]{1,0:T(8,128)(2,1)S(1)}, bf16[384,768]{1,0:T(8,128)(2,1)S(1)}, u32[]{:S(2)}, u32[]{:S(2)}) collective-permute-start(bf16[384,768]{1,0:T(8,128)(2,1)S(1)} %fusion.20), channel_id=1, source_target_pairs={{0,8},{4,20},{8,0},{12,28},{16,24},{20,4},{24,16},{28,12},{1,9},{5... | collective-permute-start | bytes 1769480 | tf_op jit(solution)/shard_map/ppermute | solution.py:252
  330.2 17.4 %collective-permute-start.31 = (bf16[96,768]{1,0:T(8,128)(2,1)S(1)}, bf16[96,768]{1,0:T(8,128)(2,1)S(1)}, u32[]{:S(2)}, u32[]{:S(2)}) collective-permute-start(bf16[96,768]{1,0:T(8,128)(2,1)S(1)} %get-tuple-element.286), channel_id=1, source_target_pairs={{0,1},{1,2},{2,3},{3,0},{4,5},{5,6},{6,7},{7,4},{8,9},{9,10},{10,1... | collective-permute-start | bytes 442376 | tf_op jit(solution)/shard_map/ppermute | solution.py:262
  330.2 17.3 %collective-permute-start.33 = (bf16[96,768]{1,0:T(8,128)(2,1)S(1)}, bf16[96,768]{1,0:T(8,128)(2,1)S(1)}, u32[]{:S(2)}, u32[]{:S(2)}) collective-permute-start(bf16[96,768]{1,0:T(8,128)(2,1)S(1)} %get-tuple-element.287), channel_id=1, source_target_pairs={{0,3},{1,0},{2,1},{3,2},{4,7},{5,4},{6,5},{7,6},{8,11},{9,8},{10,9... | collective-permute-start | bytes 442376 | tf_op jit(solution)/shard_map/ppermute | solution.py:262
  334.0 13.5 %collective-permute-start.32 = (bf16[96,768]{1,0:T(8,128)(2,1)S(1)}, bf16[96,768]{1,0:T(8,128)(2,1)S(1)}, u32[]{:S(2)}, u32[]{:S(2)}) collective-permute-start(bf16[96,768]{1,0:T(8,128)(2,1)S(1)} %get-tuple-element.288), channel_id=1, source_target_pairs={{0,2},{1,3},{2,0},{3,1},{4,6},{5,7},{6,4},{7,5},{8,10},{9,11},{10,... | collective-permute-start | bytes 442376 | tf_op jit(solution)/shard_map/ppermute | solution.py:262
  349.5 15.5 %collective-permute-start.34 = (bf16[96,4096]{1,0:T(8,128)(2,1)}, bf16[96,4096]{1,0:T(8,128)(2,1)}, u32[]{:S(2)}, u32[]{:S(2)}) collective-permute-start(bf16[96,4096]{1,0:T(8,128)(2,1)} %pad_maximum_fusion.3), channel_id=1, source_target_pairs={{0,8},{4,20},{8,0},{12,28},{16,24},{20,4},{24,16},{28,12},{1,9},{5... | collective-permute-start | bytes 2359304 | tf_op jit(solution)/shard_map/ppermute | solution.py:252
  364.9 15.5 %collective-permute-start.38 = (bf16[4,96,128]{2,1,0:T(8,128)(2,1)S(1)}, bf16[4,96,128]{2,1,0:T(8,128)(2,1)S(1)}, u32[]{:S(2)}, u32[]{:S(2)}) collective-permute-start(bf16[4,96,128]{2,1,0:T(8,128)(2,1)S(1)} %fusion.39), channel_id=1, source_target_pairs={{0,4},{4,0},{8,12},{12,8},{16,20},{20,16},{24,28},{28,24},{1,5},{5... | collective-permute-start | bytes 294920 | tf_op jit(solution)/shard_map/ppermute | solution.py:218
  375.3 12.8 %collective-permute-start.41 = (bf16[24,4096]{1,0:T(8,128)(2,1)S(1)}, bf16[24,4096]{1,0:T(8,128)(2,1)S(1)}, u32[]{:S(2)}, u32[]{:S(2)}) collective-permute-start(bf16[24,4096]{1,0:T(8,128)(2,1)S(1)} %pad_maximum_fusion.10), channel_id=1, source_target_pairs={{0,2},{1,3},{2,0},{3,1},{4,6},{5,7},{6,4},{7,5},{8,10},{9,11},{10,... | collective-permute-start | bytes 589832 | tf_op jit(solution)/shard_map/ppermute | solution.py:262
  380.2 3.0 collective-permute-start.36
  380.4 15.2 %collective-permute-start.42 = (bf16[24,4096]{1,0:T(8,128)(2,1)S(1)}, bf16[24,4096]{1,0:T(8,128)(2,1)S(1)}, u32[]{:S(2)}, u32[]{:S(2)}) collective-permute-start(bf16[24,4096]{1,0:T(8,128)(2,1)S(1)} %pad_maximum_fusion.11), channel_id=1, source_target_pairs={{0,3},{1,0},{2,1},{3,2},{4,7},{5,4},{6,5},{7,6},{8,11},{9,8},{10,9... | collective-permute-start | bytes 589832 | tf_op jit(solution)/shard_map/ppermute | solution.py:262
  381.6 14.0 %collective-permute-start.40 = (bf16[24,4096]{1,0:T(8,128)(2,1)S(1)}, bf16[24,4096]{1,0:T(8,128)(2,1)S(1)}, u32[]{:S(2)}, u32[]{:S(2)}) collective-permute-start(bf16[24,4096]{1,0:T(8,128)(2,1)S(1)} %pad_maximum_fusion.9), channel_id=1, source_target_pairs={{0,1},{1,2},{2,3},{3,0},{4,5},{5,6},{6,7},{7,4},{8,9},{9,10},{10,1... | collective-permute-start | bytes 589832 | tf_op jit(solution)/shard_map/ppermute | solution.py:262
  383.9 13.6 %collective-permute-start.39 = (bf16[2,96,2432]{2,1,0:T(8,128)(2,1)S(1)}, bf16[2,96,2432]{2,1,0:T(8,128)(2,1)S(1)}, u32[]{:S(2)}, u32[]{:S(2)}) collective-permute-start(bf16[2,96,2432]{2,1,0:T(8,128)(2,1)S(1)} %maximum_maximum_fusion), channel_id=1, source_target_pairs={{0,16},{4,12},{8,24},{12,4},{16,0},{20,28},{24,8},{28,20},{1,17},{... | collective-permute-start | bytes 2801672 | tf_op jit(solution)/shard_map/ppermute | solution.py:243
  398.0 8.6 %collective-permute-start.43 = (bf16[96,2432]{1,0:T(8,128)(2,1)S(1)}, bf16[96,2432]{1,0:T(8,128)(2,1)S(1)}, u32[]{:S(2)}, u32[]{:S(2)}) collective-permute-start(bf16[96,2432]{1,0:T(8,128)(2,1)S(1)} %pad_maximum_fusion.8), channel_id=1, source_target_pairs={{0,8},{4,20},{8,0},{12,28},{16,24},{20,4},{24,16},{28,12},{1,9},{5... | collective-permute-start | bytes 1400840 | tf_op jit(solution)/shard_map/ppermute | solution.py:252
  406.8 7.9 %collective-permute-start.44 = (bf16[24,2432]{1,0:T(8,128)(2,1)S(1)}, bf16[24,2432]{1,0:T(8,128)(2,1)S(1)}, u32[]{:S(2)}, u32[]{:S(2)}) collective-permute-start(bf16[24,2432]{1,0:T(8,128)(2,1)S(1)} %pad_maximum_fusion.14), channel_id=1, source_target_pairs={{0,1},{1,2},{2,3},{3,0},{4,5},{5,6},{6,7},{7,4},{8,9},{9,10},{10,1... | collective-permute-start | bytes 350216 | tf_op jit(solution)/shard_map/ppermute | solution.py:262
  406.9 10.5 %collective-permute-start.45 = (bf16[24,2432]{1,0:T(8,128)(2,1)S(1)}, bf16[24,2432]{1,0:T(8,128)(2,1)S(1)}, u32[]{:S(2)}, u32[]{:S(2)}) collective-permute-start(bf16[24,2432]{1,0:T(8,128)(2,1)S(1)} %pad_maximum_fusion.15), channel_id=1, source_target_pairs={{0,2},{1,3},{2,0},{3,1},{4,6},{5,7},{6,4},{7,5},{8,10},{9,11},{10,... | collective-permute-start | bytes 350216 | tf_op jit(solution)/shard_map/ppermute | solution.py:262
  409.9 7.5 %collective-permute-start.46 = (bf16[24,2432]{1,0:T(8,128)(2,1)S(1)}, bf16[24,2432]{1,0:T(8,128)(2,1)S(1)}, u32[]{:S(2)}, u32[]{:S(2)}) collective-permute-start(bf16[24,2432]{1,0:T(8,128)(2,1)S(1)} %pad_maximum_fusion.16), channel_id=1, source_target_pairs={{0,3},{1,0},{2,1},{3,2},{4,7},{5,4},{6,5},{7,6},{8,11},{9,8},{10,9... | collective-permute-start | bytes 350216 | tf_op jit(solution)/shard_map/ppermute | solution.py:262
  419.5 11.1 %all-to-all-start.1 = ((f32[32,1,128]{2,1,0:T(1,128)}), f32[32,1,128]{2,1,0:T(1,128)S(1)}, u32[]{:S(2)}, u32[]{:S(2)}) async-start(f32[32,1,128]{2,1,0:T(1,128)} %broadcast_in_dim.48), calls=%async_computation.1 | async-start | bytes 32768 | tf_op jit(solution)/shard_map/all_to_all | solution.py:282
  (57 other events, 395.9 us)
Sparse Core Ops, SparseCore 0:
  54.9 50.1 all-gather.2
  140.3 24.9 all-gather.4
